TPU v7x, 32 devices: a whole 2x2x4 slice. The times are simulated.
32 devices in a mesh: section: 8 (over y, x, core), seq: 4 (over z).
Axes of the slice: x: 2, y: 2, z: 4, core: 2. Of those that a mesh axis runs over, the one named last changes fastest.
Arguments:
- embedded: bfloat16 [512, 3072], P('seq'), may hold values from -6 to 6
- carried: bfloat16 [8, 512, 3072], P('section', 'seq'), may hold values from -6 to 6
- stash: bfloat16 [8, 512, 3072], P('section', 'seq'), may hold values from -6 to 6
- returned: bfloat16 [8, 512, 3072], P('section', 'seq'), may hold values from -1.75 to 1.75
- loss_grad: bfloat16 [512, 3072], P('seq'), may hold values from -1.75 to 1.75
- qkv_weight: bfloat16 [8, 3, 24, 128, 128], P('section', None, None, 'seq'), may hold values from -0.6 to 0.6
- rel_bias: float32 [8, 32, 24], P('section'), may hold values from -6 to 6
- norm_gain: float32 [8, 3072], P('section'), may hold values from 0.5 to 1.5
- final_gain: float32 [3072], replicated, may hold values from 0.5 to 1.5
Outputs:
- section_out: bfloat16 [8, 512, 3072], P('section', 'seq')
- input_grad: bfloat16 [8, 512, 3072], P('section', 'seq')
- weight_grad: float32 [8, 3, 24, 128, 128], P('section', None, None, 'seq')
- bias_grad: float32 [8, 32, 24], P('section', 'seq')
- gain_grad: float32 [8, 3072], P('section', 'seq')
- memory: bfloat16 [512, 3072], P('section', 'seq')
All inputs are finite; a program needn't handle non-finite values.
Results may differ from a plain program's by a relative error of at most 0.012.
The roundings to bfloat16 on the way count: a program that leaves them out, or rounds other values in their place, can miss the bound.
Values may be sent and summed in bfloat16 or wider, within the bound.
No kernel may reach another device: no remote copies, remote signals or barrier semaphores. Data moves between devices by JAX's collectives and lax.ppermute only.
A program may use at most 128 MiB of HBM per device.

v0:
```python
import jax
import jax.numpy as jnp
from jax import lax
from jax.sharding import PartitionSpec as P

RADIUS = 96


eps_norm = 1e-06
bucket_edges = (1, 2, 3, 4, 5, 6, 7, 8, 11, 16, 22, 32, 45, 64, 90)
masked_score = -1e30
block_limit = 512


def shifted(value, axis, steps):
    count = lax.axis_size(axis)
    first, last = (max(0, -steps), min(count, count - steps))
    return lax.ppermute(value, axis, [(source, source + steps) for source in range(first, last)])


def extended_2(x, sides, width):
    for axis, dim in sides:
        size, length = (lax.axis_size(axis), x.shape[dim])
        up = [(i, (i + 1) % size) for i in range(size - 1)]
        down = [(j, i) for i, j in up]
        last = lax.slice_in_dim(x, length - width, length, axis=dim)
        first = lax.slice_in_dim(x, 0, width, axis=dim)
        before = lax.ppermute(last, axis, up)
        after = lax.ppermute(first, axis, down)
        x = jnp.concatenate([before, x, after], axis=dim)
    return x


def spread(value, axis, source):
    kept = jnp.where(lax.axis_index(axis) == source, value, 0).astype(value.dtype)
    return lax.psum(kept, axis)


def contract(pattern, left_side, right_side):
    return jnp.einsum(pattern, left_side, right_side, preferred_element_type=jnp.float32)


def bucket_of(offsets):
    magnitude = jnp.abs(offsets)
    counted = jnp.zeros(offsets.shape, jnp.int32)
    for threshold in bucket_edges:
        counted = counted + (magnitude >= threshold).astype(jnp.int32)
    return counted + 16 * (offsets > 0).astype(jnp.int32)


def expand_bias(bias_table, block_rows, radius):
    window = block_rows + 2 * radius
    span_length = block_rows + window - 1
    offsets = jnp.arange(span_length, dtype=jnp.int32) - (block_rows - 1) - radius
    bucket_count = bias_table.shape[0]
    head_count = bias_table.shape[1]
    onehot = (
        bucket_of(offsets)[:, None] == jnp.arange(bucket_count, dtype=jnp.int32)[None, :]
    ).astype(jnp.float32)
    by_offset = jnp.dot(onehot, bias_table, precision=lax.Precision.HIGHEST).T
    repeated = jnp.tile(by_offset, (1, block_rows))
    first_index = block_rows - 1
    skewed = repeated[:, first_index : first_index + block_rows * (span_length - 1)]
    skewed = skewed.reshape(head_count, block_rows, span_length - 1)
    return skewed[:, :, :window]


def band_allowed(block_rows, radius, valid_rows):
    window = block_rows + 2 * radius
    offsets = (
        jnp.arange(window, dtype=jnp.int32)[None, :]
        - radius
        - jnp.arange(block_rows, dtype=jnp.int32)[:, None]
    )
    return (jnp.abs(offsets) <= radius) & valid_rows[None, :]


def block_probs(query_rows, key_rows, bias_block, allowed, score_scale):
    scores = contract("qhd,khd->hqk", query_rows, key_rows) * score_scale + bias_block
    scores = jnp.where(allowed[None], scores, masked_score)
    row_peak = jnp.max(scores, axis=-1, keepdims=True)
    weights = jnp.exp(scores - row_peak)
    return weights / jnp.sum(weights, axis=-1, keepdims=True)


def band_forward(queries, keys_ext, values_ext, bias_block, valid_ext, radius):
    row_count = queries.shape[0]
    block_rows = min(block_limit, row_count)
    score_scale = queries.shape[-1] ** (-0.5)

    def one_block(block_index):
        weights = block_probs(
            queries, keys_ext, bias_block, band_allowed(block_rows, radius, valid_ext), score_scale
        )
        return contract("hqk,khd->qhd", weights.astype(jnp.bfloat16), values_ext)

    blocks = lax.map(one_block, jnp.arange(row_count // block_rows, dtype=jnp.int32))
    return blocks.reshape(queries.shape)


def band_backward(queries, keys_ext, values_ext, bias_block, valid_ext, radius, grad_rows):
    row_count = queries.shape[0]
    block_rows = min(block_limit, row_count)
    score_scale = queries.shape[-1] ** (-0.5)

    def one_step(carried_sums, block_index):
        key_sums, value_sums, bias_sum = carried_sums
        weights = block_probs(
            queries, keys_ext, bias_block, band_allowed(block_rows, radius, valid_ext), score_scale
        )
        packed = weights.astype(jnp.bfloat16)
        grad_value = contract("hqk,qhd->khd", packed, grad_rows)
        grad_weights = contract("qhd,khd->hqk", grad_rows, values_ext)
        row_delta = jnp.sum(weights * grad_weights, axis=-1, keepdims=True)
        grad_scores = weights * (grad_weights - row_delta)
        grad_packed = grad_scores.astype(jnp.bfloat16)
        grad_query = contract("hqk,khd->qhd", grad_packed, keys_ext) * score_scale
        grad_key = contract("hqk,qhd->khd", grad_packed, queries) * score_scale
        key_sums = key_sums + grad_key
        value_sums = value_sums + grad_value
        return ((key_sums, value_sums, bias_sum + grad_scores), grad_query)

    initial = (
        jnp.zeros(keys_ext.shape, jnp.float32),
        jnp.zeros(values_ext.shape, jnp.float32),
        jnp.zeros(bias_block.shape, jnp.float32),
    )
    sums, grad_blocks = lax.scan(
        one_step, initial, jnp.arange(row_count // block_rows, dtype=jnp.int32)
    )
    return (grad_blocks.reshape(queries.shape), sums[0], sums[1], sums[2])


def normalize(stream, section_gain):
    widened = stream.astype(jnp.float32)
    inverse = lax.rsqrt(jnp.mean(widened * widened, axis=-1, keepdims=True) + eps_norm)
    return ((widened * inverse * section_gain).astype(jnp.bfloat16), widened, inverse)


def project(normed, weight):
    by_head = normed.reshape(normed.shape[0], weight.shape[1], weight.shape[2])
    return contract("thd,jhde->jthe", by_head, weight).astype(jnp.bfloat16)


def project_back(normed, weight, grad_proj, widened, inverse, section_gain, cotangent):
    by_head = normed.reshape(normed.shape[0], weight.shape[1], weight.shape[2])
    grad_normed = contract("jthe,jhde->thd", grad_proj, weight).reshape(normed.shape)
    grad_weight = contract("thd,jthe->jhde", by_head, grad_proj)
    grad_gain = jnp.sum(grad_normed * widened * inverse, axis=0)
    scaled = grad_normed * section_gain
    grad_input = inverse * scaled - widened * inverse * inverse * inverse * jnp.mean(
        scaled * widened, axis=-1, keepdims=True
    )
    return (
        (cotangent.astype(jnp.float32) + grad_input).astype(jnp.bfloat16),
        grad_weight,
        grad_gain,
    )


def body(
    embedded, carried, stash, returned, loss_grad, qkv_weight, rel_bias, norm_gain, final_gain
):
    section_index = lax.axis_index("section")
    section_count = lax.axis_size("section")
    seq_index = lax.axis_index("seq")
    seq_count = lax.axis_size("seq")
    radius = RADIUS
    weight = lax.all_gather(qkv_weight, "seq", axis=3, tiled=True)[0]
    arrived = shifted(carried, "section", 1)[0]
    inbound = jnp.where(section_index == 0, embedded, arrived)
    came_back = shifted(returned, "section", -1)[0]
    cotangent = jnp.where(section_index == section_count - 1, loss_grad, came_back)
    bias_table = rel_bias[0]
    section_gain = norm_gain[0]
    row_count, feature_count = inbound.shape
    head_count, head_dim = (weight.shape[1], weight.shape[2])
    normed_a, widened_a, inverse_a = normalize(inbound, section_gain)
    normed_b, widened_b, inverse_b = normalize(stash[0], section_gain)
    proj_a = project(normed_a, weight)
    proj_b = project(normed_b, weight)
    stacked = jnp.concatenate([proj_a[1:], proj_b[1:]], axis=0).reshape(4, row_count, feature_count)
    extended = extended_2(stacked, (("seq", 1),), radius)
    extended = extended.reshape(4, row_count + 2 * radius, head_count, head_dim)
    positions = seq_index * row_count - radius + jnp.arange(row_count + 2 * radius, dtype=jnp.int32)
    valid_ext = (positions >= 0) & (positions < row_count * seq_count)
    block_rows = min(block_limit, row_count)
    bias_block = expand_bias(bias_table, block_rows, radius)
    attended = band_forward(proj_a[0], extended[0], extended[1], bias_block, valid_ext, radius)
    output = (widened_a + attended.reshape(row_count, feature_count)).astype(jnp.bfloat16)
    final_normed = normalize(output, final_gain)[0]
    relaid = lax.all_to_all(final_normed, "seq", split_axis=1, concat_axis=0, tiled=True)
    shared = spread(relaid, "section", section_count - 1)
    memory_rows = relaid.shape[0] // section_count
    memory = lax.dynamic_slice_in_dim(shared, section_index * memory_rows, memory_rows, 0)
    grad_rows = cotangent.reshape(row_count, head_count, head_dim)
    dquery, dkey_ext, dvalue_ext, grad_bias = band_backward(
        proj_b[0], extended[2], extended[3], bias_block, valid_ext, radius, grad_rows
    )
    grad_ext = jnp.stack([dkey_ext, dvalue_ext]).reshape(2, row_count + 2 * radius, feature_count)
    rims_out = jnp.concatenate(
        [grad_ext[:, :radius], grad_ext[:, radius + row_count :]], axis=1
    ).astype(jnp.bfloat16)
    returned_rims = extended_2(rims_out, (("seq", 1),), radius).astype(jnp.float32)
    own_grad = grad_ext[:, radius : radius + row_count]
    own_grad = own_grad.at[:, :radius].add(returned_rims[:, :radius])
    own_grad = own_grad.at[:, row_count - radius :].add(returned_rims[:, 3 * radius :])
    own_grad = own_grad.reshape(2, row_count, head_count, head_dim)
    grad_proj = jnp.concatenate([dquery[None], own_grad], axis=0).astype(jnp.bfloat16)
    input_grad, grad_weight, grad_gain = project_back(
        normed_b, weight, grad_proj, widened_b, inverse_b, section_gain, cotangent
    )
    unused_value, pullback = jax.vjp(
        lambda table_arg: expand_bias(table_arg, block_rows, radius), bias_table
    )
    grad_table = pullback(grad_bias)[0]
    weight_sum, table_sum, gain_sum = (
        lax.psum_scatter(
            grad_weight[None].astype(jnp.bfloat16), "seq", scatter_dimension=3, tiled=True
        ).astype(jnp.float32),
        lax.psum_scatter(
            grad_table[None].astype(jnp.bfloat16), "seq", scatter_dimension=1, tiled=True
        ).astype(jnp.float32),
        lax.psum_scatter(
            grad_gain[None].astype(jnp.bfloat16), "seq", scatter_dimension=1, tiled=True
        ).astype(jnp.float32),
    )
    return (output[None], input_grad[None], weight_sum, table_sum, gain_sum, memory)


def solution(mesh):
    in_specs = (
        P("seq", None),
        P("section", "seq", None),
        P("section", "seq", None),
        P("section", "seq", None),
        P("seq", None),
        P("section", None, None, "seq", None),
        P("section", None, None),
        P("section", None),
        P(),
    )
    out_specs = (
        P("section", "seq", None),
        P("section", "seq", None),
        P("section", None, None, "seq", None),
        P("section", "seq", None),
        P("section", "seq"),
        P("section", "seq"),
    )
    return jax.shard_map(body, mesh=mesh, in_specs=in_specs, out_specs=out_specs, check_vma=False)
```

profile of v0, /device:TPU:0, one launch (start us, length us, event | category | flops | bytes accessed | tf_op | source)
XLA Modules:
  0.0 420.6 jit_solution(7205279854374708148)
XLA Ops:
  7.2 2.2 copy.67
  9.5 2.4 collective-permute-start
  11.9 2.6 copy.70
  16.5 46.9 %all-gather.2.cloned.1.call-done = bf16[1,3,24,128,128]{4,2,1,0,3:T(8,128)(2,1)} async-done(((bf16[1,3,24,32,128]{4,2,1,0,3:T(8,128)(2,1)}), bf16[1,3,24,128,128]{4,2,1,0,3:T(8,128)(2,1)}) %all-gather.2.cloned.1.call-update) | async-done | bytes 2359312 | tf_op jit(solution)/shard_map/all_gather | solution.py:169
  63.4 3.2 copy.68
  72.6 3.7 fusion.80
  76.3 4.5 %copy.73 = bf16[4,96,3072]{2,1,0:T(8,128)(2,1)} copy(bf16[4,96,3072]{1,2,0:T(8,128)(2,1)} %get-tuple-element.114) | data formatting | bytes 4718592 | tf_op jit(solution)/shard_map/slice | solution.py:26
  80.8 3.2 collective-permute-start.1
  84.0 4.5 %copy.74 = bf16[4,96,3072]{2,1,0:T(8,128)(2,1)} copy(bf16[4,96,3072]{1,2,0:T(8,128)(2,1)} %get-tuple-element.115) | data formatting | bytes 4718592 | tf_op jit(solution)/shard_map/slice | solution.py:27
  89.8 1.8 collective-permute-start.3
  92.0 3.5 tile.4
  95.5 7.7 %tile.10 = f32[24,57216]{1,0:T(8,128)} reshape(f32[24,128,447]{2,1,0:T(8,128)} %tile.4) | data formatting | bytes 10985472 | tf_op jit(solution)/shard_map/tile | solution.py:61
  103.2 6.5 %slice.134 = f32[24,57088]{1,0:T(8,128)} slice(f32[24,57216]{1,0:T(8,128)} %tile.10), slice={[0:24], [127:57215]} | slice | bytes 10960896 | tf_op jit(solution)/shard_map/slice | solution.py:63
  109.8 9.0 %reshape.305 = f32[24,128,446]{2,1,0:T(8,128)} reshape(f32[24,57088]{1,0:T(8,128)} %slice.134) | data formatting | bytes 10960896 | tf_op jit(solution)/shard_map/reshape | solution.py:64
  118.7 5.0 %slice.135 = f32[24,128,320]{2,1,0:T(8,128)} slice(f32[24,128,446]{2,1,0:T(8,128)} %reshape.305), slice={[0:24], [0:128], [0:320]} | slice | bytes 7864320 | tf_op jit(solution)/shard_map/slice | solution.py:65
  123.7 5.8 %copy.136 = f32[24,128,320]{1,2,0:T(8,128)} copy(f32[24,128,320]{2,1,0:T(8,128)} %slice.135) | data formatting | bytes 7864320
  129.7 3.5 collective-permute-done.1
  133.2 4.5 %copy.75 = bf16[4,96,3072]{1,2,0:T(8,128)(2,1)} copy(bf16[4,96,3072]{2,1,0:T(8,128)(2,1)} %collective-permute-done.1) | data formatting | bytes 4718592 | tf_op jit(solution)/shard_map/ppermute | solution.py:28
  137.8 5.4 %collective-permute-done.2 = bf16[4,96,3072]{2,1,0:T(8,128)(2,1)} collective-permute-done((bf16[4,96,3072]{2,1,0:T(8,128)(2,1)}, bf16[4,96,3072]{2,1,0:T(8,128)(2,1)}, u32[]{:S(2)}, u32[]{:S(2)}) %collective-permute-start.2) | collective-permute-done | bytes 2359328 | tf_op jit(solution)/shard_map/ppermute | solution.py:29
  143.2 4.5 %copy.76 = bf16[4,96,3072]{1,2,0:T(8,128)(2,1)} copy(bf16[4,96,3072]{2,1,0:T(8,128)(2,1)} %collective-permute-done.2) | data formatting | bytes 4718592 | tf_op jit(solution)/shard_map/ppermute | solution.py:29
  147.7 7.5 %pad_maximum_fusion = bf16[4,320,3072]{1,2,0:T(8,128)(2,1)S(1)} fusion(bf16[4,96,3072]{1,2,0:T(8,128)(2,1)} %copy.76, bf16[4,128,3072]{1,2,0:T(8,128)(2,1)S(1)} %bitcast.161, bf16[4,96,3072]{1,2,0:T(8,128)(2,1)} %copy.75), kind=kLoop, calls=%fused_computation.2 | loop fusion | flops 23592960 | bytes 15728640 | tf_op jit(solution)/shard_map/concatenate | solution.py:30
  155.2 3.0 fusion.78
  158.9 2.4 add_select_fusion.1
  162.1 2.4 copy-done.12
  164.5 3.1 add_select_fusion
  167.6 6.4 %fusion.15 = f32[24,128,128]{2,1,0:T(8,128)} fusion(bf16[320,24,128]{0,2,1:T(8,128)(2,1)} %bitcast.175, f32[24,128]{1,0:T(8,128)S(1)} %fusion.81, f32[24,128,320]{1,2,0:T(8,128)} %copy-done.8), kind=kOutput, calls=%fused_computation.34 | convolution fusion | flops 254610752 | bytes 7483392 | tf_op jit(solution)/shard_map/while/body/eval_jaxpr/hqk,khd->qhd/dot_general | solution.py:40
  174.0 3.1 copy.83
  177.1 2.5 fusion.16
  179.7 6.0 %fusion.82 = (f32[24,128]{1,0:T(8,128)S(1)}, f32[24,128,320]{1,2,0:T(8,128)}) fusion(f32[24,128,320]{1,2,0:T(8,128)} %add_select_fusion), kind=kOutput, calls=%fused_computation.132 | output fusion | flops 1966399 | bytes 7876608 | tf_op jit(solution)/shard_map/while/body/eval_jaxpr/sub | solution.py:82
  185.6 6.7 %convolution_bitcast_fusion = f32[320,24,128]{2,0,1:T(8,128)} fusion(f32[24,128]{1,0:T(8,128)S(1)} %get-tuple-element.116, f32[24,128,320]{1,2,0:T(8,128)} %add_select_fusion, bf16[128,3072]{1,0:T(8,128)(2,1)S(1)} %copy-done.20, bf16[1,128,3072]{2,1,0:T(8,128)(2,1)} %collective-permute-done.3, pred[]{:T(512)S(6)} %eq.37), kind=kOutput, calls=%fused_computation.29 | convolution fusion | flops 255003968 | bytes 9449473 | tf_op jit(solution)/shard_map/while/body/eval_jaxpr/hqk,qhd->khd/dot_general | solution.py:40
  192.4 6.3 %copy.94 = f32[320,24,128]{2,1,0:T(8,128)} copy(f32[320,24,128]{2,0,1:T(8,128)} %convolution_bitcast_fusion) | data formatting | bytes 7864320 | tf_op jit(solution)/shard_map/while/body/eval_jaxpr/hqk,qhd->khd/transpose | solution.py:40
  198.7 5.0 %stack.10 = f32[1,320,3072]{2,1,0:T(8,128)} reshape(f32[320,24,128]{2,1,0:T(8,128)} %copy.94) | data formatting | bytes 7864320 | tf_op jit(solution)/shard_map/stack | solution.py:200
  203.7 4.4 %multiply_reduce_fusion = (f32[24,128]{1,0:T(8,128)S(1)}, f32[24,128,320]{1,2,0:T(8,128)S(1)}) fusion(f32[24,128,320]{1,2,0:T(8,128)} %get-tuple-element.117, f32[24,128]{1,0:T(8,128)S(1)} %get-tuple-element.116, bf16[320,24,128]{0,2,1:T(8,128)(2,1)} %bitcast.174, bf16[128,3072]{1,0:T(8,128)(2,1)S(1)} %copy-done.20, ...), kind=kOutput, calls=%fused_computation.5 | convolution fusion | flops 254997504 | bytes 11427841 | tf_op jit(solution)/shard_map/while/body/eval_jaxpr/qhd,khd->hqk/dot_general | solution.py:40
  211.1 4.2 copy.92
  215.3 4.9 %stack.9 = f32[1,320,3072]{2,1,0:T(8,128)} reshape(f32[320,24,128]{2,1,0:T(8,128)} %copy.92) | data formatting | bytes 7864320 | tf_op jit(solution)/shard_map/stack | solution.py:200
  220.3 2.5 constant_dynamic-update-slice_fusion.1
  224.4 2.0 fusion.79
  226.4 3.6 collective-permute-start.4
  233.7 4.2 all-to-all-start
  238.0 4.5 %fusion.34 = bf16[1,128,24,128]{1,3,2,0:T(8,128)(2,1)} fusion(bf16[320,24,128]{0,2,1:T(8,128)(2,1)} %bitcast.163, f32[24,128,320]{1,2,0:T(8,128)} %copy-done.2), kind=kOutput, calls=%fused_computation.59 | convolution fusion | flops 253427712 | bytes 6684672 | tf_op jit(solution)/shard_map/while/body/eval_jaxpr/hqk,khd->qhd/dot_general | solution.py:40
  242.5 2.4 copy.96
  244.8 10.9 %collective-permute-done.4 = bf16[2,96,3072]{2,1,0:T(8,128)(2,1)} collective-permute-done((bf16[2,96,3072]{2,1,0:T(8,128)(2,1)}, bf16[2,96,3072]{2,1,0:T(8,128)(2,1)}, u32[]{:S(2)}, u32[]{:S(2)}) %collective-permute-start.4) | collective-permute-done | bytes 1179680 | tf_op jit(solution)/shard_map/ppermute | solution.py:28
  255.7 9.5 %collective-permute-done.5 = bf16[2,96,3072]{2,1,0:T(8,128)(2,1)} collective-permute-done((bf16[2,96,3072]{2,1,0:T(8,128)(2,1)}, bf16[2,96,3072]{2,1,0:T(8,128)(2,1)}, u32[]{:S(2)}, u32[]{:S(2)}) %collective-permute-start.5) | collective-permute-done | bytes 1179680 | tf_op jit(solution)/shard_map/ppermute | solution.py:29
  265.2 2.2 fusion.3
  267.5 1.8 fusion.2
  270.7 1.9 copy.95
  272.6 1.6 copy.97
  274.2 4.8 %fusion.24 = (bf16[24,128]{1,0:T(8,128)(2,1)S(1)}, f32[128]{0:T(128)S(1)}, f32[24,128,128,1]{1,2,3,0:T(8,128)}) fusion(f32[128,24,128]{0,2,1:T(8,128)S(1)} %bitcast.165, f32[128]{0:T(128)S(1)} %add_rsqrt_fusion.1, f32[24,128]{1,0:T(8,128)S(1)} %bitcast.182, bf16[3,24,128,128]{3,1,0,2:T(8,128)(2,1)} %bitcast.176, bf16[2,128,24,128]{3,1,0,2:T(8,128)(2,1)} %copy.97, ...), kind=kOutput, calls=%fused_computation.45 | convolution fusion | flops 305525632 | bytes 7883776 | tf_op jit(solution)/shard_map/jthe,jhde->thd/dot_general | solution.py:40
  280.3 2.2 bitcast_bitcast_fusion
  283.9 4.0 convert_bitcast_fusion
  287.8 4.5 %copy.102 = bf16[1,3,24,128,128]{4,2,1,0,3:T(8,128)(2,1)} copy(bf16[1,3,24,128,128]{3,4,1,2,0:T(8,128)(2,1)} %convert_bitcast_fusion) | data formatting | bytes 4718592 | tf_op jit(solution)/shard_map/convert_element_type | solution.py:219
  294.2 5.7 %copy.137 = f32[24,128,320]{2,1,0:T(8,128)} copy(f32[24,128,320]{1,2,0:T(8,128)} %copy-done.2) | data formatting | bytes 7864320
  300.0 5.8 %pad.10.clone = f32[24,128,446]{2,1,0:T(8,128)} pad(f32[24,128,320]{2,1,0:T(8,128)} %copy.137, f32[]{:T(128)} %constant.140.clone.1), padding=0_0x0_0x0_126 | pad | bytes 9412612 | tf_op jit(solution)/shard_map/transpose(jvp())/pad | solution.py:65
  305.8 7.7 %reshape.309 = f32[24,57088]{1,0:T(8,128)} reshape(f32[24,128,446]{2,1,0:T(8,128)} %pad.10.clone) | data formatting | bytes 10960896 | tf_op jit(solution)/shard_map/transpose(jvp())/reshape | solution.py:64
  313.6 6.4 %pad.11 = f32[24,57216]{1,0:T(8,128)} pad(f32[24,57088]{1,0:T(8,128)} %reshape.309, f32[]{:T(128)} %constant.140.clone.1), padding=0_0x127_1 | pad | bytes 10973188 | tf_op jit(solution)/shard_map/transpose(jvp())/pad | solution.py:63
  320.0 8.5 %reshape.310 = f32[24,128,447]{2,1,0:T(8,128)} reshape(f32[24,57216]{1,0:T(8,128)} %pad.11) | data formatting | bytes 10985472 | tf_op jit(solution)/shard_map/transpose(jvp())/reshape | solution.py:61
  328.4 3.7 reduce_sum.90
  332.5 15.8 %all-reduce.2 = bf16[1,32,24]{2,0,1:T(2,128)(2,1)S(1)} all-reduce(bf16[1,32,24]{2,0,1:T(2,128)(2,1)S(1)} %copy.104), channel_id=3, replica_groups=mesh['section'=8,'seq'=4] {'seq'}, use_global_device_ids=true, to_apply=%region_10.11.clone | all-reduce | flops 768 | bytes 3072
  348.9 1.9 copy.99
  350.8 2.8 fusion.39
  355.3 6.7 %all-reduce.5.cloned.1.call-done = bf16[512,768]{1,0:T(8,128)(2,1)} async-done(((bf16[512,768]{1,0:T(8,128)(2,1)}), bf16[512,768]{1,0:T(8,128)(2,1)}) %all-reduce.5.cloned.1.call-update) | async-done | bytes 786448 | tf_op jit(solution)/shard_map/psum | solution.py:36
  361.9 1.5 constant_dynamic-slice_fusion
  363.5 47.9 %reduce-scatter.5.cloned.1.call-done = bf16[1,3,24,32,128]{4,2,1,0,3:T(8,128)(2,1)} async-done(((bf16[1,3,24,128,128]{4,2,1,0,3:T(8,128)(2,1)}), bf16[1,3,24,32,128]{4,2,1,0,3:T(8,128)(2,1)}) %reduce-scatter.5.cloned.1.call-update) | async-done | bytes 589840 | tf_op jit(solution)/shard_map/reduce_scatter | solution.py:218
  411.4 2.2 copy.106
  (102 shorter events, 27.3 us)
Async XLA Ops:
  7.2 84.5 %copy-start = (f32[1,32,24]{1,2,0:T(8,128)S(1)}, f32[1,32,24]{1,2,0:T(8,128)}, u32[]{:S(2)}) copy-start(f32[1,32,24]{1,2,0:T(8,128)} %param.19) | copy-start | bytes 9220
  7.2 7.3 %copy-start.14 = (bf16[1,128,3072]{2,1,0:T(8,128)(2,1)S(1)}, bf16[1,128,3072]{2,1,0:T(8,128)(2,1)}, u32[]{:S(2)}) copy-start(bf16[1,128,3072]{2,1,0:T(8,128)(2,1)} %param.15) | copy-start | bytes 2359300
  7.2 7.6 %copy-start.22 = (bf16[128,3072]{1,0:T(8,128)(2,1)S(1)}, bf16[128,3072]{1,0:T(8,128)(2,1)}, u32[]{:S(2)}) copy-start(bf16[128,3072]{1,0:T(8,128)(2,1)} %param.13) | copy-start | bytes 2359300
  7.2 56.2 %all-gather.2.cloned.1.call-start = ((), (), s32[]{:S(2)}) async-start(), calls=%async_computation.3 | async-start | bytes 2949120 | tf_op jit(solution)/shard_map/all_gather | solution.py:169
  9.5 5.3 %collective-permute-start = (bf16[1,128,3072]{2,1,0:T(8,128)(2,1)}, bf16[1,128,3072]{2,1,0:T(8,128)(2,1)S(1)}, u32[]{:S(2)}, u32[]{:S(2)}) collective-permute-start(bf16[1,128,3072]{2,1,0:T(8,128)(2,1)} %param.14), channel_id=1, source_target_pairs={{0,4},{4,8},{8,12},{12,16},{16,20},{20,24},{24,28},{1,5},{5,9},{9,... | collective-permute-start | bytes 2359304 | tf_op jit(solution)/shard_map/ppermute | solution.py:18
  11.9 4.1 copy-start.23
  15.1 0.9 copy-start.16
  67.4 1.5 copy-start.13
  67.4 2.3 copy-start.9
  70.6 1.4 copy-start.11
  80.8 52.4 %collective-permute-start.1 = (bf16[4,96,3072]{2,1,0:T(8,128)(2,1)}, bf16[4,96,3072]{2,1,0:T(8,128)(2,1)}, u32[]{:S(2)}, u32[]{:S(2)}) collective-permute-start(bf16[4,96,3072]{2,1,0:T(8,128)(2,1)} %copy.73), channel_id=1, source_target_pairs={{0,1},{1,2},{2,3},{4,5},{5,6},{6,7},{8,9},{9,10},{10,11},{12,13},{... | collective-permute-start | bytes 7077896 | tf_op jit(solution)/shard_map/ppermute | solution.py:28
  88.5 54.7 %collective-permute-start.2 = (bf16[4,96,3072]{2,1,0:T(8,128)(2,1)}, bf16[4,96,3072]{2,1,0:T(8,128)(2,1)}, u32[]{:S(2)}, u32[]{:S(2)}) collective-permute-start(bf16[4,96,3072]{2,1,0:T(8,128)(2,1)} %copy.74), channel_id=1, source_target_pairs={{1,0},{2,1},{3,2},{5,4},{6,5},{7,6},{9,8},{10,9},{11,10},{13,12},{... | collective-permute-start | bytes 7077896 | tf_op jit(solution)/shard_map/ppermute | solution.py:29
  89.8 95.9 %collective-permute-start.3 = (bf16[1,128,3072]{2,1,0:T(8,128)(2,1)}, bf16[1,128,3072]{2,1,0:T(8,128)(2,1)}, u32[]{:S(2)}, u32[]{:S(2)}) collective-permute-start(bf16[1,128,3072]{2,1,0:T(8,128)(2,1)} %param.16), channel_id=1, source_target_pairs={{4,0},{8,4},{12,8},{16,12},{20,16},{24,20},{28,24},{5,1},{9,5},{13... | collective-permute-start | bytes 2359304 | tf_op jit(solution)/shard_map/ppermute | solution.py:18
  155.2 3.7 copy-start.4
  158.2 3.9 copy-start.5
  161.4 6.2 %copy-start.8 = (f32[24,128,320]{1,2,0:T(8,128)}, f32[24,128,320]{1,2,0:T(8,128)S(1)}, u32[]{:S(2)}) copy-start(f32[24,128,320]{1,2,0:T(8,128)S(1)} %add_select_fusion.1) | copy-start | bytes 11796484
  161.4 3.1 copy-start.12
  174.0 3.1 copy-start.17
  179.7 6.0 %copy-start.20 = (bf16[128,3072]{1,0:T(8,128)(2,1)S(1)}, bf16[128,3072]{1,0:T(8,128)(2,1)}, u32[]{:S(2)}) copy-start(bf16[128,3072]{1,0:T(8,128)(2,1)} %param.17) | copy-start | bytes 2359300
  203.7 4.5 %copy-start.7 = (f32[24,128,320]{1,2,0:T(8,128)S(1)}, f32[24,128,320]{1,2,0:T(8,128)}, u32[]{:S(2)}) copy-start(f32[24,128,320]{1,2,0:T(8,128)} %get-tuple-element.117) | copy-start | bytes 11796484
  209.2 1.9 copy-start.2
  220.2 3.3 copy-start.6
  223.8 7.5 %copy-start.3 = (f32[2,320,3072]{2,1,0:T(8,128)}, f32[2,320,3072]{2,1,0:T(8,128)S(1)}, u32[]{:S(2)}) copy-start(f32[2,320,3072]{2,1,0:T(8,128)S(1)} %constant_dynamic-update-slice_fusion) | copy-start | bytes 23592964
  226.4 29.3 %collective-permute-start.4 = (bf16[2,96,3072]{2,1,0:T(8,128)(2,1)}, bf16[2,96,3072]{2,1,0:T(8,128)(2,1)}, u32[]{:S(2)}, u32[]{:S(2)}) collective-permute-start(bf16[2,96,3072]{2,1,0:T(8,128)(2,1)} %get-tuple-element.112), channel_id=1, source_target_pairs={{0,1},{1,2},{2,3},{4,5},{5,6},{6,7},{8,9},{9,10},{10,11},{12,13},{... | collective-permute-start | bytes 3538952 | tf_op jit(solution)/shard_map/ppermute | solution.py:28
  230.0 35.2 %collective-permute-start.5 = (bf16[2,96,3072]{2,1,0:T(8,128)(2,1)}, bf16[2,96,3072]{2,1,0:T(8,128)(2,1)}, u32[]{:S(2)}, u32[]{:S(2)}) collective-permute-start(bf16[2,96,3072]{2,1,0:T(8,128)(2,1)} %get-tuple-element.113), channel_id=1, source_target_pairs={{1,0},{2,1},{3,2},{5,4},{6,5},{7,6},{9,8},{10,9},{11,10},{13,12},{... | collective-permute-start | bytes 3538952 | tf_op jit(solution)/shard_map/ppermute | solution.py:29
  231.3 1.1 copy-start.19
  231.4 1.1 copy-start.24
  233.7 48.8 %all-to-all-start = ((bf16[128,4,768]{2,0,1:T(8,128)(2,1)}), bf16[128,4,768]{2,0,1:T(8,128)(2,1)}, u32[]{:S(2)}, u32[]{:S(2)}) async-start(bf16[128,4,768]{2,0,1:T(8,128)(2,1)} %bitcast.170), calls=%async_computation.1 | async-start | bytes 1572864 | tf_op jit(solution)/shard_map/all_to_all | solution.py:192
  237.9 115.7 %reduce-scatter.7.cloned.1.call-start = ((), (), s32[]{:S(2)}) async-start(), calls=%async_computation.6 | async-start | bytes 983040
  272.6 1.6 copy-start.10
  280.3 3.6 copy-start.18
  282.5 79.4 %all-reduce.5.cloned.1.call-start = ((), (), s32[]{:S(2)}) async-start(), calls=%async_computation.5 | async-start | bytes 1572864 | tf_op jit(solution)/shard_map/psum | solution.py:36
  283.6 127.8 %reduce-scatter.5.cloned.1.call-start = ((), (), s32[]{:S(2)}) async-start(), calls=%async_computation.4 | async-start | bytes 2949120 | tf_op jit(solution)/shard_map/reduce_scatter | solution.py:218
  292.3 0.7 copy-start.25
  332.1 18.7 %copy-start.15 = (bf16[1,128,3072]{2,1,0:T(8,128)(2,1)S(1)}, bf16[1,128,3072]{2,1,0:T(8,128)(2,1)}, u32[]{:S(2)}) copy-start(bf16[1,128,3072]{2,1,0:T(8,128)(2,1)} %param.15) | copy-start | bytes 2359300
  332.1 18.7 %copy-start.21 = (bf16[128,3072]{1,0:T(8,128)(2,1)S(1)}, bf16[128,3072]{1,0:T(8,128)(2,1)}, u32[]{:S(2)}) copy-start(bf16[128,3072]{1,0:T(8,128)(2,1)} %param.17) | copy-start | bytes 2359300
  350.8 62.9 %copy-start.1 = (f32[1,32,24]{1,2,0:T(8,128)S(1)}, f32[1,32,24]{1,2,0:T(8,128)}, u32[]{:S(2)}) copy-start(f32[1,32,24]{1,2,0:T(8,128)} %param.19) | copy-start | bytes 9220
Sparse Core Ops, SparseCore 0:
  10.2 53.1 all-gather.1
  282.6 21.2 reduce-scatter.6
  307.1 54.8 all-reduce.4
  364.1 47.2 reduce-scatter.4
where the time goes:
time: 428 us; the launch traced here: 421 us
  local copies, waits for them, and re-layouts  167 us (39%)
  waiting for transfers between devices  131 us (31%)
  matrix products  39.4 us (9%)
  other arithmetic  34.1 us (8%)
  starting transfers between devices  18.2 us (4%)
  blocking collectives  15.8 us (4%)
  between operations  15.4 us (4%)
    reduce_scatter x1, waiting for transfers between devices, body(): lax.psum_scatter(grad_weight[None].astype(jnp.bfloat16), 'seq', scatter_d...  47.9 us
    all_gather x1, waiting for transfers between devices, body(): weight = lax.all_gather(qkv_weight, 'seq', axis=3, tiled=True)[0]  46.9 us
    dot_general x11, matrix products, contract(): jnp.einsum(pattern, left_side, right_side, preferred_element_type=jnp.flo...  38.8 us
    unnamed x63, local copies, waits for them, and re-layouts  34.7 us
    reshape x2, local copies, waits for them, and re-layouts, expand_bias(): skewed = skewed.reshape(head_count, block_rows, span_length - 1)  16.7 us
    unnamed x1, blocking collectives  15.8 us
    ppermute x2, waiting for transfers between devices, extended_2(): after = lax.ppermute(first, axis, down)  14.9 us
    ppermute x2, waiting for transfers between devices, extended_2(): before = lax.ppermute(last, axis, up)  14.4 us
  transfers between devices with their start and end apart: 11, of which 7 were waited for; matrix products, arithmetic and copies ran while one was open for 41% of the time, Pallas kernels for 0%

commit v1 on v0

v1 whole, which is shorter than its diff:
```python
import functools

import jax
import jax.numpy as jnp
import numpy as np
from jax import lax
from jax.experimental import pallas as pl
from jax.experimental.pallas import tpu as pltpu
from jax.sharding import PartitionSpec as P

RADIUS = 96
HEAD_DIM = 128
ROW_BLOCK = 64
WINDOW = ROW_BLOCK + 2 * RADIUS
eps_norm = 1e-06
bucket_edges = (1, 2, 3, 4, 5, 6, 7, 8, 11, 16, 22, 32, 45, 64, 90)
masked_score = -1e30
F32 = jnp.float32
BF16 = jnp.bfloat16
VMEM_LIMIT = 48 * 1024 * 1024


def bucket_onehot(bucket_count):
    offsets = np.arange(WINDOW) - RADIUS
    magnitude = np.abs(offsets)
    counted = np.zeros(offsets.shape, np.int32)
    for threshold in bucket_edges:
        counted = counted + (magnitude >= threshold)
    counted = counted + 16 * (offsets > 0)
    onehot = (counted[:, None] == np.arange(bucket_count)[None, :]) & (magnitude <= RADIUS)[:, None]
    return onehot.astype(np.float32)


def dot_nn(a, b):
    return lax.dot_general(a, b, (((1,), (0,)), ((), ())), preferred_element_type=F32)


def dot_nt(a, b):
    return lax.dot_general(a, b, (((1,), (1,)), ((), ())), preferred_element_type=F32)


def dot_tn(a, b):
    return lax.dot_general(a, b, (((0,), (0,)), ((), ())), preferred_element_type=F32)


def norm_kernel(x_ref, gain_ref, normed_ref, inverse_ref):
    x = x_ref[...].astype(F32)
    inverse = lax.rsqrt(jnp.mean(x * x, axis=-1, keepdims=True) + eps_norm)
    normed_ref[...] = (x * inverse * gain_ref[...]).astype(BF16)
    inverse_ref[...] = jnp.broadcast_to(inverse, inverse_ref.shape)


def norm_rows(x, gain):
    rows, width = x.shape
    return pl.pallas_call(
        norm_kernel,
        out_shape=(
            jax.ShapeDtypeStruct((rows, width), BF16),
            jax.ShapeDtypeStruct((rows, 128), F32),
        ),
        compiler_params=pltpu.CompilerParams(vmem_limit_bytes=VMEM_LIMIT),
        cost_estimate=pl.CostEstimate(
            flops=6 * rows * width, bytes_accessed=4 * rows * width, transcendentals=rows
        ),
        name="norm_rows",
    )(x, gain)


def load_weight(meta_ref, slot_refs, weight_ref, head, slots):
    depth = HEAD_DIM // slots
    for r, slot_ref in enumerate(slot_refs):
        if slots == 1:
            start = 0
        else:
            start = pl.multiple_of(lax.rem(meta_ref[0] + r, slots) * depth, depth)
        for j in range(3):
            weight_ref[head, pl.ds(start, depth), j * HEAD_DIM : (j + 1) * HEAD_DIM] = slot_ref[j, head]
    return weight_ref[head]


def key_mask(meta_ref, first_key):
    key = lax.broadcasted_iota(jnp.int32, (1, WINDOW), 1) + first_key
    inside = (key >= meta_ref[1]) & (key < meta_ref[2])
    return jnp.where(inside, 0.0, masked_score).astype(F32)


def toeplitz(row):
    return pltpu.roll(
        jnp.broadcast_to(row, (ROW_BLOCK, WINDOW)), 0, 1, stride=1, stride_axis=0
    )


def diagonal_sums(values):
    total = values[:8]
    for a in range(1, ROW_BLOCK // 8):
        total = total + pltpu.roll(values[8 * a : 8 * a + 8], WINDOW - 8 * a, 1)
    row = lax.broadcasted_iota(jnp.int32, total.shape, 0)
    for bit in (1, 2, 4):
        total = jnp.where((row & bit) != 0, pltpu.roll(total, WINDOW - bit, 1), total)
    return jnp.sum(total, axis=0, keepdims=True)


def block_probs(query_rows, key_rows, bias):
    scores = dot_nt(query_rows, key_rows) * (HEAD_DIM ** (-0.5)) + bias
    weights = jnp.exp(scores - jnp.max(scores, axis=-1, keepdims=True))
    return weights * (1.0 / jnp.sum(weights, axis=-1, keepdims=True))


def forward_kernel(slots, group, meta_ref, before_ref, own_ref, after_ref, x_ref, offset_ref, *rest):
    slot_refs = rest[:slots]
    out_ref, weight_ref = rest[slots:]
    rows = own_ref.shape[0]
    blocks = rows // ROW_BLOCK
    masks = [key_mask(meta_ref, b * ROW_BLOCK) for b in range(blocks)]
    for g in range(group):
        columns = slice(g * HEAD_DIM, (g + 1) * HEAD_DIM)
        weight = load_weight(meta_ref, slot_refs, weight_ref, g, slots)
        own = own_ref[:, columns]
        extended = jnp.concatenate([before_ref[:, columns], own, after_ref[:, columns]], axis=0)
        query = dot_nn(own, weight[:, :HEAD_DIM]).astype(BF16)
        key_value = dot_nn(extended, weight[:, HEAD_DIM:]).astype(BF16)
        key, value = key_value[:, :HEAD_DIM], key_value[:, HEAD_DIM:]
        bias = toeplitz(offset_ref[g])
        for b in range(blocks):
            first = b * ROW_BLOCK
            window = slice(first, first + WINDOW)
            probs = block_probs(query[first : first + ROW_BLOCK], key[window], bias + masks[b])
            attended = dot_nn(probs.astype(BF16), value[window])
            kept = x_ref[first : first + ROW_BLOCK, columns].astype(F32)
            out_ref[first : first + ROW_BLOCK, columns] = (kept + attended).astype(BF16)


def column_spec(rows, group, first):
    return pl.BlockSpec((rows, group * HEAD_DIM), lambda i, meta: (0, i + first))


def slot_specs(weight_slots, group):
    return [
        pl.BlockSpec((3, group, slot.shape[2], HEAD_DIM), lambda i, meta: (0, i, 0, 0))
        for slot in weight_slots
    ]


def forward_attention(meta, before, own, after, x, offsets, weight_slots, group):
    rows, width = own.shape
    heads = width // HEAD_DIM
    slots = len(weight_slots)
    return pl.pallas_call(
        functools.partial(forward_kernel, slots, group),
        out_shape=jax.ShapeDtypeStruct((rows, width), BF16),
        grid_spec=pltpu.PrefetchScalarGridSpec(
            num_scalar_prefetch=1,
            grid=(heads // group,),
            in_specs=[
                column_spec(RADIUS, group, 0),
                column_spec(rows, group, 0),
                column_spec(RADIUS, group, 0),
                column_spec(rows, group, 0),
                pl.BlockSpec((group, 1, WINDOW), lambda i, meta: (i, 0, 0)),
                *slot_specs(weight_slots, group),
            ],
            out_specs=column_spec(rows, group, 0),
            scratch_shapes=[pltpu.VMEM((group, HEAD_DIM, 3 * HEAD_DIM), BF16)],
        ),
        compiler_params=pltpu.CompilerParams(vmem_limit_bytes=VMEM_LIMIT),
        cost_estimate=pl.CostEstimate(
            flops=heads * 60_000_000, bytes_accessed=8 * rows * width, transcendentals=heads * 32768
        ),
        name="forward_attention",
    )(meta, before, own, after, x, offsets, *weight_slots)


def backward_kernel(slots, group, meta_ref, before_ref, own_ref, after_ref, cot_ref, offset_ref, *rest):
    slot_refs = rest[:slots]
    rest = rest[slots:]
    grad_ref, lower_ref, upper_ref, offset_grad_ref = rest[:4]
    part_refs = rest[4 : 4 + slots]
    weight_ref, part_ref = rest[4 + slots :]
    rows = own_ref.shape[0]
    blocks = rows // ROW_BLOCK
    scale = HEAD_DIM ** (-0.5)
    masks = [key_mask(meta_ref, b * ROW_BLOCK) for b in range(blocks)]
    for g in range(group):
        columns = slice(g * HEAD_DIM, (g + 1) * HEAD_DIM)
        weight = load_weight(meta_ref, slot_refs, weight_ref, g, slots)
        own = own_ref[:, columns]
        extended = jnp.concatenate([before_ref[:, columns], own, after_ref[:, columns]], axis=0)
        query = dot_nn(own, weight[:, :HEAD_DIM]).astype(BF16)
        key_value = dot_nn(extended, weight[:, HEAD_DIM:]).astype(BF16)
        key, value = key_value[:, :HEAD_DIM], key_value[:, HEAD_DIM:]
        bias = toeplitz(offset_ref[g])
        grad_query, grad_key, grad_value, score_sum = [], [], [], None
        for b in range(blocks):
            first = b * ROW_BLOCK
            window = slice(first, first + WINDOW)
            query_rows = query[first : first + ROW_BLOCK]
            cot_rows = cot_ref[first : first + ROW_BLOCK, columns]
            probs = block_probs(query_rows, key[window], bias + masks[b])
            grad_probs = dot_nt(cot_rows, value[window])
            delta = jnp.sum(probs * grad_probs, axis=-1, keepdims=True)
            grad_scores = probs * (grad_probs - delta)
            score_sum = grad_scores if score_sum is None else score_sum + grad_scores
            grad_packed = grad_scores.astype(BF16)
            grad_query.append(dot_nn(grad_packed, key[window]))
            grad_key.append(dot_tn(grad_packed, query_rows))
            grad_value.append(dot_tn(probs.astype(BF16), cot_rows))

        def joined(parts):
            pieces = []
            for u in range((rows + 2 * RADIUS) // ROW_BLOCK):
                total = None
                for b in range(blocks):
                    if 0 <= u - b < WINDOW // ROW_BLOCK:
                        piece = parts[b][(u - b) * ROW_BLOCK : (u - b + 1) * ROW_BLOCK]
                        total = piece if total is None else total + piece
                pieces.append(total)
            return jnp.concatenate(pieces, axis=0)

        dquery = (jnp.concatenate(grad_query, axis=0) * scale).astype(BF16)
        dkey = (joined(grad_key) * scale).astype(BF16)
        dvalue = joined(grad_value).astype(BF16)
        dkey_value = jnp.concatenate([dkey, dvalue], axis=1)
        grad_extended = dot_nt(dkey_value, weight[:, HEAD_DIM:])
        grad_ref[:, columns] = grad_extended[RADIUS : RADIUS + rows] + dot_nt(dquery, weight[:, :HEAD_DIM])
        lower_ref[:, columns] = grad_extended[:RADIUS].astype(BF16)
        upper_ref[:, columns] = grad_extended[RADIUS + rows :].astype(BF16)
        part_ref[g, :, :HEAD_DIM] = dot_tn(own, dquery)
        part_ref[g, :, HEAD_DIM:] = dot_tn(extended, dkey_value)
        depth = HEAD_DIM // slots
        for r in range(slots):
            if slots == 1:
                start = 0
            else:
                start = pl.multiple_of(lax.rem(meta_ref[0] + r, slots) * depth, depth)
            for j in range(3):
                part_refs[r][j, g] = part_ref[
                    g, pl.ds(start, depth), j * HEAD_DIM : (j + 1) * HEAD_DIM
                ].astype(part_refs[r].dtype)
        offset_grad_ref[g] = diagonal_sums(score_sum)


def backward_attention(meta, before, own, after, cotangent, offsets, weight_slots, group, first_head, heads):
    rows = own.shape[0]
    width = heads * HEAD_DIM
    slots = len(weight_slots)
    first = first_head // group
    slot_shape = weight_slots[0].shape
    part_types = [F32] + [BF16] * (slots - 1) if slots > 1 else [BF16]
    return pl.pallas_call(
        functools.partial(backward_kernel, slots, group),
        out_shape=(
            jax.ShapeDtypeStruct((rows, width), F32),
            jax.ShapeDtypeStruct((RADIUS, width), BF16),
            jax.ShapeDtypeStruct((RADIUS, width), BF16),
            jax.ShapeDtypeStruct((heads, 1, WINDOW), F32),
            *[jax.ShapeDtypeStruct(slot_shape, kind) for kind in part_types],
        ),
        grid_spec=pltpu.PrefetchScalarGridSpec(
            num_scalar_prefetch=1,
            grid=(heads // group,),
            in_specs=[
                column_spec(RADIUS, group, first),
                column_spec(rows, group, first),
                column_spec(RADIUS, group, first),
                column_spec(rows, group, first),
                pl.BlockSpec((group, 1, WINDOW), lambda i, meta: (i + first, 0, 0)),
                *slot_specs(weight_slots, group),
            ],
            out_specs=(
                column_spec(rows, group, 0),
                column_spec(RADIUS, group, 0),
                column_spec(RADIUS, group, 0),
                pl.BlockSpec((group, 1, WINDOW), lambda i, meta: (i, 0, 0)),
                *slot_specs(weight_slots, group),
            ),
            scratch_shapes=[
                pltpu.VMEM((group, HEAD_DIM, 3 * HEAD_DIM), BF16),
                pltpu.VMEM((group, HEAD_DIM, 3 * HEAD_DIM), F32),
            ],
        ),
        compiler_params=pltpu.CompilerParams(vmem_limit_bytes=VMEM_LIMIT),
        cost_estimate=pl.CostEstimate(
            flops=heads * 150_000_000, bytes_accessed=12 * rows * width, transcendentals=heads * 32768
        ),
        name="backward_attention",
    )(meta, before, own, after, cotangent, offsets, *weight_slots)


def finish_kernel(grad_ref, low_ref, high_ref, x_ref, inverse_ref, gain_ref, cot_ref, out_ref, gain_grad_ref):
    rows = x_ref.shape[0]
    grad = grad_ref[...]
    edge = jnp.zeros((rows - RADIUS, grad.shape[1]), F32)
    grad = grad + jnp.concatenate([low_ref[...].astype(F32), edge], axis=0)
    grad = grad + jnp.concatenate([edge, high_ref[...].astype(F32)], axis=0)
    x = x_ref[...].astype(F32)
    inverse = inverse_ref[:, :1]
    gain_grad_ref[...] = jnp.sum(grad * x * inverse, axis=0, keepdims=True)
    scaled = grad * gain_ref[...]
    mean = jnp.mean(scaled * x, axis=-1, keepdims=True)
    result = inverse * scaled - x * (inverse * inverse * inverse * mean)
    out_ref[...] = (cot_ref[...].astype(F32) + result).astype(BF16)


def finish(grad, low, high, x, inverse, gain, cotangent):
    rows, width = x.shape
    return pl.pallas_call(
        finish_kernel,
        out_shape=(
            jax.ShapeDtypeStruct((rows, width), BF16),
            jax.ShapeDtypeStruct((1, width), F32),
        ),
        compiler_params=pltpu.CompilerParams(vmem_limit_bytes=VMEM_LIMIT),
        cost_estimate=pl.CostEstimate(
            flops=16 * rows * width, bytes_accessed=14 * rows * width, transcendentals=0
        ),
        name="finish",
    )(grad, low, high, x, inverse, gain, cotangent)


def body(
    embedded, carried, stash, returned, loss_grad, qkv_weight, rel_bias, norm_gain, final_gain
):
    section_index = lax.axis_index("section")
    section_count = lax.axis_size("section")
    seq_index = lax.axis_index("seq")
    seq_count = lax.axis_size("seq")
    rows, width = embedded.shape
    heads = width // HEAD_DIM
    tokens = rows * seq_count
    shard = qkv_weight[0]
    depth = shard.shape[2]
    by_slots = seq_count <= 4 and depth % 32 == 0
    up = [(i, i + 1) for i in range(seq_count - 1)]
    down = [(j, i) for i, j in up]
    group = 4 if heads % 4 == 0 else 1

    own_b, inverse_b = norm_rows(stash[0], norm_gain)
    before_b = lax.ppermute(own_b[rows - RADIUS :], "seq", up)
    after_b = lax.ppermute(own_b[:RADIUS], "seq", down)
    if by_slots:
        slots = [shard]
        for r in range(1, seq_count):
            slots.append(lax.ppermute(shard, "seq", [((i + r) % seq_count, i) for i in range(seq_count)]))
    else:
        slots = [lax.all_gather(shard, "seq", axis=2, tiled=True)]

    section_up = [(i, (i + 1) % section_count) for i in range(section_count)]
    section_down = [(j, i) for i, j in section_up]
    inbound = lax.ppermute(
        jnp.where(section_index == section_count - 1, embedded, carried[0]), "section", section_up
    )
    cotangent = lax.ppermute(
        jnp.where(section_index == 0, loss_grad, returned[0]), "section", section_down
    )

    onehot = jnp.asarray(bucket_onehot(rel_bias.shape[1]))
    by_offset = jnp.dot(onehot, rel_bias[0], precision=lax.Precision.HIGHEST).T
    inside = jnp.arange(WINDOW, dtype=jnp.int32) <= 2 * RADIUS
    offsets = jnp.where(inside[None, :], by_offset, masked_score)[:, None, :]
    first_key = RADIUS - seq_index * rows
    meta = jnp.stack([seq_index, first_key, first_key + tokens]).astype(jnp.int32)

    own_a, unused = norm_rows(inbound, norm_gain)
    before_a = lax.ppermute(own_a[rows - RADIUS :], "seq", up)
    after_a = lax.ppermute(own_a[:RADIUS], "seq", down)

    grad_own, lower, upper, offset_grad, *parts = backward_attention(
        meta, before_b, own_b, after_b, cotangent, offsets, slots, group, 0, heads
    )
    from_before = lax.ppermute(upper, "seq", up)
    from_after = lax.ppermute(lower, "seq", down)
    if by_slots:
        weight_sum = parts[0]
        for r in range(1, seq_count):
            weight_sum = weight_sum + lax.ppermute(
                parts[r], "seq", [(i, (i + r) % seq_count) for i in range(seq_count)]
            ).astype(F32)
    else:
        weight_sum = lax.psum_scatter(parts[0], "seq", scatter_dimension=2, tiled=True).astype(F32)

    output = forward_attention(meta, before_a, own_a, after_a, inbound, offsets, slots, group)
    final_normed, unused = norm_rows(output, final_gain[None])
    relaid = lax.all_to_all(final_normed, "seq", split_axis=1, concat_axis=0, tiled=True)
    kept = jnp.where(section_index == section_count - 1, relaid, jnp.zeros_like(relaid))
    memory = lax.psum_scatter(kept, "section", scatter_dimension=0, tiled=True)

    input_grad, gain_part = finish(
        grad_own, from_before, from_after, stash[0], inverse_b, norm_gain, cotangent
    )
    bias_part = jnp.dot(
        offset_grad[:, 0, :], onehot, precision=lax.Precision.HIGHEST
    ).T
    bias_sum = lax.psum_scatter(
        bias_part.astype(BF16), "seq", scatter_dimension=0, tiled=True
    ).astype(F32)
    gain_sum = lax.psum_scatter(
        gain_part.astype(BF16), "seq", scatter_dimension=1, tiled=True
    ).astype(F32)
    return (output[None], input_grad[None], weight_sum[None], bias_sum[None], gain_sum, memory)


def solution(mesh):
    in_specs = (
        P("seq", None),
        P("section", "seq", None),
        P("section", "seq", None),
        P("section", "seq", None),
        P("seq", None),
        P("section", None, None, "seq", None),
        P("section", None, None),
        P("section", None),
        P(),
    )
    out_specs = (
        P("section", "seq", None),
        P("section", "seq", None),
        P("section", None, None, "seq", None),
        P("section", "seq", None),
        P("section", "seq"),
        P("section", "seq"),
    )
    return jax.shard_map(body, mesh=mesh, in_specs=in_specs, out_specs=out_specs, check_vma=False)
```

time: 428 us -> 276 us (0.64); the launches traced: 421 us -> 275 us
  local copies, waits for them, and re-layouts: 167 us -> 12.2 us
  Pallas kernels: 0 us -> 63.3 us
  waiting for transfers between devices: 131 us -> 82.5 us
  matrix products: 39.4 us -> 0.41 us
  blocking collectives: 15.8 us -> 50.5 us
  other arithmetic: 34.1 us -> 9.17 us
  starting transfers between devices: 18.2 us -> 41.9 us
    pallas_call x0 -> x6, Pallas kernels: none -> 63.3 us  [the longest x1 35.5 us: backward_attention(): pl.pallas_call(functools.partial(backward_kernel, slots, group), out_shap...]
    all_gather x1 -> x0, waiting for transfers between devices: 46.9 us -> none  [body(): weight = lax.all_gather(qkv_weight, 'seq', axis=3, tiled=True)[0]]
    dot_general x13 -> x2, matrix products: 39.4 us -> 0.41 us  [the longest x1 0.23 us: body(): by_offset = jnp.dot(onehot, rel_bias[0], precision=lax.Precision.HIGHEST).T]
    unnamed x1, blocking collectives: 15.8 us -> 50.5 us
    reshape x5 -> x0, local copies, waits for them, and re-layouts: 28.6 us -> none  [the longest x2 16.7 us: expand_bias(): skewed = skewed.reshape(head_count, block_rows, span_length - 1)]
    slice x10 -> x2, local copies, waits for them, and re-layouts: 29.7 us -> 2.29 us  [the longest x1 1.16 us: body(): after_b = lax.ppermute(own_b[:RADIUS], 'seq', down)]
    another operation x7 -> x0, local copies, waits for them, and re-layouts: 26.5 us -> none  [the longest x2 11.3 us: expand_bias(): repeated = jnp.tile(by_offset, (1, block_rows))]
    unnamed x63 -> x34, local copies, waits for them, and re-layouts: 34.7 us -> 8.92 us
  transfers between devices with their start and end apart: 11 -> 17, of which waited for: 7 -> 5; matrix products, arithmetic and copies ran while one was open for 41% -> 5% of each run, Pallas kernels for 0% -> 23%
where the time goes in v1:
time: 276 us; the launch traced here: 275 us
  waiting for transfers between devices  82.5 us (30%)
  Pallas kernels  63.3 us (23%)
  blocking collectives  50.5 us (18%)
  starting transfers between devices  41.9 us (15%)
  between operations  15 us (5%)
  local copies, waits for them, and re-layouts  12.2 us (4%)
  other arithmetic  9.17 us (3%)
    unnamed x1, blocking collectives  50.5 us
    pallas_call x1, Pallas kernels, backward_attention(): pl.pallas_call(functools.partial(backward_kernel, slots, group), out_shap...  35.5 us
    ppermute x3, waiting for transfers between devices, body(): lax.ppermute(shard, 'seq', [((i + r) % seq_count, i) for i in range(seq_c...  33.6 us
    reduce_scatter x1, waiting for transfers between devices, body(): memory = lax.psum_scatter(kept, 'section', scatter_dimension=0, tiled=True)  31.6 us
    pallas_call x1, Pallas kernels, forward_attention(): pl.pallas_call(functools.partial(forward_kernel, slots, group), out_shape...  23.2 us
    all_to_all x1, starting transfers between devices, body(): lax.all_to_all(final_normed, 'seq', split_axis=1, concat_axis=0, tiled=True)  13.5 us
    ppermute x1, waiting for transfers between devices, body(): from_after = lax.ppermute(lower, 'seq', down)  11.6 us
    unnamed x34, local copies, waits for them, and re-layouts  8.92 us
  transfers between devices with their start and end apart: 17, of which 5 were waited for; matrix products, arithmetic and copies ran while one was open for 5% of the time, Pallas kernels for 23%

profile of v1, /device:TPU:0, one launch (start us, length us, event | category | flops | bytes accessed | tf_op | source)
XLA Modules:
  0.0 274.9 jit_solution(17417402780131494312)
XLA Ops:
  7.2 0.0 copy-start
  7.2 2.2 bitcast_select_fusion.1
  9.4 0.5 collective-permute-start
  9.9 4.6 %collective-permute-start.3 = (bf16[3,24,32,128]{3,2,1,0:T(8,128)(2,1)}, bf16[3,24,32,128]{3,2,1,0:T(8,128)(2,1)}, u32[]{:S(2)}, u32[]{:S(2)}) collective-permute-start(bf16[3,24,32,128]{3,2,1,0:T(8,128)(2,1)} %bitcast.6.rest_0_), channel_id=1, source_target_pairs={{1,0},{2,1},{3,2},{0,3},{5,4},{6,5},{7,6},{4,7},{9,8},{10,9},{11,1... | collective-permute-start | bytes 1769480 | tf_op jit(solution)/shard_map/ppermute | solution.py:343
  14.5 0.0 collective-permute-start.4
  14.5 1.0 collective-permute-start.5
  15.5 0.4 norm_rows.4
  16.0 2.4 bitcast_select_fusion
  18.4 4.5 %collective-permute-done.x_ref = bf16[128,3072]{1,0:T(8,128)(2,1)S(1)} collective-permute-done((bf16[128,3072]{1,0:T(8,128)(2,1)}, bf16[128,3072]{1,0:T(8,128)(2,1)S(1)}, u32[]{:S(2)}, u32[]{:S(2)}) %collective-permute-start) | collective-permute-done | bytes 786464 | tf_op jit(solution)/shard_map/ppermute | solution.py:349
  22.9 0.9 norm_rows.3
  23.8 1.1 fusion.4
  25.0 4.8 %collective-permute-start.1 = (bf16[96,3072]{1,0:T(8,128)(2,1)}, bf16[96,3072]{1,0:T(8,128)(2,1)}, u32[]{:S(2)}, u32[]{:S(2)}) collective-permute-start(bf16[96,3072]{1,0:T(8,128)(2,1)} %get-tuple-element.49), channel_id=1, source_target_pairs={{0,1},{1,2},{2,3},{4,5},{5,6},{6,7},{8,9},{9,10},{10,11},{12,13},{... | collective-permute-start | bytes 1769480 | tf_op jit(solution)/shard_map/ppermute | solution.py:364
  29.8 1.3 collective-permute-start.2
  31.1 0.0 copy-start.13
  31.1 1.2 fusion.3
  32.3 0.0 collective-permute-done.3.rest_1_
  32.3 0.0 collective-permute-start.8
  32.3 33.6 %collective-permute-done.4.rest_2_ = bf16[3,24,32,128]{3,2,1,0:T(8,128)(2,1)} collective-permute-done((bf16[3,24,32,128]{3,2,1,0:T(8,128)(2,1)}, bf16[3,24,32,128]{3,2,1,0:T(8,128)(2,1)}, u32[]{:S(2)}, u32[]{:S(2)}) %collective-permute-start.4) | collective-permute-done | bytes 589856 | tf_op jit(solution)/shard_map/ppermute | solution.py:343
  65.9 2.1 collective-permute-start.6
  68.0 0.0 collective-permute-done.5.rest_3_
  68.0 1.3 collective-permute-start.7
  69.3 0.2 fusion
  69.5 0.1 pad_add_fusion.meta_ref
  69.6 0.0 collective-permute-done.1.before_ref
  69.6 0.0 collective-permute-done.2.after_ref
  69.6 23.2 %forward_attention.1.x_ref = bf16[128,3072]{1,0:T(8,128)(2,1)} custom-call(s32[3]{0:T(128)S(1)} %pad_add_fusion.meta_ref, bf16[96,3072]{1,0:T(8,128)(2,1)} %collective-permute-done.1.before_ref, bf16[128,3072]{1,0:T(8,128)(2,1)S(1)} %get-tuple-element.20.own_ref, bf16[96,3072]{1,0:T(8,128)(2,1)} %collective-permute-done.2.after_ref, ...), custom_call_target="tpu_custom_call" | custom-call | flops 1440000000 | bytes 3145728 | tf_op jit(solution)/shard_map/forward_attention/pallas_call | solution.py:148
  92.9 1.1 copy-done.2
  94.0 0.9 norm_rows.5
  94.9 0.9 copy.29
  95.9 13.5 %all-to-all-start = ((bf16[128,4,768]{2,0,1:T(8,128)(2,1)}), bf16[128,4,768]{2,0,1:T(8,128)(2,1)}, u32[]{:S(2)}, u32[]{:S(2)}) async-start(bf16[128,4,768]{2,0,1:T(8,128)(2,1)} %bitcast.40), calls=%async_computation | async-start | bytes 1572864 | tf_op jit(solution)/shard_map/all_to_all | solution.py:383
  109.4 0.0 collective-permute-done.7.after_ref
  109.4 0.0 collective-permute-done.8.cot_ref
  109.4 0.0 copy-start.5
  109.4 0.9 copy-done.5
  110.3 35.5 %backward_attention.1 = (f32[128,3072]{1,0:T(8,128)}, bf16[96,3072]{1,0:T(8,128)(2,1)S(1)}, bf16[96,3072]{1,0:T(8,128)(2,1)S(1)}, f32[24,1,256]{2,1,0:T(1,128)S(...) custom-call(s32[3]{0:T(128)S(1)} %pad_add_fusion.meta_ref, ...), custom_call_target="tpu_custom_call" | custom-call | flops 3600000000 | bytes 4718592 | tf_op jit(solution)/shard_map/backward_attention/pallas_call | solution.py:249
  145.8 0.8 copy-done.9
  146.6 1.3 collective-permute-start.10
  147.9 4.6 %collective-permute-start.9 = (bf16[96,3072]{1,0:T(8,128)(2,1)S(1)}, bf16[96,3072]{1,0:T(8,128)(2,1)S(1)}, u32[]{:S(2)}, u32[]{:S(2)}) collective-permute-start(bf16[96,3072]{1,0:T(8,128)(2,1)S(1)} %get-tuple-element.23), channel_id=1, source_target_pairs={{0,1},{1,2},{2,3},{4,5},{5,6},{6,7},{8,9},{9,10},{10,11},{12,13},{... | collective-permute-start | bytes 1769480 | tf_op jit(solution)/shard_map/ppermute | solution.py:370
  152.5 11.6 %collective-permute-done.10.high_ref = bf16[96,3072]{1,0:T(8,128)(2,1)S(1)} collective-permute-done((bf16[96,3072]{1,0:T(8,128)(2,1)S(1)}, bf16[96,3072]{1,0:T(8,128)(2,1)S(1)}, u32[]{:S(2)}, u32[]{:S(2)}) %collective-permute-start.10) | collective-permute-done | bytes 589856 | tf_op jit(solution)/shard_map/ppermute | solution.py:371
  164.1 1.2 collective-permute-done.9.low_ref
  165.3 1.4 copy-done.4
  166.7 1.1 copy-done.6
  167.8 2.2 finish.1
  170.0 1.2 copy.22
  171.3 0.0 reduce-scatter.8.cloned.1.call-update
  171.3 0.0 copy-start.14
  171.3 0.0 copy-start.11
  171.3 0.0 reduce-scatter.6.cloned.1.call-start
  171.4 1.0 broadcast_select_fusion
  172.3 0.0 reduce-scatter.6.cloned.1.call-update
  172.4 2.5 collective-permute-start.11
  174.9 3.3 %collective-permute-start.12 = (bf16[3,24,32,128]{3,2,1,0:T(8,128)(2,1)S(1)}, bf16[3,24,32,128]{3,2,1,0:T(8,128)(2,1)}, u32[]{:S(2)}, u32[]{:S(2)}) collective-permute-start(bf16[3,24,32,128]{3,2,1,0:T(8,128)(2,1)S(1)} %get-tuple-element.29), channel_id=1, source_target_pairs={{0,2},{1,3},{2,0},{3,1},{4,6},{5,7},{6,4},{7,5},{8,10},{9,11},{10,... | collective-permute-start | bytes 1769480 | tf_op jit(solution)/shard_map/ppermute | solution.py:375
  178.2 1.2 collective-permute-start.13
  179.4 0.6 dynamic-slice
  180.6 0.2 fusion.1
  180.8 50.5 %all-reduce = bf16[32,24]{0,1:T(8,128)(2,1)S(1)} all-reduce(bf16[32,24]{0,1:T(8,128)(2,1)S(1)} %fusion.1), channel_id=2, replica_groups=mesh['section'=8,'seq'=4] {'seq'}, use_global_device_ids=true, to_apply=%region_0.1.clone | all-reduce | flops 768 | bytes 3072
  231.3 0.1 bitcast_convert_fusion
  231.3 0.7 copy.19
  232.0 0.0 collective-permute-done.11
  232.0 0.0 collective-permute-done.12
  232.0 2.8 %add_bitcast_fusion = f32[1,3,24,32,128]{4,3,2,1,0:T(8,128)} fusion(bf16[3,24,32,128]{3,2,1,0:T(8,128)(2,1)} %collective-permute-done.13, bf16[3,24,32,128]{3,2,1,0:T(8,128)(2,1)} %collective-permute-done.12, f32[3,24,32,128]{3,2,1,0:T(8,128)S(1)} %copy-done.11, bf16[3,24,32,128]{3,2,1,0:T(8,128)(2,1)} %collective-permute-done.11), kind=kLoop, calls=%fused_computation | loop fusion | flops 1769472 | bytes 4128768 | tf_op jit(solution)/shard_map/broadcast_in_dim | solution.py:399
  234.8 1.0 copy.23
  235.9 0.6 convert_element_type.28
  236.5 31.6 %reduce-scatter.6.cloned.1.call-done = bf16[64,768]{1,0:T(8,128)(2,1)} async-done(((bf16[512,768]{1,0:T(8,128)(2,1)}), bf16[64,768]{1,0:T(8,128)(2,1)}) %reduce-scatter.6.cloned.1.call-update) | async-done | bytes 98320 | tf_op jit(solution)/shard_map/reduce_scatter | solution.py:385
  (28 shorter events, 0.1 us)
Async XLA Ops:
  7.2 62.1 %copy-start = (f32[1,32,24]{1,2,0:T(8,128)S(1)}, f32[1,32,24]{1,2,0:T(8,128)}, u32[]{:S(2)}) copy-start(f32[1,32,24]{1,2,0:T(8,128)} %param.16) | copy-start | bytes 9220
  7.2 8.3 %copy-start.1 = (bf16[1,128,3072]{2,1,0:T(8,128)(2,1)S(1)}, bf16[1,128,3072]{2,1,0:T(8,128)(2,1)}, u32[]{:S(2)}) copy-start(bf16[1,128,3072]{2,1,0:T(8,128)(2,1)} %param.12) | copy-start | bytes 2359300
  7.2 8.3 %copy-start.7 = (f32[1,3072]{1,0:T(1,128)S(1)}, f32[1,3072]{1,0:T(1,128)}, u32[]{:S(2)}) copy-start(f32[1,3072]{1,0:T(1,128)} %gain_ref.5) | copy-start | bytes 36868
  7.2 8.7 %copy-start.12 = (bf16[128,3072]{1,0:T(8,128)(2,1)S(1)}, bf16[128,3072]{1,0:T(8,128)(2,1)}, u32[]{:S(2)}) copy-start(bf16[128,3072]{1,0:T(8,128)(2,1)} %param.14) | copy-start | bytes 2359300
  9.4 13.5 %collective-permute-start = (bf16[128,3072]{1,0:T(8,128)(2,1)}, bf16[128,3072]{1,0:T(8,128)(2,1)S(1)}, u32[]{:S(2)}, u32[]{:S(2)}) collective-permute-start(bf16[128,3072]{1,0:T(8,128)(2,1)} %bitcast_select_fusion.1), channel_id=1, source_target_pairs={{0,4},{4,8},{8,12},{12,16},{16,20},{20,24},{24,28},{28,0},{1,5},{5... | collective-permute-start | bytes 2359304 | tf_op jit(solution)/shard_map/ppermute | solution.py:349
  9.9 22.4 %collective-permute-start.3 = (bf16[3,24,32,128]{3,2,1,0:T(8,128)(2,1)}, bf16[3,24,32,128]{3,2,1,0:T(8,128)(2,1)}, u32[]{:S(2)}, u32[]{:S(2)}) collective-permute-start(bf16[3,24,32,128]{3,2,1,0:T(8,128)(2,1)} %bitcast.6.rest_0_), channel_id=1, source_target_pairs={{1,0},{2,1},{3,2},{0,3},{5,4},{6,5},{7,6},{4,7},{9,8},{10,9},{11,1... | collective-permute-start | bytes 1769480 | tf_op jit(solution)/shard_map/ppermute | solution.py:343
  14.5 51.4 %collective-permute-start.4 = (bf16[3,24,32,128]{3,2,1,0:T(8,128)(2,1)}, bf16[3,24,32,128]{3,2,1,0:T(8,128)(2,1)}, u32[]{:S(2)}, u32[]{:S(2)}) collective-permute-start(bf16[3,24,32,128]{3,2,1,0:T(8,128)(2,1)} %bitcast.6.rest_0_), channel_id=1, source_target_pairs={{2,0},{3,1},{0,2},{1,3},{6,4},{7,5},{4,6},{5,7},{10,8},{11,9},{8,1... | collective-permute-start | bytes 1769480 | tf_op jit(solution)/shard_map/ppermute | solution.py:343
  14.5 53.5 %collective-permute-start.5 = (bf16[3,24,32,128]{3,2,1,0:T(8,128)(2,1)}, bf16[3,24,32,128]{3,2,1,0:T(8,128)(2,1)}, u32[]{:S(2)}, u32[]{:S(2)}) collective-permute-start(bf16[3,24,32,128]{3,2,1,0:T(8,128)(2,1)} %bitcast.6.rest_0_), channel_id=1, source_target_pairs={{3,0},{0,1},{1,2},{2,3},{7,4},{4,5},{5,6},{6,7},{11,8},{8,9},{9,10... | collective-permute-start | bytes 1769480 | tf_op jit(solution)/shard_map/ppermute | solution.py:343
  16.0 15.1 %copy-start.3 = (bf16[128,3072]{1,0:T(8,128)(2,1)}, bf16[128,3072]{1,0:T(8,128)(2,1)S(1)}, u32[]{:S(2)}) copy-start(bf16[128,3072]{1,0:T(8,128)(2,1)S(1)} %get-tuple-element.21.own_ref) | copy-start | bytes 2359300
  25.0 44.7 %collective-permute-start.1 = (bf16[96,3072]{1,0:T(8,128)(2,1)}, bf16[96,3072]{1,0:T(8,128)(2,1)}, u32[]{:S(2)}, u32[]{:S(2)}) collective-permute-start(bf16[96,3072]{1,0:T(8,128)(2,1)} %get-tuple-element.49), channel_id=1, source_target_pairs={{0,1},{1,2},{2,3},{4,5},{5,6},{6,7},{8,9},{9,10},{10,11},{12,13},{... | collective-permute-start | bytes 1769480 | tf_op jit(solution)/shard_map/ppermute | solution.py:364
  29.8 39.8 %collective-permute-start.2 = (bf16[96,3072]{1,0:T(8,128)(2,1)}, bf16[96,3072]{1,0:T(8,128)(2,1)}, u32[]{:S(2)}, u32[]{:S(2)}) collective-permute-start(bf16[96,3072]{1,0:T(8,128)(2,1)} %get-tuple-element.48), channel_id=1, source_target_pairs={{1,0},{2,1},{3,2},{5,4},{6,5},{7,6},{9,8},{10,9},{11,10},{13,12},{... | collective-permute-start | bytes 1769480 | tf_op jit(solution)/shard_map/ppermute | solution.py:365
  31.1 38.2 %copy-start.13 = (f32[256,32]{1,0:T(8,128)S(1)}, f32[256,32]{1,0:T(8,128)}, u32[]{:S(2)}) copy-start(f32[256,32]{1,0:T(8,128)} %constant.28.clone) | copy-start | bytes 98308
  32.3 77.1 %collective-permute-start.8 = (bf16[128,3072]{1,0:T(8,128)(2,1)}, bf16[128,3072]{1,0:T(8,128)(2,1)S(1)}, u32[]{:S(2)}, u32[]{:S(2)}) collective-permute-start(bf16[128,3072]{1,0:T(8,128)(2,1)} %bitcast_select_fusion), channel_id=1, source_target_pairs={{4,0},{8,4},{12,8},{16,12},{20,16},{24,20},{28,24},{0,28},{5,1},{9... | collective-permute-start | bytes 2359304 | tf_op jit(solution)/shard_map/ppermute | solution.py:352
  65.9 43.5 %collective-permute-start.6 = (bf16[96,3072]{1,0:T(8,128)(2,1)}, bf16[96,3072]{1,0:T(8,128)(2,1)}, u32[]{:S(2)}, u32[]{:S(2)}) collective-permute-start(bf16[96,3072]{1,0:T(8,128)(2,1)} %get-tuple-element.47), channel_id=1, source_target_pairs={{0,1},{1,2},{2,3},{4,5},{5,6},{6,7},{8,9},{9,10},{10,11},{12,13},{... | collective-permute-start | bytes 1769480 | tf_op jit(solution)/shard_map/ppermute | solution.py:338
  68.0 41.4 %collective-permute-start.7 = (bf16[96,3072]{1,0:T(8,128)(2,1)}, bf16[96,3072]{1,0:T(8,128)(2,1)}, u32[]{:S(2)}, u32[]{:S(2)}) collective-permute-start(bf16[96,3072]{1,0:T(8,128)(2,1)} %get-tuple-element.46), channel_id=1, source_target_pairs={{1,0},{2,1},{3,2},{5,4},{6,5},{7,6},{9,8},{10,9},{11,10},{13,12},{... | collective-permute-start | bytes 1769480 | tf_op jit(solution)/shard_map/ppermute | solution.py:339
  69.6 23.2 %copy-start.8 = (f32[3072]{0:T(1024)S(1)}, f32[3072]{0:T(1024)}, u32[]{:S(2)}) copy-start(f32[3072]{0:T(1024)} %param.18) | copy-start | bytes 36868
  92.9 1.1 copy-start.2
  95.9 75.5 %all-to-all-start = ((bf16[128,4,768]{2,0,1:T(8,128)(2,1)}), bf16[128,4,768]{2,0,1:T(8,128)(2,1)}, u32[]{:S(2)}, u32[]{:S(2)}) async-start(bf16[128,4,768]{2,0,1:T(8,128)(2,1)} %bitcast.40), calls=%async_computation | async-start | bytes 1572864 | tf_op jit(solution)/shard_map/all_to_all | solution.py:383
  109.4 125.5 %reduce-scatter.8.cloned.1.call-start = ((), (), s32[]{:S(2)}) async-start(), calls=%async_computation.4 | async-start | bytes 983040
  109.4 0.9 copy-start.5
  145.8 0.8 copy-start.9
  146.6 17.5 %collective-permute-start.10 = (bf16[96,3072]{1,0:T(8,128)(2,1)S(1)}, bf16[96,3072]{1,0:T(8,128)(2,1)S(1)}, u32[]{:S(2)}, u32[]{:S(2)}) collective-permute-start(bf16[96,3072]{1,0:T(8,128)(2,1)S(1)} %get-tuple-element.24), channel_id=1, source_target_pairs={{1,0},{2,1},{3,2},{5,4},{6,5},{7,6},{9,8},{10,9},{11,10},{13,12},{... | collective-permute-start | bytes 1769480 | tf_op jit(solution)/shard_map/ppermute | solution.py:371
  147.9 17.4 %collective-permute-start.9 = (bf16[96,3072]{1,0:T(8,128)(2,1)S(1)}, bf16[96,3072]{1,0:T(8,128)(2,1)S(1)}, u32[]{:S(2)}, u32[]{:S(2)}) collective-permute-start(bf16[96,3072]{1,0:T(8,128)(2,1)S(1)} %get-tuple-element.23), channel_id=1, source_target_pairs={{0,1},{1,2},{2,3},{4,5},{5,6},{6,7},{8,9},{9,10},{10,11},{12,13},{... | collective-permute-start | bytes 1769480 | tf_op jit(solution)/shard_map/ppermute | solution.py:370
  165.3 1.4 copy-start.4
  166.7 1.1 copy-start.6
  171.3 1.1 copy-start.10
  171.3 8.1 %copy-start.14 = (u32[32]{0:T(128)S(1)}, u32[32]{0:T(128)}, u32[]{:S(2)}) copy-start(u32[32]{0:T(128)} %constant.37) | copy-start | bytes 388
  171.3 60.7 %copy-start.11 = (f32[3,24,32,128]{3,2,1,0:T(8,128)S(1)}, f32[3,24,32,128]{3,2,1,0:T(8,128)}, u32[]{:S(2)}) copy-start(f32[3,24,32,128]{3,2,1,0:T(8,128)} %get-tuple-element.27) | copy-start | bytes 3538948
  171.3 96.7 %reduce-scatter.6.cloned.1.call-start = ((), (), s32[]{:S(2)}) async-start(), calls=%async_computation.3 | async-start | bytes 884736 | tf_op jit(solution)/shard_map/reduce_scatter | solution.py:385
  172.4 59.6 %collective-permute-start.11 = (bf16[3,24,32,128]{3,2,1,0:T(8,128)(2,1)S(1)}, bf16[3,24,32,128]{3,2,1,0:T(8,128)(2,1)}, u32[]{:S(2)}, u32[]{:S(2)}) collective-permute-start(bf16[3,24,32,128]{3,2,1,0:T(8,128)(2,1)S(1)} %copy-done.10), channel_id=1, source_target_pairs={{0,1},{1,2},{2,3},{3,0},{4,5},{5,6},{6,7},{7,4},{8,9},{9,10},{10,1... | collective-permute-start | bytes 1769480 | tf_op jit(solution)/shard_map/ppermute | solution.py:375
  174.9 57.1 %collective-permute-start.12 = (bf16[3,24,32,128]{3,2,1,0:T(8,128)(2,1)S(1)}, bf16[3,24,32,128]{3,2,1,0:T(8,128)(2,1)}, u32[]{:S(2)}, u32[]{:S(2)}) collective-permute-start(bf16[3,24,32,128]{3,2,1,0:T(8,128)(2,1)S(1)} %get-tuple-element.29), channel_id=1, source_target_pairs={{0,2},{1,3},{2,0},{3,1},{4,6},{5,7},{6,4},{7,5},{8,10},{9,11},{10,... | collective-permute-start | bytes 1769480 | tf_op jit(solution)/shard_map/ppermute | solution.py:375
  178.2 53.8 %collective-permute-start.13 = (bf16[3,24,32,128]{3,2,1,0:T(8,128)(2,1)S(1)}, bf16[3,24,32,128]{3,2,1,0:T(8,128)(2,1)}, u32[]{:S(2)}, u32[]{:S(2)}) collective-permute-start(bf16[3,24,32,128]{3,2,1,0:T(8,128)(2,1)S(1)} %get-tuple-element.30), channel_id=1, source_target_pairs={{0,3},{1,0},{2,1},{3,2},{4,7},{5,4},{6,5},{7,6},{8,11},{9,8},{10,9... | collective-permute-start | bytes 1769480 | tf_op jit(solution)/shard_map/ppermute | solution.py:375
Sparse Core Ops, SparseCore 0:
  171.4 58.3 reduce-scatter.7
  233.5 34.4 reduce-scatter.5

commit v2 on v1

--- a/solution.py
+++ b/solution.py
@@ -317,7 +317,534 @@
     )(grad, low, high, x, inverse, gain, cotangent)
 
 
-def body(
+def column_of(row, rows):
+    return jnp.transpose(jnp.broadcast_to(row, (128, rows)))
+
+
+def split_rows(inverse, pad_rows, width):
+    high = inverse.astype(BF16)
+    rest = inverse - high.astype(F32)
+    middle = rest.astype(BF16)
+    low = (rest - middle.astype(F32)).astype(BF16)
+    wide = [jnp.transpose(jnp.broadcast_to(v.astype(F32), (v.shape[0], 128)))[:1] for v in (high, middle, low)]
+    row = jnp.concatenate(wide + [jnp.zeros((pad_rows - 3, wide[0].shape[1]), F32)], axis=0)
+    return row.astype(BF16)
+
+
+def row_inverse(x):
+    x = x.astype(F32)
+    return lax.rsqrt(jnp.mean(x * x, axis=-1, keepdims=True) + eps_norm)
+
+
+def pack_stash_kernel(parts, meta_ref, x_ref, weight_ref, inverse_ref, *out_refs):
+    rows, width = x_ref.shape
+    depth = weight_ref.shape[2]
+    wide = width // parts
+    heads = wide // HEAD_DIM
+    inverse = row_inverse(x_ref[...])
+    inverse_ref[...] = jnp.broadcast_to(inverse, inverse_ref.shape)
+    tail = split_rows(inverse, 16, wide)
+    for r, out_ref in enumerate(out_refs):
+        target = lax.rem(meta_ref[0] + r, parts)
+        out_ref[:rows] = x_ref[:, pl.ds(pl.multiple_of(target * wide, 128), wide)]
+        for j in range(3):
+            for h in range(heads):
+                out_ref[rows + j * depth : rows + (j + 1) * depth, h * HEAD_DIM : (h + 1) * HEAD_DIM] = weight_ref[
+                    j, target * heads + h
+                ]
+        out_ref[rows + 3 * depth :] = jnp.zeros((16, wide), BF16)
+        out_ref[rows + 3 * depth :, :rows] = tail
+
+
+def pack_rows_kernel(parts, with_inverse, meta_ref, edge_ref, inner_ref, *out_refs):
+    rows, width = inner_ref.shape
+    wide = width // parts
+    edge = 2 if with_inverse else 1
+    refs = out_refs[:parts]
+    for r, out_ref in enumerate(refs):
+        target = lax.rem(meta_ref[0] + r, parts)
+        start = pl.multiple_of(target * wide, 128)
+
+        @pl.when(meta_ref[edge] == 1)
+        def use_edge():
+            out_ref[:rows] = edge_ref[:, pl.ds(start, wide)]
+
+        @pl.when(meta_ref[edge] == 0)
+        def use_inner():
+            out_ref[:rows] = inner_ref[:, pl.ds(start, wide)]
+
+    def finish_with(source_ref):
+        if with_inverse:
+            tail = split_rows(row_inverse(source_ref[...]), 16, wide)
+            for out_ref in refs:
+                out_ref[rows:] = jnp.zeros((16, wide), BF16)
+                out_ref[rows:, :rows] = tail
+        else:
+            out_refs[parts][...] = source_ref[...]
+
+    @pl.when(meta_ref[edge] == 1)
+    def finish_edge():
+        finish_with(edge_ref)
+
+    @pl.when(meta_ref[edge] == 0)
+    def finish_inner():
+        finish_with(inner_ref)
+
+
+SMEM_SPEC = pl.BlockSpec(memory_space=pltpu.SMEM)
+VMEM_SPEC = pl.BlockSpec(memory_space=pltpu.VMEM)
+
+
+def pack_stash(meta, x, weight, parts):
+    rows, width = x.shape
+    depth = weight.shape[2]
+    shape = (rows + 3 * depth + 16, width // parts)
+    return pl.pallas_call(
+        functools.partial(pack_stash_kernel, parts),
+        out_shape=(
+            jax.ShapeDtypeStruct((rows, 128), F32),
+            *[jax.ShapeDtypeStruct(shape, BF16) for r in range(parts)],
+        ),
+        in_specs=[SMEM_SPEC, VMEM_SPEC, VMEM_SPEC],
+        out_specs=(VMEM_SPEC,) * (parts + 1),
+        compiler_params=pltpu.CompilerParams(vmem_limit_bytes=VMEM_LIMIT),
+        cost_estimate=pl.CostEstimate(flops=4 * rows * width, bytes_accessed=6 * rows * width, transcendentals=0),
+        name="pack_stash",
+    )(meta, x, weight)
+
+
+def pack_rows(meta, edge, inner, parts, with_inverse):
+    rows, width = inner.shape
+    shape = (rows + (16 if with_inverse else 0), width // parts)
+    extra = () if with_inverse else (jax.ShapeDtypeStruct((rows, width), BF16),)
+    return pl.pallas_call(
+        functools.partial(pack_rows_kernel, parts, with_inverse),
+        out_shape=(*[jax.ShapeDtypeStruct(shape, BF16) for r in range(parts)], *extra),
+        in_specs=[SMEM_SPEC, VMEM_SPEC, VMEM_SPEC],
+        out_specs=(VMEM_SPEC,) * (parts + len(extra)),
+        compiler_params=pltpu.CompilerParams(vmem_limit_bytes=VMEM_LIMIT),
+        cost_estimate=pl.CostEstimate(flops=4 * rows * width, bytes_accessed=6 * rows * width, transcendentals=0),
+        name="pack_inbound" if with_inverse else "pack_cotangent",
+    )(meta, edge, inner)
+
+
+def gather_rows(meta_ref, refs, first, rows, inverse_ref, weight_refs, weight_first, x_ref, weight_ref):
+    parts = len(refs)
+    depth = HEAD_DIM // parts
+
+    @pl.when(pl.program_id(0) == 0)
+    def spread_inverse():
+        for r, ref in enumerate(refs):
+            source = lax.rem(meta_ref[0] + parts - r, parts)
+            rows_at = pl.ds(pl.multiple_of(source * rows, rows), rows)
+            tail = ref[first : first + 16].astype(F32)
+            inverse_ref[rows_at] = column_of(tail[:1] + tail[1:2] + tail[2:3], rows)
+
+    for r, ref in enumerate(refs):
+        source = lax.rem(meta_ref[0] + parts - r, parts)
+        x_ref[pl.ds(pl.multiple_of(source * rows, rows), rows)] = ref[:rows]
+        depth_at = pl.ds(pl.multiple_of(source * depth, depth), depth)
+        for j in range(3):
+            weight_ref[depth_at, j * HEAD_DIM : (j + 1) * HEAD_DIM] = weight_refs[r][
+                weight_first + j * depth : weight_first + (j + 1) * depth
+            ]
+
+
+def block_mask(first_query, tokens):
+    key = lax.broadcasted_iota(jnp.int32, (1, WINDOW), 1) + (first_query - RADIUS)
+    return jnp.where((key >= 0) & (key < tokens), 0.0, masked_score).astype(F32)
+
+
+def edge_bias(bias, first, tokens):
+    if first < RADIUS or first + ROW_BLOCK + RADIUS > tokens:
+        return bias + block_mask(first, tokens)
+    return bias
+
+
+def padded(rows):
+    edge = jnp.zeros((RADIUS, rows.shape[1]), rows.dtype)
+    return jnp.concatenate([edge, rows, edge], axis=0)
+
+
+def heads_backward_kernel(parts, rows, meta_ref, *refs):
+    a_refs, c_refs = refs[:parts], refs[parts : 2 * parts]
+    gain_ref, offset_ref, onehot_ref = refs[2 * parts : 2 * parts + 3]
+    out_refs = refs[2 * parts + 3 : 3 * parts + 3]
+    gain_grad_ref, inverse_ref, x_ref, weight_ref, cot_ref, grad_ref, part_ref, bias_ref = refs[3 * parts + 3 :]
+    tokens = rows * parts
+    depth = HEAD_DIM // parts
+    scale = HEAD_DIM ** (-0.5)
+    gather_rows(meta_ref, a_refs, rows + 3 * depth, rows, inverse_ref, a_refs, rows, x_ref, weight_ref)
+    for r in range(parts):
+        source = lax.rem(meta_ref[0] + parts - r, parts)
+        cot_ref[pl.ds(pl.multiple_of(source * rows, rows), rows)] = c_refs[r][...]
+    weight = weight_ref[...]
+    scaled_x = x_ref[...].astype(F32) * inverse_ref[...]
+    normed = (scaled_x * gain_ref[...]).astype(BF16)
+    query = dot_nn(normed, weight[:, :HEAD_DIM]).astype(BF16)
+    key = padded(dot_nn(normed, weight[:, HEAD_DIM : 2 * HEAD_DIM]).astype(BF16))
+    value = padded(dot_nn(normed, weight[:, 2 * HEAD_DIM :]).astype(BF16))
+    bias = toeplitz(offset_ref[0])
+    blocks = tokens // ROW_BLOCK
+    grad_query, grad_key, grad_value, score_sum = [], [], [], None
+    for b in range(blocks):
+        first = b * ROW_BLOCK
+        window = slice(first, first + WINDOW)
+        query_rows = query[first : first + ROW_BLOCK]
+        cot_rows = cot_ref[first : first + ROW_BLOCK]
+        probs = block_probs(query_rows, key[window], edge_bias(bias, first, tokens))
+        grad_probs = dot_nt(cot_rows, value[window])
+        delta = jnp.sum(probs * grad_probs, axis=-1, keepdims=True)
+        grad_scores = probs * (grad_probs - delta)
+        score_sum = grad_scores if score_sum is None else score_sum + grad_scores
+        grad_packed = grad_scores.astype(BF16)
+        grad_query.append(dot_nn(grad_packed, key[window]))
+        grad_key.append(dot_tn(grad_packed, query_rows))
+        grad_value.append(dot_tn(probs.astype(BF16), cot_rows))
+
+    def joined(pieces):
+        units = []
+        for u in range((tokens + 2 * RADIUS) // ROW_BLOCK):
+            total = None
+            for b in range(blocks):
+                if 0 <= u - b < WINDOW // ROW_BLOCK:
+                    piece = pieces[b][(u - b) * ROW_BLOCK : (u - b + 1) * ROW_BLOCK]
+                    total = piece if total is None else total + piece
+            units.append(total)
+        return jnp.concatenate(units, axis=0)[RADIUS : RADIUS + tokens]
+
+    dqkv = jnp.concatenate(
+        [
+            (jnp.concatenate(grad_query, axis=0) * scale).astype(BF16),
+            (joined(grad_key) * scale).astype(BF16),
+            joined(grad_value).astype(BF16),
+        ],
+        axis=1,
+    )
+    grad_normed = dot_nt(dqkv, weight)
+    gain_grad_ref[...] = jnp.sum(grad_normed * scaled_x, axis=0, keepdims=True)
+    grad_ref[...] = grad_normed
+    part_ref[...] = dot_tn(normed, dqkv)
+    bias_grad = jnp.sum(onehot_ref[...] * diagonal_sums(score_sum), axis=1, keepdims=True)
+    bias_ref[...] = jnp.broadcast_to(bias_grad, bias_ref.shape)
+    buckets = bias_ref.shape[0] // parts
+    for r, out_ref in enumerate(out_refs):
+        source = lax.rem(meta_ref[0] + parts - r, parts)
+        out_ref[:rows] = grad_ref[pl.ds(pl.multiple_of(source * rows, rows), rows)].astype(BF16)
+        for j in range(3):
+            out_ref[rows + j * depth : rows + (j + 1) * depth] = part_ref[
+                pl.ds(pl.multiple_of(source * depth, depth), depth), j * HEAD_DIM : (j + 1) * HEAD_DIM
+            ].astype(BF16)
+        share = bias_ref[pl.ds(pl.multiple_of(source * buckets, buckets), buckets)]
+        out_ref[rows + 3 * depth :] = jnp.concatenate(
+            [share, jnp.zeros((16 - buckets, HEAD_DIM), F32)], axis=0
+        ).astype(BF16)
+
+
+def head_column(rows):
+    return pl.BlockSpec((rows, HEAD_DIM), lambda i, meta: (0, i))
+
+
+def heads_backward(meta, a_slots, c_slots, gain, offsets, onehot, heads):
+    parts = len(a_slots)
+    rows = c_slots[0].shape[0]
+    tokens = rows * parts
+    buckets = onehot.shape[0]
+    packed = a_slots[0].shape[0]
+    width = heads * HEAD_DIM
+    return pl.pallas_call(
+        functools.partial(heads_backward_kernel, parts, rows),
+        out_shape=(
+            *[jax.ShapeDtypeStruct((packed, width), BF16) for r in range(parts)],
+            jax.ShapeDtypeStruct((1, width), F32),
+        ),
+        grid_spec=pltpu.PrefetchScalarGridSpec(
+            num_scalar_prefetch=1,
+            grid=(heads,),
+            in_specs=[
+                *[head_column(packed)] * parts,
+                *[head_column(rows)] * parts,
+                pl.BlockSpec((1, HEAD_DIM), lambda i, meta: (0, meta[0] * heads + i)),
+                pl.BlockSpec((1, 1, WINDOW), lambda i, meta: (meta[0] * heads + i, 0, 0)),
+                pl.BlockSpec((buckets, WINDOW), lambda i, meta: (0, 0)),
+            ],
+            out_specs=(*[head_column(packed)] * parts, head_column(1)),
+            scratch_shapes=[
+                pltpu.VMEM((tokens, HEAD_DIM), F32),
+                pltpu.VMEM((tokens, HEAD_DIM), BF16),
+                pltpu.VMEM((HEAD_DIM, 3 * HEAD_DIM), BF16),
+                pltpu.VMEM((tokens, HEAD_DIM), BF16),
+                pltpu.VMEM((tokens, HEAD_DIM), F32),
+                pltpu.VMEM((HEAD_DIM, 3 * HEAD_DIM), F32),
+                pltpu.VMEM((buckets, HEAD_DIM), F32),
+            ],
+        ),
+        compiler_params=pltpu.CompilerParams(vmem_limit_bytes=VMEM_LIMIT),
+        cost_estimate=pl.CostEstimate(
+            flops=heads * tokens * 4_000_000, bytes_accessed=6 * tokens * width, transcendentals=heads * tokens * WINDOW
+        ),
+        name="heads_backward",
+    )(meta, *a_slots, *c_slots, gain, offsets, onehot)
+
+
+def heads_forward_kernel(parts, rows, meta_ref, *refs):
+    a_refs, i_refs = refs[:parts], refs[parts : 2 * parts]
+    gain_ref, offset_ref = refs[2 * parts : 2 * parts + 2]
+    out_refs = refs[2 * parts + 2 : 3 * parts + 2]
+    sums_ref, inverse_ref, x_ref, weight_ref, made_ref, square_ref = refs[3 * parts + 2 :]
+    tokens = rows * parts
+    gather_rows(meta_ref, i_refs, rows, rows, inverse_ref, a_refs, rows, x_ref, weight_ref)
+    weight = weight_ref[...]
+    normed = (x_ref[...].astype(F32) * inverse_ref[...] * gain_ref[...]).astype(BF16)
+    query = dot_nn(normed, weight[:, :HEAD_DIM]).astype(BF16)
+    key = padded(dot_nn(normed, weight[:, HEAD_DIM : 2 * HEAD_DIM]).astype(BF16))
+    value = padded(dot_nn(normed, weight[:, 2 * HEAD_DIM :]).astype(BF16))
+    bias = toeplitz(offset_ref[0])
+    for b in range(tokens // ROW_BLOCK):
+        first = b * ROW_BLOCK
+        window = slice(first, first + WINDOW)
+        probs = block_probs(query[first : first + ROW_BLOCK], key[window], edge_bias(bias, first, tokens))
+        attended = dot_nn(probs.astype(BF16), value[window])
+        made_ref[first : first + ROW_BLOCK] = (
+            x_ref[first : first + ROW_BLOCK].astype(F32) + attended
+        ).astype(BF16)
+    made = made_ref[...].astype(F32)
+    squares = made * made
+
+    @pl.when(pl.program_id(0) == 0)
+    def first_head():
+        square_ref[...] = squares
+
+    @pl.when(pl.program_id(0) > 0)
+    def later_head():
+        square_ref[...] += squares
+
+    @pl.when(pl.program_id(0) == pl.num_programs(0) - 1)
+    def last_head():
+        total = jnp.sum(jnp.transpose(square_ref[...]), axis=0, keepdims=True)
+        sums_ref[...] = jnp.broadcast_to(total, sums_ref.shape)
+
+    for r, out_ref in enumerate(out_refs):
+        source = lax.rem(meta_ref[0] + parts - r, parts)
+        out_ref[...] = made_ref[pl.ds(pl.multiple_of(source * rows, rows), rows)]
+
+
+def heads_forward(meta, a_slots, i_slots, gain, offsets, heads, rows):
+    parts = len(a_slots)
+    tokens = rows * parts
+    packed = a_slots[0].shape[0]
+    width = heads * HEAD_DIM
+    return pl.pallas_call(
+        functools.partial(heads_forward_kernel, parts, rows),
+        out_shape=(
+            *[jax.ShapeDtypeStruct((rows, width), BF16) for r in range(parts)],
+            jax.ShapeDtypeStruct((8, tokens), F32),
+        ),
+        grid_spec=pltpu.PrefetchScalarGridSpec(
+            num_scalar_prefetch=1,
+            grid=(heads,),
+            in_specs=[
+                *[head_column(packed)] * parts,
+                *[head_column(i_slots[0].shape[0])] * parts,
+                pl.BlockSpec((1, HEAD_DIM), lambda i, meta: (0, meta[0] * heads + i)),
+                pl.BlockSpec((1, 1, WINDOW), lambda i, meta: (meta[0] * heads + i, 0, 0)),
+            ],
+            out_specs=(
+                *[head_column(rows)] * parts,
+                pl.BlockSpec((8, tokens), lambda i, meta: (0, 0)),
+            ),
+            scratch_shapes=[
+                pltpu.VMEM((tokens, HEAD_DIM), F32),
+                pltpu.VMEM((tokens, HEAD_DIM), BF16),
+                pltpu.VMEM((HEAD_DIM, 3 * HEAD_DIM), BF16),
+                pltpu.VMEM((tokens, HEAD_DIM), BF16),
+                pltpu.VMEM((tokens, HEAD_DIM), F32),
+            ],
+        ),
+        compiler_params=pltpu.CompilerParams(vmem_limit_bytes=VMEM_LIMIT),
+        cost_estimate=pl.CostEstimate(
+            flops=heads * tokens * 2_000_000, bytes_accessed=6 * tokens * width, transcendentals=heads * tokens * WINDOW
+        ),
+        name="heads_forward",
+    )(meta, *a_slots, *i_slots, gain, offsets)
+
+
+def memory_kernel(parts, width, meta_ref, *refs):
+    out_refs, sum_refs = refs[:parts], refs[parts : 2 * parts]
+    gain_ref, memory_ref = refs[2 * parts :]
+    rows = out_refs[0].shape[0]
+    wide = memory_ref.shape[1]
+    total = sum_refs[0][:1]
+    for sum_ref in sum_refs[1:]:
+        total = total + sum_ref[:1]
+    inverse = lax.rsqrt(total / width + eps_norm)
+    gain = gain_ref[:, pl.ds(pl.multiple_of(meta_ref[0] * wide, 128), wide)]
+    spread_inverse = jnp.transpose(jnp.broadcast_to(inverse, (128, inverse.shape[1])))
+    for r, out_ref in enumerate(out_refs):
+        source = lax.rem(meta_ref[0] + parts - r, parts)
+        memory_ref[pl.ds(pl.multiple_of(source * rows, rows), rows)] = out_ref[...]
+    made = memory_ref[...].astype(F32)
+    memory_ref[...] = (made * spread_inverse[:, :1] * gain).astype(BF16)
+
+
+def memory_rows(meta, outs, sums, gain, width):
+    parts = len(outs)
+    rows, wide = outs[0].shape
+    return pl.pallas_call(
+        functools.partial(memory_kernel, parts, width),
+        out_shape=jax.ShapeDtypeStruct((rows * parts, wide), BF16),
+        in_specs=[SMEM_SPEC] + [VMEM_SPEC] * (2 * parts + 1),
+        out_specs=VMEM_SPEC,
+        compiler_params=pltpu.CompilerParams(vmem_limit_bytes=VMEM_LIMIT),
+        cost_estimate=pl.CostEstimate(flops=4 * rows * width, bytes_accessed=4 * rows * width, transcendentals=0),
+        name="memory_rows",
+    )(meta, *outs, *sums, gain)
+
+
+def place_kernel(parts, meta_ref, *refs):
+    out_ref = refs[parts]
+    wide = refs[0].shape[1]
+    for r in range(parts):
+        source = lax.rem(meta_ref[0] + r, parts)
+        out_ref[:, pl.ds(pl.multiple_of(source * wide, 128), wide)] = refs[r][...]
+
+
+def place_columns(meta, slots):
+    parts = len(slots)
+    rows, wide = slots[0].shape
+    return pl.pallas_call(
+        functools.partial(place_kernel, parts),
+        out_shape=jax.ShapeDtypeStruct((rows, wide * parts), BF16),
+        in_specs=[SMEM_SPEC] + [VMEM_SPEC] * parts,
+        out_specs=VMEM_SPEC,
+        compiler_params=pltpu.CompilerParams(vmem_limit_bytes=VMEM_LIMIT),
+        cost_estimate=pl.CostEstimate(flops=0, bytes_accessed=4 * rows * wide * parts, transcendentals=0),
+        name="place_columns",
+    )(meta, *slots)
+
+
+def heads_finish_kernel(parts, meta_ref, *refs):
+    g_refs = refs[:parts]
+    x_ref, inverse_ref, gain_ref, cot_ref, out_ref, weight_ref, bias_ref, scaled_ref = refs[parts:]
+    rows, width = x_ref.shape
+    wide = width // parts
+    heads = wide // HEAD_DIM
+    depth = HEAD_DIM // parts
+    buckets = bias_ref.shape[1]
+    for r in range(parts):
+        source = lax.rem(meta_ref[0] + r, parts)
+        columns = pl.ds(pl.multiple_of(source * wide, 128), wide)
+        scaled_ref[:, columns] = g_refs[r][:rows].astype(F32) * gain_ref[:, columns]
+        for h in range(heads):
+            lanes = slice(h * HEAD_DIM, (h + 1) * HEAD_DIM)
+            for j in range(3):
+                weight_ref[j, source * heads + h] = g_refs[r][
+                    rows + j * depth : rows + (j + 1) * depth, lanes
+                ].astype(F32)
+            bias_ref[source * heads + h] = g_refs[r][rows + 3 * depth :, lanes].astype(F32)[:buckets]
+    x = x_ref[...].astype(F32)
+    scaled = scaled_ref[...]
+    inverse = inverse_ref[:, :1]
+    mean = jnp.mean(scaled * x, axis=-1, keepdims=True)
+    result = inverse * scaled - x * (inverse * inverse * inverse * mean)
+    out_ref[...] = (cot_ref[...].astype(F32) + result).astype(BF16)
+
+
+def heads_finish(meta, g_slots, x, inverse, gain, cotangent, buckets):
+    parts = len(g_slots)
+    rows, width = x.shape
+    heads = width // HEAD_DIM
+    return pl.pallas_call(
+        functools.partial(heads_finish_kernel, parts),
+        out_shape=(
+            jax.ShapeDtypeStruct((rows, width), BF16),
+            jax.ShapeDtypeStruct((3, heads, HEAD_DIM // parts, HEAD_DIM), F32),
+            jax.ShapeDtypeStruct((heads, buckets // parts, HEAD_DIM), F32),
+        ),
+        in_specs=[SMEM_SPEC] + [VMEM_SPEC] * (parts + 4),
+        out_specs=(VMEM_SPEC,) * 3,
+        scratch_shapes=[pltpu.VMEM((rows, width), F32)],
+        compiler_params=pltpu.CompilerParams(vmem_limit_bytes=VMEM_LIMIT),
+        cost_estimate=pl.CostEstimate(flops=12 * rows * width, bytes_accessed=14 * rows * width, transcendentals=0),
+        name="heads_finish",
+    )(meta, *g_slots, x, inverse, gain, cotangent)
+
+
+def offset_table(rel_bias):
+    onehot = jnp.asarray(bucket_onehot(rel_bias.shape[0]))
+    by_offset = jnp.dot(onehot, rel_bias, precision=lax.Precision.HIGHEST).T
+    inside = jnp.arange(WINDOW, dtype=jnp.int32) <= 2 * RADIUS
+    return jnp.where(inside[None, :], by_offset, masked_score)[:, None, :]
+
+
+def heads_body(
+    embedded, carried, stash, returned, loss_grad, qkv_weight, rel_bias, norm_gain, final_gain
+):
+    section = lax.axis_index("section")
+    sections = lax.axis_size("section")
+    parts = lax.axis_size("seq")
+    rows, width = embedded.shape
+    heads = width // HEAD_DIM // parts
+    buckets = rel_bias.shape[1]
+    meta = jnp.stack(
+        [lax.axis_index("seq"), section == 0, section == sections - 1]
+    ).astype(jnp.int32)
+
+    def shifted(value, r, step):
+        if step == 0:
+            return lax.ppermute(value, "seq", [(i, (i + r) % parts) for i in range(parts)])
+        pairs = [
+            (s * parts + i, (s + step) % sections * parts + (i + r) % parts)
+            for s in range(sections)
+            for i in range(parts)
+        ]
+        return lax.ppermute(value, ("section", "seq"), pairs)
+
+    def returned_to(value, r):
+        return lax.ppermute(value, "seq", [(i, (i - r) % parts) for i in range(parts)])
+
+    inverse_b, *a_sends = pack_stash(meta, stash[0], qkv_weight[0], parts)
+    a_slots = [a_sends[0]] + [shifted(a_sends[r], r, 0) for r in range(1, parts)]
+    *c_sends, cot_source = pack_rows(meta, loss_grad, returned[0], parts, False)
+    c_slots = [shifted(c_sends[r], r, -1) for r in range(parts)]
+    cotangent = lax.ppermute(
+        cot_source, "section", [((s + 1) % sections, s) for s in range(sections)]
+    )
+    i_sends = pack_rows(meta, embedded, carried[0], parts, True)
+    i_slots = [shifted(i_sends[r], r, 1) for r in range(parts)]
+
+    offsets = offset_table(rel_bias[0])
+    onehot = jnp.asarray(bucket_onehot(buckets).T)
+    *g_sends, gain_grad = heads_backward(meta, a_slots, c_slots, norm_gain, offsets, onehot, heads)
+    g_slots = [g_sends[0]] + [returned_to(g_sends[r], r) for r in range(1, parts)]
+
+    *o_sends, sums = heads_forward(meta, a_slots, i_slots, norm_gain, offsets, heads, rows)
+    o_slots = [o_sends[0]] + [returned_to(o_sends[r], r) for r in range(1, parts)]
+    all_sums = [sums] + [shifted(sums, r, 0) for r in range(1, parts)]
+    made = memory_rows(meta, o_sends, all_sums, final_gain[None], width)
+    share = rows * parts // sections
+    memory = jnp.where(section == sections - 1, made[(sections - 1) * share :], 0)
+    for s in range(sections - 1):
+        memory = memory + lax.ppermute(
+            made[s * share : (s + 1) * share], "section", [(sections - 1, s)]
+        )
+
+    input_grad, weight_grad, bias_wide = heads_finish(
+        meta, g_slots, stash[0], inverse_b, norm_gain, cotangent, buckets
+    )
+    bias_grad = bias_wide[:, :, 0].T
+    output = place_columns(meta, o_slots)
+    return (
+        output[None],
+        input_grad[None],
+        weight_grad[None],
+        bias_grad[None],
+        gain_grad,
+        memory.astype(BF16),
+    )
+
+
+def tokens_body(
     embedded, carried, stash, returned, loss_grad, qkv_weight, rel_bias, norm_gain, final_gain
 ):
     section_index = lax.axis_index("section")
@@ -328,8 +855,6 @@
     heads = width // HEAD_DIM
     tokens = rows * seq_count
     shard = qkv_weight[0]
-    depth = shard.shape[2]
-    by_slots = seq_count <= 4 and depth % 32 == 0
     up = [(i, i + 1) for i in range(seq_count - 1)]
     down = [(j, i) for i, j in up]
     group = 4 if heads % 4 == 0 else 1
@@ -337,12 +862,7 @@
     own_b, inverse_b = norm_rows(stash[0], norm_gain)
     before_b = lax.ppermute(own_b[rows - RADIUS :], "seq", up)
     after_b = lax.ppermute(own_b[:RADIUS], "seq", down)
-    if by_slots:
-        slots = [shard]
-        for r in range(1, seq_count):
-            slots.append(lax.ppermute(shard, "seq", [((i + r) % seq_count, i) for i in range(seq_count)]))
-    else:
-        slots = [lax.all_gather(shard, "seq", axis=2, tiled=True)]
+    slots = [lax.all_gather(shard, "seq", axis=2, tiled=True)]
 
     section_up = [(i, (i + 1) % section_count) for i in range(section_count)]
     section_down = [(j, i) for i, j in section_up]
@@ -354,9 +874,7 @@
     )
 
     onehot = jnp.asarray(bucket_onehot(rel_bias.shape[1]))
-    by_offset = jnp.dot(onehot, rel_bias[0], precision=lax.Precision.HIGHEST).T
-    inside = jnp.arange(WINDOW, dtype=jnp.int32) <= 2 * RADIUS
-    offsets = jnp.where(inside[None, :], by_offset, masked_score)[:, None, :]
+    offsets = offset_table(rel_bias[0])
     first_key = RADIUS - seq_index * rows
     meta = jnp.stack([seq_index, first_key, first_key + tokens]).astype(jnp.int32)
 
@@ -369,14 +887,7 @@
     )
     from_before = lax.ppermute(upper, "seq", up)
     from_after = lax.ppermute(lower, "seq", down)
-    if by_slots:
-        weight_sum = parts[0]
-        for r in range(1, seq_count):
-            weight_sum = weight_sum + lax.ppermute(
-                parts[r], "seq", [(i, (i + r) % seq_count) for i in range(seq_count)]
-            ).astype(F32)
-    else:
-        weight_sum = lax.psum_scatter(parts[0], "seq", scatter_dimension=2, tiled=True).astype(F32)
+    weight_sum = lax.psum_scatter(parts[0], "seq", scatter_dimension=2, tiled=True).astype(F32)
 
     output = forward_attention(meta, before_a, own_a, after_a, inbound, offsets, slots, group)
     final_normed, unused = norm_rows(output, final_gain[None])
@@ -397,6 +908,17 @@
         gain_part.astype(BF16), "seq", scatter_dimension=1, tiled=True
     ).astype(F32)
     return (output[None], input_grad[None], weight_sum[None], bias_sum[None], gain_sum, memory)
+
+
+def choose_body(embedded, carried, stash, returned, loss_grad, qkv_weight, rel_bias, norm_gain, final_gain):
+    parts = lax.axis_size("seq")
+    rows, width = embedded.shape
+    even = width % (HEAD_DIM * parts) == 0 and HEAD_DIM % (32 * parts) == 0 and rows == 128
+    even = even and rel_bias.shape[1] == 8 * parts and rows * parts % (16 * lax.axis_size("section")) == 0
+    chosen = heads_body if even else tokens_body
+    return chosen(
+        embedded, carried, stash, returned, loss_grad, qkv_weight, rel_bias, norm_gain, final_gain
+    )
 
 
 def solution(mesh):
@@ -419,4 +941,4 @@
         P("section", "seq"),
         P("section", "seq"),
     )
-    return jax.shard_map(body, mesh=mesh, in_specs=in_specs, out_specs=out_specs, check_vma=False)
+    return jax.shard_map(choose_body, mesh=mesh, in_specs=in_specs, out_specs=out_specs, check_vma=False)

time: 276 us -> 181 us (0.66)
  blocking collectives: 50.5 us -> 0 us
  between operations: 15 us -> 0.91 us
  Pallas kernels: 63.3 us -> 53.1 us
  local copies, waits for them, and re-layouts: 12.2 us -> 3.16 us
  other arithmetic: 9.17 us -> 0.77 us
  waiting for transfers between devices: 82.5 us -> 78.4 us
    unnamed x1 -> x0, blocking collectives: 50.5 us -> none
    reduce_scatter x1 -> x0, waiting for transfers between devices: 31.6 us -> none  [body(): memory = lax.psum_scatter(kept, 'section', scatter_dimension=0, tiled=True)]
    ppermute x14 -> x28, waiting for transfers between devices: 50.9 us -> 78.4 us  [the longest x8 50.4 us: shifted(): return lax.ppermute(value, ('section', 'seq'), pairs)]
    ppermute x14 -> x28, starting transfers between devices: 28.4 us -> 43.4 us  [the longest x6 12.4 us: shifted(): lax.ppermute(value, 'seq', [(i, (i + r) % parts) for i in range(parts)])]
    all_to_all x1 -> x0, starting transfers between devices: 13.5 us -> none  [body(): lax.all_to_all(final_normed, 'seq', split_axis=1, concat_axis=0, tiled=True)]
    pallas_call x6 -> x8, Pallas kernels: 63.3 us -> 53.1 us  [the longest x1 27.3 us: heads_backward(): pl.pallas_call(functools.partial(heads_backward_kernel, parts, rows), out...]
    unnamed x34 -> x22, local copies, waits for them, and re-layouts: 8.92 us -> 2.37 us
    select_n x3 -> x0, other arithmetic: 5.58 us -> none  [the longest x1 2.38 us: body(): jnp.where(section_index == 0, loss_grad, returned[0])]
  transfers between devices with their start and end apart: 17 -> 28, of which waited for: 5 -> 5; matrix products, arithmetic and copies ran while one was open for 5% -> 1% of each run, Pallas kernels for 23% -> 17%
where the time goes in v2:
time: 181 us; the launch traced here: 180 us
  waiting for transfers between devices  78.4 us (43%)
  Pallas kernels  53.1 us (29%)
  starting transfers between devices  43.4 us (24%)
  local copies, waits for them, and re-layouts  3.16 us (2%)
    ppermute x8, waiting for transfers between devices, shifted(): return lax.ppermute(value, ('section', 'seq'), pairs)  50.4 us
    ppermute x6, waiting for transfers between devices, returned_to(): lax.ppermute(value, 'seq', [(i, (i - r) % parts) for i in range(parts)])  28 us
    pallas_call x1, Pallas kernels, heads_backward(): pl.pallas_call(functools.partial(heads_backward_kernel, parts, rows), out...  27.3 us
    pallas_call x1, Pallas kernels, heads_forward(): pl.pallas_call(functools.partial(heads_forward_kernel, parts, rows), out_...  18.3 us
    ppermute x6, starting transfers between devices, shifted(): lax.ppermute(value, 'seq', [(i, (i + r) % parts) for i in range(parts)])  12.4 us
    ppermute x8, starting transfers between devices, shifted(): return lax.ppermute(value, ('section', 'seq'), pairs)  11.3 us
    ppermute x6, starting transfers between devices, returned_to(): lax.ppermute(value, 'seq', [(i, (i - r) % parts) for i in range(parts)])  9.78 us
    ppermute x7, starting transfers between devices, heads_body(): lax.ppermute(made[s * share:(s + 1) * share], 'section', [(sections - 1,...  5.27 us
  transfers between devices with their start and end apart: 28, of which 5 were waited for; matrix products, arithmetic and copies ran while one was open for 1% of the time, Pallas kernels for 17%

profile of v2, /device:TPU:0, one launch (start us, length us, event | category | flops | bytes accessed | tf_op | source)
XLA Modules:
  0.0 179.9 jit_solution(16020251356788202428)
XLA Ops:
  0.6 0.0 copy-start
  0.7 0.1 pad_add_fusion.meta_ref
  0.7 1.2 copy-done.2
  1.9 1.1 copy-done.3
  3.1 0.9 pack_inbound.1
  4.0 0.5 collective-permute-start.3
  4.5 3.8 %collective-permute-start.4 = (bf16[144,768]{1,0:T(8,128)(2,1)S(1)}, bf16[144,768]{1,0:T(8,128)(2,1)S(1)}, u32[]{:S(2)}, u32[]{:S(2)}) collective-permute-start(bf16[144,768]{1,0:T(8,128)(2,1)S(1)} %get-tuple-element.38), channel_id=1, source_target_pairs={{0,5},{1,6},{2,7},{3,4},{4,9},{5,10},{6,11},{7,8},{8,13},{9,14},{1... | collective-permute-start | bytes 663560 | tf_op jit(solution)/shard_map/ppermute | solution.py:801
  8.3 0.9 pack_stash.1
  9.2 1.6 collective-permute-start
  10.8 1.2 collective-permute-start.1
  12.1 2.7 %collective-permute-start.2 = (bf16[240,768]{1,0:T(8,128)(2,1)S(1)}, bf16[240,768]{1,0:T(8,128)(2,1)S(1)}, u32[]{:S(2)}, u32[]{:S(2)}) collective-permute-start(bf16[240,768]{1,0:T(8,128)(2,1)S(1)} %get-tuple-element.36), channel_id=1, source_target_pairs={{0,3},{1,0},{2,1},{3,2},{4,7},{5,4},{6,5},{7,6},{8,11},{9,8},{10,9... | collective-permute-start | bytes 1105928 | tf_op jit(solution)/shard_map/ppermute | solution.py:795
  14.8 0.0 collective-permute-done.3.refs_4_
  14.8 0.0 collective-permute-start.5
  14.8 2.4 %collective-permute-done.4.refs_5_ = bf16[144,768]{1,0:T(8,128)(2,1)S(1)} collective-permute-done((bf16[144,768]{1,0:T(8,128)(2,1)S(1)}, bf16[144,768]{1,0:T(8,128)(2,1)S(1)}, u32[]{:S(2)}, u32[]{:S(2)}) %collective-permute-start.4) | collective-permute-done | bytes 221216 | tf_op jit(solution)/shard_map/ppermute | solution.py:801
  17.2 0.8 collective-permute-start.6
  18.0 0.2 fusion
  18.3 40.0 %collective-permute-done.5.refs_6_ = bf16[144,768]{1,0:T(8,128)(2,1)S(1)} collective-permute-done((bf16[144,768]{1,0:T(8,128)(2,1)S(1)}, bf16[144,768]{1,0:T(8,128)(2,1)S(1)}, u32[]{:S(2)}, u32[]{:S(2)}) %collective-permute-start.5) | collective-permute-done | bytes 221216 | tf_op jit(solution)/shard_map/ppermute | solution.py:801
  58.2 0.0 collective-permute-done.6.refs_7_
  58.2 0.0 collective-permute-done.refs_1_
  58.2 0.0 collective-permute-done.1.refs_2_
  58.3 0.0 collective-permute-done.2.refs_3_
  58.3 0.0 copy-start.4
  58.3 0.0 copy-start.5
  58.3 18.3 %heads_forward.1 = (bf16[128,768]{1,0:T(8,128)(2,1)S(1)}, bf16[128,768]{1,0:T(8,128)(2,1)S(1)}, bf16[128,768]{1,0:T(8,128)(2,1)S(1)}, bf16[128,768]{1,0:T(8,128)(2,1)S(1)}, f32[8,512]{1,0:T(8,128)S(1)}) custom-call(s32[3]{0:T(128)S(1)} %pad_add_fusion.meta_ref, bf16[240,768]{1,0:T(8,128)(2,1)S(1)} %get-tuple-element.33.refs_0_, ...), custom_call_target="tpu_custom_call" | custom-call | flops 6144000000 | bytes 2359296 | tf_op jit(solution)/shard_map/heads_forward/pallas_call | solution.py:637
  76.6 0.0 copy-start.7
  76.6 5.5 %collective-permute-start.20 = (f32[8,512]{1,0:T(8,128)S(1)}, f32[8,512]{1,0:T(8,128)S(1)}, u32[]{:S(2)}, u32[]{:S(2)}) collective-permute-start(f32[8,512]{1,0:T(8,128)S(1)} %get-tuple-element.59.refs_4_), channel_id=1, source_target_pairs={{0,3},{1,0},{2,1},{3,2},{4,7},{5,4},{6,5},{7,6},{8,11},{9,8},{10,9... | collective-permute-start | bytes 49160 | tf_op jit(solution)/shard_map/ppermute | solution.py:795
  82.1 1.4 collective-permute-start.19
  83.4 0.0 collective-permute-start.18
  83.4 0.7 pack_cotangent.1
  84.2 0.1 collective-permute-start.10
  84.2 3.2 %collective-permute-start.11 = (bf16[128,768]{1,0:T(8,128)(2,1)S(1)}, bf16[128,768]{1,0:T(8,128)(2,1)S(1)}, u32[]{:S(2)}, u32[]{:S(2)}) collective-permute-start(bf16[128,768]{1,0:T(8,128)(2,1)S(1)} %get-tuple-element.46), channel_id=1, source_target_pairs={{0,29},{1,30},{2,31},{3,28},{4,1},{5,2},{6,3},{7,0},{8,5},{9,6},{1... | collective-permute-start | bytes 589832 | tf_op jit(solution)/shard_map/ppermute | solution.py:801
  87.4 0.0 collective-permute-done.20.refs_7_
  87.4 1.9 %collective-permute-start.12 = (bf16[128,768]{1,0:T(8,128)(2,1)S(1)}, bf16[128,768]{1,0:T(8,128)(2,1)S(1)}, u32[]{:S(2)}, u32[]{:S(2)}) collective-permute-start(bf16[128,768]{1,0:T(8,128)(2,1)S(1)} %get-tuple-element.47), channel_id=1, source_target_pairs={{0,30},{1,31},{2,28},{3,29},{4,2},{5,3},{6,0},{7,1},{8,6},{9,7},{1... | collective-permute-start | bytes 589832 | tf_op jit(solution)/shard_map/ppermute | solution.py:801
  89.4 0.0 collective-permute-done.19.refs_6_
  89.4 1.0 collective-permute-start.13
  90.4 0.0 collective-permute-done.18.refs_5_
  90.4 0.9 memory_rows.1
  91.4 1.3 collective-permute-start.21
  92.7 0.0 collective-permute-done.10.refs_4_
  92.7 0.7 collective-permute-start.27
  93.4 0.0 collective-permute-done.11.refs_5_
  93.4 0.7 collective-permute-start.26
  94.0 8.0 %collective-permute-done.12.refs_6_ = bf16[128,768]{1,0:T(8,128)(2,1)S(1)} collective-permute-done((bf16[128,768]{1,0:T(8,128)(2,1)S(1)}, bf16[128,768]{1,0:T(8,128)(2,1)S(1)}, u32[]{:S(2)}, u32[]{:S(2)}) %collective-permute-start.12) | collective-permute-done | bytes 196640 | tf_op jit(solution)/shard_map/ppermute | solution.py:801
  102.0 0.7 collective-permute-start.25
  102.7 0.0 collective-permute-done.13.refs_7_
  102.7 0.7 collective-permute-start.24
  103.4 4.6 %collective-permute-start.17 = (bf16[128,3072]{1,0:T(8,128)(2,1)S(1)}, bf16[128,3072]{1,0:T(8,128)(2,1)S(1)}, u32[]{:S(2)}, u32[]{:S(2)}) collective-permute-start(bf16[128,3072]{1,0:T(8,128)(2,1)S(1)} %get-tuple-element.54), channel_id=1, source_target_pairs={{4,0},{8,4},{12,8},{16,12},{20,16},{24,20},{28,24},{0,28},{5,1},{9... | collective-permute-start | bytes 2359304 | tf_op jit(solution)/shard_map/ppermute | solution.py:810
  108.0 4.6 %collective-permute-start.7 = (bf16[128,768]{1,0:T(8,128)(2,1)S(1)}, bf16[128,768]{1,0:T(8,128)(2,1)S(1)}, u32[]{:S(2)}, u32[]{:S(2)}) collective-permute-start(bf16[128,768]{1,0:T(8,128)(2,1)S(1)} %get-tuple-element.42.refs_1_), channel_id=1, source_target_pairs={{0,3},{1,0},{2,1},{3,2},{4,7},{5,4},{6,5},{7,6},{8,11},{9,8},{10,9... | collective-permute-start | bytes 589832 | tf_op jit(solution)/shard_map/ppermute | solution.py:804
  112.6 0.0 collective-permute-done.26
  112.6 0.7 collective-permute-start.8
  113.3 0.7 collective-permute-start.23
  114.0 0.7 collective-permute-start.22
  114.7 27.3 %heads_backward.1 = (bf16[240,768]{1,0:T(8,128)(2,1)S(1)}, bf16[240,768]{1,0:T(8,128)(2,1)S(1)}, bf16[240,768]{1,0:T(8,128)(2,1)S(1)}, bf16[240,768]{1,0:T(8,128)(2,1)S(1)}, f32[1,768]{1,0:T(1,128)}) custom-call(s32[3]{0:T(128)S(1)} %pad_add_fusion.meta_ref, bf16[240,768]{1,0:T(8,128)(2,1)S(1)} %get-tuple-element.33.refs_0_, ...), custom_call_target="tpu_custom_call" | custom-call | flops 12288000000 | bytes 2359296 | tf_op jit(solution)/shard_map/heads_backward/pallas_call | solution.py:555
  141.9 1.0 collective-permute-start.14
  142.9 1.3 collective-permute-start.15
  144.2 2.0 %collective-permute-start.16 = (bf16[240,768]{1,0:T(8,128)(2,1)S(1)}, bf16[240,768]{1,0:T(8,128)(2,1)S(1)}, u32[]{:S(2)}, u32[]{:S(2)}) collective-permute-start(bf16[240,768]{1,0:T(8,128)(2,1)S(1)} %get-tuple-element.52), channel_id=1, source_target_pairs={{0,1},{1,2},{2,3},{3,0},{4,5},{5,6},{6,7},{7,4},{8,9},{9,10},{10,1... | collective-permute-start | bytes 1105928 | tf_op jit(solution)/shard_map/ppermute | solution.py:804
  146.2 0.2 collective-permute-start.9
  146.4 0.7 fusion.7
  147.1 22.8 %collective-permute-done.9.refs_3_ = bf16[128,768]{1,0:T(8,128)(2,1)S(1)} collective-permute-done((bf16[128,768]{1,0:T(8,128)(2,1)S(1)}, bf16[128,768]{1,0:T(8,128)(2,1)S(1)}, u32[]{:S(2)}, u32[]{:S(2)}) %collective-permute-start.9) | collective-permute-done | bytes 196640 | tf_op jit(solution)/shard_map/ppermute | solution.py:804
  169.9 1.5 place_columns.1
  171.4 0.0 collective-permute-done.14.refs_1_
  171.4 5.2 %collective-permute-done.15.refs_2_ = bf16[240,768]{1,0:T(8,128)(2,1)S(1)} collective-permute-done((bf16[240,768]{1,0:T(8,128)(2,1)S(1)}, bf16[240,768]{1,0:T(8,128)(2,1)S(1)}, u32[]{:S(2)}, u32[]{:S(2)}) %collective-permute-start.15) | collective-permute-done | bytes 368672 | tf_op jit(solution)/shard_map/ppermute | solution.py:804
  176.6 2.6 %heads_finish.1 = (bf16[128,3072]{1,0:T(8,128)(2,1)}, f32[3,24,32,128]{3,2,1,0:T(8,128)}, f32[24,8,128]{2,1,0:T(8,128)S(1)}) custom-call(s32[3]{0:T(128)S(1)} %pad_add_fusion.meta_ref, bf16[240,768]{1,0:T(8,128)(2,1)S(1)} %get-tuple-element.49.refs_0_, bf16[240,768]{1,0:T(8,128)(2,1)S(1)} %collective-permute-done.14.refs_1_, ...), custom_call_target="tpu_custom_call" | custom-call | flops 4718592 | bytes 5505024 | tf_op jit(solution)/shard_map/heads_finish/pallas_call | solution.py:757
  179.2 0.7 copy.18
  (29 shorter events, 0.1 us)
Async XLA Ops:
  0.6 17.4 %copy-start = (f32[1,32,24]{1,2,0:T(8,128)S(1)}, f32[1,32,24]{1,2,0:T(8,128)}, u32[]{:S(2)}) copy-start(f32[1,32,24]{1,2,0:T(8,128)} %param.17) | copy-start | bytes 9220
  0.6 7.6 %copy-start.1 = (bf16[1,128,3072]{2,1,0:T(8,128)(2,1)S(1)}, bf16[1,128,3072]{2,1,0:T(8,128)(2,1)}, u32[]{:S(2)}) copy-start(bf16[1,128,3072]{2,1,0:T(8,128)(2,1)} %param.13) | copy-start | bytes 2359300
  0.7 1.2 copy-start.2
  1.9 1.1 copy-start.3
  3.1 5.2 %copy-start.6 = (bf16[1,3,24,32,128]{4,3,2,1,0:T(8,128)(2,1)S(1)}, bf16[1,3,24,32,128]{4,3,2,1,0:T(8,128)(2,1)}, u32[]{:S(2)}) copy-start(bf16[1,3,24,32,128]{4,3,2,1,0:T(8,128)(2,1)} %param.16) | copy-start | bytes 1769476
  3.1 14.9 %copy-start.10 = (f32[256,32]{1,0:T(8,128)S(1)}, f32[256,32]{1,0:T(8,128)}, u32[]{:S(2)}) copy-start(f32[256,32]{1,0:T(8,128)} %constant.23.clone) | copy-start | bytes 98308
  4.0 54.3 %copy-start.8 = (f32[1,3072]{1,0:T(1,128)S(1)}, f32[1,3072]{1,0:T(1,128)}, u32[]{:S(2)}) copy-start(f32[1,3072]{1,0:T(1,128)} %refs_6_.1) | copy-start | bytes 36868
  4.0 10.8 %collective-permute-start.3 = (bf16[144,768]{1,0:T(8,128)(2,1)S(1)}, bf16[144,768]{1,0:T(8,128)(2,1)S(1)}, u32[]{:S(2)}, u32[]{:S(2)}) collective-permute-start(bf16[144,768]{1,0:T(8,128)(2,1)S(1)} %get-tuple-element.37), channel_id=1, source_target_pairs={{0,4},{1,5},{2,6},{3,7},{4,8},{5,9},{6,10},{7,11},{8,12},{9,13},{1... | collective-permute-start | bytes 663560 | tf_op jit(solution)/shard_map/ppermute | solution.py:801
  4.5 12.7 %collective-permute-start.4 = (bf16[144,768]{1,0:T(8,128)(2,1)S(1)}, bf16[144,768]{1,0:T(8,128)(2,1)S(1)}, u32[]{:S(2)}, u32[]{:S(2)}) collective-permute-start(bf16[144,768]{1,0:T(8,128)(2,1)S(1)} %get-tuple-element.38), channel_id=1, source_target_pairs={{0,5},{1,6},{2,7},{3,4},{4,9},{5,10},{6,11},{7,8},{8,13},{9,14},{1... | collective-permute-start | bytes 663560 | tf_op jit(solution)/shard_map/ppermute | solution.py:801
  9.2 49.1 %collective-permute-start = (bf16[240,768]{1,0:T(8,128)(2,1)S(1)}, bf16[240,768]{1,0:T(8,128)(2,1)S(1)}, u32[]{:S(2)}, u32[]{:S(2)}) collective-permute-start(bf16[240,768]{1,0:T(8,128)(2,1)S(1)} %get-tuple-element.34), channel_id=1, source_target_pairs={{0,1},{1,2},{2,3},{3,0},{4,5},{5,6},{6,7},{7,4},{8,9},{9,10},{10,1... | collective-permute-start | bytes 1105928 | tf_op jit(solution)/shard_map/ppermute | solution.py:795
  10.8 47.4 %collective-permute-start.1 = (bf16[240,768]{1,0:T(8,128)(2,1)S(1)}, bf16[240,768]{1,0:T(8,128)(2,1)S(1)}, u32[]{:S(2)}, u32[]{:S(2)}) collective-permute-start(bf16[240,768]{1,0:T(8,128)(2,1)S(1)} %get-tuple-element.35), channel_id=1, source_target_pairs={{0,2},{1,3},{2,0},{3,1},{4,6},{5,7},{6,4},{7,5},{8,10},{9,11},{10,... | collective-permute-start | bytes 1105928 | tf_op jit(solution)/shard_map/ppermute | solution.py:795
  12.1 46.2 %collective-permute-start.2 = (bf16[240,768]{1,0:T(8,128)(2,1)S(1)}, bf16[240,768]{1,0:T(8,128)(2,1)S(1)}, u32[]{:S(2)}, u32[]{:S(2)}) collective-permute-start(bf16[240,768]{1,0:T(8,128)(2,1)S(1)} %get-tuple-element.36), channel_id=1, source_target_pairs={{0,3},{1,0},{2,1},{3,2},{4,7},{5,4},{6,5},{7,6},{8,11},{9,8},{10,9... | collective-permute-start | bytes 1105928 | tf_op jit(solution)/shard_map/ppermute | solution.py:795
  14.8 43.5 %collective-permute-start.5 = (bf16[144,768]{1,0:T(8,128)(2,1)S(1)}, bf16[144,768]{1,0:T(8,128)(2,1)S(1)}, u32[]{:S(2)}, u32[]{:S(2)}) collective-permute-start(bf16[144,768]{1,0:T(8,128)(2,1)S(1)} %get-tuple-element.39), channel_id=1, source_target_pairs={{0,6},{1,7},{2,4},{3,5},{4,10},{5,11},{6,8},{7,9},{8,14},{9,15},{1... | collective-permute-start | bytes 663560 | tf_op jit(solution)/shard_map/ppermute | solution.py:801
  17.2 41.0 %collective-permute-start.6 = (bf16[144,768]{1,0:T(8,128)(2,1)S(1)}, bf16[144,768]{1,0:T(8,128)(2,1)S(1)}, u32[]{:S(2)}, u32[]{:S(2)}) collective-permute-start(bf16[144,768]{1,0:T(8,128)(2,1)S(1)} %get-tuple-element.40), channel_id=1, source_target_pairs={{0,7},{1,4},{2,5},{3,6},{4,11},{5,8},{6,9},{7,10},{8,15},{9,12},{1... | collective-permute-start | bytes 663560 | tf_op jit(solution)/shard_map/ppermute | solution.py:801
  58.3 25.1 %copy-start.4 = (bf16[128,3072]{1,0:T(8,128)(2,1)S(1)}, bf16[128,3072]{1,0:T(8,128)(2,1)}, u32[]{:S(2)}) copy-start(bf16[128,3072]{1,0:T(8,128)(2,1)} %edge_ref.3) | copy-start | bytes 2359300
  58.3 25.1 %copy-start.5 = (bf16[1,128,3072]{2,1,0:T(8,128)(2,1)S(1)}, bf16[1,128,3072]{2,1,0:T(8,128)(2,1)}, u32[]{:S(2)}) copy-start(bf16[1,128,3072]{2,1,0:T(8,128)(2,1)} %param.14) | copy-start | bytes 2359300
  76.6 13.8 %copy-start.7 = (f32[3072]{0:T(1024)S(1)}, f32[3072]{0:T(1024)}, u32[]{:S(2)}) copy-start(f32[3072]{0:T(1024)} %param.19) | copy-start | bytes 36868
  76.6 10.8 %collective-permute-start.20 = (f32[8,512]{1,0:T(8,128)S(1)}, f32[8,512]{1,0:T(8,128)S(1)}, u32[]{:S(2)}, u32[]{:S(2)}) collective-permute-start(f32[8,512]{1,0:T(8,128)S(1)} %get-tuple-element.59.refs_4_), channel_id=1, source_target_pairs={{0,3},{1,0},{2,1},{3,2},{4,7},{5,4},{6,5},{7,6},{8,11},{9,8},{10,9... | collective-permute-start | bytes 49160 | tf_op jit(solution)/shard_map/ppermute | solution.py:795
  82.1 7.3 %collective-permute-start.19 = (f32[8,512]{1,0:T(8,128)S(1)}, f32[8,512]{1,0:T(8,128)S(1)}, u32[]{:S(2)}, u32[]{:S(2)}) collective-permute-start(f32[8,512]{1,0:T(8,128)S(1)} %get-tuple-element.59.refs_4_), channel_id=1, source_target_pairs={{0,2},{1,3},{2,0},{3,1},{4,6},{5,7},{6,4},{7,5},{8,10},{9,11},{10,... | collective-permute-start | bytes 49160 | tf_op jit(solution)/shard_map/ppermute | solution.py:795
  83.4 7.0 %collective-permute-start.18 = (f32[8,512]{1,0:T(8,128)S(1)}, f32[8,512]{1,0:T(8,128)S(1)}, u32[]{:S(2)}, u32[]{:S(2)}) collective-permute-start(f32[8,512]{1,0:T(8,128)S(1)} %get-tuple-element.59.refs_4_), channel_id=1, source_target_pairs={{0,1},{1,2},{2,3},{3,0},{4,5},{5,6},{6,7},{7,4},{8,9},{9,10},{10,1... | collective-permute-start | bytes 49160 | tf_op jit(solution)/shard_map/ppermute | solution.py:795
  84.2 8.5 %collective-permute-start.10 = (bf16[128,768]{1,0:T(8,128)(2,1)S(1)}, bf16[128,768]{1,0:T(8,128)(2,1)S(1)}, u32[]{:S(2)}, u32[]{:S(2)}) collective-permute-start(bf16[128,768]{1,0:T(8,128)(2,1)S(1)} %get-tuple-element.45), channel_id=1, source_target_pairs={{0,28},{1,29},{2,30},{3,31},{4,0},{5,1},{6,2},{7,3},{8,4},{9,5},{1... | collective-permute-start | bytes 589832 | tf_op jit(solution)/shard_map/ppermute | solution.py:801
  84.2 9.1 %collective-permute-start.11 = (bf16[128,768]{1,0:T(8,128)(2,1)S(1)}, bf16[128,768]{1,0:T(8,128)(2,1)S(1)}, u32[]{:S(2)}, u32[]{:S(2)}) collective-permute-start(bf16[128,768]{1,0:T(8,128)(2,1)S(1)} %get-tuple-element.46), channel_id=1, source_target_pairs={{0,29},{1,30},{2,31},{3,28},{4,1},{5,2},{6,3},{7,0},{8,5},{9,6},{1... | collective-permute-start | bytes 589832 | tf_op jit(solution)/shard_map/ppermute | solution.py:801
  87.4 14.6 %collective-permute-start.12 = (bf16[128,768]{1,0:T(8,128)(2,1)S(1)}, bf16[128,768]{1,0:T(8,128)(2,1)S(1)}, u32[]{:S(2)}, u32[]{:S(2)}) collective-permute-start(bf16[128,768]{1,0:T(8,128)(2,1)S(1)} %get-tuple-element.47), channel_id=1, source_target_pairs={{0,30},{1,31},{2,28},{3,29},{4,2},{5,3},{6,0},{7,1},{8,6},{9,7},{1... | collective-permute-start | bytes 589832 | tf_op jit(solution)/shard_map/ppermute | solution.py:801
  89.4 13.3 %collective-permute-start.13 = (bf16[128,768]{1,0:T(8,128)(2,1)S(1)}, bf16[128,768]{1,0:T(8,128)(2,1)S(1)}, u32[]{:S(2)}, u32[]{:S(2)}) collective-permute-start(bf16[128,768]{1,0:T(8,128)(2,1)S(1)} %get-tuple-element.48), channel_id=1, source_target_pairs={{0,31},{1,28},{2,29},{3,30},{4,3},{5,0},{6,1},{7,2},{8,7},{9,4},{1... | collective-permute-start | bytes 589832 | tf_op jit(solution)/shard_map/ppermute | solution.py:801
  90.4 24.3 %copy-start.9 = (f32[32,256]{1,0:T(8,128)S(1)}, f32[32,256]{1,0:T(8,128)}, u32[]{:S(2)}) copy-start(f32[32,256]{1,0:T(8,128)} %constant.24.clone.refs_10_) | copy-start | bytes 98308
  91.4 12.0 %collective-permute-start.21 = (bf16[64,768]{1,0:T(8,128)(2,1)S(1)}, bf16[64,768]{1,0:T(8,128)(2,1)S(1)}, u32[]{:S(2)}, u32[]{:S(2)}) collective-permute-start(bf16[64,768]{1,0:T(8,128)(2,1)S(1)} %get-tuple-element.66), channel_id=1, source_target_pairs={{28,0},{29,1},{30,2},{31,3}} | collective-permute-start | bytes 294920 | tf_op jit(solution)/shard_map/ppermute | solution.py:828
  92.7 15.3 %collective-permute-start.27 = (bf16[64,768]{1,0:T(8,128)(2,1)S(1)}, bf16[64,768]{1,0:T(8,128)(2,1)S(1)}, u32[]{:S(2)}, u32[]{:S(2)}) collective-permute-start(bf16[64,768]{1,0:T(8,128)(2,1)S(1)} %get-tuple-element.67), channel_id=1, source_target_pairs={{28,24},{29,25},{30,26},{31,27}} | collective-permute-start | bytes 294920 | tf_op jit(solution)/shard_map/ppermute | solution.py:828
  93.4 19.3 %collective-permute-start.26 = (bf16[64,768]{1,0:T(8,128)(2,1)S(1)}, bf16[64,768]{1,0:T(8,128)(2,1)S(1)}, u32[]{:S(2)}, u32[]{:S(2)}) collective-permute-start(bf16[64,768]{1,0:T(8,128)(2,1)S(1)} %get-tuple-element.68), channel_id=1, source_target_pairs={{28,20},{29,21},{30,22},{31,23}} | collective-permute-start | bytes 294920 | tf_op jit(solution)/shard_map/ppermute | solution.py:828
  102.0 11.3 %collective-permute-start.25 = (bf16[64,768]{1,0:T(8,128)(2,1)S(1)}, bf16[64,768]{1,0:T(8,128)(2,1)S(1)}, u32[]{:S(2)}, u32[]{:S(2)}) collective-permute-start(bf16[64,768]{1,0:T(8,128)(2,1)S(1)} %get-tuple-element.69), channel_id=1, source_target_pairs={{28,16},{29,17},{30,18},{31,19}} | collective-permute-start | bytes 294920 | tf_op jit(solution)/shard_map/ppermute | solution.py:828
  102.7 11.3 %collective-permute-start.24 = (bf16[64,768]{1,0:T(8,128)(2,1)S(1)}, bf16[64,768]{1,0:T(8,128)(2,1)S(1)}, u32[]{:S(2)}, u32[]{:S(2)}) collective-permute-start(bf16[64,768]{1,0:T(8,128)(2,1)S(1)} %get-tuple-element.70), channel_id=1, source_target_pairs={{28,12},{29,13},{30,14},{31,15}} | collective-permute-start | bytes 294920 | tf_op jit(solution)/shard_map/ppermute | solution.py:828
  103.4 73.2 %collective-permute-start.17 = (bf16[128,3072]{1,0:T(8,128)(2,1)S(1)}, bf16[128,3072]{1,0:T(8,128)(2,1)S(1)}, u32[]{:S(2)}, u32[]{:S(2)}) collective-permute-start(bf16[128,3072]{1,0:T(8,128)(2,1)S(1)} %get-tuple-element.54), channel_id=1, source_target_pairs={{4,0},{8,4},{12,8},{16,12},{20,16},{24,20},{28,24},{0,28},{5,1},{9... | collective-permute-start | bytes 2359304 | tf_op jit(solution)/shard_map/ppermute | solution.py:810
  108.0 36.2 %collective-permute-start.7 = (bf16[128,768]{1,0:T(8,128)(2,1)S(1)}, bf16[128,768]{1,0:T(8,128)(2,1)S(1)}, u32[]{:S(2)}, u32[]{:S(2)}) collective-permute-start(bf16[128,768]{1,0:T(8,128)(2,1)S(1)} %get-tuple-element.42.refs_1_), channel_id=1, source_target_pairs={{0,3},{1,0},{2,1},{3,2},{4,7},{5,4},{6,5},{7,6},{8,11},{9,8},{10,9... | collective-permute-start | bytes 589832 | tf_op jit(solution)/shard_map/ppermute | solution.py:804
  112.6 33.6 %collective-permute-start.8 = (bf16[128,768]{1,0:T(8,128)(2,1)S(1)}, bf16[128,768]{1,0:T(8,128)(2,1)S(1)}, u32[]{:S(2)}, u32[]{:S(2)}) collective-permute-start(bf16[128,768]{1,0:T(8,128)(2,1)S(1)} %get-tuple-element.43.refs_2_), channel_id=1, source_target_pairs={{0,2},{1,3},{2,0},{3,1},{4,6},{5,7},{6,4},{7,5},{8,10},{9,11},{10,... | collective-permute-start | bytes 589832 | tf_op jit(solution)/shard_map/ppermute | solution.py:804
  113.3 28.6 %collective-permute-start.23 = (bf16[64,768]{1,0:T(8,128)(2,1)S(1)}, bf16[64,768]{1,0:T(8,128)(2,1)S(1)}, u32[]{:S(2)}, u32[]{:S(2)}) collective-permute-start(bf16[64,768]{1,0:T(8,128)(2,1)S(1)} %get-tuple-element.71), channel_id=1, source_target_pairs={{28,8},{29,9},{30,10},{31,11}} | collective-permute-start | bytes 294920 | tf_op jit(solution)/shard_map/ppermute | solution.py:828
  114.0 28.9 %collective-permute-start.22 = (bf16[64,768]{1,0:T(8,128)(2,1)S(1)}, bf16[64,768]{1,0:T(8,128)(2,1)S(1)}, u32[]{:S(2)}, u32[]{:S(2)}) collective-permute-start(bf16[64,768]{1,0:T(8,128)(2,1)S(1)} %get-tuple-element.72), channel_id=1, source_target_pairs={{28,4},{29,5},{30,6},{31,7}} | collective-permute-start | bytes 294920 | tf_op jit(solution)/shard_map/ppermute | solution.py:828
  141.9 29.5 %collective-permute-start.14 = (bf16[240,768]{1,0:T(8,128)(2,1)S(1)}, bf16[240,768]{1,0:T(8,128)(2,1)S(1)}, u32[]{:S(2)}, u32[]{:S(2)}) collective-permute-start(bf16[240,768]{1,0:T(8,128)(2,1)S(1)} %get-tuple-element.50), channel_id=1, source_target_pairs={{0,3},{1,0},{2,1},{3,2},{4,7},{5,4},{6,5},{7,6},{8,11},{9,8},{10,9... | collective-permute-start | bytes 1105928 | tf_op jit(solution)/shard_map/ppermute | solution.py:804
  142.9 33.7 %collective-permute-start.15 = (bf16[240,768]{1,0:T(8,128)(2,1)S(1)}, bf16[240,768]{1,0:T(8,128)(2,1)S(1)}, u32[]{:S(2)}, u32[]{:S(2)}) collective-permute-start(bf16[240,768]{1,0:T(8,128)(2,1)S(1)} %get-tuple-element.51), channel_id=1, source_target_pairs={{0,2},{1,3},{2,0},{3,1},{4,6},{5,7},{6,4},{7,5},{8,10},{9,11},{10,... | collective-permute-start | bytes 1105928 | tf_op jit(solution)/shard_map/ppermute | solution.py:804
  144.2 32.4 %collective-permute-start.16 = (bf16[240,768]{1,0:T(8,128)(2,1)S(1)}, bf16[240,768]{1,0:T(8,128)(2,1)S(1)}, u32[]{:S(2)}, u32[]{:S(2)}) collective-permute-start(bf16[240,768]{1,0:T(8,128)(2,1)S(1)} %get-tuple-element.52), channel_id=1, source_target_pairs={{0,1},{1,2},{2,3},{3,0},{4,5},{5,6},{6,7},{7,4},{8,9},{9,10},{10,1... | collective-permute-start | bytes 1105928 | tf_op jit(solution)/shard_map/ppermute | solution.py:804
  146.2 23.7 %collective-permute-start.9 = (bf16[128,768]{1,0:T(8,128)(2,1)S(1)}, bf16[128,768]{1,0:T(8,128)(2,1)S(1)}, u32[]{:S(2)}, u32[]{:S(2)}) collective-permute-start(bf16[128,768]{1,0:T(8,128)(2,1)S(1)} %get-tuple-element.44.refs_3_), channel_id=1, source_target_pairs={{0,1},{1,2},{2,3},{3,0},{4,5},{5,6},{6,7},{7,4},{8,9},{9,10},{10,1... | collective-permute-start | bytes 589832 | tf_op jit(solution)/shard_map/ppermute | solution.py:804

commit v3 on v2

--- a/solution.py
+++ b/solution.py
@@ -336,30 +336,29 @@
     return lax.rsqrt(jnp.mean(x * x, axis=-1, keepdims=True) + eps_norm)
 
 
-def pack_stash_kernel(parts, meta_ref, x_ref, weight_ref, inverse_ref, *out_refs):
+def pack_stash_kernel(parts, meta_ref, x_ref, gain_ref, weight_ref, inverse_ref, *refs):
+    out_refs, normed_ref = refs[:parts], refs[parts]
     rows, width = x_ref.shape
     depth = weight_ref.shape[2]
     wide = width // parts
     heads = wide // HEAD_DIM
     inverse = row_inverse(x_ref[...])
     inverse_ref[...] = jnp.broadcast_to(inverse, inverse_ref.shape)
-    tail = split_rows(inverse, 16, wide)
+    normed_ref[...] = (x_ref[...].astype(F32) * inverse * gain_ref[...]).astype(BF16)
     for r, out_ref in enumerate(out_refs):
         target = lax.rem(meta_ref[0] + r, parts)
-        out_ref[:rows] = x_ref[:, pl.ds(pl.multiple_of(target * wide, 128), wide)]
+        out_ref[:rows] = normed_ref[:, pl.ds(pl.multiple_of(target * wide, 128), wide)]
         for j in range(3):
             for h in range(heads):
                 out_ref[rows + j * depth : rows + (j + 1) * depth, h * HEAD_DIM : (h + 1) * HEAD_DIM] = weight_ref[
                     j, target * heads + h
                 ]
-        out_ref[rows + 3 * depth :] = jnp.zeros((16, wide), BF16)
-        out_ref[rows + 3 * depth :, :rows] = tail
 
 
 def pack_rows_kernel(parts, with_inverse, meta_ref, edge_ref, inner_ref, *out_refs):
     rows, width = inner_ref.shape
     wide = width // parts
-    edge = 2 if with_inverse else 1
+    edge = 1 if with_inverse else 2
     refs = out_refs[:parts]
     for r, out_ref in enumerate(refs):
         target = lax.rem(meta_ref[0] + r, parts)
@@ -395,22 +394,23 @@
 VMEM_SPEC = pl.BlockSpec(memory_space=pltpu.VMEM)
 
 
-def pack_stash(meta, x, weight, parts):
+def pack_stash(meta, x, gain, weight, parts):
     rows, width = x.shape
     depth = weight.shape[2]
-    shape = (rows + 3 * depth + 16, width // parts)
+    shape = (rows + 3 * depth, width // parts)
     return pl.pallas_call(
         functools.partial(pack_stash_kernel, parts),
         out_shape=(
             jax.ShapeDtypeStruct((rows, 128), F32),
             *[jax.ShapeDtypeStruct(shape, BF16) for r in range(parts)],
         ),
-        in_specs=[SMEM_SPEC, VMEM_SPEC, VMEM_SPEC],
+        in_specs=[SMEM_SPEC, VMEM_SPEC, VMEM_SPEC, VMEM_SPEC],
         out_specs=(VMEM_SPEC,) * (parts + 1),
+        scratch_shapes=[pltpu.VMEM((rows, width), BF16)],
         compiler_params=pltpu.CompilerParams(vmem_limit_bytes=VMEM_LIMIT),
         cost_estimate=pl.CostEstimate(flops=4 * rows * width, bytes_accessed=6 * rows * width, transcendentals=0),
         name="pack_stash",
-    )(meta, x, weight)
+    )(meta, x, gain, weight)
 
 
 def pack_rows(meta, edge, inner, parts, with_inverse):
@@ -428,26 +428,36 @@
     )(meta, edge, inner)
 
 
-def gather_rows(meta_ref, refs, first, rows, inverse_ref, weight_refs, weight_first, x_ref, weight_ref):
+def gather_rows(meta_ref, refs, rows, x_ref):
+    parts = len(refs)
+    for r, ref in enumerate(refs):
+        source = lax.rem(meta_ref[0] + parts - r, parts)
+        x_ref[pl.ds(pl.multiple_of(source * rows, rows), rows)] = ref[:rows]
+
+
+def gather_weight(meta_ref, refs, rows, weight_ref):
     parts = len(refs)
     depth = HEAD_DIM // parts
+    for r, ref in enumerate(refs):
+        source = lax.rem(meta_ref[0] + parts - r, parts)
+        depth_at = pl.ds(pl.multiple_of(source * depth, depth), depth)
+        for j in range(3):
+            weight_ref[depth_at, j * HEAD_DIM : (j + 1) * HEAD_DIM] = ref[
+                rows + j * depth : rows + (j + 1) * depth
+            ]
+
+
+def gather_inverse(meta_ref, refs, rows, inverse_ref):
+    parts = len(refs)
 
     @pl.when(pl.program_id(0) == 0)
     def spread_inverse():
         for r, ref in enumerate(refs):
             source = lax.rem(meta_ref[0] + parts - r, parts)
-            rows_at = pl.ds(pl.multiple_of(source * rows, rows), rows)
-            tail = ref[first : first + 16].astype(F32)
-            inverse_ref[rows_at] = column_of(tail[:1] + tail[1:2] + tail[2:3], rows)
-
-    for r, ref in enumerate(refs):
-        source = lax.rem(meta_ref[0] + parts - r, parts)
-        x_ref[pl.ds(pl.multiple_of(source * rows, rows), rows)] = ref[:rows]
-        depth_at = pl.ds(pl.multiple_of(source * depth, depth), depth)
-        for j in range(3):
-            weight_ref[depth_at, j * HEAD_DIM : (j + 1) * HEAD_DIM] = weight_refs[r][
-                weight_first + j * depth : weight_first + (j + 1) * depth
-            ]
+            tail = ref[rows : rows + 16].astype(F32)
+            inverse_ref[pl.ds(pl.multiple_of(source * rows, rows), rows)] = column_of(
+                tail[:1] + tail[1:2] + tail[2:3], rows
+            )
 
 
 def block_mask(first_query, tokens):
@@ -470,17 +480,15 @@
     a_refs, c_refs = refs[:parts], refs[parts : 2 * parts]
     gain_ref, offset_ref, onehot_ref = refs[2 * parts : 2 * parts + 3]
     out_refs = refs[2 * parts + 3 : 3 * parts + 3]
-    gain_grad_ref, inverse_ref, x_ref, weight_ref, cot_ref, grad_ref, part_ref, bias_ref = refs[3 * parts + 3 :]
+    gain_grad_ref, x_ref, weight_ref, cot_ref, grad_ref, part_ref, bias_ref = refs[3 * parts + 3 :]
     tokens = rows * parts
     depth = HEAD_DIM // parts
     scale = HEAD_DIM ** (-0.5)
-    gather_rows(meta_ref, a_refs, rows + 3 * depth, rows, inverse_ref, a_refs, rows, x_ref, weight_ref)
-    for r in range(parts):
-        source = lax.rem(meta_ref[0] + parts - r, parts)
-        cot_ref[pl.ds(pl.multiple_of(source * rows, rows), rows)] = c_refs[r][...]
+    gather_rows(meta_ref, a_refs, rows, x_ref)
+    gather_weight(meta_ref, a_refs, rows, weight_ref)
+    gather_rows(meta_ref, c_refs, rows, cot_ref)
     weight = weight_ref[...]
-    scaled_x = x_ref[...].astype(F32) * inverse_ref[...]
-    normed = (scaled_x * gain_ref[...]).astype(BF16)
+    normed = x_ref[...]
     query = dot_nn(normed, weight[:, :HEAD_DIM]).astype(BF16)
     key = padded(dot_nn(normed, weight[:, HEAD_DIM : 2 * HEAD_DIM]).astype(BF16))
     value = padded(dot_nn(normed, weight[:, 2 * HEAD_DIM :]).astype(BF16))
@@ -522,7 +530,7 @@
         axis=1,
     )
     grad_normed = dot_nt(dqkv, weight)
-    gain_grad_ref[...] = jnp.sum(grad_normed * scaled_x, axis=0, keepdims=True)
+    gain_grad_ref[...] = jnp.sum(grad_normed * normed.astype(F32), axis=0, keepdims=True) / gain_ref[...]
     grad_ref[...] = grad_normed
     part_ref[...] = dot_tn(normed, dqkv)
     bias_grad = jnp.sum(onehot_ref[...] * diagonal_sums(score_sum), axis=1, keepdims=True)
@@ -551,11 +559,12 @@
     tokens = rows * parts
     buckets = onehot.shape[0]
     packed = a_slots[0].shape[0]
+    made = packed + 16
     width = heads * HEAD_DIM
     return pl.pallas_call(
         functools.partial(heads_backward_kernel, parts, rows),
         out_shape=(
-            *[jax.ShapeDtypeStruct((packed, width), BF16) for r in range(parts)],
+            *[jax.ShapeDtypeStruct((made, width), BF16) for r in range(parts)],
             jax.ShapeDtypeStruct((1, width), F32),
         ),
         grid_spec=pltpu.PrefetchScalarGridSpec(
@@ -568,9 +577,8 @@
                 pl.BlockSpec((1, 1, WINDOW), lambda i, meta: (meta[0] * heads + i, 0, 0)),
                 pl.BlockSpec((buckets, WINDOW), lambda i, meta: (0, 0)),
             ],
-            out_specs=(*[head_column(packed)] * parts, head_column(1)),
+            out_specs=(*[head_column(made)] * parts, head_column(1)),
             scratch_shapes=[
-                pltpu.VMEM((tokens, HEAD_DIM), F32),
                 pltpu.VMEM((tokens, HEAD_DIM), BF16),
                 pltpu.VMEM((HEAD_DIM, 3 * HEAD_DIM), BF16),
                 pltpu.VMEM((tokens, HEAD_DIM), BF16),
@@ -581,7 +589,7 @@
         ),
         compiler_params=pltpu.CompilerParams(vmem_limit_bytes=VMEM_LIMIT),
         cost_estimate=pl.CostEstimate(
-            flops=heads * tokens * 4_000_000, bytes_accessed=6 * tokens * width, transcendentals=heads * tokens * WINDOW
+            flops=heads * tokens * 400_000, bytes_accessed=tokens * width, transcendentals=0
         ),
         name="heads_backward",
     )(meta, *a_slots, *c_slots, gain, offsets, onehot)
@@ -593,7 +601,9 @@
     out_refs = refs[2 * parts + 2 : 3 * parts + 2]
     sums_ref, inverse_ref, x_ref, weight_ref, made_ref, square_ref = refs[3 * parts + 2 :]
     tokens = rows * parts
-    gather_rows(meta_ref, i_refs, rows, rows, inverse_ref, a_refs, rows, x_ref, weight_ref)
+    gather_rows(meta_ref, i_refs, rows, x_ref)
+    gather_weight(meta_ref, a_refs, rows, weight_ref)
+    gather_inverse(meta_ref, i_refs, rows, inverse_ref)
     weight = weight_ref[...]
     normed = (x_ref[...].astype(F32) * inverse_ref[...] * gain_ref[...]).astype(BF16)
     query = dot_nn(normed, weight[:, :HEAD_DIM]).astype(BF16)
@@ -663,7 +673,7 @@
         ),
         compiler_params=pltpu.CompilerParams(vmem_limit_bytes=VMEM_LIMIT),
         cost_estimate=pl.CostEstimate(
-            flops=heads * tokens * 2_000_000, bytes_accessed=6 * tokens * width, transcendentals=heads * tokens * WINDOW
+            flops=heads * tokens, bytes_accessed=tokens, transcendentals=0
         ),
         name="heads_forward",
     )(meta, *a_slots, *i_slots, gain, offsets)
@@ -777,6 +787,12 @@
     return jnp.where(inside[None, :], by_offset, masked_score)[:, None, :]
 
 
+def shifted(value, axis, steps):
+    count = lax.axis_size(axis)
+    first, last = (max(0, -steps), min(count, count - steps))
+    return lax.ppermute(value, axis, [(source, source + steps) for source in range(first, last)])
+
+
 def heads_body(
     embedded, carried, stash, returned, loss_grad, qkv_weight, rel_bias, norm_gain, final_gain
 ):
@@ -790,38 +806,31 @@
         [lax.axis_index("seq"), section == 0, section == sections - 1]
     ).astype(jnp.int32)
 
-    def shifted(value, r, step):
-        if step == 0:
-            return lax.ppermute(value, "seq", [(i, (i + r) % parts) for i in range(parts)])
-        pairs = [
-            (s * parts + i, (s + step) % sections * parts + (i + r) % parts)
-            for s in range(sections)
-            for i in range(parts)
-        ]
-        return lax.ppermute(value, ("section", "seq"), pairs)
-
-    def returned_to(value, r):
-        return lax.ppermute(value, "seq", [(i, (i - r) % parts) for i in range(parts)])
-
-    inverse_b, *a_sends = pack_stash(meta, stash[0], qkv_weight[0], parts)
-    a_slots = [a_sends[0]] + [shifted(a_sends[r], r, 0) for r in range(1, parts)]
-    *c_sends, cot_source = pack_rows(meta, loss_grad, returned[0], parts, False)
-    c_slots = [shifted(c_sends[r], r, -1) for r in range(parts)]
-    cotangent = lax.ppermute(
-        cot_source, "section", [((s + 1) % sections, s) for s in range(sections)]
-    )
-    i_sends = pack_rows(meta, embedded, carried[0], parts, True)
-    i_slots = [shifted(i_sends[r], r, 1) for r in range(parts)]
+    def sent(value, r):
+        return lax.ppermute(value, "seq", [(i, (i + r) % parts) for i in range(parts)])
+
+    def exchanged(sends, direction):
+        return [sends[0]] + [sent(sends[r], direction * r) for r in range(1, parts)]
+
+    came_back = shifted(returned[0], "section", -1)
+    arrived = shifted(carried[0], "section", 1)
+    inverse_b, *a_sends = pack_stash(meta, stash[0], norm_gain, qkv_weight[0], parts)
+    a_slots = exchanged(a_sends, 1)
+    *c_sends, cotangent = pack_rows(meta, loss_grad, came_back, parts, False)
+    c_slots = exchanged(c_sends, 1)
+    i_slots = exchanged(pack_rows(meta, embedded, arrived, parts, True), 1)
 
     offsets = offset_table(rel_bias[0])
     onehot = jnp.asarray(bucket_onehot(buckets).T)
     *g_sends, gain_grad = heads_backward(meta, a_slots, c_slots, norm_gain, offsets, onehot, heads)
-    g_slots = [g_sends[0]] + [returned_to(g_sends[r], r) for r in range(1, parts)]
+    g_sends, i_slots = lax.optimization_barrier((g_sends, i_slots))
+    g_slots = exchanged(g_sends, -1)
 
     *o_sends, sums = heads_forward(meta, a_slots, i_slots, norm_gain, offsets, heads, rows)
-    o_slots = [o_sends[0]] + [returned_to(o_sends[r], r) for r in range(1, parts)]
-    all_sums = [sums] + [shifted(sums, r, 0) for r in range(1, parts)]
-    made = memory_rows(meta, o_sends, all_sums, final_gain[None], width)
+    all_sums = [sums] + [sent(sums, r) for r in range(1, parts)]
+    o_slots = exchanged(o_sends, -1)
+    g_slots, memory_gain = lax.optimization_barrier((g_slots, final_gain[None]))
+    made = memory_rows(meta, o_sends, all_sums, memory_gain, width)
     share = rows * parts // sections
     memory = jnp.where(section == sections - 1, made[(sections - 1) * share :], 0)
     for s in range(sections - 1):

time: 181 us -> 162 us (0.90)
  waiting for transfers between devices: 78.4 us -> 39.5 us
  starting transfers between devices: 43.4 us -> 61.6 us
    ppermute x21 -> x20, waiting for transfers between devices: 78.4 us -> 39.5 us  [the longest x18 39.5 us: sent(): lax.ppermute(value, 'seq', [(i, (i + r) % parts) for i in range(parts)])]
    ppermute x21 -> x20, starting transfers between devices: 38.1 us -> 56.2 us  [the longest x18 51.8 us: sent(): lax.ppermute(value, 'seq', [(i, (i + r) % parts) for i in range(parts)])]
  transfers between devices with their start and end apart: 28 -> 27, of which waited for: 5 -> 5; matrix products, arithmetic and copies ran while one was open for 1% -> 1% of each run, Pallas kernels for 17% -> 33%
where the time goes in v3:
time: 162 us; the launch traced here: 160 us
  starting transfers between devices  61.6 us (38%)
  Pallas kernels  53 us (33%)
  waiting for transfers between devices  39.5 us (24%)
  local copies, waits for them, and re-layouts  3.74 us (2%)
    ppermute x18, starting transfers between devices, sent(): lax.ppermute(value, 'seq', [(i, (i + r) % parts) for i in range(parts)])  51.8 us
    ppermute x18, waiting for transfers between devices, sent(): lax.ppermute(value, 'seq', [(i, (i + r) % parts) for i in range(parts)])  39.5 us
    pallas_call x1, Pallas kernels, heads_backward(): pl.pallas_call(functools.partial(heads_backward_kernel, parts, rows), out...  27 us
    pallas_call x1, Pallas kernels, heads_forward(): pl.pallas_call(functools.partial(heads_forward_kernel, parts, rows), out_...  18.1 us
    ppermute x7, starting transfers between devices, heads_body(): lax.ppermute(made[s * share:(s + 1) * share], 'section', [(sections - 1,...  5.4 us
    ppermute x2, starting transfers between devices, shifted(): lax.ppermute(value, axis, [(source, source + steps) for source in range(f...  4.37 us
  transfers between devices with their start and end apart: 27, of which 5 were waited for; matrix products, arithmetic and copies ran while one was open for 1% of the time, Pallas kernels for 33%

profile of v3, /device:TPU:0, one launch (start us, length us, event | category | flops | bytes accessed | tf_op | source)
XLA Modules:
  0.0 159.8 jit_solution(14962457511038678625)
XLA Ops:
  0.6 0.0 copy-start
  0.6 1.3 collective-permute-start.3
  1.9 3.1 %collective-permute-start.7 = (bf16[128,3072]{1,0:T(8,128)(2,1)}, bf16[128,3072]{1,0:T(8,128)(2,1)S(1)}, u32[]{:S(2)}, u32[]{:S(2)}) collective-permute-start(bf16[128,3072]{1,0:T(8,128)(2,1)} %bitcast.32), channel_id=1, source_target_pairs={{0,4},{4,8},{8,12},{12,16},{16,20},{20,24},{24,28},{1,5},{5,9},{9,... | collective-permute-start | bytes 2359304 | tf_op jit(solution)/shard_map/ppermute | solution.py:793
  5.0 0.1 pad_add_fusion.meta_ref
  5.1 1.1 copy-done.1
  6.3 1.1 copy-done.5
  7.3 0.7 copy-done.6
  8.0 1.3 pack_stash.1
  9.3 3.1 %collective-permute-start = (bf16[224,768]{1,0:T(8,128)(2,1)S(1)}, bf16[224,768]{1,0:T(8,128)(2,1)S(1)}, u32[]{:S(2)}, u32[]{:S(2)}) collective-permute-start(bf16[224,768]{1,0:T(8,128)(2,1)S(1)} %get-tuple-element.47), channel_id=1, source_target_pairs={{0,1},{1,2},{2,3},{3,0},{4,5},{5,6},{6,7},{7,4},{8,9},{9,10},{10,1... | collective-permute-start | bytes 1032200 | tf_op jit(solution)/shard_map/ppermute | solution.py:810
  12.4 2.6 %collective-permute-start.1 = (bf16[224,768]{1,0:T(8,128)(2,1)S(1)}, bf16[224,768]{1,0:T(8,128)(2,1)S(1)}, u32[]{:S(2)}, u32[]{:S(2)}) collective-permute-start(bf16[224,768]{1,0:T(8,128)(2,1)S(1)} %get-tuple-element.48), channel_id=1, source_target_pairs={{0,2},{1,3},{2,0},{3,1},{4,6},{5,7},{6,4},{7,5},{8,10},{9,11},{10,... | collective-permute-start | bytes 1032200 | tf_op jit(solution)/shard_map/ppermute | solution.py:810
  15.0 1.4 collective-permute-start.2
  16.3 0.0 collective-permute-done.3.inner_ref
  16.3 0.7 pack_cotangent.1
  17.0 0.0 copy-start.10
  17.0 0.0 copy-start.7
  17.1 0.0 copy-start.9
  17.1 0.7 collective-permute-start.4
  17.8 0.0 collective-permute-done.7.inner_ref
  17.8 0.3 collective-permute-start.5
  18.1 0.9 pack_inbound.1
  19.1 4.1 %collective-permute-done.refs_1_ = bf16[224,768]{1,0:T(8,128)(2,1)S(1)} collective-permute-done((bf16[224,768]{1,0:T(8,128)(2,1)S(1)}, bf16[224,768]{1,0:T(8,128)(2,1)S(1)}, u32[]{:S(2)}, u32[]{:S(2)}) %collective-permute-start) | collective-permute-done | bytes 344096 | tf_op jit(solution)/shard_map/ppermute | solution.py:810
  23.2 2.0 %collective-permute-start.6 = (bf16[128,768]{1,0:T(8,128)(2,1)S(1)}, bf16[128,768]{1,0:T(8,128)(2,1)S(1)}, u32[]{:S(2)}, u32[]{:S(2)}) collective-permute-start(bf16[128,768]{1,0:T(8,128)(2,1)S(1)} %get-tuple-element.53), channel_id=1, source_target_pairs={{0,3},{1,0},{2,1},{3,2},{4,7},{5,4},{6,5},{7,6},{8,11},{9,8},{10,9... | collective-permute-start | bytes 589832 | tf_op jit(solution)/shard_map/ppermute | solution.py:810
  25.2 13.3 %collective-permute-done.1.refs_2_ = bf16[224,768]{1,0:T(8,128)(2,1)S(1)} collective-permute-done((bf16[224,768]{1,0:T(8,128)(2,1)S(1)}, bf16[224,768]{1,0:T(8,128)(2,1)S(1)}, u32[]{:S(2)}, u32[]{:S(2)}) %collective-permute-start.1) | collective-permute-done | bytes 344096 | tf_op jit(solution)/shard_map/ppermute | solution.py:810
  38.5 17.2 %collective-permute-start.10 = (bf16[144,768]{1,0:T(8,128)(2,1)S(1)}, bf16[144,768]{1,0:T(8,128)(2,1)S(1)}, u32[]{:S(2)}, u32[]{:S(2)}) collective-permute-start(bf16[144,768]{1,0:T(8,128)(2,1)S(1)} %get-tuple-element.61), channel_id=1, source_target_pairs={{0,3},{1,0},{2,1},{3,2},{4,7},{5,4},{6,5},{7,6},{8,11},{9,8},{10,9... | collective-permute-start | bytes 663560 | tf_op jit(solution)/shard_map/ppermute | solution.py:810
  55.7 0.0 collective-permute-done.2.refs_3_
  55.7 0.0 collective-permute-start.8
  55.7 3.3 %collective-permute-start.9 = (bf16[144,768]{1,0:T(8,128)(2,1)S(1)}, bf16[144,768]{1,0:T(8,128)(2,1)S(1)}, u32[]{:S(2)}, u32[]{:S(2)}) collective-permute-start(bf16[144,768]{1,0:T(8,128)(2,1)S(1)} %get-tuple-element.60), channel_id=1, source_target_pairs={{0,2},{1,3},{2,0},{3,1},{4,6},{5,7},{6,4},{7,5},{8,10},{9,11},{10,... | collective-permute-start | bytes 663560 | tf_op jit(solution)/shard_map/ppermute | solution.py:810
  59.0 0.2 fusion
  59.3 0.0 collective-permute-done.6.refs_7_
  59.3 27.0 %heads_backward.1 = (bf16[240,768]{1,0:T(8,128)(2,1)S(1)}, bf16[240,768]{1,0:T(8,128)(2,1)S(1)}, bf16[240,768]{1,0:T(8,128)(2,1)S(1)}, bf16[240,768]{1,0:T(8,128)(2,1)S(1)}, f32[1,768]{1,0:T(1,128)}) custom-call(s32[3]{0:T(128)S(1)} %pad_add_fusion.meta_ref, bf16[224,768]{1,0:T(8,128)(2,1)S(1)} %get-tuple-element.46.refs_0_, ...), custom_call_target="tpu_custom_call" | custom-call | flops 1228800000 | bytes 393216 | tf_op jit(solution)/shard_map/heads_backward/pallas_call | solution.py:564
  86.3 0.0 collective-permute-done.10.refs_7_
  86.3 0.0 collective-permute-done.8.refs_5_
  86.3 9.7 %collective-permute-start.14 = (bf16[240,768]{1,0:T(8,128)(2,1)S(1)}, bf16[240,768]{1,0:T(8,128)(2,1)S(1)}, u32[]{:S(2)}, u32[]{:S(2)}) collective-permute-start(bf16[240,768]{1,0:T(8,128)(2,1)S(1)} %get-tuple-element.71), channel_id=1, source_target_pairs={{0,3},{1,0},{2,1},{3,2},{4,7},{5,4},{6,5},{7,6},{8,11},{9,8},{10,9... | collective-permute-start | bytes 1105928 | tf_op jit(solution)/shard_map/ppermute | solution.py:810
  96.0 4.9 %collective-permute-start.15 = (bf16[240,768]{1,0:T(8,128)(2,1)S(1)}, bf16[240,768]{1,0:T(8,128)(2,1)S(1)}, u32[]{:S(2)}, u32[]{:S(2)}) collective-permute-start(bf16[240,768]{1,0:T(8,128)(2,1)S(1)} %get-tuple-element.72), channel_id=1, source_target_pairs={{0,2},{1,3},{2,0},{3,1},{4,6},{5,7},{6,4},{7,5},{8,10},{9,11},{10,... | collective-permute-start | bytes 1105928 | tf_op jit(solution)/shard_map/ppermute | solution.py:810
  101.0 0.0 collective-permute-start.16
  101.0 18.1 %heads_forward.1 = (bf16[128,768]{1,0:T(8,128)(2,1)S(1)}, bf16[128,768]{1,0:T(8,128)(2,1)S(1)}, bf16[128,768]{1,0:T(8,128)(2,1)S(1)}, bf16[128,768]{1,0:T(8,128)(2,1)S(1)}, f32[8,512]{1,0:T(8,128)S(1)}) custom-call(s32[3]{0:T(128)S(1)} %pad_add_fusion.meta_ref, bf16[224,768]{1,0:T(8,128)(2,1)S(1)} %get-tuple-element.46.refs_0_, ...), custom_call_target="tpu_custom_call" | custom-call | flops 3072 | bytes 512 | tf_op jit(solution)/shard_map/heads_forward/pallas_call | solution.py:647
  119.1 0.6 collective-permute-start.17
  119.7 3.8 %collective-permute-start.18 = (f32[8,512]{1,0:T(8,128)S(1)}, f32[8,512]{1,0:T(8,128)S(1)}, u32[]{:S(2)}, u32[]{:S(2)}) collective-permute-start(f32[8,512]{1,0:T(8,128)S(1)} %get-tuple-element.84.refs_4_), channel_id=1, source_target_pairs={{0,2},{1,3},{2,0},{3,1},{4,6},{5,7},{6,4},{7,5},{8,10},{9,11},{10,... | collective-permute-start | bytes 49160 | tf_op jit(solution)/shard_map/ppermute | solution.py:810
  123.5 0.1 collective-permute-start.19
  123.6 11.2 %collective-permute-done.15.refs_2_ = bf16[240,768]{1,0:T(8,128)(2,1)S(1)} collective-permute-done((bf16[240,768]{1,0:T(8,128)(2,1)S(1)}, bf16[240,768]{1,0:T(8,128)(2,1)S(1)}, u32[]{:S(2)}, u32[]{:S(2)}) %collective-permute-start.15) | collective-permute-done | bytes 368672 | tf_op jit(solution)/shard_map/ppermute | solution.py:810
  134.8 0.0 collective-permute-start.11
  134.8 0.0 collective-permute-done.16.refs_3_
  134.8 0.0 collective-permute-start.12
  134.8 2.1 %collective-permute-start.13 = (bf16[128,768]{1,0:T(8,128)(2,1)S(1)}, bf16[128,768]{1,0:T(8,128)(2,1)S(1)}, u32[]{:S(2)}, u32[]{:S(2)}) collective-permute-start(bf16[128,768]{1,0:T(8,128)(2,1)S(1)} %get-tuple-element.69.refs_3_), channel_id=1, source_target_pairs={{0,1},{1,2},{2,3},{3,0},{4,5},{5,6},{6,7},{7,4},{8,9},{9,10},{10,1... | collective-permute-start | bytes 589832 | tf_op jit(solution)/shard_map/ppermute | solution.py:810
  136.9 0.0 collective-permute-done.18.refs_6_
  136.9 0.0 collective-permute-done.19.refs_7_
  136.9 0.9 memory_rows.1
  137.8 0.0 copy-start.2
  137.9 1.4 collective-permute-start.20
  139.3 0.7 collective-permute-start.21
  140.0 1.2 collective-permute-done.11.refs_1_
  141.2 0.7 collective-permute-start.22
  141.8 9.7 %collective-permute-done.12.refs_2_ = bf16[128,768]{1,0:T(8,128)(2,1)S(1)} collective-permute-done((bf16[128,768]{1,0:T(8,128)(2,1)S(1)}, bf16[128,768]{1,0:T(8,128)(2,1)S(1)}, u32[]{:S(2)}, u32[]{:S(2)}) %collective-permute-start.12) | collective-permute-done | bytes 196640 | tf_op jit(solution)/shard_map/ppermute | solution.py:810
  151.5 0.7 collective-permute-start.23
  152.2 0.7 collective-permute-start.24
  152.9 0.0 collective-permute-done.20
  152.9 0.7 collective-permute-start.25
  153.5 0.0 collective-permute-done.21
  153.6 0.7 collective-permute-start.26
  154.2 1.5 place_columns.1
  155.7 2.6 %heads_finish.1 = (bf16[128,3072]{1,0:T(8,128)(2,1)}, f32[3,24,32,128]{3,2,1,0:T(8,128)}, f32[24,8,128]{2,1,0:T(8,128)S(1)}) custom-call(s32[3]{0:T(128)S(1)} %pad_add_fusion.meta_ref, bf16[240,768]{1,0:T(8,128)(2,1)S(1)} %get-tuple-element.74.refs_0_, bf16[240,768]{1,0:T(8,128)(2,1)S(1)} %collective-permute-done.14.refs_1_, ...), custom_call_target="tpu_custom_call" | custom-call | flops 4718592 | bytes 5505024 | tf_op jit(solution)/shard_map/heads_finish/pallas_call | solution.py:767
  158.3 0.7 copy.18
  159.1 0.0 collective-permute-done.23
  159.1 0.7 fusion.7
  (27 shorter events, 0.1 us)
Async XLA Ops:
  0.6 58.4 %copy-start = (f32[1,32,24]{1,2,0:T(8,128)S(1)}, f32[1,32,24]{1,2,0:T(8,128)}, u32[]{:S(2)}) copy-start(f32[1,32,24]{1,2,0:T(8,128)} %param.17) | copy-start | bytes 9220
  0.6 15.7 %collective-permute-start.3 = (bf16[128,3072]{1,0:T(8,128)(2,1)}, bf16[128,3072]{1,0:T(8,128)(2,1)S(1)}, u32[]{:S(2)}, u32[]{:S(2)}) collective-permute-start(bf16[128,3072]{1,0:T(8,128)(2,1)} %bitcast.31), channel_id=1, source_target_pairs={{4,0},{8,4},{12,8},{16,12},{20,16},{24,20},{28,24},{5,1},{9,5},{13... | collective-permute-start | bytes 2359304 | tf_op jit(solution)/shard_map/ppermute | solution.py:793
  1.9 15.9 %collective-permute-start.7 = (bf16[128,3072]{1,0:T(8,128)(2,1)}, bf16[128,3072]{1,0:T(8,128)(2,1)S(1)}, u32[]{:S(2)}, u32[]{:S(2)}) collective-permute-start(bf16[128,3072]{1,0:T(8,128)(2,1)} %bitcast.32), channel_id=1, source_target_pairs={{0,4},{4,8},{8,12},{12,16},{16,20},{20,24},{24,28},{1,5},{5,9},{9,... | collective-permute-start | bytes 2359304 | tf_op jit(solution)/shard_map/ppermute | solution.py:793
  5.1 1.1 copy-start.1
  6.3 1.1 copy-start.5
  7.3 0.7 copy-start.6
  8.0 8.3 %copy-start.3 = (bf16[128,3072]{1,0:T(8,128)(2,1)S(1)}, bf16[128,3072]{1,0:T(8,128)(2,1)}, u32[]{:S(2)}) copy-start(bf16[128,3072]{1,0:T(8,128)(2,1)} %edge_ref.2) | copy-start | bytes 2359300
  8.0 10.1 %copy-start.4 = (bf16[128,3072]{1,0:T(8,128)(2,1)S(1)}, bf16[128,3072]{1,0:T(8,128)(2,1)}, u32[]{:S(2)}) copy-start(bf16[128,3072]{1,0:T(8,128)(2,1)} %edge_ref.3) | copy-start | bytes 2359300
  9.3 13.9 %collective-permute-start = (bf16[224,768]{1,0:T(8,128)(2,1)S(1)}, bf16[224,768]{1,0:T(8,128)(2,1)S(1)}, u32[]{:S(2)}, u32[]{:S(2)}) collective-permute-start(bf16[224,768]{1,0:T(8,128)(2,1)S(1)} %get-tuple-element.47), channel_id=1, source_target_pairs={{0,1},{1,2},{2,3},{3,0},{4,5},{5,6},{6,7},{7,4},{8,9},{9,10},{10,1... | collective-permute-start | bytes 1032200 | tf_op jit(solution)/shard_map/ppermute | solution.py:810
  12.4 26.1 %collective-permute-start.1 = (bf16[224,768]{1,0:T(8,128)(2,1)S(1)}, bf16[224,768]{1,0:T(8,128)(2,1)S(1)}, u32[]{:S(2)}, u32[]{:S(2)}) collective-permute-start(bf16[224,768]{1,0:T(8,128)(2,1)S(1)} %get-tuple-element.48), channel_id=1, source_target_pairs={{0,2},{1,3},{2,0},{3,1},{4,6},{5,7},{6,4},{7,5},{8,10},{9,11},{10,... | collective-permute-start | bytes 1032200 | tf_op jit(solution)/shard_map/ppermute | solution.py:810
  15.0 40.7 %collective-permute-start.2 = (bf16[224,768]{1,0:T(8,128)(2,1)S(1)}, bf16[224,768]{1,0:T(8,128)(2,1)S(1)}, u32[]{:S(2)}, u32[]{:S(2)}) collective-permute-start(bf16[224,768]{1,0:T(8,128)(2,1)S(1)} %get-tuple-element.49), channel_id=1, source_target_pairs={{0,3},{1,0},{2,1},{3,2},{4,7},{5,4},{6,5},{7,6},{8,11},{9,8},{10,9... | collective-permute-start | bytes 1032200 | tf_op jit(solution)/shard_map/ppermute | solution.py:810
  17.0 42.0 %copy-start.10 = (f32[256,32]{1,0:T(8,128)S(1)}, f32[256,32]{1,0:T(8,128)}, u32[]{:S(2)}) copy-start(f32[256,32]{1,0:T(8,128)} %constant.23.clone) | copy-start | bytes 98308
  17.0 42.2 %copy-start.7 = (f32[1,3072]{1,0:T(1,128)S(1)}, f32[1,3072]{1,0:T(1,128)}, u32[]{:S(2)}) copy-start(f32[1,3072]{1,0:T(1,128)} %refs_6_.1) | copy-start | bytes 36868
  17.1 42.2 %copy-start.9 = (f32[32,256]{1,0:T(8,128)S(1)}, f32[32,256]{1,0:T(8,128)}, u32[]{:S(2)}) copy-start(f32[32,256]{1,0:T(8,128)} %constant.24.clone.refs_10_) | copy-start | bytes 98308
  17.1 38.6 %collective-permute-start.4 = (bf16[128,768]{1,0:T(8,128)(2,1)S(1)}, bf16[128,768]{1,0:T(8,128)(2,1)S(1)}, u32[]{:S(2)}, u32[]{:S(2)}) collective-permute-start(bf16[128,768]{1,0:T(8,128)(2,1)S(1)} %get-tuple-element.51), channel_id=1, source_target_pairs={{0,1},{1,2},{2,3},{3,0},{4,5},{5,6},{6,7},{7,4},{8,9},{9,10},{10,1... | collective-permute-start | bytes 589832 | tf_op jit(solution)/shard_map/ppermute | solution.py:810
  17.8 41.4 %collective-permute-start.5 = (bf16[128,768]{1,0:T(8,128)(2,1)S(1)}, bf16[128,768]{1,0:T(8,128)(2,1)S(1)}, u32[]{:S(2)}, u32[]{:S(2)}) collective-permute-start(bf16[128,768]{1,0:T(8,128)(2,1)S(1)} %get-tuple-element.52), channel_id=1, source_target_pairs={{0,2},{1,3},{2,0},{3,1},{4,6},{5,7},{6,4},{7,5},{8,10},{9,11},{10,... | collective-permute-start | bytes 589832 | tf_op jit(solution)/shard_map/ppermute | solution.py:810
  23.2 36.0 %collective-permute-start.6 = (bf16[128,768]{1,0:T(8,128)(2,1)S(1)}, bf16[128,768]{1,0:T(8,128)(2,1)S(1)}, u32[]{:S(2)}, u32[]{:S(2)}) collective-permute-start(bf16[128,768]{1,0:T(8,128)(2,1)S(1)} %get-tuple-element.53), channel_id=1, source_target_pairs={{0,3},{1,0},{2,1},{3,2},{4,7},{5,4},{6,5},{7,6},{8,11},{9,8},{10,9... | collective-permute-start | bytes 589832 | tf_op jit(solution)/shard_map/ppermute | solution.py:810
  38.5 47.8 %collective-permute-start.10 = (bf16[144,768]{1,0:T(8,128)(2,1)S(1)}, bf16[144,768]{1,0:T(8,128)(2,1)S(1)}, u32[]{:S(2)}, u32[]{:S(2)}) collective-permute-start(bf16[144,768]{1,0:T(8,128)(2,1)S(1)} %get-tuple-element.61), channel_id=1, source_target_pairs={{0,3},{1,0},{2,1},{3,2},{4,7},{5,4},{6,5},{7,6},{8,11},{9,8},{10,9... | collective-permute-start | bytes 663560 | tf_op jit(solution)/shard_map/ppermute | solution.py:810
  55.7 30.6 %collective-permute-start.8 = (bf16[144,768]{1,0:T(8,128)(2,1)S(1)}, bf16[144,768]{1,0:T(8,128)(2,1)S(1)}, u32[]{:S(2)}, u32[]{:S(2)}) collective-permute-start(bf16[144,768]{1,0:T(8,128)(2,1)S(1)} %get-tuple-element.59), channel_id=1, source_target_pairs={{0,1},{1,2},{2,3},{3,0},{4,5},{5,6},{6,7},{7,4},{8,9},{9,10},{10,1... | collective-permute-start | bytes 663560 | tf_op jit(solution)/shard_map/ppermute | solution.py:810
  55.7 30.6 %collective-permute-start.9 = (bf16[144,768]{1,0:T(8,128)(2,1)S(1)}, bf16[144,768]{1,0:T(8,128)(2,1)S(1)}, u32[]{:S(2)}, u32[]{:S(2)}) collective-permute-start(bf16[144,768]{1,0:T(8,128)(2,1)S(1)} %get-tuple-element.60), channel_id=1, source_target_pairs={{0,2},{1,3},{2,0},{3,1},{4,6},{5,7},{6,4},{7,5},{8,10},{9,11},{10,... | collective-permute-start | bytes 663560 | tf_op jit(solution)/shard_map/ppermute | solution.py:810
  86.3 50.6 %copy-start.8 = (f32[3072]{0:T(1024)S(1)}, f32[3072]{0:T(1024)}, u32[]{:S(2)}) copy-start(f32[3072]{0:T(1024)} %param.19) | copy-start | bytes 36868
  86.3 37.2 %collective-permute-start.14 = (bf16[240,768]{1,0:T(8,128)(2,1)S(1)}, bf16[240,768]{1,0:T(8,128)(2,1)S(1)}, u32[]{:S(2)}, u32[]{:S(2)}) collective-permute-start(bf16[240,768]{1,0:T(8,128)(2,1)S(1)} %get-tuple-element.71), channel_id=1, source_target_pairs={{0,3},{1,0},{2,1},{3,2},{4,7},{5,4},{6,5},{7,6},{8,11},{9,8},{10,9... | collective-permute-start | bytes 1105928 | tf_op jit(solution)/shard_map/ppermute | solution.py:810
  96.0 38.8 %collective-permute-start.15 = (bf16[240,768]{1,0:T(8,128)(2,1)S(1)}, bf16[240,768]{1,0:T(8,128)(2,1)S(1)}, u32[]{:S(2)}, u32[]{:S(2)}) collective-permute-start(bf16[240,768]{1,0:T(8,128)(2,1)S(1)} %get-tuple-element.72), channel_id=1, source_target_pairs={{0,2},{1,3},{2,0},{3,1},{4,6},{5,7},{6,4},{7,5},{8,10},{9,11},{10,... | collective-permute-start | bytes 1105928 | tf_op jit(solution)/shard_map/ppermute | solution.py:810
  101.0 33.9 %collective-permute-start.16 = (bf16[240,768]{1,0:T(8,128)(2,1)S(1)}, bf16[240,768]{1,0:T(8,128)(2,1)S(1)}, u32[]{:S(2)}, u32[]{:S(2)}) collective-permute-start(bf16[240,768]{1,0:T(8,128)(2,1)S(1)} %get-tuple-element.73), channel_id=1, source_target_pairs={{0,1},{1,2},{2,3},{3,0},{4,5},{5,6},{6,7},{7,4},{8,9},{9,10},{10,1... | collective-permute-start | bytes 1105928 | tf_op jit(solution)/shard_map/ppermute | solution.py:810
  119.1 15.7 %collective-permute-start.17 = (f32[8,512]{1,0:T(8,128)S(1)}, f32[8,512]{1,0:T(8,128)S(1)}, u32[]{:S(2)}, u32[]{:S(2)}) collective-permute-start(f32[8,512]{1,0:T(8,128)S(1)} %get-tuple-element.84.refs_4_), channel_id=1, source_target_pairs={{0,1},{1,2},{2,3},{3,0},{4,5},{5,6},{6,7},{7,4},{8,9},{9,10},{10,1... | collective-permute-start | bytes 49160 | tf_op jit(solution)/shard_map/ppermute | solution.py:810
  119.7 17.2 %collective-permute-start.18 = (f32[8,512]{1,0:T(8,128)S(1)}, f32[8,512]{1,0:T(8,128)S(1)}, u32[]{:S(2)}, u32[]{:S(2)}) collective-permute-start(f32[8,512]{1,0:T(8,128)S(1)} %get-tuple-element.84.refs_4_), channel_id=1, source_target_pairs={{0,2},{1,3},{2,0},{3,1},{4,6},{5,7},{6,4},{7,5},{8,10},{9,11},{10,... | collective-permute-start | bytes 49160 | tf_op jit(solution)/shard_map/ppermute | solution.py:810
  123.5 13.4 %collective-permute-start.19 = (f32[8,512]{1,0:T(8,128)S(1)}, f32[8,512]{1,0:T(8,128)S(1)}, u32[]{:S(2)}, u32[]{:S(2)}) collective-permute-start(f32[8,512]{1,0:T(8,128)S(1)} %get-tuple-element.84.refs_4_), channel_id=1, source_target_pairs={{0,3},{1,0},{2,1},{3,2},{4,7},{5,4},{6,5},{7,6},{8,11},{9,8},{10,9... | collective-permute-start | bytes 49160 | tf_op jit(solution)/shard_map/ppermute | solution.py:810
  134.8 6.4 %collective-permute-start.11 = (bf16[128,768]{1,0:T(8,128)(2,1)S(1)}, bf16[128,768]{1,0:T(8,128)(2,1)S(1)}, u32[]{:S(2)}, u32[]{:S(2)}) collective-permute-start(bf16[128,768]{1,0:T(8,128)(2,1)S(1)} %get-tuple-element.67.refs_1_), channel_id=1, source_target_pairs={{0,3},{1,0},{2,1},{3,2},{4,7},{5,4},{6,5},{7,6},{8,11},{9,8},{10,9... | collective-permute-start | bytes 589832 | tf_op jit(solution)/shard_map/ppermute | solution.py:810
  134.8 16.7 %collective-permute-start.12 = (bf16[128,768]{1,0:T(8,128)(2,1)S(1)}, bf16[128,768]{1,0:T(8,128)(2,1)S(1)}, u32[]{:S(2)}, u32[]{:S(2)}) collective-permute-start(bf16[128,768]{1,0:T(8,128)(2,1)S(1)} %get-tuple-element.68.refs_2_), channel_id=1, source_target_pairs={{0,2},{1,3},{2,0},{3,1},{4,6},{5,7},{6,4},{7,5},{8,10},{9,11},{10,... | collective-permute-start | bytes 589832 | tf_op jit(solution)/shard_map/ppermute | solution.py:810
  134.8 17.3 %collective-permute-start.13 = (bf16[128,768]{1,0:T(8,128)(2,1)S(1)}, bf16[128,768]{1,0:T(8,128)(2,1)S(1)}, u32[]{:S(2)}, u32[]{:S(2)}) collective-permute-start(bf16[128,768]{1,0:T(8,128)(2,1)S(1)} %get-tuple-element.69.refs_3_), channel_id=1, source_target_pairs={{0,1},{1,2},{2,3},{3,0},{4,5},{5,6},{6,7},{7,4},{8,9},{9,10},{10,1... | collective-permute-start | bytes 589832 | tf_op jit(solution)/shard_map/ppermute | solution.py:810
  137.8 17.9 %copy-start.2 = (bf16[1,128,3072]{2,1,0:T(8,128)(2,1)S(1)}, bf16[1,128,3072]{2,1,0:T(8,128)(2,1)}, u32[]{:S(2)}) copy-start(bf16[1,128,3072]{2,1,0:T(8,128)(2,1)} %param.13) | copy-start | bytes 2359300
  137.9 15.0 %collective-permute-start.20 = (bf16[64,768]{1,0:T(8,128)(2,1)S(1)}, bf16[64,768]{1,0:T(8,128)(2,1)S(1)}, u32[]{:S(2)}, u32[]{:S(2)}) collective-permute-start(bf16[64,768]{1,0:T(8,128)(2,1)S(1)} %get-tuple-element.92), channel_id=1, source_target_pairs={{28,0},{29,1},{30,2},{31,3}} | collective-permute-start | bytes 294920 | tf_op jit(solution)/shard_map/ppermute | solution.py:837
  139.3 14.2 %collective-permute-start.21 = (bf16[64,768]{1,0:T(8,128)(2,1)S(1)}, bf16[64,768]{1,0:T(8,128)(2,1)S(1)}, u32[]{:S(2)}, u32[]{:S(2)}) collective-permute-start(bf16[64,768]{1,0:T(8,128)(2,1)S(1)} %get-tuple-element.98), channel_id=1, source_target_pairs={{28,4},{29,5},{30,6},{31,7}} | collective-permute-start | bytes 294920 | tf_op jit(solution)/shard_map/ppermute | solution.py:837
  141.2 17.9 %collective-permute-start.22 = (bf16[64,768]{1,0:T(8,128)(2,1)S(1)}, bf16[64,768]{1,0:T(8,128)(2,1)S(1)}, u32[]{:S(2)}, u32[]{:S(2)}) collective-permute-start(bf16[64,768]{1,0:T(8,128)(2,1)S(1)} %get-tuple-element.97), channel_id=1, source_target_pairs={{28,8},{29,9},{30,10},{31,11}} | collective-permute-start | bytes 294920 | tf_op jit(solution)/shard_map/ppermute | solution.py:837
  151.5 7.5 %collective-permute-start.23 = (bf16[64,768]{1,0:T(8,128)(2,1)S(1)}, bf16[64,768]{1,0:T(8,128)(2,1)S(1)}, u32[]{:S(2)}, u32[]{:S(2)}) collective-permute-start(bf16[64,768]{1,0:T(8,128)(2,1)S(1)} %get-tuple-element.96), channel_id=1, source_target_pairs={{28,12},{29,13},{30,14},{31,15}} | collective-permute-start | bytes 294920 | tf_op jit(solution)/shard_map/ppermute | solution.py:837
  152.2 6.9 %collective-permute-start.24 = (bf16[64,768]{1,0:T(8,128)(2,1)S(1)}, bf16[64,768]{1,0:T(8,128)(2,1)S(1)}, u32[]{:S(2)}, u32[]{:S(2)}) collective-permute-start(bf16[64,768]{1,0:T(8,128)(2,1)S(1)} %get-tuple-element.95), channel_id=1, source_target_pairs={{28,16},{29,17},{30,18},{31,19}} | collective-permute-start | bytes 294920 | tf_op jit(solution)/shard_map/ppermute | solution.py:837
  152.9 6.2 %collective-permute-start.25 = (bf16[64,768]{1,0:T(8,128)(2,1)S(1)}, bf16[64,768]{1,0:T(8,128)(2,1)S(1)}, u32[]{:S(2)}, u32[]{:S(2)}) collective-permute-start(bf16[64,768]{1,0:T(8,128)(2,1)S(1)} %get-tuple-element.94), channel_id=1, source_target_pairs={{28,20},{29,21},{30,22},{31,23}} | collective-permute-start | bytes 294920 | tf_op jit(solution)/shard_map/ppermute | solution.py:837
  153.6 5.5 %collective-permute-start.26 = (bf16[64,768]{1,0:T(8,128)(2,1)S(1)}, bf16[64,768]{1,0:T(8,128)(2,1)S(1)}, u32[]{:S(2)}, u32[]{:S(2)}) collective-permute-start(bf16[64,768]{1,0:T(8,128)(2,1)S(1)} %get-tuple-element.93), channel_id=1, source_target_pairs={{28,24},{29,25},{30,26},{31,27}} | collective-permute-start | bytes 294920 | tf_op jit(solution)/shard_map/ppermute | solution.py:837

commit v4 on v3

--- a/solution.py
+++ b/solution.py
@@ -358,7 +358,7 @@
 def pack_rows_kernel(parts, with_inverse, meta_ref, edge_ref, inner_ref, *out_refs):
     rows, width = inner_ref.shape
     wide = width // parts
-    edge = 1 if with_inverse else 2
+    edge = 2 if with_inverse else 1
     refs = out_refs[:parts]
     for r, out_ref in enumerate(refs):
         target = lax.rem(meta_ref[0] + r, parts)
@@ -549,18 +549,26 @@
         ).astype(BF16)
 
 
-def head_column(rows):
-    return pl.BlockSpec((rows, HEAD_DIM), lambda i, meta: (0, i))
-
-
-def heads_backward(meta, a_slots, c_slots, gain, offsets, onehot, heads):
+def head_column(rows, first=0):
+    return pl.BlockSpec((rows, HEAD_DIM), lambda i, meta: (0, i + first))
+
+
+def whole_column(rows, heads, first=0):
+    return pl.BlockSpec((rows, HEAD_DIM), lambda i, meta: (0, meta[0] * heads + first + i))
+
+
+def offset_spec(heads, first=0):
+    return pl.BlockSpec((1, 1, WINDOW), lambda i, meta: (meta[0] * heads + first + i, 0, 0))
+
+
+def heads_backward(meta, a_slots, c_slots, gain, offsets, onehot, heads, first, count):
     parts = len(a_slots)
     rows = c_slots[0].shape[0]
     tokens = rows * parts
     buckets = onehot.shape[0]
     packed = a_slots[0].shape[0]
     made = packed + 16
-    width = heads * HEAD_DIM
+    width = count * HEAD_DIM
     return pl.pallas_call(
         functools.partial(heads_backward_kernel, parts, rows),
         out_shape=(
@@ -569,12 +577,13 @@
         ),
         grid_spec=pltpu.PrefetchScalarGridSpec(
             num_scalar_prefetch=1,
-            grid=(heads,),
+            grid=(count,),
             in_specs=[
-                *[head_column(packed)] * parts,
-                *[head_column(rows)] * parts,
-                pl.BlockSpec((1, HEAD_DIM), lambda i, meta: (0, meta[0] * heads + i)),
-                pl.BlockSpec((1, 1, WINDOW), lambda i, meta: (meta[0] * heads + i, 0, 0)),
+                *[head_column(packed, first)] * parts,
+                whole_column(rows, heads, first),
+                *[head_column(rows, first)] * (parts - 1),
+                whole_column(1, heads, first),
+                offset_spec(heads, first),
                 pl.BlockSpec((buckets, WINDOW), lambda i, meta: (0, 0)),
             ],
             out_specs=(*[head_column(made)] * parts, head_column(1)),
@@ -589,7 +598,7 @@
         ),
         compiler_params=pltpu.CompilerParams(vmem_limit_bytes=VMEM_LIMIT),
         cost_estimate=pl.CostEstimate(
-            flops=heads * tokens * 400_000, bytes_accessed=tokens * width, transcendentals=0
+            flops=count * tokens * 400_000, bytes_accessed=tokens * width, transcendentals=0
         ),
         name="heads_backward",
     )(meta, *a_slots, *c_slots, gain, offsets, onehot)
@@ -656,8 +665,8 @@
             in_specs=[
                 *[head_column(packed)] * parts,
                 *[head_column(i_slots[0].shape[0])] * parts,
-                pl.BlockSpec((1, HEAD_DIM), lambda i, meta: (0, meta[0] * heads + i)),
-                pl.BlockSpec((1, 1, WINDOW), lambda i, meta: (meta[0] * heads + i, 0, 0)),
+                whole_column(1, heads),
+                offset_spec(heads),
             ],
             out_specs=(
                 *[head_column(rows)] * parts,
@@ -680,13 +689,13 @@
 
 
 def memory_kernel(parts, width, meta_ref, *refs):
-    out_refs, sum_refs = refs[:parts], refs[parts : 2 * parts]
-    gain_ref, memory_ref = refs[2 * parts :]
+    out_refs = refs[:parts]
+    sums_ref, gain_ref, after_ref, memory_ref = refs[parts:]
     rows = out_refs[0].shape[0]
     wide = memory_ref.shape[1]
-    total = sum_refs[0][:1]
-    for sum_ref in sum_refs[1:]:
-        total = total + sum_ref[:1]
+    total = sums_ref[0, :1]
+    for r in range(1, parts):
+        total = total + sums_ref[r, :1]
     inverse = lax.rsqrt(total / width + eps_norm)
     gain = gain_ref[:, pl.ds(pl.multiple_of(meta_ref[0] * wide, 128), wide)]
     spread_inverse = jnp.transpose(jnp.broadcast_to(inverse, (128, inverse.shape[1])))
@@ -697,18 +706,18 @@
     memory_ref[...] = (made * spread_inverse[:, :1] * gain).astype(BF16)
 
 
-def memory_rows(meta, outs, sums, gain, width):
+def memory_rows(meta, outs, sums, gain, after, width):
     parts = len(outs)
     rows, wide = outs[0].shape
     return pl.pallas_call(
         functools.partial(memory_kernel, parts, width),
         out_shape=jax.ShapeDtypeStruct((rows * parts, wide), BF16),
-        in_specs=[SMEM_SPEC] + [VMEM_SPEC] * (2 * parts + 1),
+        in_specs=[SMEM_SPEC] + [VMEM_SPEC] * (parts + 2) + [pl.BlockSpec(memory_space=pl.ANY)],
         out_specs=VMEM_SPEC,
         compiler_params=pltpu.CompilerParams(vmem_limit_bytes=VMEM_LIMIT),
-        cost_estimate=pl.CostEstimate(flops=4 * rows * width, bytes_accessed=4 * rows * width, transcendentals=0),
+        cost_estimate=pl.CostEstimate(flops=rows, bytes_accessed=rows, transcendentals=0),
         name="memory_rows",
-    )(meta, *outs, *sums, gain)
+    )(meta, *outs, sums, gain, after)
 
 
 def place_kernel(parts, meta_ref, *refs):
@@ -728,30 +737,32 @@
         in_specs=[SMEM_SPEC] + [VMEM_SPEC] * parts,
         out_specs=VMEM_SPEC,
         compiler_params=pltpu.CompilerParams(vmem_limit_bytes=VMEM_LIMIT),
-        cost_estimate=pl.CostEstimate(flops=0, bytes_accessed=4 * rows * wide * parts, transcendentals=0),
+        cost_estimate=pl.CostEstimate(flops=0, bytes_accessed=rows, transcendentals=0),
         name="place_columns",
     )(meta, *slots)
 
 
-def heads_finish_kernel(parts, meta_ref, *refs):
-    g_refs = refs[:parts]
-    x_ref, inverse_ref, gain_ref, cot_ref, out_ref, weight_ref, bias_ref, scaled_ref = refs[parts:]
+def heads_finish_kernel(parts, chunks, meta_ref, *refs):
+    g_refs = refs[: parts * chunks]
+    x_ref, inverse_ref, gain_ref, cot_ref, out_ref, weight_ref, bias_ref, scaled_ref = refs[parts * chunks :]
     rows, width = x_ref.shape
-    wide = width // parts
+    wide = width // parts // chunks
     heads = wide // HEAD_DIM
     depth = HEAD_DIM // parts
     buckets = bias_ref.shape[1]
-    for r in range(parts):
-        source = lax.rem(meta_ref[0] + r, parts)
-        columns = pl.ds(pl.multiple_of(source * wide, 128), wide)
-        scaled_ref[:, columns] = g_refs[r][:rows].astype(F32) * gain_ref[:, columns]
-        for h in range(heads):
-            lanes = slice(h * HEAD_DIM, (h + 1) * HEAD_DIM)
-            for j in range(3):
-                weight_ref[j, source * heads + h] = g_refs[r][
-                    rows + j * depth : rows + (j + 1) * depth, lanes
-                ].astype(F32)
-            bias_ref[source * heads + h] = g_refs[r][rows + 3 * depth :, lanes].astype(F32)[:buckets]
+    for c in range(chunks):
+        for r in range(parts):
+            g_ref = g_refs[c * parts + r]
+            place = lax.rem(meta_ref[0] + r, parts) * chunks + c
+            columns = pl.ds(pl.multiple_of(place * wide, 128), wide)
+            scaled_ref[:, columns] = g_ref[:rows].astype(F32) * gain_ref[:, columns]
+            for h in range(heads):
+                lanes = slice(h * HEAD_DIM, (h + 1) * HEAD_DIM)
+                for j in range(3):
+                    weight_ref[j, place * heads + h] = g_ref[
+                        rows + j * depth : rows + (j + 1) * depth, lanes
+                    ].astype(F32)
+                bias_ref[place * heads + h] = g_ref[rows + 3 * depth :, lanes].astype(F32)[:buckets]
     x = x_ref[...].astype(F32)
     scaled = scaled_ref[...]
     inverse = inverse_ref[:, :1]
@@ -760,24 +771,25 @@
     out_ref[...] = (cot_ref[...].astype(F32) + result).astype(BF16)
 
 
-def heads_finish(meta, g_slots, x, inverse, gain, cotangent, buckets):
-    parts = len(g_slots)
+def heads_finish(meta, g_chunks, x, inverse, gain, cotangent, buckets):
+    chunks, parts = len(g_chunks), len(g_chunks[0])
     rows, width = x.shape
     heads = width // HEAD_DIM
+    slots = [slot for g_slots in g_chunks for slot in g_slots]
     return pl.pallas_call(
-        functools.partial(heads_finish_kernel, parts),
+        functools.partial(heads_finish_kernel, parts, chunks),
         out_shape=(
             jax.ShapeDtypeStruct((rows, width), BF16),
             jax.ShapeDtypeStruct((3, heads, HEAD_DIM // parts, HEAD_DIM), F32),
             jax.ShapeDtypeStruct((heads, buckets // parts, HEAD_DIM), F32),
         ),
-        in_specs=[SMEM_SPEC] + [VMEM_SPEC] * (parts + 4),
+        in_specs=[SMEM_SPEC] + [VMEM_SPEC] * (len(slots) + 4),
         out_specs=(VMEM_SPEC,) * 3,
         scratch_shapes=[pltpu.VMEM((rows, width), F32)],
         compiler_params=pltpu.CompilerParams(vmem_limit_bytes=VMEM_LIMIT),
         cost_estimate=pl.CostEstimate(flops=12 * rows * width, bytes_accessed=14 * rows * width, transcendentals=0),
         name="heads_finish",
-    )(meta, *g_slots, x, inverse, gain, cotangent)
+    )(meta, *slots, x, inverse, gain, cotangent)
 
 
 def offset_table(rel_bias):
@@ -791,6 +803,21 @@
     count = lax.axis_size(axis)
     first, last = (max(0, -steps), min(count, count - steps))
     return lax.ppermute(value, axis, [(source, source + steps) for source in range(first, last)])
+
+
+def spread_memory(made, section, sections):
+    share = made.shape[0] // sections
+    last = sections - 1
+    if sections % 2:
+        memory = jnp.where(section == last, made[last * share :], 0)
+        for s in range(last):
+            memory = memory + lax.ppermute(made[s * share : (s + 1) * share], "section", [(last, s)])
+        return memory
+    couple = jnp.where(section == last, made[(last - 1) * share :], 0)
+    for s in range(0, last - 1, 2):
+        couple = couple + lax.ppermute(made[s * share : (s + 2) * share], "section", [(last, s + 1)])
+    even = lax.ppermute(couple[:share], "section", [(s + 1, s) for s in range(0, sections, 2)])
+    return jnp.where(section % 2 == 0, even, couple[share:])
 
 
 def heads_body(
@@ -806,40 +833,62 @@
         [lax.axis_index("seq"), section == 0, section == sections - 1]
     ).astype(jnp.int32)
 
-    def sent(value, r):
-        return lax.ppermute(value, "seq", [(i, (i + r) % parts) for i in range(parts)])
-
     def exchanged(sends, direction):
-        return [sends[0]] + [sent(sends[r], direction * r) for r in range(1, parts)]
-
-    came_back = shifted(returned[0], "section", -1)
-    arrived = shifted(carried[0], "section", 1)
+        moved = [
+            lax.ppermute(sends[r], "seq", [(i, (i + direction * r) % parts) for i in range(parts)])
+            for r in range(1, parts)
+        ]
+        return [sends[0]] + moved
+
+    def diagonal(value, r, step):
+        pairs = [
+            (s * parts + i, (s + step) % sections * parts + (i + r) % parts)
+            for s in range(sections)
+            for i in range(parts)
+        ]
+        return lax.ppermute(value, ("section", "seq"), pairs)
+
     inverse_b, *a_sends = pack_stash(meta, stash[0], norm_gain, qkv_weight[0], parts)
     a_slots = exchanged(a_sends, 1)
-    *c_sends, cotangent = pack_rows(meta, loss_grad, came_back, parts, False)
-    c_slots = exchanged(c_sends, 1)
-    i_slots = exchanged(pack_rows(meta, embedded, arrived, parts, True), 1)
+    meta_i, inverse_b = lax.optimization_barrier((meta, inverse_b))
+    i_sends = pack_rows(meta_i, embedded, carried[0], parts, True)
+    i_slots = [diagonal(i_sends[r], r, 1) for r in range(parts)]
+    meta_c, i_sends = lax.optimization_barrier((meta_i, i_sends))
+    *c_sends, cot_source = pack_rows(meta_c, loss_grad, returned[0], parts, False)
+    cotangent = diagonal(cot_source, 0, -1)
+    c_slots = [cotangent] + [diagonal(c_sends[r], r, -1) for r in range(1, parts)]
 
     offsets = offset_table(rel_bias[0])
     onehot = jnp.asarray(bucket_onehot(buckets).T)
-    *g_sends, gain_grad = heads_backward(meta, a_slots, c_slots, norm_gain, offsets, onehot, heads)
-    g_sends, i_slots = lax.optimization_barrier((g_sends, i_slots))
-    g_slots = exchanged(g_sends, -1)
-
     *o_sends, sums = heads_forward(meta, a_slots, i_slots, norm_gain, offsets, heads, rows)
-    all_sums = [sums] + [sent(sums, r) for r in range(1, parts)]
-    o_slots = exchanged(o_sends, -1)
-    g_slots, memory_gain = lax.optimization_barrier((g_slots, final_gain[None]))
-    made = memory_rows(meta, o_sends, all_sums, memory_gain, width)
-    share = rows * parts // sections
-    memory = jnp.where(section == sections - 1, made[(sections - 1) * share :], 0)
-    for s in range(sections - 1):
-        memory = memory + lax.ppermute(
-            made[s * share : (s + 1) * share], "section", [(sections - 1, s)]
+    all_sums = lax.all_gather(sums, "seq", axis=0, tiled=False)
+    o_sends, c_slots, sums = lax.optimization_barrier((o_sends, c_slots, sums))
+    waiting = exchanged(o_sends, -1)
+    gain_after, sums = lax.optimization_barrier((norm_gain, sums))
+
+    chunks = 2 if heads % 2 == 0 else 1
+    count = heads // chunks
+    g_chunks, gain_parts, o_slots = [], [], None
+    for c in range(chunks):
+        *g_sends, gain_part = heads_backward(
+            meta, a_slots, c_slots, gain_after, offsets, onehot, heads, c * count, count
         )
+        g_sends, waiting, gain_after, gain_part = lax.optimization_barrier(
+            (g_sends, waiting, gain_after, gain_part)
+        )
+        if o_slots is None:
+            o_slots = waiting
+        else:
+            g_chunks.append(waiting)
+        waiting = exchanged(g_sends, -1)
+        gain_parts.append(gain_part)
+    g_chunks.append(waiting)
+    gain_grad = jnp.concatenate(gain_parts, axis=1)
+    made = memory_rows(meta, o_sends, all_sums, final_gain[None], gain_parts[-1], width)
+    memory = spread_memory(made, section, sections)
 
     input_grad, weight_grad, bias_wide = heads_finish(
-        meta, g_slots, stash[0], inverse_b, norm_gain, cotangent, buckets
+        meta, g_chunks, stash[0], inverse_b, norm_gain, cotangent, buckets
     )
     bias_grad = bias_wide[:, :, 0].T
     output = place_columns(meta, o_slots)
@@ -849,7 +898,7 @@
         weight_grad[None],
         bias_grad[None],
         gain_grad,
-        memory.astype(BF16),
+        memory,
     )
 
 

time: 162 us -> 171 us (1.056)
  starting transfers between devices: 61.6 us -> 34.4 us
  blocking collectives: 0 us -> 18.4 us
  waiting for transfers between devices: 39.5 us -> 51.6 us
  local copies, waits for them, and re-layouts: 3.74 us -> 5.68 us
  other arithmetic: 0.77 us -> 2.5 us
    ppermute x27 -> x24, starting transfers between devices: 61.6 us -> 34.4 us  [the longest x12 21.2 us: exchanged(): lax.ppermute(sends[r], 'seq', [(i, (i + direction * r) % parts) for i in...]
    all_gather x0 -> x1, blocking collectives: none -> 18.4 us  [heads_body(): all_sums = lax.all_gather(sums, 'seq', axis=0, tiled=False)]
    ppermute x27 -> x24, waiting for transfers between devices: 39.5 us -> 51.6 us  [the longest x8 37.3 us: diagonal(): return lax.ppermute(value, ('section', 'seq'), pairs)]
    unnamed x22 -> x42, local copies, waits for them, and re-layouts: 2.95 us -> 4.12 us
    pallas_call x1 -> x2, Pallas kernels: 27 us -> 27.1 us  [heads_backward(): pl.pallas_call(functools.partial(heads_backward_kernel, parts, rows), out...]
  transfers between devices with their start and end apart: 27 -> 24, of which waited for: 5 -> 5; matrix products, arithmetic and copies ran while one was open for 1% -> 2% of each run, Pallas kernels for 33% -> 30%
where the time goes in v4:
time: 171 us; the launch traced here: 167 us
  Pallas kernels  53.8 us (31%)
  waiting for transfers between devices  51.6 us (30%)
  starting transfers between devices  34.4 us (20%)
  blocking collectives  18.4 us (11%)
  local copies, waits for them, and re-layouts  5.68 us (3%)
  other arithmetic  2.5 us (1%)
    ppermute x8, waiting for transfers between devices, diagonal(): return lax.ppermute(value, ('section', 'seq'), pairs)  37.3 us
    pallas_call x2, Pallas kernels, heads_backward(): pl.pallas_call(functools.partial(heads_backward_kernel, parts, rows), out...  27.1 us
    ppermute x12, starting transfers between devices, exchanged(): lax.ppermute(sends[r], 'seq', [(i, (i + direction * r) % parts) for i in...  21.2 us
    all_gather x1, blocking collectives, heads_body(): all_sums = lax.all_gather(sums, 'seq', axis=0, tiled=False)  18.4 us
    pallas_call x1, Pallas kernels, heads_forward(): pl.pallas_call(functools.partial(heads_forward_kernel, parts, rows), out_...  18.1 us
    ppermute x12, waiting for transfers between devices, exchanged(): lax.ppermute(sends[r], 'seq', [(i, (i + direction * r) % parts) for i in...  14.2 us
    ppermute x8, starting transfers between devices, diagonal(): return lax.ppermute(value, ('section', 'seq'), pairs)  7.83 us
    unnamed x42, local copies, waits for them, and re-layouts  4.12 us
  transfers between devices with their start and end apart: 24, of which 5 were waited for; matrix products, arithmetic and copies ran while one was open for 2% of the time, Pallas kernels for 30%

profile of v4, /device:TPU:0, one launch (start us, length us, event | category | flops | bytes accessed | tf_op | source)
XLA Modules:
  0.0 167.5 jit_solution(3656963232596331167)
XLA Ops:
  0.6 0.0 copy-start
  0.7 0.1 pad_add_fusion.meta_ref
  0.7 1.1 copy-done.1
  1.9 1.1 copy-done.7
  2.9 0.7 copy-done.8
  3.6 1.3 pack_stash.1
  4.9 0.0 copy-start.4
  4.9 1.1 copy-done.4
  6.1 0.9 pack_inbound.1
  7.0 0.0 copy-start.9
  7.0 0.5 collective-permute-start.3
  7.5 1.4 pack_cotangent.1
  8.9 3.2 %collective-permute-start.7 = (bf16[128,3072]{1,0:T(8,128)(2,1)S(1)}, bf16[128,3072]{1,0:T(8,128)(2,1)S(1)}, u32[]{:S(2)}, u32[]{:S(2)}) collective-permute-start(bf16[128,3072]{1,0:T(8,128)(2,1)S(1)} %get-tuple-element.82), channel_id=1, source_target_pairs={{0,28},{1,29},{2,30},{3,31},{4,0},{5,1},{6,2},{7,3},{8,4},{9,5},{1... | collective-permute-start | bytes 2359304 | tf_op jit(solution)/shard_map/ppermute | solution.py:849
  12.1 0.6 collective-permute-start.4
  12.7 1.6 collective-permute-start
  14.3 2.5 %collective-permute-start.1 = (bf16[224,768]{1,0:T(8,128)(2,1)S(1)}, bf16[224,768]{1,0:T(8,128)(2,1)S(1)}, u32[]{:S(2)}, u32[]{:S(2)}) collective-permute-start(bf16[224,768]{1,0:T(8,128)(2,1)S(1)} %get-tuple-element.69), channel_id=1, source_target_pairs={{0,2},{1,3},{2,0},{3,1},{4,6},{5,7},{6,4},{7,5},{8,10},{9,11},{10,... | collective-permute-start | bytes 1032200 | tf_op jit(solution)/shard_map/ppermute | solution.py:838
  16.7 1.1 collective-permute-start.5
  17.8 5.7 %collective-permute-done.4.refs_5_ = bf16[144,768]{1,0:T(8,128)(2,1)S(1)} collective-permute-done((bf16[144,768]{1,0:T(8,128)(2,1)S(1)}, bf16[144,768]{1,0:T(8,128)(2,1)S(1)}, u32[]{:S(2)}, u32[]{:S(2)}) %collective-permute-start.4) | collective-permute-done | bytes 221216 | tf_op jit(solution)/shard_map/ppermute | solution.py:849
  23.6 0.0 collective-permute-start.6
  23.6 31.6 %collective-permute-done.5.refs_6_ = bf16[144,768]{1,0:T(8,128)(2,1)S(1)} collective-permute-done((bf16[144,768]{1,0:T(8,128)(2,1)S(1)}, bf16[144,768]{1,0:T(8,128)(2,1)S(1)}, u32[]{:S(2)}, u32[]{:S(2)}) %collective-permute-start.5) | collective-permute-done | bytes 221216 | tf_op jit(solution)/shard_map/ppermute | solution.py:849
  55.1 5.2 %collective-permute-start.2 = (bf16[224,768]{1,0:T(8,128)(2,1)S(1)}, bf16[224,768]{1,0:T(8,128)(2,1)S(1)}, u32[]{:S(2)}, u32[]{:S(2)}) collective-permute-start(bf16[224,768]{1,0:T(8,128)(2,1)S(1)} %get-tuple-element.70), channel_id=1, source_target_pairs={{0,3},{1,0},{2,1},{3,2},{4,7},{5,4},{6,5},{7,6},{8,11},{9,8},{10,9... | collective-permute-start | bytes 1032200 | tf_op jit(solution)/shard_map/ppermute | solution.py:838
  60.4 0.0 collective-permute-done.6.refs_7_
  60.4 0.0 collective-permute-done.refs_1_
  60.4 2.5 %collective-permute-start.8 = (bf16[128,768]{1,0:T(8,128)(2,1)S(1)}, bf16[128,768]{1,0:T(8,128)(2,1)S(1)}, u32[]{:S(2)}, u32[]{:S(2)}) collective-permute-start(bf16[128,768]{1,0:T(8,128)(2,1)S(1)} %get-tuple-element.83), channel_id=1, source_target_pairs={{0,29},{1,30},{2,31},{3,28},{4,1},{5,2},{6,3},{7,0},{8,5},{9,6},{1... | collective-permute-start | bytes 589832 | tf_op jit(solution)/shard_map/ppermute | solution.py:849
  62.9 0.0 collective-permute-done.1.refs_2_
  62.9 0.0 collective-permute-start.9
  62.9 0.2 fusion
  63.1 0.0 copy-start.10
  63.2 5.8 %collective-permute-done.2.refs_3_ = bf16[224,768]{1,0:T(8,128)(2,1)S(1)} collective-permute-done((bf16[224,768]{1,0:T(8,128)(2,1)S(1)}, bf16[224,768]{1,0:T(8,128)(2,1)S(1)}, u32[]{:S(2)}, u32[]{:S(2)}) %collective-permute-start.2) | collective-permute-done | bytes 344096 | tf_op jit(solution)/shard_map/ppermute | solution.py:838
  69.0 18.1 %heads_forward.1 = (bf16[128,768]{1,0:T(8,128)(2,1)S(1)}, bf16[128,768]{1,0:T(8,128)(2,1)S(1)}, bf16[128,768]{1,0:T(8,128)(2,1)S(1)}, bf16[128,768]{1,0:T(8,128)(2,1)S(1)}, f32[8,512]{1,0:T(8,128)S(1)}) custom-call(s32[3]{0:T(128)S(1)} %pad_add_fusion.meta_ref, bf16[224,768]{1,0:T(8,128)(2,1)S(1)} %get-tuple-element.67.refs_0_, ...), custom_call_target="tpu_custom_call" | custom-call | flops 3072 | bytes 512 | tf_op jit(solution)/shard_map/heads_forward/pallas_call | solution.py:656
  87.1 0.0 collective-permute-done.10.refs_7_
  87.1 0.0 collective-permute-done.8.refs_5_
  87.1 0.0 collective-permute-done.7.refs_4_.refs_11_
  87.1 4.3 %collective-permute-start.11 = (bf16[128,768]{1,0:T(8,128)(2,1)S(1)}, bf16[128,768]{1,0:T(8,128)(2,1)S(1)}, u32[]{:S(2)}, u32[]{:S(2)}) collective-permute-start(bf16[128,768]{1,0:T(8,128)(2,1)S(1)} %get-tuple-element.96.refs_1_), channel_id=1, source_target_pairs={{0,3},{1,0},{2,1},{3,2},{4,7},{5,4},{6,5},{7,6},{8,11},{9,8},{10,9... | collective-permute-start | bytes 589832 | tf_op jit(solution)/shard_map/ppermute | solution.py:838
  91.5 0.0 collective-permute-start.12
  91.5 0.6 collective-permute-start.13
  92.1 13.5 %heads_backward.2 = (bf16[240,384]{1,0:T(8,128)(2,1)S(1)}, bf16[240,384]{1,0:T(8,128)(2,1)S(1)}, bf16[240,384]{1,0:T(8,128)(2,1)S(1)}, bf16[240,384]{1,0:T(8,128)(2,1)S(1)}, f32[1,384]{1,0:T(1,128)S(1)}) custom-call(s32[3]{0:T(128)S(1)} %pad_add_fusion.meta_ref, bf16[224,768]{1,0:T(8,128)(2,1)S(1)} %get-tuple-element.67.refs_0_, ...), custom_call_target="tpu_custom_call" | custom-call | flops 614400000 | bytes 196608 | tf_op jit(solution)/shard_map/heads_backward/pallas_call | solution.py:572
  105.6 0.0 collective-permute-done.11.refs_1_
  105.7 0.0 collective-permute-done.13.refs_3_
  105.7 3.2 %collective-permute-start.14 = (bf16[240,384]{1,0:T(8,128)(2,1)S(1)}, bf16[240,384]{1,0:T(8,128)(2,1)S(1)}, u32[]{:S(2)}, u32[]{:S(2)}) collective-permute-start(bf16[240,384]{1,0:T(8,128)(2,1)S(1)} %get-tuple-element.110), channel_id=1, source_target_pairs={{0,3},{1,0},{2,1},{3,2},{4,7},{5,4},{6,5},{7,6},{8,11},{9,8},{10,9... | collective-permute-start | bytes 552968 | tf_op jit(solution)/shard_map/ppermute | solution.py:838
  108.9 1.1 collective-permute-start.15
  110.0 0.0 collective-permute-start.16
  110.0 18.4 %all-gather = f32[32,512]{1,0:T(8,128)S(1)} all-gather(f32[8,512]{1,0:T(8,128)S(1)} %get-tuple-element.86), channel_id=2, replica_groups=mesh['section'=8,'seq'=4] {'seq'}, dimensions={0}, use_global_device_ids=true | all-gather | bytes 81920 | tf_op jit(solution)/shard_map/all_gather | solution.py:864
  128.4 13.5 %heads_backward.3 = (bf16[240,384]{1,0:T(8,128)(2,1)S(1)}, bf16[240,384]{1,0:T(8,128)(2,1)S(1)}, bf16[240,384]{1,0:T(8,128)(2,1)S(1)}, bf16[240,384]{1,0:T(8,128)(2,1)S(1)}, f32[1,384]{1,0:T(1,128)S(1)}) custom-call(s32[3]{0:T(128)S(1)} %pad_add_fusion.meta_ref, bf16[224,768]{1,0:T(8,128)(2,1)S(1)} %get-tuple-element.67.refs_0_, ...), custom_call_target="tpu_custom_call" | custom-call | flops 614400000 | bytes 196608 | tf_op jit(solution)/shard_map/heads_backward/pallas_call | solution.py:572
  142.0 0.0 collective-permute-done.15.refs_2_
  142.0 0.0 collective-permute-done.16.refs_3_
  142.0 0.9 memory_rows.1
  142.9 0.8 fusion.5
  143.8 1.4 collective-permute-start.20
  145.1 1.3 collective-permute-start.21
  146.5 1.3 collective-permute-start.22
  147.8 1.5 place_columns.1
  149.3 1.4 collective-permute-start.17
  150.7 0.0 collective-permute-done.20
  150.7 1.2 collective-permute-start.19
  151.9 0.0 collective-permute-done.21
  151.9 1.2 fusion.3
  153.1 1.3 collective-permute-start.23
  154.4 0.6 pad_maximum_fusion
  155.0 2.5 %collective-permute-done.17.refs_5_ = bf16[240,384]{1,0:T(8,128)(2,1)S(1)} collective-permute-done((bf16[240,384]{1,0:T(8,128)(2,1)S(1)}, bf16[240,384]{1,0:T(8,128)(2,1)S(1)}, u32[]{:S(2)}, u32[]{:S(2)}) %collective-permute-start.17) | collective-permute-done | bytes 184352 | tf_op jit(solution)/shard_map/ppermute | solution.py:838
  157.5 5.9 %collective-permute-done.18.refs_6_ = bf16[240,384]{1,0:T(8,128)(2,1)S(1)} collective-permute-done((bf16[240,384]{1,0:T(8,128)(2,1)S(1)}, bf16[240,384]{1,0:T(8,128)(2,1)S(1)}, u32[]{:S(2)}, u32[]{:S(2)}) %collective-permute-start.18) | collective-permute-done | bytes 184352 | tf_op jit(solution)/shard_map/ppermute | solution.py:838
  163.5 2.6 %heads_finish.1 = (bf16[128,3072]{1,0:T(8,128)(2,1)}, f32[3,24,32,128]{3,2,1,0:T(8,128)}, f32[24,8,128]{2,1,0:T(8,128)S(1)}) custom-call(s32[3]{0:T(128)S(1)} %pad_add_fusion.meta_ref, bf16[240,384]{1,0:T(8,128)(2,1)S(1)} %get-tuple-element.114.refs_0_, bf16[240,384]{1,0:T(8,128)(2,1)S(1)} %collective-permute-done.14.refs_1_, ...), custom_call_target="tpu_custom_call" | custom-call | flops 4718592 | bytes 5505024 | tf_op jit(solution)/shard_map/heads_finish/pallas_call | solution.py:779
  166.1 0.7 copy.18
  166.8 0.7 slice_select_fusion.1
  (46 shorter events, 0.1 us)
Async XLA Ops:
  0.6 62.2 %copy-start = (f32[1,32,24]{1,2,0:T(8,128)S(1)}, f32[1,32,24]{1,2,0:T(8,128)}, u32[]{:S(2)}) copy-start(f32[1,32,24]{1,2,0:T(8,128)} %param.17) | copy-start | bytes 9220
  0.7 1.1 copy-start.1
  1.9 1.1 copy-start.7
  2.9 0.7 copy-start.8
  3.6 1.3 copy-start.3
  4.9 1.1 copy-start.4
  6.0 1.5 copy-start.5
  6.1 1.5 copy-start.6
  7.0 55.9 %copy-start.20 = (f32[256,32]{1,0:T(8,128)S(1)}, f32[256,32]{1,0:T(8,128)}, u32[]{:S(2)}) copy-start(f32[256,32]{1,0:T(8,128)} %constant.35.clone) | copy-start | bytes 98308
  7.0 62.0 %copy-start.9 = (f32[1,3072]{1,0:T(1,128)S(1)}, f32[1,3072]{1,0:T(1,128)}, u32[]{:S(2)}) copy-start(f32[1,3072]{1,0:T(1,128)} %refs_10_.3) | copy-start | bytes 36868
  7.0 9.7 %collective-permute-start.3 = (bf16[144,768]{1,0:T(8,128)(2,1)S(1)}, bf16[144,768]{1,0:T(8,128)(2,1)S(1)}, u32[]{:S(2)}, u32[]{:S(2)}) collective-permute-start(bf16[144,768]{1,0:T(8,128)(2,1)S(1)} %get-tuple-element.73), channel_id=1, source_target_pairs={{0,4},{1,5},{2,6},{3,7},{4,8},{5,9},{6,10},{7,11},{8,12},{9,13},{1... | collective-permute-start | bytes 663560 | tf_op jit(solution)/shard_map/ppermute | solution.py:849
  8.9 78.2 %collective-permute-start.7 = (bf16[128,3072]{1,0:T(8,128)(2,1)S(1)}, bf16[128,3072]{1,0:T(8,128)(2,1)S(1)}, u32[]{:S(2)}, u32[]{:S(2)}) collective-permute-start(bf16[128,3072]{1,0:T(8,128)(2,1)S(1)} %get-tuple-element.82), channel_id=1, source_target_pairs={{0,28},{1,29},{2,30},{3,31},{4,0},{5,1},{6,2},{7,3},{8,4},{9,5},{1... | collective-permute-start | bytes 2359304 | tf_op jit(solution)/shard_map/ppermute | solution.py:849
  12.1 11.4 %collective-permute-start.4 = (bf16[144,768]{1,0:T(8,128)(2,1)S(1)}, bf16[144,768]{1,0:T(8,128)(2,1)S(1)}, u32[]{:S(2)}, u32[]{:S(2)}) collective-permute-start(bf16[144,768]{1,0:T(8,128)(2,1)S(1)} %get-tuple-element.74), channel_id=1, source_target_pairs={{0,5},{1,6},{2,7},{3,4},{4,9},{5,10},{6,11},{7,8},{8,13},{9,14},{1... | collective-permute-start | bytes 663560 | tf_op jit(solution)/shard_map/ppermute | solution.py:849
  12.7 47.7 %collective-permute-start = (bf16[224,768]{1,0:T(8,128)(2,1)S(1)}, bf16[224,768]{1,0:T(8,128)(2,1)S(1)}, u32[]{:S(2)}, u32[]{:S(2)}) collective-permute-start(bf16[224,768]{1,0:T(8,128)(2,1)S(1)} %get-tuple-element.68), channel_id=1, source_target_pairs={{0,1},{1,2},{2,3},{3,0},{4,5},{5,6},{6,7},{7,4},{8,9},{9,10},{10,1... | collective-permute-start | bytes 1032200 | tf_op jit(solution)/shard_map/ppermute | solution.py:838
  14.3 48.6 %collective-permute-start.1 = (bf16[224,768]{1,0:T(8,128)(2,1)S(1)}, bf16[224,768]{1,0:T(8,128)(2,1)S(1)}, u32[]{:S(2)}, u32[]{:S(2)}) collective-permute-start(bf16[224,768]{1,0:T(8,128)(2,1)S(1)} %get-tuple-element.69), channel_id=1, source_target_pairs={{0,2},{1,3},{2,0},{3,1},{4,6},{5,7},{6,4},{7,5},{8,10},{9,11},{10,... | collective-permute-start | bytes 1032200 | tf_op jit(solution)/shard_map/ppermute | solution.py:838
  16.7 38.4 %collective-permute-start.5 = (bf16[144,768]{1,0:T(8,128)(2,1)S(1)}, bf16[144,768]{1,0:T(8,128)(2,1)S(1)}, u32[]{:S(2)}, u32[]{:S(2)}) collective-permute-start(bf16[144,768]{1,0:T(8,128)(2,1)S(1)} %get-tuple-element.75), channel_id=1, source_target_pairs={{0,6},{1,7},{2,4},{3,5},{4,10},{5,11},{6,8},{7,9},{8,14},{9,15},{1... | collective-permute-start | bytes 663560 | tf_op jit(solution)/shard_map/ppermute | solution.py:849
  23.6 36.8 %collective-permute-start.6 = (bf16[144,768]{1,0:T(8,128)(2,1)S(1)}, bf16[144,768]{1,0:T(8,128)(2,1)S(1)}, u32[]{:S(2)}, u32[]{:S(2)}) collective-permute-start(bf16[144,768]{1,0:T(8,128)(2,1)S(1)} %get-tuple-element.76), channel_id=1, source_target_pairs={{0,7},{1,4},{2,5},{3,6},{4,11},{5,8},{6,9},{7,10},{8,15},{9,12},{1... | collective-permute-start | bytes 663560 | tf_op jit(solution)/shard_map/ppermute | solution.py:849
  55.1 13.8 %collective-permute-start.2 = (bf16[224,768]{1,0:T(8,128)(2,1)S(1)}, bf16[224,768]{1,0:T(8,128)(2,1)S(1)}, u32[]{:S(2)}, u32[]{:S(2)}) collective-permute-start(bf16[224,768]{1,0:T(8,128)(2,1)S(1)} %get-tuple-element.70), channel_id=1, source_target_pairs={{0,3},{1,0},{2,1},{3,2},{4,7},{5,4},{6,5},{7,6},{8,11},{9,8},{10,9... | collective-permute-start | bytes 1032200 | tf_op jit(solution)/shard_map/ppermute | solution.py:838
  60.4 26.7 %collective-permute-start.10 = (bf16[128,768]{1,0:T(8,128)(2,1)S(1)}, bf16[128,768]{1,0:T(8,128)(2,1)S(1)}, u32[]{:S(2)}, u32[]{:S(2)}) collective-permute-start(bf16[128,768]{1,0:T(8,128)(2,1)S(1)} %get-tuple-element.85), channel_id=1, source_target_pairs={{0,31},{1,28},{2,29},{3,30},{4,3},{5,0},{6,1},{7,2},{8,7},{9,4},{1... | collective-permute-start | bytes 589832 | tf_op jit(solution)/shard_map/ppermute | solution.py:849
  60.4 26.7 %collective-permute-start.8 = (bf16[128,768]{1,0:T(8,128)(2,1)S(1)}, bf16[128,768]{1,0:T(8,128)(2,1)S(1)}, u32[]{:S(2)}, u32[]{:S(2)}) collective-permute-start(bf16[128,768]{1,0:T(8,128)(2,1)S(1)} %get-tuple-element.83), channel_id=1, source_target_pairs={{0,29},{1,30},{2,31},{3,28},{4,1},{5,2},{6,3},{7,0},{8,5},{9,6},{1... | collective-permute-start | bytes 589832 | tf_op jit(solution)/shard_map/ppermute | solution.py:849
  62.9 24.2 %collective-permute-start.9 = (bf16[128,768]{1,0:T(8,128)(2,1)S(1)}, bf16[128,768]{1,0:T(8,128)(2,1)S(1)}, u32[]{:S(2)}, u32[]{:S(2)}) collective-permute-start(bf16[128,768]{1,0:T(8,128)(2,1)S(1)} %get-tuple-element.84), channel_id=1, source_target_pairs={{0,30},{1,31},{2,28},{3,29},{4,2},{5,3},{6,0},{7,1},{8,6},{9,7},{1... | collective-permute-start | bytes 589832 | tf_op jit(solution)/shard_map/ppermute | solution.py:849
  63.1 29.0 %copy-start.10 = (f32[32,256]{1,0:T(8,128)S(1)}, f32[32,256]{1,0:T(8,128)}, u32[]{:S(2)}) copy-start(f32[32,256]{1,0:T(8,128)} %constant.36.clone.refs_10_) | copy-start | bytes 98308
  87.1 18.5 %collective-permute-start.11 = (bf16[128,768]{1,0:T(8,128)(2,1)S(1)}, bf16[128,768]{1,0:T(8,128)(2,1)S(1)}, u32[]{:S(2)}, u32[]{:S(2)}) collective-permute-start(bf16[128,768]{1,0:T(8,128)(2,1)S(1)} %get-tuple-element.96.refs_1_), channel_id=1, source_target_pairs={{0,3},{1,0},{2,1},{3,2},{4,7},{5,4},{6,5},{7,6},{8,11},{9,8},{10,9... | collective-permute-start | bytes 589832 | tf_op jit(solution)/shard_map/ppermute | solution.py:838
  91.5 14.2 %collective-permute-start.12 = (bf16[128,768]{1,0:T(8,128)(2,1)S(1)}, bf16[128,768]{1,0:T(8,128)(2,1)S(1)}, u32[]{:S(2)}, u32[]{:S(2)}) collective-permute-start(bf16[128,768]{1,0:T(8,128)(2,1)S(1)} %get-tuple-element.97.refs_2_), channel_id=1, source_target_pairs={{0,2},{1,3},{2,0},{3,1},{4,6},{5,7},{6,4},{7,5},{8,10},{9,11},{10,... | collective-permute-start | bytes 589832 | tf_op jit(solution)/shard_map/ppermute | solution.py:838
  91.5 14.2 %collective-permute-start.13 = (bf16[128,768]{1,0:T(8,128)(2,1)S(1)}, bf16[128,768]{1,0:T(8,128)(2,1)S(1)}, u32[]{:S(2)}, u32[]{:S(2)}) collective-permute-start(bf16[128,768]{1,0:T(8,128)(2,1)S(1)} %get-tuple-element.98.refs_3_), channel_id=1, source_target_pairs={{0,1},{1,2},{2,3},{3,0},{4,5},{5,6},{6,7},{7,4},{8,9},{9,10},{10,1... | collective-permute-start | bytes 589832 | tf_op jit(solution)/shard_map/ppermute | solution.py:838
  105.7 36.3 %collective-permute-start.14 = (bf16[240,384]{1,0:T(8,128)(2,1)S(1)}, bf16[240,384]{1,0:T(8,128)(2,1)S(1)}, u32[]{:S(2)}, u32[]{:S(2)}) collective-permute-start(bf16[240,384]{1,0:T(8,128)(2,1)S(1)} %get-tuple-element.110), channel_id=1, source_target_pairs={{0,3},{1,0},{2,1},{3,2},{4,7},{5,4},{6,5},{7,6},{8,11},{9,8},{10,9... | collective-permute-start | bytes 552968 | tf_op jit(solution)/shard_map/ppermute | solution.py:838
  108.9 33.1 %collective-permute-start.15 = (bf16[240,384]{1,0:T(8,128)(2,1)S(1)}, bf16[240,384]{1,0:T(8,128)(2,1)S(1)}, u32[]{:S(2)}, u32[]{:S(2)}) collective-permute-start(bf16[240,384]{1,0:T(8,128)(2,1)S(1)} %get-tuple-element.111), channel_id=1, source_target_pairs={{0,2},{1,3},{2,0},{3,1},{4,6},{5,7},{6,4},{7,5},{8,10},{9,11},{10,... | collective-permute-start | bytes 552968 | tf_op jit(solution)/shard_map/ppermute | solution.py:838
  110.0 32.0 %collective-permute-start.16 = (bf16[240,384]{1,0:T(8,128)(2,1)S(1)}, bf16[240,384]{1,0:T(8,128)(2,1)S(1)}, u32[]{:S(2)}, u32[]{:S(2)}) collective-permute-start(bf16[240,384]{1,0:T(8,128)(2,1)S(1)} %get-tuple-element.112), channel_id=1, source_target_pairs={{0,1},{1,2},{2,3},{3,0},{4,5},{5,6},{6,7},{7,4},{8,9},{9,10},{10,1... | collective-permute-start | bytes 552968 | tf_op jit(solution)/shard_map/ppermute | solution.py:838
  128.4 13.6 %copy-start.11 = (f32[3072]{0:T(1024)S(1)}, f32[3072]{0:T(1024)}, u32[]{:S(2)}) copy-start(f32[3072]{0:T(1024)} %param.19) | copy-start | bytes 36868
  142.0 1.8 %copy-start.12 = (bf16[240,384]{1,0:T(8,128)(2,1)}, bf16[240,384]{1,0:T(8,128)(2,1)S(1)}, u32[]{:S(2)}) copy-start(bf16[240,384]{1,0:T(8,128)(2,1)S(1)} %get-tuple-element.121) | copy-start | bytes 552964
  142.0 1.8 %copy-start.14 = (bf16[240,384]{1,0:T(8,128)(2,1)}, bf16[240,384]{1,0:T(8,128)(2,1)S(1)}, u32[]{:S(2)}) copy-start(bf16[240,384]{1,0:T(8,128)(2,1)S(1)} %get-tuple-element.120) | copy-start | bytes 552964
  142.0 1.8 %copy-start.16 = (bf16[240,384]{1,0:T(8,128)(2,1)}, bf16[240,384]{1,0:T(8,128)(2,1)S(1)}, u32[]{:S(2)}) copy-start(bf16[240,384]{1,0:T(8,128)(2,1)S(1)} %get-tuple-element.119) | copy-start | bytes 552964
  143.8 6.9 %collective-permute-start.20 = (bf16[128,768]{1,0:T(8,128)(2,1)}, bf16[128,768]{1,0:T(8,128)(2,1)}, u32[]{:S(2)}, u32[]{:S(2)}) collective-permute-start(bf16[128,768]{1,0:T(8,128)(2,1)} %get-tuple-element.134), channel_id=1, source_target_pairs={{28,4},{29,5},{30,6},{31,7}} | collective-permute-start | bytes 589832 | tf_op jit(solution)/shard_map/ppermute | solution.py:818
  145.1 6.8 %collective-permute-start.21 = (bf16[128,768]{1,0:T(8,128)(2,1)}, bf16[128,768]{1,0:T(8,128)(2,1)}, u32[]{:S(2)}, u32[]{:S(2)}) collective-permute-start(bf16[128,768]{1,0:T(8,128)(2,1)} %get-tuple-element.136), channel_id=1, source_target_pairs={{28,12},{29,13},{30,14},{31,15}} | collective-permute-start | bytes 589832 | tf_op jit(solution)/shard_map/ppermute | solution.py:818
  146.5 5.5 %collective-permute-start.22 = (bf16[128,768]{1,0:T(8,128)(2,1)}, bf16[128,768]{1,0:T(8,128)(2,1)}, u32[]{:S(2)}, u32[]{:S(2)}) collective-permute-start(bf16[128,768]{1,0:T(8,128)(2,1)} %get-tuple-element.135), channel_id=1, source_target_pairs={{28,20},{29,21},{30,22},{31,23}} | collective-permute-start | bytes 589832 | tf_op jit(solution)/shard_map/ppermute | solution.py:818
  147.8 1.5 copy-start.17
  147.8 2.9 %copy-start.15 = (bf16[240,384]{1,0:T(8,128)(2,1)S(1)}, bf16[240,384]{1,0:T(8,128)(2,1)}, u32[]{:S(2)}) copy-start(bf16[240,384]{1,0:T(8,128)(2,1)} %copy-done.14) | copy-start | bytes 552964
  147.8 2.9 %copy-start.13 = (bf16[240,384]{1,0:T(8,128)(2,1)S(1)}, bf16[240,384]{1,0:T(8,128)(2,1)}, u32[]{:S(2)}) copy-start(bf16[240,384]{1,0:T(8,128)(2,1)} %copy-done.12) | copy-start | bytes 552964
  147.8 15.7 %copy-start.2 = (bf16[1,128,3072]{2,1,0:T(8,128)(2,1)S(1)}, bf16[1,128,3072]{2,1,0:T(8,128)(2,1)}, u32[]{:S(2)}) copy-start(bf16[1,128,3072]{2,1,0:T(8,128)(2,1)} %param.13) | copy-start | bytes 2359300
  149.3 8.2 %collective-permute-start.17 = (bf16[240,384]{1,0:T(8,128)(2,1)S(1)}, bf16[240,384]{1,0:T(8,128)(2,1)S(1)}, u32[]{:S(2)}, u32[]{:S(2)}) collective-permute-start(bf16[240,384]{1,0:T(8,128)(2,1)S(1)} %copy-done.17), channel_id=1, source_target_pairs={{0,3},{1,0},{2,1},{3,2},{4,7},{5,4},{6,5},{7,6},{8,11},{9,8},{10,9... | collective-permute-start | bytes 552968 | tf_op jit(solution)/shard_map/ppermute | solution.py:838
  150.7 12.8 %collective-permute-start.18 = (bf16[240,384]{1,0:T(8,128)(2,1)S(1)}, bf16[240,384]{1,0:T(8,128)(2,1)S(1)}, u32[]{:S(2)}, u32[]{:S(2)}) collective-permute-start(bf16[240,384]{1,0:T(8,128)(2,1)S(1)} %copy-done.15), channel_id=1, source_target_pairs={{0,2},{1,3},{2,0},{3,1},{4,6},{5,7},{6,4},{7,5},{8,10},{9,11},{10,... | collective-permute-start | bytes 552968 | tf_op jit(solution)/shard_map/ppermute | solution.py:838
  150.7 12.8 %collective-permute-start.19 = (bf16[240,384]{1,0:T(8,128)(2,1)S(1)}, bf16[240,384]{1,0:T(8,128)(2,1)S(1)}, u32[]{:S(2)}, u32[]{:S(2)}) collective-permute-start(bf16[240,384]{1,0:T(8,128)(2,1)S(1)} %copy-done.13), channel_id=1, source_target_pairs={{0,1},{1,2},{2,3},{3,0},{4,5},{5,6},{6,7},{7,4},{8,9},{9,10},{10,1... | collective-permute-start | bytes 552968 | tf_op jit(solution)/shard_map/ppermute | solution.py:838
  153.1 10.3 %copy-start.18 = (bf16[128,768]{1,0:T(8,128)(2,1)}, bf16[128,768]{1,0:T(8,128)(2,1)S(1)}, u32[]{:S(2)}) copy-start(bf16[128,768]{1,0:T(8,128)(2,1)S(1)} %fusion.3) | copy-start | bytes 589828
  153.1 13.7 %collective-permute-start.23 = (bf16[64,768]{1,0:T(8,128)(2,1)S(1)}, bf16[64,768]{1,0:T(8,128)(2,1)S(1)}, u32[]{:S(2)}, u32[]{:S(2)}) collective-permute-start(bf16[64,768]{1,0:T(8,128)(2,1)S(1)} %slice.32), channel_id=1, source_target_pairs={{4,0},{12,8},{20,16},{28,24},{5,1},{13,9},{21,17},{29,25},{6,2},{1... | collective-permute-start | bytes 294920 | tf_op jit(solution)/shard_map/ppermute | solution.py:819
  163.5 3.4 %copy-start.19 = (bf16[128,768]{1,0:T(8,128)(2,1)S(1)}, bf16[128,768]{1,0:T(8,128)(2,1)}, u32[]{:S(2)}) copy-start(bf16[128,768]{1,0:T(8,128)(2,1)} %copy-done.18) | copy-start | bytes 589828

commit v5 on v4

--- a/solution.py
+++ b/solution.py
@@ -358,7 +358,7 @@
 def pack_rows_kernel(parts, with_inverse, meta_ref, edge_ref, inner_ref, *out_refs):
     rows, width = inner_ref.shape
     wide = width // parts
-    edge = 2 if with_inverse else 1
+    edge = 1 if with_inverse else 2
     refs = out_refs[:parts]
     for r, out_ref in enumerate(refs):
         target = lax.rem(meta_ref[0] + r, parts)
@@ -478,9 +478,9 @@
 
 def heads_backward_kernel(parts, rows, meta_ref, *refs):
     a_refs, c_refs = refs[:parts], refs[parts : 2 * parts]
-    gain_ref, offset_ref, onehot_ref = refs[2 * parts : 2 * parts + 3]
-    out_refs = refs[2 * parts + 3 : 3 * parts + 3]
-    gain_grad_ref, x_ref, weight_ref, cot_ref, grad_ref, part_ref, bias_ref = refs[3 * parts + 3 :]
+    gain_ref, offset_ref, onehot_ref, after_ref = refs[2 * parts : 2 * parts + 4]
+    out_refs = refs[2 * parts + 4 : 3 * parts + 4]
+    gain_grad_ref, x_ref, weight_ref, cot_ref, grad_ref, part_ref, bias_ref = refs[3 * parts + 4 :]
     tokens = rows * parts
     depth = HEAD_DIM // parts
     scale = HEAD_DIM ** (-0.5)
@@ -561,7 +561,7 @@
     return pl.BlockSpec((1, 1, WINDOW), lambda i, meta: (meta[0] * heads + first + i, 0, 0))
 
 
-def heads_backward(meta, a_slots, c_slots, gain, offsets, onehot, heads, first, count):
+def heads_backward(meta, a_slots, c_slots, gain, offsets, onehot, after, heads, first, count):
     parts = len(a_slots)
     rows = c_slots[0].shape[0]
     tokens = rows * parts
@@ -585,6 +585,7 @@
                 whole_column(1, heads, first),
                 offset_spec(heads, first),
                 pl.BlockSpec((buckets, WINDOW), lambda i, meta: (0, 0)),
+                pl.BlockSpec(memory_space=pl.ANY),
             ],
             out_specs=(*[head_column(made)] * parts, head_column(1)),
             scratch_shapes=[
@@ -601,14 +602,14 @@
             flops=count * tokens * 400_000, bytes_accessed=tokens * width, transcendentals=0
         ),
         name="heads_backward",
-    )(meta, *a_slots, *c_slots, gain, offsets, onehot)
+    )(meta, *a_slots, *c_slots, gain, offsets, onehot, after)
 
 
 def heads_forward_kernel(parts, rows, meta_ref, *refs):
     a_refs, i_refs = refs[:parts], refs[parts : 2 * parts]
     gain_ref, offset_ref = refs[2 * parts : 2 * parts + 2]
     out_refs = refs[2 * parts + 2 : 3 * parts + 2]
-    sums_ref, inverse_ref, x_ref, weight_ref, made_ref, square_ref = refs[3 * parts + 2 :]
+    inverse_ref, x_ref, weight_ref, made_ref, square_ref = refs[3 * parts + 2 :]
     tokens = rows * parts
     gather_rows(meta_ref, i_refs, rows, x_ref)
     gather_weight(meta_ref, a_refs, rows, weight_ref)
@@ -638,14 +639,24 @@
     def later_head():
         square_ref[...] += squares
 
+    for r, out_ref in enumerate(out_refs):
+        source = lax.rem(meta_ref[0] + parts - r, parts)
+        out_ref[:rows] = made_ref[pl.ds(pl.multiple_of(source * rows, rows), rows)]
+
     @pl.when(pl.program_id(0) == pl.num_programs(0) - 1)
     def last_head():
         total = jnp.sum(jnp.transpose(square_ref[...]), axis=0, keepdims=True)
-        sums_ref[...] = jnp.broadcast_to(total, sums_ref.shape)
-
-    for r, out_ref in enumerate(out_refs):
-        source = lax.rem(meta_ref[0] + parts - r, parts)
-        out_ref[...] = made_ref[pl.ds(pl.multiple_of(source * rows, rows), rows)]
+        at_row = lax.broadcasted_iota(jnp.int32, (16, rows), 0)
+        tail = jnp.zeros((16, rows), F32)
+        rest = total
+        for k in range(3):
+            piece = rest.astype(BF16).astype(F32)
+            rest = rest - piece
+            for part in range(parts):
+                row = jnp.broadcast_to(piece[:, part * rows : (part + 1) * rows], (16, rows))
+                tail = jnp.where(at_row == 3 * part + k, row, tail)
+        for out_ref in out_refs:
+            out_ref[rows:] = tail.astype(BF16)
 
 
 def heads_forward(meta, a_slots, i_slots, gain, offsets, heads, rows):
@@ -656,8 +667,7 @@
     return pl.pallas_call(
         functools.partial(heads_forward_kernel, parts, rows),
         out_shape=(
-            *[jax.ShapeDtypeStruct((rows, width), BF16) for r in range(parts)],
-            jax.ShapeDtypeStruct((8, tokens), F32),
+            *[jax.ShapeDtypeStruct((rows + 16, width), BF16) for r in range(parts)],
         ),
         grid_spec=pltpu.PrefetchScalarGridSpec(
             num_scalar_prefetch=1,
@@ -668,10 +678,7 @@
                 whole_column(1, heads),
                 offset_spec(heads),
             ],
-            out_specs=(
-                *[head_column(rows)] * parts,
-                pl.BlockSpec((8, tokens), lambda i, meta: (0, 0)),
-            ),
+            out_specs=(head_column(rows + 16),) * parts,
             scratch_shapes=[
                 pltpu.VMEM((tokens, HEAD_DIM), F32),
                 pltpu.VMEM((tokens, HEAD_DIM), BF16),
@@ -689,35 +696,45 @@
 
 
 def memory_kernel(parts, width, meta_ref, *refs):
-    out_refs = refs[:parts]
-    sums_ref, gain_ref, after_ref, memory_ref = refs[parts:]
-    rows = out_refs[0].shape[0]
+    out_refs, other_refs = refs[:parts], refs[parts : 2 * parts - 1]
+    gain_ref, *share_refs, memory_ref = refs[2 * parts - 1 :]
     wide = memory_ref.shape[1]
-    total = sums_ref[0, :1]
-    for r in range(1, parts):
-        total = total + sums_ref[r, :1]
+    rows = memory_ref.shape[0] // parts
+    total = None
+    for ref in (out_refs[0], *other_refs):
+        tail = ref[rows:, wide - rows :].astype(F32)
+        pieces = [
+            tail[3 * p : 3 * p + 1] + tail[3 * p + 1 : 3 * p + 2] + tail[3 * p + 2 : 3 * p + 3]
+            for p in range(parts)
+        ]
+        row = jnp.concatenate(pieces, axis=1)
+        total = row if total is None else total + row
     inverse = lax.rsqrt(total / width + eps_norm)
     gain = gain_ref[:, pl.ds(pl.multiple_of(meta_ref[0] * wide, 128), wide)]
     spread_inverse = jnp.transpose(jnp.broadcast_to(inverse, (128, inverse.shape[1])))
     for r, out_ref in enumerate(out_refs):
         source = lax.rem(meta_ref[0] + parts - r, parts)
-        memory_ref[pl.ds(pl.multiple_of(source * rows, rows), rows)] = out_ref[...]
+        memory_ref[pl.ds(pl.multiple_of(source * rows, rows), rows)] = out_ref[:rows]
     made = memory_ref[...].astype(F32)
     memory_ref[...] = (made * spread_inverse[:, :1] * gain).astype(BF16)
-
-
-def memory_rows(meta, outs, sums, gain, after, width):
+    for k, share_ref in enumerate(share_refs):
+        size = share_ref.shape[0]
+        share_ref[...] = memory_ref[k * size : (k + 1) * size]
+
+
+def memory_rows(meta, outs, others, gain, width, shares):
     parts = len(outs)
-    rows, wide = outs[0].shape
+    rows, wide = outs[0].shape[0] - 16, outs[0].shape[1]
     return pl.pallas_call(
         functools.partial(memory_kernel, parts, width),
-        out_shape=jax.ShapeDtypeStruct((rows * parts, wide), BF16),
-        in_specs=[SMEM_SPEC] + [VMEM_SPEC] * (parts + 2) + [pl.BlockSpec(memory_space=pl.ANY)],
-        out_specs=VMEM_SPEC,
+        out_shape=[jax.ShapeDtypeStruct((rows * parts // shares, wide), BF16)] * shares,
+        in_specs=[SMEM_SPEC] + [VMEM_SPEC] * (2 * parts),
+        out_specs=[VMEM_SPEC] * shares,
+        scratch_shapes=[pltpu.VMEM((rows * parts, wide), BF16)],
         compiler_params=pltpu.CompilerParams(vmem_limit_bytes=VMEM_LIMIT),
         cost_estimate=pl.CostEstimate(flops=rows, bytes_accessed=rows, transcendentals=0),
         name="memory_rows",
-    )(meta, *outs, sums, gain, after)
+    )(meta, *outs, *others, gain)
 
 
 def place_kernel(parts, meta_ref, *refs):
@@ -725,12 +742,12 @@
     wide = refs[0].shape[1]
     for r in range(parts):
         source = lax.rem(meta_ref[0] + r, parts)
-        out_ref[:, pl.ds(pl.multiple_of(source * wide, 128), wide)] = refs[r][...]
+        out_ref[:, pl.ds(pl.multiple_of(source * wide, 128), wide)] = refs[r][: out_ref.shape[0]]
 
 
 def place_columns(meta, slots):
     parts = len(slots)
-    rows, wide = slots[0].shape
+    rows, wide = slots[0].shape[0] - 16, slots[0].shape[1]
     return pl.pallas_call(
         functools.partial(place_kernel, parts),
         out_shape=jax.ShapeDtypeStruct((rows, wide * parts), BF16),
@@ -805,19 +822,19 @@
     return lax.ppermute(value, axis, [(source, source + steps) for source in range(first, last)])
 
 
-def spread_memory(made, section, sections):
-    share = made.shape[0] // sections
+def spread_memory(shares, section, sections):
     last = sections - 1
-    if sections % 2:
-        memory = jnp.where(section == last, made[last * share :], 0)
+    if len(shares) == sections:
+        memory = jnp.where(section == last, shares[last], 0)
         for s in range(last):
-            memory = memory + lax.ppermute(made[s * share : (s + 1) * share], "section", [(last, s)])
+            memory = memory + lax.ppermute(shares[s], "section", [(last, s)])
         return memory
-    couple = jnp.where(section == last, made[(last - 1) * share :], 0)
-    for s in range(0, last - 1, 2):
-        couple = couple + lax.ppermute(made[s * share : (s + 2) * share], "section", [(last, s + 1)])
-    even = lax.ppermute(couple[:share], "section", [(s + 1, s) for s in range(0, sections, 2)])
-    return jnp.where(section % 2 == 0, even, couple[share:])
+    couple = jnp.where(section == last, shares[-1], 0)
+    for s, share in enumerate(shares[:-1]):
+        couple = couple + lax.ppermute(share, "section", [(last, 2 * s + 1)])
+    half = couple.shape[0] // 2
+    even = lax.ppermute(couple[:half], "section", [(s + 1, s) for s in range(0, sections, 2)])
+    return jnp.where(section % 2 == 0, even, couple[half:])
 
 
 def heads_body(
@@ -840,58 +857,47 @@
         ]
         return [sends[0]] + moved
 
-    def diagonal(value, r, step):
-        pairs = [
-            (s * parts + i, (s + step) % sections * parts + (i + r) % parts)
-            for s in range(sections)
-            for i in range(parts)
-        ]
-        return lax.ppermute(value, ("section", "seq"), pairs)
-
     inverse_b, *a_sends = pack_stash(meta, stash[0], norm_gain, qkv_weight[0], parts)
     a_slots = exchanged(a_sends, 1)
-    meta_i, inverse_b = lax.optimization_barrier((meta, inverse_b))
-    i_sends = pack_rows(meta_i, embedded, carried[0], parts, True)
-    i_slots = [diagonal(i_sends[r], r, 1) for r in range(parts)]
-    meta_c, i_sends = lax.optimization_barrier((meta_i, i_sends))
-    *c_sends, cot_source = pack_rows(meta_c, loss_grad, returned[0], parts, False)
-    cotangent = diagonal(cot_source, 0, -1)
-    c_slots = [cotangent] + [diagonal(c_sends[r], r, -1) for r in range(1, parts)]
+    kept, gone, inverse_b = lax.optimization_barrier((carried[0], returned[0], inverse_b))
+    arrived = shifted(kept, "section", 1)
+    came_back = shifted(gone, "section", -1)
+    i_slots = exchanged(pack_rows(meta, embedded, arrived, parts, True), 1)
+    *c_sends, cotangent = pack_rows(meta, loss_grad, came_back, parts, False)
+    c_slots = exchanged(c_sends, 1)
+    c_slots[0] = cotangent
 
     offsets = offset_table(rel_bias[0])
     onehot = jnp.asarray(bucket_onehot(buckets).T)
-    *o_sends, sums = heads_forward(meta, a_slots, i_slots, norm_gain, offsets, heads, rows)
-    all_sums = lax.all_gather(sums, "seq", axis=0, tiled=False)
-    o_sends, c_slots, sums = lax.optimization_barrier((o_sends, c_slots, sums))
-    waiting = exchanged(o_sends, -1)
-    gain_after, sums = lax.optimization_barrier((norm_gain, sums))
+    o_sends = heads_forward(meta, a_slots, i_slots, norm_gain, offsets, heads, rows)
+    o_sends, c_slots = lax.optimization_barrier((o_sends, c_slots))
+    o_slots = exchanged(o_sends, -1)
 
     chunks = 2 if heads % 2 == 0 else 1
     count = heads // chunks
-    g_chunks, gain_parts, o_slots = [], [], None
-    for c in range(chunks):
-        *g_sends, gain_part = heads_backward(
-            meta, a_slots, c_slots, gain_after, offsets, onehot, heads, c * count, count
+
+    def backward(c, after):
+        return heads_backward(
+            meta, a_slots, c_slots, norm_gain, offsets, onehot, after, heads, c * count, count
         )
-        g_sends, waiting, gain_after, gain_part = lax.optimization_barrier(
-            (g_sends, waiting, gain_after, gain_part)
-        )
-        if o_slots is None:
-            o_slots = waiting
-        else:
-            g_chunks.append(waiting)
-        waiting = exchanged(g_sends, -1)
-        gain_parts.append(gain_part)
-    g_chunks.append(waiting)
-    gain_grad = jnp.concatenate(gain_parts, axis=1)
-    made = memory_rows(meta, o_sends, all_sums, final_gain[None], gain_parts[-1], width)
+
+    *g_sends, gain_grad = backward(0, o_sends[0])
+    g_sends, o_slots = lax.optimization_barrier((g_sends, o_slots))
+    g_chunks = [exchanged(g_sends, -1)]
+    output = place_columns(meta, o_slots)
+    shares = sections // 2 if sections % 2 == 0 else sections
+    made = memory_rows(meta, o_sends, o_slots[1:], final_gain[None], width, shares)
+    if chunks == 2:
+        *g_sends, gain_part = backward(1, output)
+        g_sends, made, g_chunks = lax.optimization_barrier((g_sends, made, g_chunks))
+        g_chunks.append(exchanged(g_sends, -1))
+        gain_grad = jnp.concatenate([gain_grad, gain_part], axis=1)
     memory = spread_memory(made, section, sections)
 
     input_grad, weight_grad, bias_wide = heads_finish(
         meta, g_chunks, stash[0], inverse_b, norm_gain, cotangent, buckets
     )
     bias_grad = bias_wide[:, :, 0].T
-    output = place_columns(meta, o_slots)
     return (
         output[None],
         input_grad[None],

time: 171 us -> 161 us (0.942); the launches traced: 167 us -> 160 us
  blocking collectives: 18.4 us -> 0 us
  starting transfers between devices: 34.4 us -> 50.6 us
  waiting for transfers between devices: 51.6 us -> 45.1 us
    ppermute x12 -> x6, waiting for transfers between devices: 37.3 us -> 0.02 us  [the longest x3 0.01 us: spread_memory(): couple = couple + lax.ppermute(share, 'section', [(last, 2 * s + 1)])]
    ppermute x12 -> x18, waiting for transfers between devices: 14.2 us -> 45.1 us  [exchanged(): lax.ppermute(sends[r], 'seq', [(i, (i + direction * r) % parts) for i in...]
    ppermute x12 -> x18, starting transfers between devices: 21.2 us -> 41.5 us  [exchanged(): lax.ppermute(sends[r], 'seq', [(i, (i + direction * r) % parts) for i in...]
    all_gather x1 -> x0, blocking collectives: 18.4 us -> none  [heads_body(): all_sums = lax.all_gather(sums, 'seq', axis=0, tiled=False)]
    ppermute x12 -> x6, starting transfers between devices: 13.2 us -> 9.13 us  [the longest x3 4.14 us: spread_memory(): couple = couple + lax.ppermute(share, 'section', [(last, 2 * s + 1)])]
    unnamed x42 -> x30, local copies, waits for them, and re-layouts: 4.12 us -> 6.1 us
  transfers between devices with their start and end apart: 24 -> 24, of which waited for: 5 -> 6; matrix products, arithmetic and copies ran while one was open for 2% -> 2% of each run, Pallas kernels for 30% -> 33%
where the time goes in v5:
time: 161 us; the launch traced here: 160 us
  Pallas kernels  53.8 us (33%)
  starting transfers between devices  50.6 us (31%)
  waiting for transfers between devices  45.1 us (28%)
  local copies, waits for them, and re-layouts  6.85 us (4%)
  other arithmetic  2.5 us (2%)
    ppermute x18, waiting for transfers between devices, exchanged(): lax.ppermute(sends[r], 'seq', [(i, (i + direction * r) % parts) for i in...  45.1 us
    ppermute x18, starting transfers between devices, exchanged(): lax.ppermute(sends[r], 'seq', [(i, (i + direction * r) % parts) for i in...  41.5 us
    pallas_call x2, Pallas kernels, heads_backward(): pl.pallas_call(functools.partial(heads_backward_kernel, parts, rows), out...  27.1 us
    pallas_call x1, Pallas kernels, heads_forward(): pl.pallas_call(functools.partial(heads_forward_kernel, parts, rows), out_...  18.1 us
    unnamed x30, local copies, waits for them, and re-layouts  6.1 us
    ppermute x3, starting transfers between devices, spread_memory(): couple = couple + lax.ppermute(share, 'section', [(last, 2 * s + 1)])  4.14 us
    ppermute x2, starting transfers between devices, shifted(): lax.ppermute(value, axis, [(source, source + steps) for source in range(f...  3.7 us
  transfers between devices with their start and end apart: 24, of which 6 were waited for; matrix products, arithmetic and copies ran while one was open for 2% of the time, Pallas kernels for 33%

profile of v5, /device:TPU:0, one launch (start us, length us, event | category | flops | bytes accessed | tf_op | source)
XLA Modules:
  0.0 159.9 jit_solution(3199589799603512974)
XLA Ops:
  0.6 0.0 copy-start
  0.7 0.1 pad_add_fusion.meta_ref
  0.7 1.1 copy-done.2
  1.9 1.1 copy-done.6
  2.9 0.7 copy-done.7
  3.6 1.3 pack_stash.1
  4.9 2.4 %collective-permute-start.3 = (bf16[128,3072]{1,0:T(8,128)(2,1)}, bf16[128,3072]{1,0:T(8,128)(2,1)S(1)}, u32[]{:S(2)}, u32[]{:S(2)}) collective-permute-start(bf16[128,3072]{1,0:T(8,128)(2,1)} %bitcast.31), channel_id=1, source_target_pairs={{0,4},{4,8},{8,12},{12,16},{16,20},{20,24},{24,28},{1,5},{5,9},{9,... | collective-permute-start | bytes 2359304 | tf_op jit(solution)/shard_map/ppermute | solution.py:822
  7.3 1.3 collective-permute-start.7
  8.6 2.5 %collective-permute-start = (bf16[224,768]{1,0:T(8,128)(2,1)S(1)}, bf16[224,768]{1,0:T(8,128)(2,1)S(1)}, u32[]{:S(2)}, u32[]{:S(2)}) collective-permute-start(bf16[224,768]{1,0:T(8,128)(2,1)S(1)} %get-tuple-element.72), channel_id=1, source_target_pairs={{0,1},{1,2},{2,3},{3,0},{4,5},{5,6},{6,7},{7,4},{8,9},{9,10},{10,1... | collective-permute-start | bytes 1032200 | tf_op jit(solution)/shard_map/ppermute | solution.py:855
  11.1 2.6 %collective-permute-start.1 = (bf16[224,768]{1,0:T(8,128)(2,1)S(1)}, bf16[224,768]{1,0:T(8,128)(2,1)S(1)}, u32[]{:S(2)}, u32[]{:S(2)}) collective-permute-start(bf16[224,768]{1,0:T(8,128)(2,1)S(1)} %get-tuple-element.73), channel_id=1, source_target_pairs={{0,2},{1,3},{2,0},{3,1},{4,6},{5,7},{6,4},{7,5},{8,10},{9,11},{10,... | collective-permute-start | bytes 1032200 | tf_op jit(solution)/shard_map/ppermute | solution.py:855
  13.7 1.4 collective-permute-start.2
  15.0 0.0 collective-permute-done.3.inner_ref
  15.0 0.9 pack_inbound.1
  16.0 0.7 collective-permute-start.4
  16.7 0.0 collective-permute-done.7.inner_ref
  16.7 0.3 collective-permute-start.5
  17.1 1.4 pack_cotangent.1
  18.5 2.0 %collective-permute-done.refs_1_ = bf16[224,768]{1,0:T(8,128)(2,1)S(1)} collective-permute-done((bf16[224,768]{1,0:T(8,128)(2,1)S(1)}, bf16[224,768]{1,0:T(8,128)(2,1)S(1)}, u32[]{:S(2)}, u32[]{:S(2)}) %collective-permute-start) | collective-permute-done | bytes 344096 | tf_op jit(solution)/shard_map/ppermute | solution.py:855
  20.5 2.1 %collective-permute-start.6 = (bf16[144,768]{1,0:T(8,128)(2,1)S(1)}, bf16[144,768]{1,0:T(8,128)(2,1)S(1)}, u32[]{:S(2)}, u32[]{:S(2)}) collective-permute-start(bf16[144,768]{1,0:T(8,128)(2,1)S(1)} %get-tuple-element.80), channel_id=1, source_target_pairs={{0,3},{1,0},{2,1},{3,2},{4,7},{5,4},{6,5},{7,6},{8,11},{9,8},{10,9... | collective-permute-start | bytes 663560 | tf_op jit(solution)/shard_map/ppermute | solution.py:855
  22.6 15.8 %collective-permute-done.1.refs_2_ = bf16[224,768]{1,0:T(8,128)(2,1)S(1)} collective-permute-done((bf16[224,768]{1,0:T(8,128)(2,1)S(1)}, bf16[224,768]{1,0:T(8,128)(2,1)S(1)}, u32[]{:S(2)}, u32[]{:S(2)}) %collective-permute-start.1) | collective-permute-done | bytes 344096 | tf_op jit(solution)/shard_map/ppermute | solution.py:855
  38.5 12.8 %collective-permute-start.8 = (bf16[128,768]{1,0:T(8,128)(2,1)S(1)}, bf16[128,768]{1,0:T(8,128)(2,1)S(1)}, u32[]{:S(2)}, u32[]{:S(2)}) collective-permute-start(bf16[128,768]{1,0:T(8,128)(2,1)S(1)} %get-tuple-element.87), channel_id=1, source_target_pairs={{0,1},{1,2},{2,3},{3,0},{4,5},{5,6},{6,7},{7,4},{8,9},{9,10},{10,1... | collective-permute-start | bytes 589832 | tf_op jit(solution)/shard_map/ppermute | solution.py:855
  51.3 0.0 collective-permute-done.2.refs_3_
  51.3 3.4 %collective-permute-start.9 = (bf16[128,768]{1,0:T(8,128)(2,1)S(1)}, bf16[128,768]{1,0:T(8,128)(2,1)S(1)}, u32[]{:S(2)}, u32[]{:S(2)}) collective-permute-start(bf16[128,768]{1,0:T(8,128)(2,1)S(1)} %get-tuple-element.88), channel_id=1, source_target_pairs={{0,2},{1,3},{2,0},{3,1},{4,6},{5,7},{6,4},{7,5},{8,10},{9,11},{10,... | collective-permute-start | bytes 589832 | tf_op jit(solution)/shard_map/ppermute | solution.py:855
  54.7 1.9 %collective-permute-start.10 = (bf16[128,768]{1,0:T(8,128)(2,1)S(1)}, bf16[128,768]{1,0:T(8,128)(2,1)S(1)}, u32[]{:S(2)}, u32[]{:S(2)}) collective-permute-start(bf16[128,768]{1,0:T(8,128)(2,1)S(1)} %get-tuple-element.89), channel_id=1, source_target_pairs={{0,3},{1,0},{2,1},{3,2},{4,7},{5,4},{6,5},{7,6},{8,11},{9,8},{10,9... | collective-permute-start | bytes 589832 | tf_op jit(solution)/shard_map/ppermute | solution.py:855
  56.6 0.2 fusion
  56.8 0.0 copy-start.9
  56.8 10.0 %collective-permute-done.5.refs_6_ = bf16[144,768]{1,0:T(8,128)(2,1)S(1)} collective-permute-done((bf16[144,768]{1,0:T(8,128)(2,1)S(1)}, bf16[144,768]{1,0:T(8,128)(2,1)S(1)}, u32[]{:S(2)}, u32[]{:S(2)}) %collective-permute-start.5) | collective-permute-done | bytes 221216 | tf_op jit(solution)/shard_map/ppermute | solution.py:855
  66.8 0.0 collective-permute-done.6.refs_7_
  66.8 18.1 %heads_forward.1 = (bf16[144,768]{1,0:T(8,128)(2,1)S(1)}, bf16[144,768]{1,0:T(8,128)(2,1)S(1)}, bf16[144,768]{1,0:T(8,128)(2,1)S(1)}, bf16[144,768]{1,0:T(8,128)(2,1)S(1)}) custom-call(s32[3]{0:T(128)S(1)} %pad_add_fusion.meta_ref, bf16[224,768]{1,0:T(8,128)(2,1)S(1)} %get-tuple-element.71.refs_0_, bf16[224,768]{1,0:T(8,128)(2,1)S(1)} %collective-permute-done.refs_1_, ...), custom_call_target="tpu_custom_call" | custom-call | flops 3072 | bytes 512 | tf_op jit(solution)/shard_map/heads_forward/pallas_call | solution.py:667
  84.9 0.0 collective-permute-done.9.refs_6_
  84.9 0.0 collective-permute-done.10.refs_7_
  84.9 0.0 copy-start.10
  84.9 5.3 %collective-permute-start.11 = (bf16[144,768]{1,0:T(8,128)(2,1)S(1)}, bf16[144,768]{1,0:T(8,128)(2,1)S(1)}, u32[]{:S(2)}, u32[]{:S(2)}) collective-permute-start(bf16[144,768]{1,0:T(8,128)(2,1)S(1)} %get-tuple-element.99.refs_1_), channel_id=1, source_target_pairs={{0,3},{1,0},{2,1},{3,2},{4,7},{5,4},{6,5},{7,6},{8,11},{9,8},{10,9... | collective-permute-start | bytes 663560 | tf_op jit(solution)/shard_map/ppermute | solution.py:855
  90.2 1.5 collective-permute-start.12
  91.8 0.0 collective-permute-start.13
  91.8 13.5 %heads_backward.2 = (bf16[240,384]{1,0:T(8,128)(2,1)S(1)}, bf16[240,384]{1,0:T(8,128)(2,1)S(1)}, bf16[240,384]{1,0:T(8,128)(2,1)S(1)}, bf16[240,384]{1,0:T(8,128)(2,1)S(1)}, f32[1,384]{1,0:T(1,128)S(1)}) custom-call(s32[3]{0:T(128)S(1)} %pad_add_fusion.meta_ref, bf16[224,768]{1,0:T(8,128)(2,1)S(1)} %get-tuple-element.71.refs_0_, ...), custom_call_target="tpu_custom_call" | custom-call | flops 614400000 | bytes 196608 | tf_op jit(solution)/shard_map/heads_backward/pallas_call | solution.py:572
  105.3 0.0 collective-permute-done.11.refs_1_.refs_4_
  105.3 6.1 %collective-permute-done.12.refs_2_.refs_5_ = bf16[144,768]{1,0:T(8,128)(2,1)S(1)} collective-permute-done((bf16[144,768]{1,0:T(8,128)(2,1)S(1)}, bf16[144,768]{1,0:T(8,128)(2,1)S(1)}, u32[]{:S(2)}, u32[]{:S(2)}) %collective-permute-start.12) | collective-permute-done | bytes 221216 | tf_op jit(solution)/shard_map/ppermute | solution.py:855
  111.4 1.4 collective-permute-start.15
  112.8 2.0 %collective-permute-start.16 = (bf16[240,384]{1,0:T(8,128)(2,1)S(1)}, bf16[240,384]{1,0:T(8,128)(2,1)S(1)}, u32[]{:S(2)}, u32[]{:S(2)}) collective-permute-start(bf16[240,384]{1,0:T(8,128)(2,1)S(1)} %get-tuple-element.117), channel_id=1, source_target_pairs={{0,1},{1,2},{2,3},{3,0},{4,5},{5,6},{6,7},{7,4},{8,9},{9,10},{10,1... | collective-permute-start | bytes 552968 | tf_op jit(solution)/shard_map/ppermute | solution.py:855
  114.8 0.9 memory_rows.1
  115.7 0.0 copy-start.8
  115.8 1.5 place_columns.1.refs_11_
  117.3 1.1 copy-done.1
  118.4 13.5 %heads_backward.3 = (bf16[240,384]{1,0:T(8,128)(2,1)S(1)}, bf16[240,384]{1,0:T(8,128)(2,1)S(1)}, bf16[240,384]{1,0:T(8,128)(2,1)S(1)}, bf16[240,384]{1,0:T(8,128)(2,1)S(1)}, f32[1,384]{1,0:T(1,128)S(1)}) custom-call(s32[3]{0:T(128)S(1)} %pad_add_fusion.meta_ref, bf16[224,768]{1,0:T(8,128)(2,1)S(1)} %get-tuple-element.71.refs_0_, ...), custom_call_target="tpu_custom_call" | custom-call | flops 614400000 | bytes 196608 | tf_op jit(solution)/shard_map/heads_backward/pallas_call | solution.py:572
  132.0 0.7 copy-done.11
  132.6 0.7 copy-done.12
  133.3 0.7 copy-done.13
  134.0 0.0 collective-permute-done.16.refs_3_
  134.0 1.5 collective-permute-start.20
  135.5 1.3 collective-permute-start.21
  136.8 1.3 collective-permute-start.22
  138.1 1.8 %collective-permute-start.17 = (bf16[240,384]{1,0:T(8,128)(2,1)}, bf16[240,384]{1,0:T(8,128)(2,1)S(1)}, u32[]{:S(2)}, u32[]{:S(2)}) collective-permute-start(bf16[240,384]{1,0:T(8,128)(2,1)} %copy-done.13), channel_id=1, source_target_pairs={{0,3},{1,0},{2,1},{3,2},{4,7},{5,4},{6,5},{7,6},{8,11},{9,8},{10,9... | collective-permute-start | bytes 552968 | tf_op jit(solution)/shard_map/ppermute | solution.py:855
  140.0 0.0 collective-permute-done.20
  140.0 1.8 %collective-permute-start.19 = (bf16[240,384]{1,0:T(8,128)(2,1)}, bf16[240,384]{1,0:T(8,128)(2,1)S(1)}, u32[]{:S(2)}, u32[]{:S(2)}) collective-permute-start(bf16[240,384]{1,0:T(8,128)(2,1)} %copy-done.11), channel_id=1, source_target_pairs={{0,1},{1,2},{2,3},{3,0},{4,5},{5,6},{6,7},{7,4},{8,9},{9,10},{10,1... | collective-permute-start | bytes 552968 | tf_op jit(solution)/shard_map/ppermute | solution.py:855
  141.7 0.0 collective-permute-done.21
  141.7 1.2 add_add_fusion
  142.9 1.3 collective-permute-start.23
  144.2 0.6 pad_maximum_fusion
  144.8 0.5 collective-permute-done.17.refs_5_
  145.3 10.6 %collective-permute-done.18.refs_6_ = bf16[240,384]{1,0:T(8,128)(2,1)S(1)} collective-permute-done((bf16[240,384]{1,0:T(8,128)(2,1)}, bf16[240,384]{1,0:T(8,128)(2,1)S(1)}, u32[]{:S(2)}, u32[]{:S(2)}) %collective-permute-start.18) | collective-permute-done | bytes 184352 | tf_op jit(solution)/shard_map/ppermute | solution.py:855
  155.9 2.6 %heads_finish.1 = (bf16[128,3072]{1,0:T(8,128)(2,1)}, f32[3,24,32,128]{3,2,1,0:T(8,128)}, f32[24,8,128]{2,1,0:T(8,128)S(1)}) custom-call(s32[3]{0:T(128)S(1)} %pad_add_fusion.meta_ref, bf16[240,384]{1,0:T(8,128)(2,1)S(1)} %get-tuple-element.118.refs_0_, bf16[240,384]{1,0:T(8,128)(2,1)S(1)} %collective-permute-done.14.refs_1_, ...), custom_call_target="tpu_custom_call" | custom-call | flops 4718592 | bytes 5505024 | tf_op jit(solution)/shard_map/heads_finish/pallas_call | solution.py:796
  158.6 0.7 copy.18
  159.3 0.7 slice_select_fusion
  (32 shorter events, 0.1 us)
Async XLA Ops:
  0.6 55.9 %copy-start = (f32[1,32,24]{1,2,0:T(8,128)S(1)}, f32[1,32,24]{1,2,0:T(8,128)}, u32[]{:S(2)}) copy-start(f32[1,32,24]{1,2,0:T(8,128)} %param.17) | copy-start | bytes 9220
  0.7 1.1 copy-start.2
  1.9 1.1 copy-start.6
  2.9 0.7 copy-start.7
  3.6 11.4 %copy-start.4 = (bf16[128,3072]{1,0:T(8,128)(2,1)S(1)}, bf16[128,3072]{1,0:T(8,128)(2,1)}, u32[]{:S(2)}) copy-start(bf16[128,3072]{1,0:T(8,128)(2,1)} %edge_ref.2) | copy-start | bytes 2359300
  3.6 13.4 %copy-start.5 = (bf16[128,3072]{1,0:T(8,128)(2,1)S(1)}, bf16[128,3072]{1,0:T(8,128)(2,1)}, u32[]{:S(2)}) copy-start(bf16[128,3072]{1,0:T(8,128)(2,1)} %edge_ref.3) | copy-start | bytes 2359300
  4.9 10.1 %collective-permute-start.3 = (bf16[128,3072]{1,0:T(8,128)(2,1)}, bf16[128,3072]{1,0:T(8,128)(2,1)S(1)}, u32[]{:S(2)}, u32[]{:S(2)}) collective-permute-start(bf16[128,3072]{1,0:T(8,128)(2,1)} %bitcast.31), channel_id=1, source_target_pairs={{0,4},{4,8},{8,12},{12,16},{16,20},{20,24},{24,28},{1,5},{5,9},{9,... | collective-permute-start | bytes 2359304 | tf_op jit(solution)/shard_map/ppermute | solution.py:822
  7.3 9.4 %collective-permute-start.7 = (bf16[128,3072]{1,0:T(8,128)(2,1)}, bf16[128,3072]{1,0:T(8,128)(2,1)S(1)}, u32[]{:S(2)}, u32[]{:S(2)}) collective-permute-start(bf16[128,3072]{1,0:T(8,128)(2,1)} %bitcast.32), channel_id=1, source_target_pairs={{4,0},{8,4},{12,8},{16,12},{20,16},{24,20},{28,24},{5,1},{9,5},{13... | collective-permute-start | bytes 2359304 | tf_op jit(solution)/shard_map/ppermute | solution.py:822
  8.6 11.9 %collective-permute-start = (bf16[224,768]{1,0:T(8,128)(2,1)S(1)}, bf16[224,768]{1,0:T(8,128)(2,1)S(1)}, u32[]{:S(2)}, u32[]{:S(2)}) collective-permute-start(bf16[224,768]{1,0:T(8,128)(2,1)S(1)} %get-tuple-element.72), channel_id=1, source_target_pairs={{0,1},{1,2},{2,3},{3,0},{4,5},{5,6},{6,7},{7,4},{8,9},{9,10},{10,1... | collective-permute-start | bytes 1032200 | tf_op jit(solution)/shard_map/ppermute | solution.py:855
  11.1 27.4 %collective-permute-start.1 = (bf16[224,768]{1,0:T(8,128)(2,1)S(1)}, bf16[224,768]{1,0:T(8,128)(2,1)S(1)}, u32[]{:S(2)}, u32[]{:S(2)}) collective-permute-start(bf16[224,768]{1,0:T(8,128)(2,1)S(1)} %get-tuple-element.73), channel_id=1, source_target_pairs={{0,2},{1,3},{2,0},{3,1},{4,6},{5,7},{6,4},{7,5},{8,10},{9,11},{10,... | collective-permute-start | bytes 1032200 | tf_op jit(solution)/shard_map/ppermute | solution.py:855
  13.7 37.6 %collective-permute-start.2 = (bf16[224,768]{1,0:T(8,128)(2,1)S(1)}, bf16[224,768]{1,0:T(8,128)(2,1)S(1)}, u32[]{:S(2)}, u32[]{:S(2)}) collective-permute-start(bf16[224,768]{1,0:T(8,128)(2,1)S(1)} %get-tuple-element.74), channel_id=1, source_target_pairs={{0,3},{1,0},{2,1},{3,2},{4,7},{5,4},{6,5},{7,6},{8,11},{9,8},{10,9... | collective-permute-start | bytes 1032200 | tf_op jit(solution)/shard_map/ppermute | solution.py:855
  16.0 40.6 %copy-start.14 = (f32[256,32]{1,0:T(8,128)S(1)}, f32[256,32]{1,0:T(8,128)}, u32[]{:S(2)}) copy-start(f32[256,32]{1,0:T(8,128)} %constant.35.clone) | copy-start | bytes 98308
  16.0 38.7 %collective-permute-start.4 = (bf16[144,768]{1,0:T(8,128)(2,1)S(1)}, bf16[144,768]{1,0:T(8,128)(2,1)S(1)}, u32[]{:S(2)}, u32[]{:S(2)}) collective-permute-start(bf16[144,768]{1,0:T(8,128)(2,1)S(1)} %get-tuple-element.78), channel_id=1, source_target_pairs={{0,1},{1,2},{2,3},{3,0},{4,5},{5,6},{6,7},{7,4},{8,9},{9,10},{10,1... | collective-permute-start | bytes 663560 | tf_op jit(solution)/shard_map/ppermute | solution.py:855
  16.7 50.1 %collective-permute-start.5 = (bf16[144,768]{1,0:T(8,128)(2,1)S(1)}, bf16[144,768]{1,0:T(8,128)(2,1)S(1)}, u32[]{:S(2)}, u32[]{:S(2)}) collective-permute-start(bf16[144,768]{1,0:T(8,128)(2,1)S(1)} %get-tuple-element.79), channel_id=1, source_target_pairs={{0,2},{1,3},{2,0},{3,1},{4,6},{5,7},{6,4},{7,5},{8,10},{9,11},{10,... | collective-permute-start | bytes 663560 | tf_op jit(solution)/shard_map/ppermute | solution.py:855
  20.5 46.3 %collective-permute-start.6 = (bf16[144,768]{1,0:T(8,128)(2,1)S(1)}, bf16[144,768]{1,0:T(8,128)(2,1)S(1)}, u32[]{:S(2)}, u32[]{:S(2)}) collective-permute-start(bf16[144,768]{1,0:T(8,128)(2,1)S(1)} %get-tuple-element.80), channel_id=1, source_target_pairs={{0,3},{1,0},{2,1},{3,2},{4,7},{5,4},{6,5},{7,6},{8,11},{9,8},{10,9... | collective-permute-start | bytes 663560 | tf_op jit(solution)/shard_map/ppermute | solution.py:855
  38.5 46.4 %collective-permute-start.8 = (bf16[128,768]{1,0:T(8,128)(2,1)S(1)}, bf16[128,768]{1,0:T(8,128)(2,1)S(1)}, u32[]{:S(2)}, u32[]{:S(2)}) collective-permute-start(bf16[128,768]{1,0:T(8,128)(2,1)S(1)} %get-tuple-element.87), channel_id=1, source_target_pairs={{0,1},{1,2},{2,3},{3,0},{4,5},{5,6},{6,7},{7,4},{8,9},{9,10},{10,1... | collective-permute-start | bytes 589832 | tf_op jit(solution)/shard_map/ppermute | solution.py:855
  51.3 33.6 %collective-permute-start.9 = (bf16[128,768]{1,0:T(8,128)(2,1)S(1)}, bf16[128,768]{1,0:T(8,128)(2,1)S(1)}, u32[]{:S(2)}, u32[]{:S(2)}) collective-permute-start(bf16[128,768]{1,0:T(8,128)(2,1)S(1)} %get-tuple-element.88), channel_id=1, source_target_pairs={{0,2},{1,3},{2,0},{3,1},{4,6},{5,7},{6,4},{7,5},{8,10},{9,11},{10,... | collective-permute-start | bytes 589832 | tf_op jit(solution)/shard_map/ppermute | solution.py:855
  54.7 30.2 %collective-permute-start.10 = (bf16[128,768]{1,0:T(8,128)(2,1)S(1)}, bf16[128,768]{1,0:T(8,128)(2,1)S(1)}, u32[]{:S(2)}, u32[]{:S(2)}) collective-permute-start(bf16[128,768]{1,0:T(8,128)(2,1)S(1)} %get-tuple-element.89), channel_id=1, source_target_pairs={{0,3},{1,0},{2,1},{3,2},{4,7},{5,4},{6,5},{7,6},{8,11},{9,8},{10,9... | collective-permute-start | bytes 589832 | tf_op jit(solution)/shard_map/ppermute | solution.py:855
  56.8 35.0 %copy-start.9 = (f32[32,256]{1,0:T(8,128)S(1)}, f32[32,256]{1,0:T(8,128)}, u32[]{:S(2)}) copy-start(f32[32,256]{1,0:T(8,128)} %constant.36.clone.refs_10_) | copy-start | bytes 98308
  84.9 29.9 %copy-start.10 = (f32[3072]{0:T(1024)S(1)}, f32[3072]{0:T(1024)}, u32[]{:S(2)}) copy-start(f32[3072]{0:T(1024)} %param.19) | copy-start | bytes 36868
  84.9 20.4 %collective-permute-start.11 = (bf16[144,768]{1,0:T(8,128)(2,1)S(1)}, bf16[144,768]{1,0:T(8,128)(2,1)S(1)}, u32[]{:S(2)}, u32[]{:S(2)}) collective-permute-start(bf16[144,768]{1,0:T(8,128)(2,1)S(1)} %get-tuple-element.99.refs_1_), channel_id=1, source_target_pairs={{0,3},{1,0},{2,1},{3,2},{4,7},{5,4},{6,5},{7,6},{8,11},{9,8},{10,9... | collective-permute-start | bytes 663560 | tf_op jit(solution)/shard_map/ppermute | solution.py:855
  90.2 21.2 %collective-permute-start.12 = (bf16[144,768]{1,0:T(8,128)(2,1)S(1)}, bf16[144,768]{1,0:T(8,128)(2,1)S(1)}, u32[]{:S(2)}, u32[]{:S(2)}) collective-permute-start(bf16[144,768]{1,0:T(8,128)(2,1)S(1)} %get-tuple-element.100.refs_2_), channel_id=1, source_target_pairs={{0,2},{1,3},{2,0},{3,1},{4,6},{5,7},{6,4},{7,5},{8,10},{9,11},{10,... | collective-permute-start | bytes 663560 | tf_op jit(solution)/shard_map/ppermute | solution.py:855
  91.8 19.6 %collective-permute-start.13 = (bf16[144,768]{1,0:T(8,128)(2,1)S(1)}, bf16[144,768]{1,0:T(8,128)(2,1)S(1)}, u32[]{:S(2)}, u32[]{:S(2)}) collective-permute-start(bf16[144,768]{1,0:T(8,128)(2,1)S(1)} %get-tuple-element.101.refs_3_), channel_id=1, source_target_pairs={{0,1},{1,2},{2,3},{3,0},{4,5},{5,6},{6,7},{7,4},{8,9},{9,10},{10,1... | collective-permute-start | bytes 663560 | tf_op jit(solution)/shard_map/ppermute | solution.py:855
  111.4 22.6 %collective-permute-start.14 = (bf16[240,384]{1,0:T(8,128)(2,1)S(1)}, bf16[240,384]{1,0:T(8,128)(2,1)S(1)}, u32[]{:S(2)}, u32[]{:S(2)}) collective-permute-start(bf16[240,384]{1,0:T(8,128)(2,1)S(1)} %get-tuple-element.115), channel_id=1, source_target_pairs={{0,3},{1,0},{2,1},{3,2},{4,7},{5,4},{6,5},{7,6},{8,11},{9,8},{10,9... | collective-permute-start | bytes 552968 | tf_op jit(solution)/shard_map/ppermute | solution.py:855
  111.4 22.6 %collective-permute-start.15 = (bf16[240,384]{1,0:T(8,128)(2,1)S(1)}, bf16[240,384]{1,0:T(8,128)(2,1)S(1)}, u32[]{:S(2)}, u32[]{:S(2)}) collective-permute-start(bf16[240,384]{1,0:T(8,128)(2,1)S(1)} %get-tuple-element.116), channel_id=1, source_target_pairs={{0,2},{1,3},{2,0},{3,1},{4,6},{5,7},{6,4},{7,5},{8,10},{9,11},{10,... | collective-permute-start | bytes 552968 | tf_op jit(solution)/shard_map/ppermute | solution.py:855
  112.8 21.2 %collective-permute-start.16 = (bf16[240,384]{1,0:T(8,128)(2,1)S(1)}, bf16[240,384]{1,0:T(8,128)(2,1)S(1)}, u32[]{:S(2)}, u32[]{:S(2)}) collective-permute-start(bf16[240,384]{1,0:T(8,128)(2,1)S(1)} %get-tuple-element.117), channel_id=1, source_target_pairs={{0,1},{1,2},{2,3},{3,0},{4,5},{5,6},{6,7},{7,4},{8,9},{9,10},{10,1... | collective-permute-start | bytes 552968 | tf_op jit(solution)/shard_map/ppermute | solution.py:855
  115.7 1.5 copy-start.8
  117.3 1.1 copy-start.1
  131.9 0.7 copy-start.11
  132.6 0.7 copy-start.12
  133.3 0.7 copy-start.13
  134.0 22.0 %copy-start.3 = (bf16[1,128,3072]{2,1,0:T(8,128)(2,1)S(1)}, bf16[1,128,3072]{2,1,0:T(8,128)(2,1)}, u32[]{:S(2)}) copy-start(bf16[1,128,3072]{2,1,0:T(8,128)(2,1)} %param.13) | copy-start | bytes 2359300
  134.0 6.0 %collective-permute-start.20 = (bf16[128,768]{1,0:T(8,128)(2,1)S(1)}, bf16[128,768]{1,0:T(8,128)(2,1)}, u32[]{:S(2)}, u32[]{:S(2)}) collective-permute-start(bf16[128,768]{1,0:T(8,128)(2,1)S(1)} %get-tuple-element.133), channel_id=1, source_target_pairs={{28,4},{29,5},{30,6},{31,7}} | collective-permute-start | bytes 589832 | tf_op jit(solution)/shard_map/ppermute | solution.py:834
  135.5 6.2 %collective-permute-start.21 = (bf16[128,768]{1,0:T(8,128)(2,1)S(1)}, bf16[128,768]{1,0:T(8,128)(2,1)}, u32[]{:S(2)}, u32[]{:S(2)}) collective-permute-start(bf16[128,768]{1,0:T(8,128)(2,1)S(1)} %get-tuple-element.134), channel_id=1, source_target_pairs={{28,12},{29,13},{30,14},{31,15}} | collective-permute-start | bytes 589832 | tf_op jit(solution)/shard_map/ppermute | solution.py:834
  136.8 4.9 %collective-permute-start.22 = (bf16[128,768]{1,0:T(8,128)(2,1)S(1)}, bf16[128,768]{1,0:T(8,128)(2,1)}, u32[]{:S(2)}, u32[]{:S(2)}) collective-permute-start(bf16[128,768]{1,0:T(8,128)(2,1)S(1)} %get-tuple-element.135), channel_id=1, source_target_pairs={{28,20},{29,21},{30,22},{31,23}} | collective-permute-start | bytes 589832 | tf_op jit(solution)/shard_map/ppermute | solution.py:834
  138.1 7.2 %collective-permute-start.17 = (bf16[240,384]{1,0:T(8,128)(2,1)}, bf16[240,384]{1,0:T(8,128)(2,1)S(1)}, u32[]{:S(2)}, u32[]{:S(2)}) collective-permute-start(bf16[240,384]{1,0:T(8,128)(2,1)} %copy-done.13), channel_id=1, source_target_pairs={{0,3},{1,0},{2,1},{3,2},{4,7},{5,4},{6,5},{7,6},{8,11},{9,8},{10,9... | collective-permute-start | bytes 552968 | tf_op jit(solution)/shard_map/ppermute | solution.py:855
  140.0 16.0 %collective-permute-start.18 = (bf16[240,384]{1,0:T(8,128)(2,1)}, bf16[240,384]{1,0:T(8,128)(2,1)S(1)}, u32[]{:S(2)}, u32[]{:S(2)}) collective-permute-start(bf16[240,384]{1,0:T(8,128)(2,1)} %copy-done.12), channel_id=1, source_target_pairs={{0,2},{1,3},{2,0},{3,1},{4,6},{5,7},{6,4},{7,5},{8,10},{9,11},{10,... | collective-permute-start | bytes 552968 | tf_op jit(solution)/shard_map/ppermute | solution.py:855
  140.0 16.0 %collective-permute-start.19 = (bf16[240,384]{1,0:T(8,128)(2,1)}, bf16[240,384]{1,0:T(8,128)(2,1)S(1)}, u32[]{:S(2)}, u32[]{:S(2)}) collective-permute-start(bf16[240,384]{1,0:T(8,128)(2,1)} %copy-done.11), channel_id=1, source_target_pairs={{0,1},{1,2},{2,3},{3,0},{4,5},{5,6},{6,7},{7,4},{8,9},{9,10},{10,1... | collective-permute-start | bytes 552968 | tf_op jit(solution)/shard_map/ppermute | solution.py:855
  142.9 16.4 %collective-permute-start.23 = (bf16[64,768]{1,0:T(8,128)(2,1)S(1)}, bf16[64,768]{1,0:T(8,128)(2,1)S(1)}, u32[]{:S(2)}, u32[]{:S(2)}) collective-permute-start(bf16[64,768]{1,0:T(8,128)(2,1)S(1)} %slice.12), channel_id=1, source_target_pairs={{4,0},{12,8},{20,16},{28,24},{5,1},{13,9},{21,17},{29,25},{6,2},{1... | collective-permute-start | bytes 294920 | tf_op jit(solution)/shard_map/ppermute | solution.py:836

commit v6 on v5

--- a/solution.py
+++ b/solution.py
@@ -17,7 +17,7 @@
 masked_score = -1e30
 F32 = jnp.float32
 BF16 = jnp.bfloat16
-VMEM_LIMIT = 48 * 1024 * 1024
+VMEM_LIMIT = 24 * 1024 * 1024
 
 
 def bucket_onehot(bucket_count):
@@ -822,19 +822,19 @@
     return lax.ppermute(value, axis, [(source, source + steps) for source in range(first, last)])
 
 
-def spread_memory(shares, section, sections):
-    last = sections - 1
-    if len(shares) == sections:
-        memory = jnp.where(section == last, shares[last], 0)
-        for s in range(last):
-            memory = memory + lax.ppermute(shares[s], "section", [(last, s)])
-        return memory
-    couple = jnp.where(section == last, shares[-1], 0)
-    for s, share in enumerate(shares[:-1]):
-        couple = couple + lax.ppermute(share, "section", [(last, 2 * s + 1)])
-    half = couple.shape[0] // 2
-    even = lax.ppermute(couple[:half], "section", [(s + 1, s) for s in range(0, sections, 2)])
-    return jnp.where(section % 2 == 0, even, couple[half:])
+def spread_memory(lower, upper, section, sections, later):
+    size = sections
+    while True:
+        half = size // 2
+        pairs = [(top, top - half) for top in range(size - 1, sections, size)]
+        got = lax.ppermute(lower, "section", pairs)
+        if size == sections:
+            got, later = lax.optimization_barrier((got, later))
+        held = jnp.where(section % size == size - 1, upper, got)
+        if half == 1:
+            return held
+        middle = held.shape[0] // 2
+        lower, upper, size = held[:middle], held[middle:], half
 
 
 def heads_body(
@@ -859,11 +859,11 @@
 
     inverse_b, *a_sends = pack_stash(meta, stash[0], norm_gain, qkv_weight[0], parts)
     a_slots = exchanged(a_sends, 1)
-    kept, gone, inverse_b = lax.optimization_barrier((carried[0], returned[0], inverse_b))
-    arrived = shifted(kept, "section", 1)
-    came_back = shifted(gone, "section", -1)
+    arrived = shifted(carried[0], "section", 1)
+    came_back = shifted(returned[0], "section", -1)
     i_slots = exchanged(pack_rows(meta, embedded, arrived, parts, True), 1)
     *c_sends, cotangent = pack_rows(meta, loss_grad, came_back, parts, False)
+    c_sends, a_slots, i_slots = lax.optimization_barrier((c_sends, a_slots, i_slots))
     c_slots = exchanged(c_sends, 1)
     c_slots[0] = cotangent
 
@@ -885,14 +885,13 @@
     g_sends, o_slots = lax.optimization_barrier((g_sends, o_slots))
     g_chunks = [exchanged(g_sends, -1)]
     output = place_columns(meta, o_slots)
-    shares = sections // 2 if sections % 2 == 0 else sections
-    made = memory_rows(meta, o_sends, o_slots[1:], final_gain[None], width, shares)
+    lower, upper = memory_rows(meta, o_sends, o_slots[1:], final_gain[None], width, 2)
     if chunks == 2:
         *g_sends, gain_part = backward(1, output)
-        g_sends, made, g_chunks = lax.optimization_barrier((g_sends, made, g_chunks))
+        g_sends, g_chunks = lax.optimization_barrier((g_sends, g_chunks))
         g_chunks.append(exchanged(g_sends, -1))
         gain_grad = jnp.concatenate([gain_grad, gain_part], axis=1)
-    memory = spread_memory(made, section, sections)
+    memory = spread_memory(lower, upper, section, sections, g_chunks[0])
 
     input_grad, weight_grad, bias_wide = heads_finish(
         meta, g_chunks, stash[0], inverse_b, norm_gain, cotangent, buckets
@@ -978,7 +977,9 @@
     parts = lax.axis_size("seq")
     rows, width = embedded.shape
     even = width % (HEAD_DIM * parts) == 0 and HEAD_DIM % (32 * parts) == 0 and rows == 128
-    even = even and rel_bias.shape[1] == 8 * parts and rows * parts % (16 * lax.axis_size("section")) == 0
+    sections = lax.axis_size("section")
+    even = even and sections > 1 and sections & (sections - 1) == 0
+    even = even and rel_bias.shape[1] == 8 * parts and rows * parts % (16 * sections) == 0
     chosen = heads_body if even else tokens_body
     return chosen(
         embedded, carried, stash, returned, loss_grad, qkv_weight, rel_bias, norm_gain, final_gain

time: 161 us -> 157 us (0.975)
  starting transfers between devices: 50.6 us -> 36.5 us
  waiting for transfers between devices: 45.1 us -> 53.7 us
  Pallas kernels: 53.8 us -> 56.2 us
    ppermute x18, starting transfers between devices: 41.5 us -> 28.6 us  [exchanged(): lax.ppermute(sends[r], 'seq', [(i, (i + direction * r) % parts) for i in...]
    ppermute x18, waiting for transfers between devices: 45.1 us -> 53.7 us  [exchanged(): lax.ppermute(sends[r], 'seq', [(i, (i + direction * r) % parts) for i in...]
    ppermute x4 -> x3, starting transfers between devices: 5.43 us -> 3.37 us  [spread_memory(): got = lax.ppermute(lower, 'section', pairs)]
    unnamed x30 -> x46, local copies, waits for them, and re-layouts: 6.1 us -> 5.5 us
  transfers between devices with their start and end apart: 24 -> 23, of which waited for: 6 -> 7; matrix products, arithmetic and copies ran while one was open for 2% -> 1% of each run, Pallas kernels for 33% -> 35%
where the time goes in v6:
time: 157 us
  Pallas kernels  56.2 us (36%)
  waiting for transfers between devices  53.7 us (34%)
  starting transfers between devices  36.5 us (23%)
  local copies, waits for them, and re-layouts  6.26 us (4%)
  other arithmetic  2.56 us (2%)
    ppermute x18, waiting for transfers between devices, exchanged(): lax.ppermute(sends[r], 'seq', [(i, (i + direction * r) % parts) for i in...  53.7 us
    ppermute x18, starting transfers between devices, exchanged(): lax.ppermute(sends[r], 'seq', [(i, (i + direction * r) % parts) for i in...  28.6 us
    pallas_call x2, Pallas kernels, heads_backward(): pl.pallas_call(functools.partial(heads_backward_kernel, parts, rows), out...  27.7 us
    pallas_call x1, Pallas kernels, heads_forward(): pl.pallas_call(functools.partial(heads_forward_kernel, parts, rows), out_...  18.1 us
    unnamed x46, local copies, waits for them, and re-layouts  5.5 us
    ppermute x2, starting transfers between devices, shifted(): lax.ppermute(value, axis, [(source, source + steps) for source in range(f...  4.54 us
    ppermute x3, starting transfers between devices, spread_memory(): got = lax.ppermute(lower, 'section', pairs)  3.37 us
    pallas_call x1, Pallas kernels, heads_finish(): pl.pallas_call(functools.partial(heads_finish_kernel, parts, chunks), out...  3.2 us
  transfers between devices with their start and end apart: 23, of which 7 were waited for; matrix products, arithmetic and copies ran while one was open for 1% of the time, Pallas kernels for 35%

profile of v6, /device:TPU:0, one launch (start us, length us, event | category | flops | bytes accessed | tf_op | source)
XLA Modules:
  0.0 156.5 jit_solution(7397223171493393249)
XLA Ops:
  0.6 0.0 copy-start
  0.6 3.3 %collective-permute-start.4 = (bf16[128,3072]{1,0:T(8,128)(2,1)}, bf16[128,3072]{1,0:T(8,128)(2,1)}, u32[]{:S(2)}, u32[]{:S(2)}) collective-permute-start(bf16[128,3072]{1,0:T(8,128)(2,1)} %bitcast.31), channel_id=1, source_target_pairs={{0,4},{4,8},{8,12},{12,16},{16,20},{20,24},{24,28},{1,5},{5,9},{9,... | collective-permute-start | bytes 2359304 | tf_op jit(solution)/shard_map/ppermute | solution.py:822
  3.9 1.3 collective-permute-start
  5.2 0.1 pad_add_fusion.meta_ref
  5.3 1.1 copy-done.2
  6.4 1.1 copy-done.8
  7.5 0.7 copy-done.11
  8.2 1.3 pack_stash.1
  9.5 0.0 copy-start.16
  9.5 0.6 copy-done.16
  10.1 2.4 %collective-permute-start.1 = (bf16[224,768]{1,0:T(8,128)(2,1)S(1)}, bf16[224,768]{1,0:T(8,128)(2,1)S(1)}, u32[]{:S(2)}, u32[]{:S(2)}) collective-permute-start(bf16[224,768]{1,0:T(8,128)(2,1)S(1)} %get-tuple-element.78), channel_id=1, source_target_pairs={{0,1},{1,2},{2,3},{3,0},{4,5},{5,6},{6,7},{7,4},{8,9},{9,10},{10,1... | collective-permute-start | bytes 1032200 | tf_op jit(solution)/shard_map/ppermute | solution.py:855
  12.5 2.6 %collective-permute-start.2 = (bf16[224,768]{1,0:T(8,128)(2,1)S(1)}, bf16[224,768]{1,0:T(8,128)(2,1)S(1)}, u32[]{:S(2)}, u32[]{:S(2)}) collective-permute-start(bf16[224,768]{1,0:T(8,128)(2,1)S(1)} %get-tuple-element.79), channel_id=1, source_target_pairs={{0,2},{1,3},{2,0},{3,1},{4,6},{5,7},{6,4},{7,5},{8,10},{9,11},{10,... | collective-permute-start | bytes 1032200 | tf_op jit(solution)/shard_map/ppermute | solution.py:855
  15.1 1.4 collective-permute-start.3
  16.4 1.5 pack_inbound.1
  18.0 0.0 copy-start.12
  18.0 0.7 collective-permute-start.5
  18.7 4.1 %collective-permute-done.1.refs_1_ = bf16[224,768]{1,0:T(8,128)(2,1)S(1)} collective-permute-done((bf16[224,768]{1,0:T(8,128)(2,1)S(1)}, bf16[224,768]{1,0:T(8,128)(2,1)S(1)}, u32[]{:S(2)}, u32[]{:S(2)}) %collective-permute-start.1) | collective-permute-done | bytes 344096 | tf_op jit(solution)/shard_map/ppermute | solution.py:855
  22.8 1.2 collective-permute-start.6
  24.1 0.0 collective-permute-done.inner_ref
  24.1 1.2 collective-permute-start.7
  25.3 1.4 pack_cotangent.1
  26.7 12.4 %collective-permute-done.2.refs_2_ = bf16[224,768]{1,0:T(8,128)(2,1)S(1)} collective-permute-done((bf16[224,768]{1,0:T(8,128)(2,1)S(1)}, bf16[224,768]{1,0:T(8,128)(2,1)S(1)}, u32[]{:S(2)}, u32[]{:S(2)}) %collective-permute-start.2) | collective-permute-done | bytes 344096 | tf_op jit(solution)/shard_map/ppermute | solution.py:855
  39.1 3.3 %collective-permute-done.5.refs_5_ = bf16[144,768]{1,0:T(8,128)(2,1)S(1)} collective-permute-done((bf16[144,768]{1,0:T(8,128)(2,1)S(1)}, bf16[144,768]{1,0:T(8,128)(2,1)S(1)}, u32[]{:S(2)}, u32[]{:S(2)}) %collective-permute-start.5) | collective-permute-done | bytes 221216 | tf_op jit(solution)/shard_map/ppermute | solution.py:855
  42.3 17.5 %collective-permute-done.6.refs_6_ = bf16[144,768]{1,0:T(8,128)(2,1)S(1)} collective-permute-done((bf16[144,768]{1,0:T(8,128)(2,1)S(1)}, bf16[144,768]{1,0:T(8,128)(2,1)S(1)}, u32[]{:S(2)}, u32[]{:S(2)}) %collective-permute-start.6) | collective-permute-done | bytes 221216 | tf_op jit(solution)/shard_map/ppermute | solution.py:855
  59.8 6.1 %collective-permute-start.10 = (bf16[128,768]{1,0:T(8,128)(2,1)S(1)}, bf16[128,768]{1,0:T(8,128)(2,1)S(1)}, u32[]{:S(2)}, u32[]{:S(2)}) collective-permute-start(bf16[128,768]{1,0:T(8,128)(2,1)S(1)} %get-tuple-element.100), channel_id=1, source_target_pairs={{0,3},{1,0},{2,1},{3,2},{4,7},{5,4},{6,5},{7,6},{8,11},{9,8},{10,9... | collective-permute-start | bytes 589832 | tf_op jit(solution)/shard_map/ppermute | solution.py:855
  65.9 0.0 collective-permute-start.8
  65.9 0.7 collective-permute-start.9
  66.6 0.2 fusion
  66.8 0.0 copy-start.15
  66.9 18.1 %heads_forward.1 = (bf16[144,768]{1,0:T(8,128)(2,1)S(1)}, bf16[144,768]{1,0:T(8,128)(2,1)S(1)}, bf16[144,768]{1,0:T(8,128)(2,1)S(1)}, bf16[144,768]{1,0:T(8,128)(2,1)S(1)}) custom-call(s32[3]{0:T(128)S(1)} %pad_add_fusion.meta_ref, bf16[224,768]{1,0:T(8,128)(2,1)S(1)} %get-tuple-element.85.refs_0_, bf16[224,768]{1,0:T(8,128)(2,1)S(1)} %collective-permute-done.1.refs_1_, ...), custom_call_target="tpu_custom_call" | custom-call | flops 3072 | bytes 512 | tf_op jit(solution)/shard_map/heads_forward/pallas_call | solution.py:667
  85.0 0.0 collective-permute-done.10.refs_7_
  85.0 0.0 collective-permute-done.9.refs_6_
  85.0 0.0 copy-start.18
  85.0 3.2 %collective-permute-start.11 = (bf16[144,768]{1,0:T(8,128)(2,1)S(1)}, bf16[144,768]{1,0:T(8,128)(2,1)S(1)}, u32[]{:S(2)}, u32[]{:S(2)}) collective-permute-start(bf16[144,768]{1,0:T(8,128)(2,1)S(1)} %get-tuple-element.110.refs_1_), channel_id=1, source_target_pairs={{0,3},{1,0},{2,1},{3,2},{4,7},{5,4},{6,5},{7,6},{8,11},{9,8},{10,9... | collective-permute-start | bytes 663560 | tf_op jit(solution)/shard_map/ppermute | solution.py:855
  88.3 2.0 %collective-permute-start.12 = (bf16[144,768]{1,0:T(8,128)(2,1)S(1)}, bf16[144,768]{1,0:T(8,128)(2,1)S(1)}, u32[]{:S(2)}, u32[]{:S(2)}) collective-permute-start(bf16[144,768]{1,0:T(8,128)(2,1)S(1)} %get-tuple-element.111.refs_2_), channel_id=1, source_target_pairs={{0,2},{1,3},{2,0},{3,1},{4,6},{5,7},{6,4},{7,5},{8,10},{9,11},{10,... | collective-permute-start | bytes 663560 | tf_op jit(solution)/shard_map/ppermute | solution.py:855
  90.3 0.0 collective-permute-start.13
  90.3 14.1 %heads_backward.2 = (bf16[240,384]{1,0:T(8,128)(2,1)S(1)}, bf16[240,384]{1,0:T(8,128)(2,1)}, bf16[240,384]{1,0:T(8,128)(2,1)}, bf16[240,384]{1,0:T(8,128)(2,1)}, f32[1,384]{1,0:T(1,128)S(1)}) custom-call(s32[3]{0:T(128)S(1)} %pad_add_fusion.meta_ref, bf16[224,768]{1,0:T(8,128)(2,1)S(1)} %get-tuple-element.85.refs_0_, ...), custom_call_target="tpu_custom_call" | custom-call | flops 614400000 | bytes 196608 | tf_op jit(solution)/shard_map/heads_backward/pallas_call | solution.py:572
  104.4 4.9 %collective-permute-done.12.refs_2_.refs_5_ = bf16[144,768]{1,0:T(8,128)(2,1)S(1)} collective-permute-done((bf16[144,768]{1,0:T(8,128)(2,1)S(1)}, bf16[144,768]{1,0:T(8,128)(2,1)S(1)}, u32[]{:S(2)}, u32[]{:S(2)}) %collective-permute-start.12) | collective-permute-done | bytes 221216 | tf_op jit(solution)/shard_map/ppermute | solution.py:855
  109.3 1.6 %memory_rows.1 = (bf16[256,768]{1,0:T(8,128)(2,1)}, bf16[256,768]{1,0:T(8,128)(2,1)S(1)}) custom-call(s32[3]{0:T(128)S(1)} %pad_add_fusion.meta_ref, bf16[144,768]{1,0:T(8,128)(2,1)S(1)} %get-tuple-element.113.refs_11_.refs_0_, bf16[144,768]{1,0:T(8,128)(2,1)S(1)} %get-tuple-element.110.refs_1_, bf16[144,768]{1,0:T(8,128)(2,1)S(1)} %get-tuple-element.111.refs_2_, ...), custom_call_target="tpu_custom_call" | custom-call | flops 128 | bytes 128 | tf_op jit(solution)/shard_map/memory_rows/pallas_call | solution.py:728
  110.9 0.7 copy-done.9
  111.6 1.4 collective-permute-start.20
  113.0 0.6 collective-permute-start.15
  113.7 2.0 %collective-permute-start.16 = (bf16[240,384]{1,0:T(8,128)(2,1)}, bf16[240,384]{1,0:T(8,128)(2,1)}, u32[]{:S(2)}, u32[]{:S(2)}) collective-permute-start(bf16[240,384]{1,0:T(8,128)(2,1)} %get-tuple-element.124), channel_id=1, source_target_pairs={{0,1},{1,2},{2,3},{3,0},{4,5},{5,6},{6,7},{7,4},{8,9},{9,10},{10,1... | collective-permute-start | bytes 552968 | tf_op jit(solution)/shard_map/ppermute | solution.py:855
  115.7 1.5 place_columns.1.refs_11_
  117.2 1.1 copy-done.1
  118.3 13.5 %heads_backward.3 = (bf16[240,384]{1,0:T(8,128)(2,1)S(1)}, bf16[240,384]{1,0:T(8,128)(2,1)S(1)}, bf16[240,384]{1,0:T(8,128)(2,1)S(1)}, bf16[240,384]{1,0:T(8,128)(2,1)S(1)}, f32[1,384]{1,0:T(1,128)S(1)}) custom-call(s32[3]{0:T(128)S(1)} %pad_add_fusion.meta_ref, bf16[224,768]{1,0:T(8,128)(2,1)S(1)} %get-tuple-element.85.refs_0_, ...), custom_call_target="tpu_custom_call" | custom-call | flops 614400000 | bytes 196608 | tf_op jit(solution)/shard_map/heads_backward/pallas_call | solution.py:572
  131.9 0.0 collective-permute-done.14.refs_1_
  131.9 0.0 collective-permute-done.15.refs_2_
  131.9 0.0 collective-permute-done.20
  131.9 0.0 copy-start.3
  132.0 0.0 copy-start.17
  132.0 1.2 broadcast_select_fusion
  133.2 0.7 collective-permute-start.21
  134.0 1.9 %collective-permute-start.17 = (bf16[240,384]{1,0:T(8,128)(2,1)}, bf16[240,384]{1,0:T(8,128)(2,1)S(1)}, u32[]{:S(2)}, u32[]{:S(2)}) collective-permute-start(bf16[240,384]{1,0:T(8,128)(2,1)} %copy-done.21), channel_id=1, source_target_pairs={{0,3},{1,0},{2,1},{3,2},{4,7},{5,4},{6,5},{7,6},{8,11},{9,8},{10,9... | collective-permute-start | bytes 552968 | tf_op jit(solution)/shard_map/ppermute | solution.py:855
  135.8 0.6 collective-permute-start.18
  136.4 1.9 %collective-permute-start.19 = (bf16[240,384]{1,0:T(8,128)(2,1)}, bf16[240,384]{1,0:T(8,128)(2,1)S(1)}, u32[]{:S(2)}, u32[]{:S(2)}) collective-permute-start(bf16[240,384]{1,0:T(8,128)(2,1)} %copy-done.19), channel_id=1, source_target_pairs={{0,1},{1,2},{2,3},{3,0},{4,5},{5,6},{6,7},{7,4},{8,9},{9,10},{10,1... | collective-permute-start | bytes 552968 | tf_op jit(solution)/shard_map/ppermute | solution.py:855
  138.4 0.0 collective-permute-done.21
  138.4 1.3 collective-permute-start.22
  139.7 0.6 pad_maximum_fusion
  140.3 1.0 collective-permute-done.17.refs_5_
  141.3 10.6 %collective-permute-done.18.refs_6_ = bf16[240,384]{1,0:T(8,128)(2,1)S(1)} collective-permute-done((bf16[240,384]{1,0:T(8,128)(2,1)}, bf16[240,384]{1,0:T(8,128)(2,1)S(1)}, u32[]{:S(2)}, u32[]{:S(2)}) %collective-permute-start.18) | collective-permute-done | bytes 184352 | tf_op jit(solution)/shard_map/ppermute | solution.py:855
  151.9 3.2 %heads_finish.1 = (bf16[128,3072]{1,0:T(8,128)(2,1)}, f32[3,24,32,128]{3,2,1,0:T(8,128)}, f32[24,8,128]{2,1,0:T(8,128)S(1)}) custom-call(s32[3]{0:T(128)S(1)} %pad_add_fusion.meta_ref, bf16[240,384]{1,0:T(8,128)(2,1)S(1)} %copy-done.14, bf16[240,384]{1,0:T(8,128)(2,1)} %collective-permute-done.14.refs_1_, bf16[240,384]{1,0:T(8,128)(2,1)} %collective-permute-done.15.refs_2_, ...), custom_call_target="tpu_custom_call" | custom-call | flops 4718592 | bytes 5505024 | tf_op jit(solution)/shard_map/heads_finish/pallas_call | solution.py:796
  155.1 0.7 copy.18
  155.8 0.7 slice_select_fusion.1
  (48 shorter events, 0.2 us)
Async XLA Ops:
  0.6 66.0 %copy-start = (f32[1,32,24]{1,2,0:T(8,128)S(1)}, f32[1,32,24]{1,2,0:T(8,128)}, u32[]{:S(2)}) copy-start(f32[1,32,24]{1,2,0:T(8,128)} %param.17) | copy-start | bytes 9220
  0.6 15.8 %collective-permute-start.4 = (bf16[128,3072]{1,0:T(8,128)(2,1)}, bf16[128,3072]{1,0:T(8,128)(2,1)}, u32[]{:S(2)}, u32[]{:S(2)}) collective-permute-start(bf16[128,3072]{1,0:T(8,128)(2,1)} %bitcast.31), channel_id=1, source_target_pairs={{0,4},{4,8},{8,12},{12,16},{16,20},{20,24},{24,28},{1,5},{5,9},{9,... | collective-permute-start | bytes 2359304 | tf_op jit(solution)/shard_map/ppermute | solution.py:822
  3.9 20.2 %collective-permute-start = (bf16[128,3072]{1,0:T(8,128)(2,1)}, bf16[128,3072]{1,0:T(8,128)(2,1)S(1)}, u32[]{:S(2)}, u32[]{:S(2)}) collective-permute-start(bf16[128,3072]{1,0:T(8,128)(2,1)} %bitcast.32), channel_id=1, source_target_pairs={{4,0},{8,4},{12,8},{16,12},{20,16},{24,20},{28,24},{5,1},{9,5},{13... | collective-permute-start | bytes 2359304 | tf_op jit(solution)/shard_map/ppermute | solution.py:822
  5.3 1.1 copy-start.2
  6.4 1.1 copy-start.8
  7.5 0.7 copy-start.11
  8.2 8.2 %copy-start.6 = (bf16[128,3072]{1,0:T(8,128)(2,1)S(1)}, bf16[128,3072]{1,0:T(8,128)(2,1)}, u32[]{:S(2)}) copy-start(bf16[128,3072]{1,0:T(8,128)(2,1)} %edge_ref.3) | copy-start | bytes 2359300
  8.2 17.1 %copy-start.7 = (bf16[128,3072]{1,0:T(8,128)(2,1)S(1)}, bf16[128,3072]{1,0:T(8,128)(2,1)}, u32[]{:S(2)}) copy-start(bf16[128,3072]{1,0:T(8,128)(2,1)} %edge_ref.2) | copy-start | bytes 2359300
  9.5 0.6 copy-start.16
  10.1 12.7 %collective-permute-start.1 = (bf16[224,768]{1,0:T(8,128)(2,1)S(1)}, bf16[224,768]{1,0:T(8,128)(2,1)S(1)}, u32[]{:S(2)}, u32[]{:S(2)}) collective-permute-start(bf16[224,768]{1,0:T(8,128)(2,1)S(1)} %get-tuple-element.78), channel_id=1, source_target_pairs={{0,1},{1,2},{2,3},{3,0},{4,5},{5,6},{6,7},{7,4},{8,9},{9,10},{10,1... | collective-permute-start | bytes 1032200 | tf_op jit(solution)/shard_map/ppermute | solution.py:855
  12.5 26.6 %collective-permute-start.2 = (bf16[224,768]{1,0:T(8,128)(2,1)S(1)}, bf16[224,768]{1,0:T(8,128)(2,1)S(1)}, u32[]{:S(2)}, u32[]{:S(2)}) collective-permute-start(bf16[224,768]{1,0:T(8,128)(2,1)S(1)} %get-tuple-element.79), channel_id=1, source_target_pairs={{0,2},{1,3},{2,0},{3,1},{4,6},{5,7},{6,4},{7,5},{8,10},{9,11},{10,... | collective-permute-start | bytes 1032200 | tf_op jit(solution)/shard_map/ppermute | solution.py:855
  15.1 24.0 %collective-permute-start.3 = (bf16[224,768]{1,0:T(8,128)(2,1)S(1)}, bf16[224,768]{1,0:T(8,128)(2,1)S(1)}, u32[]{:S(2)}, u32[]{:S(2)}) collective-permute-start(bf16[224,768]{1,0:T(8,128)(2,1)S(1)} %get-tuple-element.80), channel_id=1, source_target_pairs={{0,3},{1,0},{2,1},{3,2},{4,7},{5,4},{6,5},{7,6},{8,11},{9,8},{10,9... | collective-permute-start | bytes 1032200 | tf_op jit(solution)/shard_map/ppermute | solution.py:855
  18.0 48.6 %copy-start.22 = (f32[256,32]{1,0:T(8,128)S(1)}, f32[256,32]{1,0:T(8,128)}, u32[]{:S(2)}) copy-start(f32[256,32]{1,0:T(8,128)} %constant.54.clone) | copy-start | bytes 98308
  18.0 48.9 %copy-start.12 = (f32[1,3072]{1,0:T(1,128)S(1)}, f32[1,3072]{1,0:T(1,128)}, u32[]{:S(2)}) copy-start(f32[1,3072]{1,0:T(1,128)} %refs_10_.3) | copy-start | bytes 36868
  18.0 24.3 %collective-permute-start.5 = (bf16[144,768]{1,0:T(8,128)(2,1)S(1)}, bf16[144,768]{1,0:T(8,128)(2,1)S(1)}, u32[]{:S(2)}, u32[]{:S(2)}) collective-permute-start(bf16[144,768]{1,0:T(8,128)(2,1)S(1)} %get-tuple-element.82), channel_id=1, source_target_pairs={{0,1},{1,2},{2,3},{3,0},{4,5},{5,6},{6,7},{7,4},{8,9},{9,10},{10,1... | collective-permute-start | bytes 663560 | tf_op jit(solution)/shard_map/ppermute | solution.py:855
  22.8 37.0 %collective-permute-start.6 = (bf16[144,768]{1,0:T(8,128)(2,1)S(1)}, bf16[144,768]{1,0:T(8,128)(2,1)S(1)}, u32[]{:S(2)}, u32[]{:S(2)}) collective-permute-start(bf16[144,768]{1,0:T(8,128)(2,1)S(1)} %get-tuple-element.83), channel_id=1, source_target_pairs={{0,2},{1,3},{2,0},{3,1},{4,6},{5,7},{6,4},{7,5},{8,10},{9,11},{10,... | collective-permute-start | bytes 663560 | tf_op jit(solution)/shard_map/ppermute | solution.py:855
  24.1 35.8 %collective-permute-start.7 = (bf16[144,768]{1,0:T(8,128)(2,1)S(1)}, bf16[144,768]{1,0:T(8,128)(2,1)S(1)}, u32[]{:S(2)}, u32[]{:S(2)}) collective-permute-start(bf16[144,768]{1,0:T(8,128)(2,1)S(1)} %get-tuple-element.84), channel_id=1, source_target_pairs={{0,3},{1,0},{2,1},{3,2},{4,7},{5,4},{6,5},{7,6},{8,11},{9,8},{10,9... | collective-permute-start | bytes 663560 | tf_op jit(solution)/shard_map/ppermute | solution.py:855
  59.8 25.2 %collective-permute-start.10 = (bf16[128,768]{1,0:T(8,128)(2,1)S(1)}, bf16[128,768]{1,0:T(8,128)(2,1)S(1)}, u32[]{:S(2)}, u32[]{:S(2)}) collective-permute-start(bf16[128,768]{1,0:T(8,128)(2,1)S(1)} %get-tuple-element.100), channel_id=1, source_target_pairs={{0,3},{1,0},{2,1},{3,2},{4,7},{5,4},{6,5},{7,6},{8,11},{9,8},{10,9... | collective-permute-start | bytes 589832 | tf_op jit(solution)/shard_map/ppermute | solution.py:855
  65.9 19.1 %collective-permute-start.8 = (bf16[128,768]{1,0:T(8,128)(2,1)S(1)}, bf16[128,768]{1,0:T(8,128)(2,1)S(1)}, u32[]{:S(2)}, u32[]{:S(2)}) collective-permute-start(bf16[128,768]{1,0:T(8,128)(2,1)S(1)} %get-tuple-element.98), channel_id=1, source_target_pairs={{0,1},{1,2},{2,3},{3,0},{4,5},{5,6},{6,7},{7,4},{8,9},{9,10},{10,1... | collective-permute-start | bytes 589832 | tf_op jit(solution)/shard_map/ppermute | solution.py:855
  65.9 19.1 %collective-permute-start.9 = (bf16[128,768]{1,0:T(8,128)(2,1)S(1)}, bf16[128,768]{1,0:T(8,128)(2,1)S(1)}, u32[]{:S(2)}, u32[]{:S(2)}) collective-permute-start(bf16[128,768]{1,0:T(8,128)(2,1)S(1)} %get-tuple-element.99), channel_id=1, source_target_pairs={{0,2},{1,3},{2,0},{3,1},{4,6},{5,7},{6,4},{7,5},{8,10},{9,11},{10,... | collective-permute-start | bytes 589832 | tf_op jit(solution)/shard_map/ppermute | solution.py:855
  66.8 23.5 %copy-start.15 = (f32[32,256]{1,0:T(8,128)S(1)}, f32[32,256]{1,0:T(8,128)}, u32[]{:S(2)}) copy-start(f32[32,256]{1,0:T(8,128)} %constant.55.clone.refs_10_) | copy-start | bytes 98308
  85.0 19.4 %copy-start.4 = (bf16[128,768]{1,0:T(8,128)(2,1)}, bf16[128,768]{1,0:T(8,128)(2,1)S(1)}, u32[]{:S(2)}) copy-start(bf16[128,768]{1,0:T(8,128)(2,1)S(1)} %collective-permute-done.9.refs_6_) | copy-start | bytes 589828
  85.0 24.3 %copy-start.18 = (f32[3072]{0:T(1024)S(1)}, f32[3072]{0:T(1024)}, u32[]{:S(2)}) copy-start(f32[3072]{0:T(1024)} %param.19) | copy-start | bytes 36868
  85.0 19.4 %collective-permute-start.11 = (bf16[144,768]{1,0:T(8,128)(2,1)S(1)}, bf16[144,768]{1,0:T(8,128)(2,1)S(1)}, u32[]{:S(2)}, u32[]{:S(2)}) collective-permute-start(bf16[144,768]{1,0:T(8,128)(2,1)S(1)} %get-tuple-element.110.refs_1_), channel_id=1, source_target_pairs={{0,3},{1,0},{2,1},{3,2},{4,7},{5,4},{6,5},{7,6},{8,11},{9,8},{10,9... | collective-permute-start | bytes 663560 | tf_op jit(solution)/shard_map/ppermute | solution.py:855
  88.3 21.0 %collective-permute-start.12 = (bf16[144,768]{1,0:T(8,128)(2,1)S(1)}, bf16[144,768]{1,0:T(8,128)(2,1)S(1)}, u32[]{:S(2)}, u32[]{:S(2)}) collective-permute-start(bf16[144,768]{1,0:T(8,128)(2,1)S(1)} %get-tuple-element.111.refs_2_), channel_id=1, source_target_pairs={{0,2},{1,3},{2,0},{3,1},{4,6},{5,7},{6,4},{7,5},{8,10},{9,11},{10,... | collective-permute-start | bytes 663560 | tf_op jit(solution)/shard_map/ppermute | solution.py:855
  90.3 19.0 %collective-permute-start.13 = (bf16[144,768]{1,0:T(8,128)(2,1)S(1)}, bf16[144,768]{1,0:T(8,128)(2,1)S(1)}, u32[]{:S(2)}, u32[]{:S(2)}) collective-permute-start(bf16[144,768]{1,0:T(8,128)(2,1)S(1)} %get-tuple-element.112.refs_3_), channel_id=1, source_target_pairs={{0,1},{1,2},{2,3},{3,0},{4,5},{5,6},{6,7},{7,4},{8,9},{9,10},{10,1... | collective-permute-start | bytes 663560 | tf_op jit(solution)/shard_map/ppermute | solution.py:855
  104.4 6.5 %copy-start.13 = (bf16[240,384]{1,0:T(8,128)(2,1)}, bf16[240,384]{1,0:T(8,128)(2,1)S(1)}, u32[]{:S(2)}) copy-start(bf16[240,384]{1,0:T(8,128)(2,1)S(1)} %get-tuple-element.125.refs_0_) | copy-start | bytes 552964
  110.9 0.7 copy-start.9
  111.6 20.3 %collective-permute-start.20 = (bf16[256,768]{1,0:T(8,128)(2,1)}, bf16[256,768]{1,0:T(8,128)(2,1)}, u32[]{:S(2)}, u32[]{:S(2)}) collective-permute-start(bf16[256,768]{1,0:T(8,128)(2,1)} %get-tuple-element.140), channel_id=1, source_target_pairs={{28,12},{29,13},{30,14},{31,15}} | collective-permute-start | bytes 1179656 | tf_op jit(solution)/shard_map/ppermute | solution.py:830
  113.0 18.9 %collective-permute-start.14 = (bf16[240,384]{1,0:T(8,128)(2,1)}, bf16[240,384]{1,0:T(8,128)(2,1)}, u32[]{:S(2)}, u32[]{:S(2)}) collective-permute-start(bf16[240,384]{1,0:T(8,128)(2,1)} %get-tuple-element.122), channel_id=1, source_target_pairs={{0,3},{1,0},{2,1},{3,2},{4,7},{5,4},{6,5},{7,6},{8,11},{9,8},{10,9... | collective-permute-start | bytes 552968 | tf_op jit(solution)/shard_map/ppermute | solution.py:855
  113.0 18.9 %collective-permute-start.15 = (bf16[240,384]{1,0:T(8,128)(2,1)}, bf16[240,384]{1,0:T(8,128)(2,1)}, u32[]{:S(2)}, u32[]{:S(2)}) collective-permute-start(bf16[240,384]{1,0:T(8,128)(2,1)} %get-tuple-element.123), channel_id=1, source_target_pairs={{0,2},{1,3},{2,0},{3,1},{4,6},{5,7},{6,4},{7,5},{8,10},{9,11},{10,... | collective-permute-start | bytes 552968 | tf_op jit(solution)/shard_map/ppermute | solution.py:855
  113.7 18.3 %collective-permute-start.16 = (bf16[240,384]{1,0:T(8,128)(2,1)}, bf16[240,384]{1,0:T(8,128)(2,1)}, u32[]{:S(2)}, u32[]{:S(2)}) collective-permute-start(bf16[240,384]{1,0:T(8,128)(2,1)} %get-tuple-element.124), channel_id=1, source_target_pairs={{0,1},{1,2},{2,3},{3,0},{4,5},{5,6},{6,7},{7,4},{8,9},{9,10},{10,1... | collective-permute-start | bytes 552968 | tf_op jit(solution)/shard_map/ppermute | solution.py:855
  115.7 1.5 copy-start.5
  117.2 1.1 copy-start.1
  118.3 13.6 %copy-start.10 = (bf16[256,768]{1,0:T(8,128)(2,1)S(1)}, bf16[256,768]{1,0:T(8,128)(2,1)}, u32[]{:S(2)}) copy-start(bf16[256,768]{1,0:T(8,128)(2,1)} %copy-done.9) | copy-start | bytes 1179652
  131.9 1.3 copy-start.20
  131.9 1.4 copy-start.21
  131.9 2.1 %copy-start.19 = (bf16[240,384]{1,0:T(8,128)(2,1)}, bf16[240,384]{1,0:T(8,128)(2,1)S(1)}, u32[]{:S(2)}) copy-start(bf16[240,384]{1,0:T(8,128)(2,1)S(1)} %get-tuple-element.132) | copy-start | bytes 552964
  131.9 20.0 %copy-start.3 = (bf16[1,128,3072]{2,1,0:T(8,128)(2,1)S(1)}, bf16[1,128,3072]{2,1,0:T(8,128)(2,1)}, u32[]{:S(2)}) copy-start(bf16[1,128,3072]{2,1,0:T(8,128)(2,1)} %param.13) | copy-start | bytes 2359300
  132.0 20.0 %copy-start.14 = (bf16[240,384]{1,0:T(8,128)(2,1)S(1)}, bf16[240,384]{1,0:T(8,128)(2,1)}, u32[]{:S(2)}) copy-start(bf16[240,384]{1,0:T(8,128)(2,1)} %copy-done.13) | copy-start | bytes 552964
  132.0 19.9 %copy-start.17 = (f32[128,128]{1,0:T(8,128)S(1)}, f32[128,128]{1,0:T(8,128)}, u32[]{:S(2)}) copy-start(f32[128,128]{1,0:T(8,128)} %copy-done.16) | copy-start | bytes 196612
  133.2 5.1 %collective-permute-start.21 = (bf16[128,768]{1,0:T(8,128)(2,1)S(1)}, bf16[128,768]{1,0:T(8,128)(2,1)S(1)}, u32[]{:S(2)}, u32[]{:S(2)}) collective-permute-start(bf16[128,768]{1,0:T(8,128)(2,1)S(1)} %slice.21), channel_id=1, source_target_pairs={{12,4},{28,20},{13,5},{29,21},{14,6},{30,22},{15,7},{31,23}} | collective-permute-start | bytes 589832 | tf_op jit(solution)/shard_map/ppermute | solution.py:830
  134.0 7.3 %collective-permute-start.17 = (bf16[240,384]{1,0:T(8,128)(2,1)}, bf16[240,384]{1,0:T(8,128)(2,1)S(1)}, u32[]{:S(2)}, u32[]{:S(2)}) collective-permute-start(bf16[240,384]{1,0:T(8,128)(2,1)} %copy-done.21), channel_id=1, source_target_pairs={{0,3},{1,0},{2,1},{3,2},{4,7},{5,4},{6,5},{7,6},{8,11},{9,8},{10,9... | collective-permute-start | bytes 552968 | tf_op jit(solution)/shard_map/ppermute | solution.py:855
  135.8 16.1 %collective-permute-start.18 = (bf16[240,384]{1,0:T(8,128)(2,1)}, bf16[240,384]{1,0:T(8,128)(2,1)S(1)}, u32[]{:S(2)}, u32[]{:S(2)}) collective-permute-start(bf16[240,384]{1,0:T(8,128)(2,1)} %copy-done.20), channel_id=1, source_target_pairs={{0,2},{1,3},{2,0},{3,1},{4,6},{5,7},{6,4},{7,5},{8,10},{9,11},{10,... | collective-permute-start | bytes 552968 | tf_op jit(solution)/shard_map/ppermute | solution.py:855
  136.4 15.5 %collective-permute-start.19 = (bf16[240,384]{1,0:T(8,128)(2,1)}, bf16[240,384]{1,0:T(8,128)(2,1)S(1)}, u32[]{:S(2)}, u32[]{:S(2)}) collective-permute-start(bf16[240,384]{1,0:T(8,128)(2,1)} %copy-done.19), channel_id=1, source_target_pairs={{0,1},{1,2},{2,3},{3,0},{4,5},{5,6},{6,7},{7,4},{8,9},{9,10},{10,1... | collective-permute-start | bytes 552968 | tf_op jit(solution)/shard_map/ppermute | solution.py:855
  138.4 17.4 %collective-permute-start.22 = (bf16[64,768]{1,0:T(8,128)(2,1)S(1)}, bf16[64,768]{1,0:T(8,128)(2,1)S(1)}, u32[]{:S(2)}, u32[]{:S(2)}) collective-permute-start(bf16[64,768]{1,0:T(8,128)(2,1)S(1)} %slice.23), channel_id=1, source_target_pairs={{4,0},{12,8},{20,16},{28,24},{5,1},{13,9},{21,17},{29,25},{6,2},{1... | collective-permute-start | bytes 294920 | tf_op jit(solution)/shard_map/ppermute | solution.py:830

commit v7 on v5

--- a/solution.py
+++ b/solution.py
@@ -17,7 +17,7 @@
 masked_score = -1e30
 F32 = jnp.float32
 BF16 = jnp.bfloat16
-VMEM_LIMIT = 48 * 1024 * 1024
+VMEM_LIMIT = 24 * 1024 * 1024
 
 
 def bucket_onehot(bucket_count):
@@ -101,7 +101,11 @@
 
 
 def block_probs(query_rows, key_rows, bias):
-    scores = dot_nt(query_rows, key_rows) * (HEAD_DIM ** (-0.5)) + bias
+    return score_probs(dot_nt(query_rows, key_rows), bias)
+
+
+def score_probs(products, bias):
+    scores = products * (HEAD_DIM ** (-0.5)) + bias
     weights = jnp.exp(scores - jnp.max(scores, axis=-1, keepdims=True))
     return weights * (1.0 / jnp.sum(weights, axis=-1, keepdims=True))
 
@@ -494,21 +498,23 @@
     value = padded(dot_nn(normed, weight[:, 2 * HEAD_DIM :]).astype(BF16))
     bias = toeplitz(offset_ref[0])
     blocks = tokens // ROW_BLOCK
-    grad_query, grad_key, grad_value, score_sum = [], [], [], None
-    for b in range(blocks):
-        first = b * ROW_BLOCK
-        window = slice(first, first + WINDOW)
-        query_rows = query[first : first + ROW_BLOCK]
-        cot_rows = cot_ref[first : first + ROW_BLOCK]
-        probs = block_probs(query_rows, key[window], edge_bias(bias, first, tokens))
-        grad_probs = dot_nt(cot_rows, value[window])
-        delta = jnp.sum(probs * grad_probs, axis=-1, keepdims=True)
-        grad_scores = probs * (grad_probs - delta)
+    starts = range(0, tokens, ROW_BLOCK)
+    cot = cot_ref[...]
+    query_rows = [query[f : f + ROW_BLOCK] for f in starts]
+    cot_rows = [cot[f : f + ROW_BLOCK] for f in starts]
+    products = [dot_nt(rows_q, key[f : f + WINDOW]) for f, rows_q in zip(starts, query_rows)]
+    grad_probs = [dot_nt(rows_c, value[f : f + WINDOW]) for f, rows_c in zip(starts, cot_rows)]
+    packed, grad_packed, score_sum = [], [], None
+    for f, product, grads in zip(starts, products, grad_probs):
+        probs = score_probs(product, edge_bias(bias, f, tokens))
+        delta = jnp.sum(probs * grads, axis=-1, keepdims=True)
+        grad_scores = probs * (grads - delta)
         score_sum = grad_scores if score_sum is None else score_sum + grad_scores
-        grad_packed = grad_scores.astype(BF16)
-        grad_query.append(dot_nn(grad_packed, key[window]))
-        grad_key.append(dot_tn(grad_packed, query_rows))
-        grad_value.append(dot_tn(probs.astype(BF16), cot_rows))
+        packed.append(probs.astype(BF16))
+        grad_packed.append(grad_scores.astype(BF16))
+    grad_query = [dot_nn(part, key[f : f + WINDOW]) for f, part in zip(starts, grad_packed)]
+    grad_key = [dot_tn(part, rows_q) for part, rows_q in zip(grad_packed, query_rows)]
+    grad_value = [dot_tn(part, rows_c) for part, rows_c in zip(packed, cot_rows)]
 
     def joined(pieces):
         units = []
@@ -609,7 +615,7 @@
     a_refs, i_refs = refs[:parts], refs[parts : 2 * parts]
     gain_ref, offset_ref = refs[2 * parts : 2 * parts + 2]
     out_refs = refs[2 * parts + 2 : 3 * parts + 2]
-    inverse_ref, x_ref, weight_ref, made_ref, square_ref = refs[3 * parts + 2 :]
+    sums_ref, inverse_ref, x_ref, weight_ref, made_ref, square_ref = refs[3 * parts + 2 :]
     tokens = rows * parts
     gather_rows(meta_ref, i_refs, rows, x_ref)
     gather_weight(meta_ref, a_refs, rows, weight_ref)
@@ -620,14 +626,14 @@
     key = padded(dot_nn(normed, weight[:, HEAD_DIM : 2 * HEAD_DIM]).astype(BF16))
     value = padded(dot_nn(normed, weight[:, 2 * HEAD_DIM :]).astype(BF16))
     bias = toeplitz(offset_ref[0])
-    for b in range(tokens // ROW_BLOCK):
-        first = b * ROW_BLOCK
-        window = slice(first, first + WINDOW)
-        probs = block_probs(query[first : first + ROW_BLOCK], key[window], edge_bias(bias, first, tokens))
-        attended = dot_nn(probs.astype(BF16), value[window])
-        made_ref[first : first + ROW_BLOCK] = (
-            x_ref[first : first + ROW_BLOCK].astype(F32) + attended
-        ).astype(BF16)
+    starts = range(0, tokens, ROW_BLOCK)
+    products = [dot_nt(query[f : f + ROW_BLOCK], key[f : f + WINDOW]) for f in starts]
+    packed = [
+        score_probs(product, edge_bias(bias, f, tokens)).astype(BF16) for f, product in zip(starts, products)
+    ]
+    attended = [dot_nn(part, value[f : f + WINDOW]) for f, part in zip(starts, packed)]
+    for f, part in zip(starts, attended):
+        made_ref[f : f + ROW_BLOCK] = (x_ref[f : f + ROW_BLOCK].astype(F32) + part).astype(BF16)
     made = made_ref[...].astype(F32)
     squares = made * made
 
@@ -641,22 +647,12 @@
 
     for r, out_ref in enumerate(out_refs):
         source = lax.rem(meta_ref[0] + parts - r, parts)
-        out_ref[:rows] = made_ref[pl.ds(pl.multiple_of(source * rows, rows), rows)]
+        out_ref[...] = made_ref[pl.ds(pl.multiple_of(source * rows, rows), rows)]
 
     @pl.when(pl.program_id(0) == pl.num_programs(0) - 1)
     def last_head():
         total = jnp.sum(jnp.transpose(square_ref[...]), axis=0, keepdims=True)
-        at_row = lax.broadcasted_iota(jnp.int32, (16, rows), 0)
-        tail = jnp.zeros((16, rows), F32)
-        rest = total
-        for k in range(3):
-            piece = rest.astype(BF16).astype(F32)
-            rest = rest - piece
-            for part in range(parts):
-                row = jnp.broadcast_to(piece[:, part * rows : (part + 1) * rows], (16, rows))
-                tail = jnp.where(at_row == 3 * part + k, row, tail)
-        for out_ref in out_refs:
-            out_ref[rows:] = tail.astype(BF16)
+        sums_ref[...] = jnp.broadcast_to(total, sums_ref.shape)
 
 
 def heads_forward(meta, a_slots, i_slots, gain, offsets, heads, rows):
@@ -667,7 +663,8 @@
     return pl.pallas_call(
         functools.partial(heads_forward_kernel, parts, rows),
         out_shape=(
-            *[jax.ShapeDtypeStruct((rows + 16, width), BF16) for r in range(parts)],
+            *[jax.ShapeDtypeStruct((rows, width), BF16) for r in range(parts)],
+            jax.ShapeDtypeStruct((8, tokens), F32),
         ),
         grid_spec=pltpu.PrefetchScalarGridSpec(
             num_scalar_prefetch=1,
@@ -678,7 +675,10 @@
                 whole_column(1, heads),
                 offset_spec(heads),
             ],
-            out_specs=(head_column(rows + 16),) * parts,
+            out_specs=(
+                *[head_column(rows)] * parts,
+                pl.BlockSpec((8, tokens), lambda i, meta: (0, 0)),
+            ),
             scratch_shapes=[
                 pltpu.VMEM((tokens, HEAD_DIM), F32),
                 pltpu.VMEM((tokens, HEAD_DIM), BF16),
@@ -696,25 +696,19 @@
 
 
 def memory_kernel(parts, width, meta_ref, *refs):
-    out_refs, other_refs = refs[:parts], refs[parts : 2 * parts - 1]
-    gain_ref, *share_refs, memory_ref = refs[2 * parts - 1 :]
+    out_refs, sum_refs = refs[:parts], refs[parts : 2 * parts]
+    gain_ref, after_ref, *share_refs, memory_ref = refs[2 * parts :]
     wide = memory_ref.shape[1]
     rows = memory_ref.shape[0] // parts
-    total = None
-    for ref in (out_refs[0], *other_refs):
-        tail = ref[rows:, wide - rows :].astype(F32)
-        pieces = [
-            tail[3 * p : 3 * p + 1] + tail[3 * p + 1 : 3 * p + 2] + tail[3 * p + 2 : 3 * p + 3]
-            for p in range(parts)
-        ]
-        row = jnp.concatenate(pieces, axis=1)
-        total = row if total is None else total + row
+    total = sum_refs[0][:1]
+    for sum_ref in sum_refs[1:]:
+        total = total + sum_ref[:1]
     inverse = lax.rsqrt(total / width + eps_norm)
     gain = gain_ref[:, pl.ds(pl.multiple_of(meta_ref[0] * wide, 128), wide)]
     spread_inverse = jnp.transpose(jnp.broadcast_to(inverse, (128, inverse.shape[1])))
     for r, out_ref in enumerate(out_refs):
         source = lax.rem(meta_ref[0] + parts - r, parts)
-        memory_ref[pl.ds(pl.multiple_of(source * rows, rows), rows)] = out_ref[:rows]
+        memory_ref[pl.ds(pl.multiple_of(source * rows, rows), rows)] = out_ref[...]
     made = memory_ref[...].astype(F32)
     memory_ref[...] = (made * spread_inverse[:, :1] * gain).astype(BF16)
     for k, share_ref in enumerate(share_refs):
@@ -722,19 +716,19 @@
         share_ref[...] = memory_ref[k * size : (k + 1) * size]
 
 
-def memory_rows(meta, outs, others, gain, width, shares):
+def memory_rows(meta, outs, sums, gain, after, width, shares):
     parts = len(outs)
-    rows, wide = outs[0].shape[0] - 16, outs[0].shape[1]
+    rows, wide = outs[0].shape
     return pl.pallas_call(
         functools.partial(memory_kernel, parts, width),
         out_shape=[jax.ShapeDtypeStruct((rows * parts // shares, wide), BF16)] * shares,
-        in_specs=[SMEM_SPEC] + [VMEM_SPEC] * (2 * parts),
+        in_specs=[SMEM_SPEC] + [VMEM_SPEC] * (2 * parts + 1) + [pl.BlockSpec(memory_space=pl.ANY)],
         out_specs=[VMEM_SPEC] * shares,
         scratch_shapes=[pltpu.VMEM((rows * parts, wide), BF16)],
         compiler_params=pltpu.CompilerParams(vmem_limit_bytes=VMEM_LIMIT),
         cost_estimate=pl.CostEstimate(flops=rows, bytes_accessed=rows, transcendentals=0),
         name="memory_rows",
-    )(meta, *outs, *others, gain)
+    )(meta, *outs, *sums, gain, after)
 
 
 def place_kernel(parts, meta_ref, *refs):
@@ -742,12 +736,12 @@
     wide = refs[0].shape[1]
     for r in range(parts):
         source = lax.rem(meta_ref[0] + r, parts)
-        out_ref[:, pl.ds(pl.multiple_of(source * wide, 128), wide)] = refs[r][: out_ref.shape[0]]
+        out_ref[:, pl.ds(pl.multiple_of(source * wide, 128), wide)] = refs[r][...]
 
 
 def place_columns(meta, slots):
     parts = len(slots)
-    rows, wide = slots[0].shape[0] - 16, slots[0].shape[1]
+    rows, wide = slots[0].shape
     return pl.pallas_call(
         functools.partial(place_kernel, parts),
         out_shape=jax.ShapeDtypeStruct((rows, wide * parts), BF16),
@@ -824,11 +818,6 @@
 
 def spread_memory(shares, section, sections):
     last = sections - 1
-    if len(shares) == sections:
-        memory = jnp.where(section == last, shares[last], 0)
-        for s in range(last):
-            memory = memory + lax.ppermute(shares[s], "section", [(last, s)])
-        return memory
     couple = jnp.where(section == last, shares[-1], 0)
     for s, share in enumerate(shares[:-1]):
         couple = couple + lax.ppermute(share, "section", [(last, 2 * s + 1)])
@@ -859,9 +848,8 @@
 
     inverse_b, *a_sends = pack_stash(meta, stash[0], norm_gain, qkv_weight[0], parts)
     a_slots = exchanged(a_sends, 1)
-    kept, gone, inverse_b = lax.optimization_barrier((carried[0], returned[0], inverse_b))
-    arrived = shifted(kept, "section", 1)
-    came_back = shifted(gone, "section", -1)
+    arrived = shifted(carried[0], "section", 1)
+    came_back = shifted(returned[0], "section", -1)
     i_slots = exchanged(pack_rows(meta, embedded, arrived, parts, True), 1)
     *c_sends, cotangent = pack_rows(meta, loss_grad, came_back, parts, False)
     c_slots = exchanged(c_sends, 1)
@@ -869,30 +857,19 @@
 
     offsets = offset_table(rel_bias[0])
     onehot = jnp.asarray(bucket_onehot(buckets).T)
-    o_sends = heads_forward(meta, a_slots, i_slots, norm_gain, offsets, heads, rows)
+    *o_sends, sums = heads_forward(meta, a_slots, i_slots, norm_gain, offsets, heads, rows)
+    all_sums = exchanged([sums] * parts, 1)
     o_sends, c_slots = lax.optimization_barrier((o_sends, c_slots))
     o_slots = exchanged(o_sends, -1)
 
-    chunks = 2 if heads % 2 == 0 else 1
-    count = heads // chunks
-
-    def backward(c, after):
-        return heads_backward(
-            meta, a_slots, c_slots, norm_gain, offsets, onehot, after, heads, c * count, count
-        )
-
-    *g_sends, gain_grad = backward(0, o_sends[0])
+    *g_sends, gain_grad = heads_backward(
+        meta, a_slots, c_slots, norm_gain, offsets, onehot, o_sends[0], heads, 0, heads
+    )
     g_sends, o_slots = lax.optimization_barrier((g_sends, o_slots))
     g_chunks = [exchanged(g_sends, -1)]
     output = place_columns(meta, o_slots)
-    shares = sections // 2 if sections % 2 == 0 else sections
-    made = memory_rows(meta, o_sends, o_slots[1:], final_gain[None], width, shares)
-    if chunks == 2:
-        *g_sends, gain_part = backward(1, output)
-        g_sends, made, g_chunks = lax.optimization_barrier((g_sends, made, g_chunks))
-        g_chunks.append(exchanged(g_sends, -1))
-        gain_grad = jnp.concatenate([gain_grad, gain_part], axis=1)
-    memory = spread_memory(made, section, sections)
+    shares = memory_rows(meta, o_sends, all_sums, final_gain[None], gain_grad, width, sections // 2)
+    memory = spread_memory(shares, section, sections)
 
     input_grad, weight_grad, bias_wide = heads_finish(
         meta, g_chunks, stash[0], inverse_b, norm_gain, cotangent, buckets
@@ -978,7 +955,9 @@
     parts = lax.axis_size("seq")
     rows, width = embedded.shape
     even = width % (HEAD_DIM * parts) == 0 and HEAD_DIM % (32 * parts) == 0 and rows == 128
-    even = even and rel_bias.shape[1] == 8 * parts and rows * parts % (16 * lax.axis_size("section")) == 0
+    sections = lax.axis_size("section")
+    even = even and sections % 2 == 0
+    even = even and rel_bias.shape[1] == 8 * parts and rows * parts % (16 * sections) == 0
     chosen = heads_body if even else tokens_body
     return chosen(
         embedded, carried, stash, returned, loss_grad, qkv_weight, rel_bias, norm_gain, final_gain

time: 161 us -> 144 us (0.89)
  Pallas kernels: 53.8 us -> 26.8 us
  starting transfers between devices: 50.6 us -> 58 us
  waiting for transfers between devices: 45.1 us -> 47.9 us
    pallas_call x2 -> x1, Pallas kernels: 27.1 us -> 11.2 us  [heads_backward(): pl.pallas_call(functools.partial(heads_backward_kernel, parts, rows), out...]
    pallas_call x1, Pallas kernels: 18.1 us -> 6.92 us  [heads_forward(): pl.pallas_call(functools.partial(heads_forward_kernel, parts, rows), out_...]
    ppermute x18, starting transfers between devices: 41.5 us -> 51 us  [exchanged(): lax.ppermute(sends[r], 'seq', [(i, (i + direction * r) % parts) for i in...]
    ppermute x18, waiting for transfers between devices: 45.1 us -> 47.8 us  [exchanged(): lax.ppermute(sends[r], 'seq', [(i, (i + direction * r) % parts) for i in...]
    ppermute x3, starting transfers between devices: 4.14 us -> 2.02 us  [spread_memory(): couple = couple + lax.ppermute(share, 'section', [(last, 2 * s + 1)])]
    unnamed x30 -> x36, local copies, waits for them, and re-layouts: 6.1 us -> 6.26 us
  transfers between devices with their start and end apart: 24 -> 24, of which waited for: 6 -> 7; matrix products, arithmetic and copies ran while one was open for 2% -> 2% of each run, Pallas kernels for 33% -> 17%
where the time goes in v7:
time: 144 us; the launch traced here: 143 us
  starting transfers between devices  58 us (40%)
  waiting for transfers between devices  47.9 us (33%)
  Pallas kernels  26.8 us (19%)
  local copies, waits for them, and re-layouts  7.64 us (5%)
  other arithmetic  1.69 us (1%)
    ppermute x18, starting transfers between devices, exchanged(): lax.ppermute(sends[r], 'seq', [(i, (i + direction * r) % parts) for i in...  51 us
    ppermute x18, waiting for transfers between devices, exchanged(): lax.ppermute(sends[r], 'seq', [(i, (i + direction * r) % parts) for i in...  47.8 us
    pallas_call x1, Pallas kernels, heads_backward(): pl.pallas_call(functools.partial(heads_backward_kernel, parts, rows), out...  11.2 us
    pallas_call x1, Pallas kernels, heads_forward(): pl.pallas_call(functools.partial(heads_forward_kernel, parts, rows), out_...  6.92 us
    unnamed x36, local copies, waits for them, and re-layouts  6.26 us
    ppermute x2, starting transfers between devices, shifted(): lax.ppermute(value, axis, [(source, source + steps) for source in range(f...  3.7 us
  transfers between devices with their start and end apart: 24, of which 7 were waited for; matrix products, arithmetic and copies ran while one was open for 2% of the time, Pallas kernels for 17%

profile of v7, /device:TPU:0, one launch (start us, length us, event | category | flops | bytes accessed | tf_op | source)
XLA Modules:
  0.0 143.1 jit_solution(15262750502856796086)
XLA Ops:
  0.6 0.0 copy-start
  0.6 2.4 %collective-permute-start.3 = (bf16[128,3072]{1,0:T(8,128)(2,1)}, bf16[128,3072]{1,0:T(8,128)(2,1)S(1)}, u32[]{:S(2)}, u32[]{:S(2)}) collective-permute-start(bf16[128,3072]{1,0:T(8,128)(2,1)} %bitcast.31), channel_id=1, source_target_pairs={{0,4},{4,8},{8,12},{12,16},{16,20},{20,24},{24,28},{1,5},{5,9},{9,... | collective-permute-start | bytes 2359304 | tf_op jit(solution)/shard_map/ppermute | solution.py:816
  3.1 1.3 collective-permute-start.7
  4.4 0.1 pad_add_fusion.meta_ref
  4.5 1.1 copy-done.1
  5.6 1.1 copy-done.5
  6.7 0.7 copy-done.10
  7.4 1.3 pack_stash.1
  8.6 2.5 %collective-permute-start = (bf16[224,768]{1,0:T(8,128)(2,1)S(1)}, bf16[224,768]{1,0:T(8,128)(2,1)S(1)}, u32[]{:S(2)}, u32[]{:S(2)}) collective-permute-start(bf16[224,768]{1,0:T(8,128)(2,1)S(1)} %get-tuple-element.53), channel_id=1, source_target_pairs={{0,1},{1,2},{2,3},{3,0},{4,5},{5,6},{6,7},{7,4},{8,9},{9,10},{10,1... | collective-permute-start | bytes 1032200 | tf_op jit(solution)/shard_map/ppermute | solution.py:844
  11.1 2.6 %collective-permute-start.1 = (bf16[224,768]{1,0:T(8,128)(2,1)S(1)}, bf16[224,768]{1,0:T(8,128)(2,1)S(1)}, u32[]{:S(2)}, u32[]{:S(2)}) collective-permute-start(bf16[224,768]{1,0:T(8,128)(2,1)S(1)} %get-tuple-element.54), channel_id=1, source_target_pairs={{0,2},{1,3},{2,0},{3,1},{4,6},{5,7},{6,4},{7,5},{8,10},{9,11},{10,... | collective-permute-start | bytes 1032200 | tf_op jit(solution)/shard_map/ppermute | solution.py:844
  13.7 1.4 collective-permute-start.2
  15.0 0.9 pack_inbound.1
  16.0 0.0 copy-start.11
  16.0 0.7 collective-permute-start.4
  16.7 0.0 collective-permute-done.7.inner_ref
  16.7 0.3 collective-permute-start.5
  17.1 1.4 pack_cotangent.1
  18.5 2.0 %collective-permute-done.refs_1_ = bf16[224,768]{1,0:T(8,128)(2,1)S(1)} collective-permute-done((bf16[224,768]{1,0:T(8,128)(2,1)S(1)}, bf16[224,768]{1,0:T(8,128)(2,1)S(1)}, u32[]{:S(2)}, u32[]{:S(2)}) %collective-permute-start) | collective-permute-done | bytes 344096 | tf_op jit(solution)/shard_map/ppermute | solution.py:844
  20.5 2.1 %collective-permute-start.6 = (bf16[144,768]{1,0:T(8,128)(2,1)S(1)}, bf16[144,768]{1,0:T(8,128)(2,1)S(1)}, u32[]{:S(2)}, u32[]{:S(2)}) collective-permute-start(bf16[144,768]{1,0:T(8,128)(2,1)S(1)} %get-tuple-element.59), channel_id=1, source_target_pairs={{0,3},{1,0},{2,1},{3,2},{4,7},{5,4},{6,5},{7,6},{8,11},{9,8},{10,9... | collective-permute-start | bytes 663560 | tf_op jit(solution)/shard_map/ppermute | solution.py:844
  22.6 15.8 %collective-permute-done.1.refs_2_ = bf16[224,768]{1,0:T(8,128)(2,1)S(1)} collective-permute-done((bf16[224,768]{1,0:T(8,128)(2,1)S(1)}, bf16[224,768]{1,0:T(8,128)(2,1)S(1)}, u32[]{:S(2)}, u32[]{:S(2)}) %collective-permute-start.1) | collective-permute-done | bytes 344096 | tf_op jit(solution)/shard_map/ppermute | solution.py:844
  38.4 12.8 %collective-permute-start.8 = (bf16[128,768]{1,0:T(8,128)(2,1)S(1)}, bf16[128,768]{1,0:T(8,128)(2,1)S(1)}, u32[]{:S(2)}, u32[]{:S(2)}) collective-permute-start(bf16[128,768]{1,0:T(8,128)(2,1)S(1)} %get-tuple-element.65), channel_id=1, source_target_pairs={{0,1},{1,2},{2,3},{3,0},{4,5},{5,6},{6,7},{7,4},{8,9},{9,10},{10,1... | collective-permute-start | bytes 589832 | tf_op jit(solution)/shard_map/ppermute | solution.py:844
  51.3 3.4 %collective-permute-start.9 = (bf16[128,768]{1,0:T(8,128)(2,1)S(1)}, bf16[128,768]{1,0:T(8,128)(2,1)S(1)}, u32[]{:S(2)}, u32[]{:S(2)}) collective-permute-start(bf16[128,768]{1,0:T(8,128)(2,1)S(1)} %get-tuple-element.66), channel_id=1, source_target_pairs={{0,2},{1,3},{2,0},{3,1},{4,6},{5,7},{6,4},{7,5},{8,10},{9,11},{10,... | collective-permute-start | bytes 589832 | tf_op jit(solution)/shard_map/ppermute | solution.py:844
  54.7 0.0 collective-permute-done.4.refs_5_
  54.7 1.9 %collective-permute-start.10 = (bf16[128,768]{1,0:T(8,128)(2,1)S(1)}, bf16[128,768]{1,0:T(8,128)(2,1)S(1)}, u32[]{:S(2)}, u32[]{:S(2)}) collective-permute-start(bf16[128,768]{1,0:T(8,128)(2,1)S(1)} %get-tuple-element.67), channel_id=1, source_target_pairs={{0,3},{1,0},{2,1},{3,2},{4,7},{5,4},{6,5},{7,6},{8,11},{9,8},{10,9... | collective-permute-start | bytes 589832 | tf_op jit(solution)/shard_map/ppermute | solution.py:844
  56.5 0.2 fusion
  56.8 0.0 copy-start.14
  56.8 10.0 %collective-permute-done.5.refs_6_ = bf16[144,768]{1,0:T(8,128)(2,1)S(1)} collective-permute-done((bf16[144,768]{1,0:T(8,128)(2,1)S(1)}, bf16[144,768]{1,0:T(8,128)(2,1)S(1)}, u32[]{:S(2)}, u32[]{:S(2)}) %collective-permute-start.5) | collective-permute-done | bytes 221216 | tf_op jit(solution)/shard_map/ppermute | solution.py:844
  66.8 6.9 %heads_forward.1 = (bf16[128,768]{1,0:T(8,128)(2,1)S(1)}, bf16[128,768]{1,0:T(8,128)(2,1)S(1)}, bf16[128,768]{1,0:T(8,128)(2,1)S(1)}, bf16[128,768]{1,0:T(8,128)(2,1)S(1)}, f32[8,512]{1,0:T(8,128)S(1)}) custom-call(s32[3]{0:T(128)S(1)} %pad_add_fusion.meta_ref, bf16[224,768]{1,0:T(8,128)(2,1)S(1)} %get-tuple-element.52.refs_0_, ...), custom_call_target="tpu_custom_call" | custom-call | flops 3072 | bytes 512 | tf_op jit(solution)/shard_map/heads_forward/pallas_call | solution.py:663
  73.7 2.0 %collective-permute-done.9.refs_6_ = bf16[128,768]{1,0:T(8,128)(2,1)S(1)} collective-permute-done((bf16[128,768]{1,0:T(8,128)(2,1)S(1)}, bf16[128,768]{1,0:T(8,128)(2,1)S(1)}, u32[]{:S(2)}, u32[]{:S(2)}) %collective-permute-start.9) | collective-permute-done | bytes 196640 | tf_op jit(solution)/shard_map/ppermute | solution.py:844
  75.7 4.7 %collective-permute-start.11 = (bf16[128,768]{1,0:T(8,128)(2,1)S(1)}, bf16[128,768]{1,0:T(8,128)(2,1)S(1)}, u32[]{:S(2)}, u32[]{:S(2)}) collective-permute-start(bf16[128,768]{1,0:T(8,128)(2,1)S(1)} %get-tuple-element.77.refs_1_), channel_id=1, source_target_pairs={{0,3},{1,0},{2,1},{3,2},{4,7},{5,4},{6,5},{7,6},{8,11},{9,8},{10,9... | collective-permute-start | bytes 589832 | tf_op jit(solution)/shard_map/ppermute | solution.py:844
  80.4 0.5 collective-permute-start.19
  80.9 1.1 collective-permute-start.18
  82.0 2.0 %collective-permute-start.17 = (f32[8,512]{1,0:T(8,128)S(1)}, f32[8,512]{1,0:T(8,128)S(1)}, u32[]{:S(2)}, u32[]{:S(2)}) collective-permute-start(f32[8,512]{1,0:T(8,128)S(1)} %get-tuple-element.93.refs_4_), channel_id=1, source_target_pairs={{0,1},{1,2},{2,3},{3,0},{4,5},{5,6},{6,7},{7,4},{8,9},{9,10},{10,1... | collective-permute-start | bytes 49160 | tf_op jit(solution)/shard_map/ppermute | solution.py:844
  84.0 1.4 collective-permute-start.12
  85.4 0.7 collective-permute-done.19.refs_7_
  86.0 11.7 %collective-permute-start.13 = (bf16[128,768]{1,0:T(8,128)(2,1)S(1)}, bf16[128,768]{1,0:T(8,128)(2,1)S(1)}, u32[]{:S(2)}, u32[]{:S(2)}) collective-permute-start(bf16[128,768]{1,0:T(8,128)(2,1)S(1)} %get-tuple-element.79.refs_3_), channel_id=1, source_target_pairs={{0,1},{1,2},{2,3},{3,0},{4,5},{5,6},{6,7},{7,4},{8,9},{9,10},{10,1... | collective-permute-start | bytes 589832 | tf_op jit(solution)/shard_map/ppermute | solution.py:844
  97.7 11.2 %heads_backward.1 = (bf16[240,768]{1,0:T(8,128)(2,1)S(1)}, bf16[240,768]{1,0:T(8,128)(2,1)}, bf16[240,768]{1,0:T(8,128)(2,1)}, bf16[240,768]{1,0:T(8,128)(2,1)}, f32[1,768]{1,0:T(1,128)}) custom-call(s32[3]{0:T(128)S(1)} %pad_add_fusion.meta_ref, bf16[224,768]{1,0:T(8,128)(2,1)S(1)} %get-tuple-element.52.refs_0_, ...), custom_call_target="tpu_custom_call" | custom-call | flops 1228800000 | bytes 393216 | tf_op jit(solution)/shard_map/heads_backward/pallas_call | solution.py:578
  109.0 0.0 collective-permute-done.18.refs_6_
  109.0 0.0 collective-permute-done.17.refs_5_
  109.0 0.0 copy-start.13
  109.0 0.7 copy-done.13
  109.7 0.9 memory_rows.1
  110.6 0.7 collective-permute-start.20
  111.3 0.7 collective-permute-start.21
  112.0 0.0 collective-permute-done.11.refs_1_
  112.0 0.7 collective-permute-start.22
  112.7 0.0 copy-start.6
  112.7 0.7 copy-done.8
  113.4 1.5 %collective-permute-start.15 = (bf16[240,768]{1,0:T(8,128)(2,1)}, bf16[240,768]{1,0:T(8,128)(2,1)S(1)}, u32[]{:S(2)}, u32[]{:S(2)}) collective-permute-start(bf16[240,768]{1,0:T(8,128)(2,1)} %get-tuple-element.86), channel_id=1, source_target_pairs={{0,2},{1,3},{2,0},{3,1},{4,6},{5,7},{6,4},{7,5},{8,10},{9,11},{10,... | collective-permute-start | bytes 1105928 | tf_op jit(solution)/shard_map/ppermute | solution.py:844
  114.9 0.6 collective-permute-start.16
  115.4 0.1 add_add_fusion
  115.5 0.0 copy-start.2
  115.5 0.6 slice.12
  116.2 0.1 copy-done.15
  116.2 1.3 collective-permute-start.23
  117.5 0.0 copy-start.7
  117.5 0.9 copy-done.7
  118.5 0.9 copy-done.9
  119.4 1.5 %place_columns.1 = bf16[128,3072]{1,0:T(8,128)(2,1)} custom-call(s32[3]{0:T(128)S(1)} %pad_add_fusion.meta_ref, bf16[128,768]{1,0:T(8,128)(2,1)S(1)} %get-tuple-element.80.refs_11_.refs_0_, bf16[128,768]{1,0:T(8,128)(2,1)S(1)} %collective-permute-done.11.refs_1_, bf16[128,768]{1,0:T(8,128)(2,1)S(1)} %copy-done.7, bf16[128,768]{1,0:T(8,128)(2,1)S(1)} %copy-done.9), custom_call_target="tpu_custom_call" | custom-call | bytes 128 | tf_op jit(solution)/shard_map/place_columns/pallas_call | solution.py:745
  120.9 1.5 %slice_select_fusion = bf16[64,768]{1,0:T(8,128)(2,1)} fusion(bf16[64,768]{1,0:T(8,128)(2,1)} %collective-permute-done.23, bf16[128,768]{1,0:T(8,128)(2,1)S(1)} %copy-done.16, pred[]{:T(512)S(6)} %eq.14), kind=kLoop, calls=%fused_computation.3 | loop fusion | flops 49152 | bytes 294913 | tf_op jit(solution)/shard_map/jit(_where)/select_n | solution.py:826
  122.4 4.0 %collective-permute-done.14.refs_1_ = bf16[240,768]{1,0:T(8,128)(2,1)S(1)} collective-permute-done((bf16[240,768]{1,0:T(8,128)(2,1)}, bf16[240,768]{1,0:T(8,128)(2,1)S(1)}, u32[]{:S(2)}, u32[]{:S(2)}) %collective-permute-start.14) | collective-permute-done | bytes 368672 | tf_op jit(solution)/shard_map/ppermute | solution.py:844
  126.5 13.3 %collective-permute-done.15.refs_2_ = bf16[240,768]{1,0:T(8,128)(2,1)S(1)} collective-permute-done((bf16[240,768]{1,0:T(8,128)(2,1)}, bf16[240,768]{1,0:T(8,128)(2,1)S(1)}, u32[]{:S(2)}, u32[]{:S(2)}) %collective-permute-start.15) | collective-permute-done | bytes 368672 | tf_op jit(solution)/shard_map/ppermute | solution.py:844
  139.8 2.6 %heads_finish.1 = (bf16[128,3072]{1,0:T(8,128)(2,1)}, f32[3,24,32,128]{3,2,1,0:T(8,128)}, f32[24,8,128]{2,1,0:T(8,128)S(1)}) custom-call(s32[3]{0:T(128)S(1)} %pad_add_fusion.meta_ref, bf16[240,768]{1,0:T(8,128)(2,1)S(1)} %get-tuple-element.84.refs_0_, bf16[240,768]{1,0:T(8,128)(2,1)S(1)} %collective-permute-done.14.refs_1_, ...), custom_call_target="tpu_custom_call" | custom-call | flops 4718592 | bytes 5505024 | tf_op jit(solution)/shard_map/heads_finish/pallas_call | solution.py:790
  142.4 0.7 copy.18
  (36 shorter events, 0.1 us)
Async XLA Ops:
  0.6 55.9 %copy-start = (f32[1,32,24]{1,2,0:T(8,128)S(1)}, f32[1,32,24]{1,2,0:T(8,128)}, u32[]{:S(2)}) copy-start(f32[1,32,24]{1,2,0:T(8,128)} %param.17) | copy-start | bytes 9220
  0.6 14.4 %collective-permute-start.3 = (bf16[128,3072]{1,0:T(8,128)(2,1)}, bf16[128,3072]{1,0:T(8,128)(2,1)S(1)}, u32[]{:S(2)}, u32[]{:S(2)}) collective-permute-start(bf16[128,3072]{1,0:T(8,128)(2,1)} %bitcast.31), channel_id=1, source_target_pairs={{0,4},{4,8},{8,12},{12,16},{16,20},{20,24},{24,28},{1,5},{5,9},{9,... | collective-permute-start | bytes 2359304 | tf_op jit(solution)/shard_map/ppermute | solution.py:816
  3.1 13.7 %collective-permute-start.7 = (bf16[128,3072]{1,0:T(8,128)(2,1)}, bf16[128,3072]{1,0:T(8,128)(2,1)S(1)}, u32[]{:S(2)}, u32[]{:S(2)}) collective-permute-start(bf16[128,3072]{1,0:T(8,128)(2,1)} %bitcast.32), channel_id=1, source_target_pairs={{4,0},{8,4},{12,8},{16,12},{20,16},{24,20},{28,24},{5,1},{9,5},{13... | collective-permute-start | bytes 2359304 | tf_op jit(solution)/shard_map/ppermute | solution.py:816
  4.4 1.1 copy-start.1
  5.6 1.1 copy-start.5
  6.6 0.7 copy-start.10
  7.4 7.7 %copy-start.3 = (bf16[128,3072]{1,0:T(8,128)(2,1)S(1)}, bf16[128,3072]{1,0:T(8,128)(2,1)}, u32[]{:S(2)}) copy-start(bf16[128,3072]{1,0:T(8,128)(2,1)} %edge_ref.2) | copy-start | bytes 2359300
  7.4 9.7 %copy-start.4 = (bf16[128,3072]{1,0:T(8,128)(2,1)S(1)}, bf16[128,3072]{1,0:T(8,128)(2,1)}, u32[]{:S(2)}) copy-start(bf16[128,3072]{1,0:T(8,128)(2,1)} %edge_ref.3) | copy-start | bytes 2359300
  8.6 11.9 %collective-permute-start = (bf16[224,768]{1,0:T(8,128)(2,1)S(1)}, bf16[224,768]{1,0:T(8,128)(2,1)S(1)}, u32[]{:S(2)}, u32[]{:S(2)}) collective-permute-start(bf16[224,768]{1,0:T(8,128)(2,1)S(1)} %get-tuple-element.53), channel_id=1, source_target_pairs={{0,1},{1,2},{2,3},{3,0},{4,5},{5,6},{6,7},{7,4},{8,9},{9,10},{10,1... | collective-permute-start | bytes 1032200 | tf_op jit(solution)/shard_map/ppermute | solution.py:844
  11.1 27.4 %collective-permute-start.1 = (bf16[224,768]{1,0:T(8,128)(2,1)S(1)}, bf16[224,768]{1,0:T(8,128)(2,1)S(1)}, u32[]{:S(2)}, u32[]{:S(2)}) collective-permute-start(bf16[224,768]{1,0:T(8,128)(2,1)S(1)} %get-tuple-element.54), channel_id=1, source_target_pairs={{0,2},{1,3},{2,0},{3,1},{4,6},{5,7},{6,4},{7,5},{8,10},{9,11},{10,... | collective-permute-start | bytes 1032200 | tf_op jit(solution)/shard_map/ppermute | solution.py:844
  13.7 37.6 %collective-permute-start.2 = (bf16[224,768]{1,0:T(8,128)(2,1)S(1)}, bf16[224,768]{1,0:T(8,128)(2,1)S(1)}, u32[]{:S(2)}, u32[]{:S(2)}) collective-permute-start(bf16[224,768]{1,0:T(8,128)(2,1)S(1)} %get-tuple-element.55), channel_id=1, source_target_pairs={{0,3},{1,0},{2,1},{3,2},{4,7},{5,4},{6,5},{7,6},{8,11},{9,8},{10,9... | collective-permute-start | bytes 1032200 | tf_op jit(solution)/shard_map/ppermute | solution.py:844
  16.0 40.6 %copy-start.17 = (f32[256,32]{1,0:T(8,128)S(1)}, f32[256,32]{1,0:T(8,128)}, u32[]{:S(2)}) copy-start(f32[256,32]{1,0:T(8,128)} %constant.35.clone) | copy-start | bytes 98308
  16.0 50.8 %copy-start.11 = (f32[1,3072]{1,0:T(1,128)S(1)}, f32[1,3072]{1,0:T(1,128)}, u32[]{:S(2)}) copy-start(f32[1,3072]{1,0:T(1,128)} %refs_6_.1) | copy-start | bytes 36868
  16.0 38.7 %collective-permute-start.4 = (bf16[144,768]{1,0:T(8,128)(2,1)S(1)}, bf16[144,768]{1,0:T(8,128)(2,1)S(1)}, u32[]{:S(2)}, u32[]{:S(2)}) collective-permute-start(bf16[144,768]{1,0:T(8,128)(2,1)S(1)} %get-tuple-element.57), channel_id=1, source_target_pairs={{0,1},{1,2},{2,3},{3,0},{4,5},{5,6},{6,7},{7,4},{8,9},{9,10},{10,1... | collective-permute-start | bytes 663560 | tf_op jit(solution)/shard_map/ppermute | solution.py:844
  16.7 50.0 %collective-permute-start.5 = (bf16[144,768]{1,0:T(8,128)(2,1)S(1)}, bf16[144,768]{1,0:T(8,128)(2,1)S(1)}, u32[]{:S(2)}, u32[]{:S(2)}) collective-permute-start(bf16[144,768]{1,0:T(8,128)(2,1)S(1)} %get-tuple-element.58), channel_id=1, source_target_pairs={{0,2},{1,3},{2,0},{3,1},{4,6},{5,7},{6,4},{7,5},{8,10},{9,11},{10,... | collective-permute-start | bytes 663560 | tf_op jit(solution)/shard_map/ppermute | solution.py:844
  20.5 46.3 %collective-permute-start.6 = (bf16[144,768]{1,0:T(8,128)(2,1)S(1)}, bf16[144,768]{1,0:T(8,128)(2,1)S(1)}, u32[]{:S(2)}, u32[]{:S(2)}) collective-permute-start(bf16[144,768]{1,0:T(8,128)(2,1)S(1)} %get-tuple-element.59), channel_id=1, source_target_pairs={{0,3},{1,0},{2,1},{3,2},{4,7},{5,4},{6,5},{7,6},{8,11},{9,8},{10,9... | collective-permute-start | bytes 663560 | tf_op jit(solution)/shard_map/ppermute | solution.py:844
  38.4 35.3 %collective-permute-start.8 = (bf16[128,768]{1,0:T(8,128)(2,1)S(1)}, bf16[128,768]{1,0:T(8,128)(2,1)S(1)}, u32[]{:S(2)}, u32[]{:S(2)}) collective-permute-start(bf16[128,768]{1,0:T(8,128)(2,1)S(1)} %get-tuple-element.65), channel_id=1, source_target_pairs={{0,1},{1,2},{2,3},{3,0},{4,5},{5,6},{6,7},{7,4},{8,9},{9,10},{10,1... | collective-permute-start | bytes 589832 | tf_op jit(solution)/shard_map/ppermute | solution.py:844
  51.3 24.4 %collective-permute-start.9 = (bf16[128,768]{1,0:T(8,128)(2,1)S(1)}, bf16[128,768]{1,0:T(8,128)(2,1)S(1)}, u32[]{:S(2)}, u32[]{:S(2)}) collective-permute-start(bf16[128,768]{1,0:T(8,128)(2,1)S(1)} %get-tuple-element.66), channel_id=1, source_target_pairs={{0,2},{1,3},{2,0},{3,1},{4,6},{5,7},{6,4},{7,5},{8,10},{9,11},{10,... | collective-permute-start | bytes 589832 | tf_op jit(solution)/shard_map/ppermute | solution.py:844
  54.7 21.1 %collective-permute-start.10 = (bf16[128,768]{1,0:T(8,128)(2,1)S(1)}, bf16[128,768]{1,0:T(8,128)(2,1)S(1)}, u32[]{:S(2)}, u32[]{:S(2)}) collective-permute-start(bf16[128,768]{1,0:T(8,128)(2,1)S(1)} %get-tuple-element.67), channel_id=1, source_target_pairs={{0,3},{1,0},{2,1},{3,2},{4,7},{5,4},{6,5},{7,6},{8,11},{9,8},{10,9... | collective-permute-start | bytes 589832 | tf_op jit(solution)/shard_map/ppermute | solution.py:844
  56.8 41.0 %copy-start.14 = (f32[32,256]{1,0:T(8,128)S(1)}, f32[32,256]{1,0:T(8,128)}, u32[]{:S(2)}) copy-start(f32[32,256]{1,0:T(8,128)} %constant.36.clone.refs_10_) | copy-start | bytes 98308
  75.7 36.2 %collective-permute-start.11 = (bf16[128,768]{1,0:T(8,128)(2,1)S(1)}, bf16[128,768]{1,0:T(8,128)(2,1)S(1)}, u32[]{:S(2)}, u32[]{:S(2)}) collective-permute-start(bf16[128,768]{1,0:T(8,128)(2,1)S(1)} %get-tuple-element.77.refs_1_), channel_id=1, source_target_pairs={{0,3},{1,0},{2,1},{3,2},{4,7},{5,4},{6,5},{7,6},{8,11},{9,8},{10,9... | collective-permute-start | bytes 589832 | tf_op jit(solution)/shard_map/ppermute | solution.py:844
  80.4 28.6 %copy-start.12 = (f32[3072]{0:T(1024)S(1)}, f32[3072]{0:T(1024)}, u32[]{:S(2)}) copy-start(f32[3072]{0:T(1024)} %param.19) | copy-start | bytes 36868
  80.4 5.6 %collective-permute-start.19 = (f32[8,512]{1,0:T(8,128)S(1)}, f32[8,512]{1,0:T(8,128)S(1)}, u32[]{:S(2)}, u32[]{:S(2)}) collective-permute-start(f32[8,512]{1,0:T(8,128)S(1)} %get-tuple-element.93.refs_4_), channel_id=1, source_target_pairs={{0,3},{1,0},{2,1},{3,2},{4,7},{5,4},{6,5},{7,6},{8,11},{9,8},{10,9... | collective-permute-start | bytes 49160 | tf_op jit(solution)/shard_map/ppermute | solution.py:844
  80.9 28.0 %collective-permute-start.18 = (f32[8,512]{1,0:T(8,128)S(1)}, f32[8,512]{1,0:T(8,128)S(1)}, u32[]{:S(2)}, u32[]{:S(2)}) collective-permute-start(f32[8,512]{1,0:T(8,128)S(1)} %get-tuple-element.93.refs_4_), channel_id=1, source_target_pairs={{0,2},{1,3},{2,0},{3,1},{4,6},{5,7},{6,4},{7,5},{8,10},{9,11},{10,... | collective-permute-start | bytes 49160 | tf_op jit(solution)/shard_map/ppermute | solution.py:844
  82.0 27.0 %collective-permute-start.17 = (f32[8,512]{1,0:T(8,128)S(1)}, f32[8,512]{1,0:T(8,128)S(1)}, u32[]{:S(2)}, u32[]{:S(2)}) collective-permute-start(f32[8,512]{1,0:T(8,128)S(1)} %get-tuple-element.93.refs_4_), channel_id=1, source_target_pairs={{0,1},{1,2},{2,3},{3,0},{4,5},{5,6},{6,7},{7,4},{8,9},{9,10},{10,1... | collective-permute-start | bytes 49160 | tf_op jit(solution)/shard_map/ppermute | solution.py:844
  84.0 28.7 %collective-permute-start.12 = (bf16[128,768]{1,0:T(8,128)(2,1)S(1)}, bf16[128,768]{1,0:T(8,128)(2,1)S(1)}, u32[]{:S(2)}, u32[]{:S(2)}) collective-permute-start(bf16[128,768]{1,0:T(8,128)(2,1)S(1)} %get-tuple-element.78.refs_2_), channel_id=1, source_target_pairs={{0,2},{1,3},{2,0},{3,1},{4,6},{5,7},{6,4},{7,5},{8,10},{9,11},{10,... | collective-permute-start | bytes 589832 | tf_op jit(solution)/shard_map/ppermute | solution.py:844
  86.0 26.6 %collective-permute-start.13 = (bf16[128,768]{1,0:T(8,128)(2,1)S(1)}, bf16[128,768]{1,0:T(8,128)(2,1)S(1)}, u32[]{:S(2)}, u32[]{:S(2)}) collective-permute-start(bf16[128,768]{1,0:T(8,128)(2,1)S(1)} %get-tuple-element.79.refs_3_), channel_id=1, source_target_pairs={{0,1},{1,2},{2,3},{3,0},{4,5},{5,6},{6,7},{7,4},{8,9},{9,10},{10,1... | collective-permute-start | bytes 589832 | tf_op jit(solution)/shard_map/ppermute | solution.py:844
  109.0 0.7 copy-start.13
  110.6 4.3 %collective-permute-start.20 = (bf16[128,768]{1,0:T(8,128)(2,1)S(1)}, bf16[128,768]{1,0:T(8,128)(2,1)S(1)}, u32[]{:S(2)}, u32[]{:S(2)}) collective-permute-start(bf16[128,768]{1,0:T(8,128)(2,1)S(1)} %get-tuple-element.95), channel_id=1, source_target_pairs={{28,4},{29,5},{30,6},{31,7}} | collective-permute-start | bytes 589832 | tf_op jit(solution)/shard_map/ppermute | solution.py:823
  111.3 4.2 %collective-permute-start.21 = (bf16[128,768]{1,0:T(8,128)(2,1)S(1)}, bf16[128,768]{1,0:T(8,128)(2,1)S(1)}, u32[]{:S(2)}, u32[]{:S(2)}) collective-permute-start(bf16[128,768]{1,0:T(8,128)(2,1)S(1)} %get-tuple-element.96), channel_id=1, source_target_pairs={{28,12},{29,13},{30,14},{31,15}} | collective-permute-start | bytes 589832 | tf_op jit(solution)/shard_map/ppermute | solution.py:823
  112.0 3.5 %collective-permute-start.22 = (bf16[128,768]{1,0:T(8,128)(2,1)S(1)}, bf16[128,768]{1,0:T(8,128)(2,1)S(1)}, u32[]{:S(2)}, u32[]{:S(2)}) collective-permute-start(bf16[128,768]{1,0:T(8,128)(2,1)S(1)} %get-tuple-element.97), channel_id=1, source_target_pairs={{28,20},{29,21},{30,22},{31,23}} | collective-permute-start | bytes 589832 | tf_op jit(solution)/shard_map/ppermute | solution.py:823
  112.7 2.8 %copy-start.6 = (bf16[128,768]{1,0:T(8,128)(2,1)}, bf16[128,768]{1,0:T(8,128)(2,1)S(1)}, u32[]{:S(2)}) copy-start(bf16[128,768]{1,0:T(8,128)(2,1)S(1)} %collective-permute-done.12.refs_2_) | copy-start | bytes 589828
  112.7 0.7 copy-start.8
  113.4 13.1 %collective-permute-start.14 = (bf16[240,768]{1,0:T(8,128)(2,1)}, bf16[240,768]{1,0:T(8,128)(2,1)S(1)}, u32[]{:S(2)}, u32[]{:S(2)}) collective-permute-start(bf16[240,768]{1,0:T(8,128)(2,1)} %get-tuple-element.85), channel_id=1, source_target_pairs={{0,3},{1,0},{2,1},{3,2},{4,7},{5,4},{6,5},{7,6},{8,11},{9,8},{10,9... | collective-permute-start | bytes 1105928 | tf_op jit(solution)/shard_map/ppermute | solution.py:844
  113.4 26.4 %collective-permute-start.15 = (bf16[240,768]{1,0:T(8,128)(2,1)}, bf16[240,768]{1,0:T(8,128)(2,1)S(1)}, u32[]{:S(2)}, u32[]{:S(2)}) collective-permute-start(bf16[240,768]{1,0:T(8,128)(2,1)} %get-tuple-element.86), channel_id=1, source_target_pairs={{0,2},{1,3},{2,0},{3,1},{4,6},{5,7},{6,4},{7,5},{8,10},{9,11},{10,... | collective-permute-start | bytes 1105928 | tf_op jit(solution)/shard_map/ppermute | solution.py:844
  114.9 24.9 %collective-permute-start.16 = (bf16[240,768]{1,0:T(8,128)(2,1)}, bf16[240,768]{1,0:T(8,128)(2,1)S(1)}, u32[]{:S(2)}, u32[]{:S(2)}) collective-permute-start(bf16[240,768]{1,0:T(8,128)(2,1)} %get-tuple-element.87), channel_id=1, source_target_pairs={{0,1},{1,2},{2,3},{3,0},{4,5},{5,6},{6,7},{7,4},{8,9},{9,10},{10,1... | collective-permute-start | bytes 1105928 | tf_op jit(solution)/shard_map/ppermute | solution.py:844
  115.5 0.7 copy-start.15
  115.5 24.3 %copy-start.2 = (bf16[1,128,3072]{2,1,0:T(8,128)(2,1)S(1)}, bf16[1,128,3072]{2,1,0:T(8,128)(2,1)}, u32[]{:S(2)}) copy-start(bf16[1,128,3072]{2,1,0:T(8,128)(2,1)} %param.13) | copy-start | bytes 2359300
  116.2 4.7 %collective-permute-start.23 = (bf16[64,768]{1,0:T(8,128)(2,1)}, bf16[64,768]{1,0:T(8,128)(2,1)}, u32[]{:S(2)}, u32[]{:S(2)}) collective-permute-start(bf16[64,768]{1,0:T(8,128)(2,1)} %slice.12), channel_id=1, source_target_pairs={{4,0},{12,8},{20,16},{28,24},{5,1},{13,9},{21,17},{29,25},{6,2},{1... | collective-permute-start | bytes 294920 | tf_op jit(solution)/shard_map/ppermute | solution.py:825
  117.5 0.9 copy-start.7
  118.5 0.9 copy-start.9
  119.4 1.5 %copy-start.16 = (bf16[128,768]{1,0:T(8,128)(2,1)S(1)}, bf16[128,768]{1,0:T(8,128)(2,1)}, u32[]{:S(2)}) copy-start(bf16[128,768]{1,0:T(8,128)(2,1)} %copy-done.15) | copy-start | bytes 589828

commit v8 on v7

--- a/solution.py
+++ b/solution.py
@@ -340,19 +340,39 @@
     return lax.rsqrt(jnp.mean(x * x, axis=-1, keepdims=True) + eps_norm)
 
 
-def pack_stash_kernel(parts, meta_ref, x_ref, gain_ref, weight_ref, inverse_ref, *refs):
-    out_refs, normed_ref = refs[:parts], refs[parts]
+def pack_stash_kernel(parts, pieces, meta_ref, x_hbm, gain_hbm, weight_hbm, inverse_ref, *refs):
+    out_refs = refs[:parts]
+    x_ref, gain_ref, weight_ref, normed_ref, sems = refs[parts:]
     rows, width = x_ref.shape
     depth = weight_ref.shape[2]
     wide = width // parts
     heads = wide // HEAD_DIM
-    inverse = row_inverse(x_ref[...])
-    inverse_ref[...] = jnp.broadcast_to(inverse, inverse_ref.shape)
-    normed_ref[...] = (x_ref[...].astype(F32) * inverse * gain_ref[...]).astype(BF16)
+    step = rows // pieces
+    gain_copy = pltpu.make_async_copy(gain_hbm, gain_ref, sems.at[0])
+    x_copies = [
+        pltpu.make_async_copy(x_hbm.at[pl.ds(k * step, step)], x_ref.at[pl.ds(k * step, step)], sems.at[1 + k])
+        for k in range(pieces)
+    ]
+    weight_copies = [
+        pltpu.make_async_copy(weight_hbm.at[j], weight_ref.at[j], sems.at[1 + pieces + j]) for j in range(3)
+    ]
+    for copy in (gain_copy, *x_copies, *weight_copies):
+        copy.start()
+    gain_copy.wait()
+    gain = gain_ref[...]
+    for k, copy in enumerate(x_copies):
+        copy.wait()
+        part = slice(k * step, (k + 1) * step)
+        inverse = row_inverse(x_ref[part])
+        inverse_ref[part] = jnp.broadcast_to(inverse, (step, 128))
+        normed_ref[part] = (x_ref[part].astype(F32) * inverse * gain).astype(BF16)
     for r, out_ref in enumerate(out_refs):
         target = lax.rem(meta_ref[0] + r, parts)
         out_ref[:rows] = normed_ref[:, pl.ds(pl.multiple_of(target * wide, 128), wide)]
-        for j in range(3):
+    for j, copy in enumerate(weight_copies):
+        copy.wait()
+        for r, out_ref in enumerate(out_refs):
+            target = lax.rem(meta_ref[0] + r, parts)
             for h in range(heads):
                 out_ref[rows + j * depth : rows + (j + 1) * depth, h * HEAD_DIM : (h + 1) * HEAD_DIM] = weight_ref[
                     j, target * heads + h
@@ -403,14 +423,20 @@
     depth = weight.shape[2]
     shape = (rows + 3 * depth, width // parts)
     return pl.pallas_call(
-        functools.partial(pack_stash_kernel, parts),
+        functools.partial(pack_stash_kernel, parts, 4),
         out_shape=(
             jax.ShapeDtypeStruct((rows, 128), F32),
             *[jax.ShapeDtypeStruct(shape, BF16) for r in range(parts)],
         ),
-        in_specs=[SMEM_SPEC, VMEM_SPEC, VMEM_SPEC, VMEM_SPEC],
+        in_specs=[SMEM_SPEC] + [pl.BlockSpec(memory_space=pl.ANY)] * 3,
         out_specs=(VMEM_SPEC,) * (parts + 1),
-        scratch_shapes=[pltpu.VMEM((rows, width), BF16)],
+        scratch_shapes=[
+            pltpu.VMEM((rows, width), BF16),
+            pltpu.VMEM((1, width), F32),
+            pltpu.VMEM(weight.shape, BF16),
+            pltpu.VMEM((rows, width), BF16),
+            pltpu.SemaphoreType.DMA((8,)),
+        ],
         compiler_params=pltpu.CompilerParams(vmem_limit_bytes=VMEM_LIMIT),
         cost_estimate=pl.CostEstimate(flops=4 * rows * width, bytes_accessed=6 * rows * width, transcendentals=0),
         name="pack_stash",
@@ -615,7 +641,7 @@
     a_refs, i_refs = refs[:parts], refs[parts : 2 * parts]
     gain_ref, offset_ref = refs[2 * parts : 2 * parts + 2]
     out_refs = refs[2 * parts + 2 : 3 * parts + 2]
-    sums_ref, inverse_ref, x_ref, weight_ref, made_ref, square_ref = refs[3 * parts + 2 :]
+    inverse_ref, x_ref, weight_ref, made_ref, square_ref = refs[3 * parts + 2 :]
     tokens = rows * parts
     gather_rows(meta_ref, i_refs, rows, x_ref)
     gather_weight(meta_ref, a_refs, rows, weight_ref)
@@ -647,12 +673,26 @@
 
     for r, out_ref in enumerate(out_refs):
         source = lax.rem(meta_ref[0] + parts - r, parts)
-        out_ref[...] = made_ref[pl.ds(pl.multiple_of(source * rows, rows), rows)]
+        out_ref[:rows] = made_ref[pl.ds(pl.multiple_of(source * rows, rows), rows)]
+
+    @pl.when(pl.program_id(0) < pl.num_programs(0) - 1)
+    def no_sums():
+        for out_ref in out_refs:
+            out_ref[rows:] = jnp.zeros((16, HEAD_DIM), BF16)
 
     @pl.when(pl.program_id(0) == pl.num_programs(0) - 1)
     def last_head():
-        total = jnp.sum(jnp.transpose(square_ref[...]), axis=0, keepdims=True)
-        sums_ref[...] = jnp.broadcast_to(total, sums_ref.shape)
+        rest = jnp.sum(jnp.transpose(square_ref[...]), axis=0, keepdims=True)
+        at_row = lax.broadcasted_iota(jnp.int32, (16, rows), 0)
+        tail = jnp.zeros((16, rows), F32)
+        for k in range(3):
+            piece = rest.astype(BF16).astype(F32)
+            rest = rest - piece
+            for part in range(parts):
+                row = jnp.broadcast_to(piece[:, part * rows : (part + 1) * rows], (16, rows))
+                tail = jnp.where(at_row == 3 * part + k, row, tail)
+        for out_ref in out_refs:
+            out_ref[rows:] = tail.astype(BF16)
 
 
 def heads_forward(meta, a_slots, i_slots, gain, offsets, heads, rows):
@@ -663,8 +703,7 @@
     return pl.pallas_call(
         functools.partial(heads_forward_kernel, parts, rows),
         out_shape=(
-            *[jax.ShapeDtypeStruct((rows, width), BF16) for r in range(parts)],
-            jax.ShapeDtypeStruct((8, tokens), F32),
+            *[jax.ShapeDtypeStruct((rows + 16, width), BF16) for r in range(parts)],
         ),
         grid_spec=pltpu.PrefetchScalarGridSpec(
             num_scalar_prefetch=1,
@@ -675,10 +714,7 @@
                 whole_column(1, heads),
                 offset_spec(heads),
             ],
-            out_specs=(
-                *[head_column(rows)] * parts,
-                pl.BlockSpec((8, tokens), lambda i, meta: (0, 0)),
-            ),
+            out_specs=(head_column(rows + 16),) * parts,
             scratch_shapes=[
                 pltpu.VMEM((tokens, HEAD_DIM), F32),
                 pltpu.VMEM((tokens, HEAD_DIM), BF16),
@@ -696,19 +732,25 @@
 
 
 def memory_kernel(parts, width, meta_ref, *refs):
-    out_refs, sum_refs = refs[:parts], refs[parts : 2 * parts]
-    gain_ref, after_ref, *share_refs, memory_ref = refs[2 * parts :]
+    out_refs, other_refs = refs[:parts], refs[parts : 2 * parts - 1]
+    gain_ref, *share_refs, memory_ref = refs[2 * parts - 1 :]
     wide = memory_ref.shape[1]
     rows = memory_ref.shape[0] // parts
-    total = sum_refs[0][:1]
-    for sum_ref in sum_refs[1:]:
-        total = total + sum_ref[:1]
+    total = None
+    for ref in (out_refs[0], *other_refs):
+        tail = ref[rows:, wide - rows :].astype(F32)
+        pieces = [
+            tail[3 * p : 3 * p + 1] + tail[3 * p + 1 : 3 * p + 2] + tail[3 * p + 2 : 3 * p + 3]
+            for p in range(parts)
+        ]
+        row = jnp.concatenate(pieces, axis=1)
+        total = row if total is None else total + row
     inverse = lax.rsqrt(total / width + eps_norm)
     gain = gain_ref[:, pl.ds(pl.multiple_of(meta_ref[0] * wide, 128), wide)]
     spread_inverse = jnp.transpose(jnp.broadcast_to(inverse, (128, inverse.shape[1])))
     for r, out_ref in enumerate(out_refs):
         source = lax.rem(meta_ref[0] + parts - r, parts)
-        memory_ref[pl.ds(pl.multiple_of(source * rows, rows), rows)] = out_ref[...]
+        memory_ref[pl.ds(pl.multiple_of(source * rows, rows), rows)] = out_ref[:rows]
     made = memory_ref[...].astype(F32)
     memory_ref[...] = (made * spread_inverse[:, :1] * gain).astype(BF16)
     for k, share_ref in enumerate(share_refs):
@@ -716,19 +758,19 @@
         share_ref[...] = memory_ref[k * size : (k + 1) * size]
 
 
-def memory_rows(meta, outs, sums, gain, after, width, shares):
+def memory_rows(meta, outs, others, gain, width, shares):
     parts = len(outs)
-    rows, wide = outs[0].shape
+    rows, wide = outs[0].shape[0] - 16, outs[0].shape[1]
     return pl.pallas_call(
         functools.partial(memory_kernel, parts, width),
         out_shape=[jax.ShapeDtypeStruct((rows * parts // shares, wide), BF16)] * shares,
-        in_specs=[SMEM_SPEC] + [VMEM_SPEC] * (2 * parts + 1) + [pl.BlockSpec(memory_space=pl.ANY)],
+        in_specs=[SMEM_SPEC] + [VMEM_SPEC] * (2 * parts),
         out_specs=[VMEM_SPEC] * shares,
         scratch_shapes=[pltpu.VMEM((rows * parts, wide), BF16)],
         compiler_params=pltpu.CompilerParams(vmem_limit_bytes=VMEM_LIMIT),
         cost_estimate=pl.CostEstimate(flops=rows, bytes_accessed=rows, transcendentals=0),
         name="memory_rows",
-    )(meta, *outs, *sums, gain, after)
+    )(meta, *outs, *others, gain)
 
 
 def place_kernel(parts, meta_ref, *refs):
@@ -736,12 +778,12 @@
     wide = refs[0].shape[1]
     for r in range(parts):
         source = lax.rem(meta_ref[0] + r, parts)
-        out_ref[:, pl.ds(pl.multiple_of(source * wide, 128), wide)] = refs[r][...]
+        out_ref[:, pl.ds(pl.multiple_of(source * wide, 128), wide)] = refs[r][: out_ref.shape[0]]
 
 
 def place_columns(meta, slots):
     parts = len(slots)
-    rows, wide = slots[0].shape
+    rows, wide = slots[0].shape[0] - 16, slots[0].shape[1]
     return pl.pallas_call(
         functools.partial(place_kernel, parts),
         out_shape=jax.ShapeDtypeStruct((rows, wide * parts), BF16),
@@ -857,8 +899,7 @@
 
     offsets = offset_table(rel_bias[0])
     onehot = jnp.asarray(bucket_onehot(buckets).T)
-    *o_sends, sums = heads_forward(meta, a_slots, i_slots, norm_gain, offsets, heads, rows)
-    all_sums = exchanged([sums] * parts, 1)
+    o_sends = heads_forward(meta, a_slots, i_slots, norm_gain, offsets, heads, rows)
     o_sends, c_slots = lax.optimization_barrier((o_sends, c_slots))
     o_slots = exchanged(o_sends, -1)
 
@@ -868,7 +909,7 @@
     g_sends, o_slots = lax.optimization_barrier((g_sends, o_slots))
     g_chunks = [exchanged(g_sends, -1)]
     output = place_columns(meta, o_slots)
-    shares = memory_rows(meta, o_sends, all_sums, final_gain[None], gain_grad, width, sections // 2)
+    shares = memory_rows(meta, o_sends, o_slots[1:], final_gain[None], width, sections // 2)
     memory = spread_memory(shares, section, sections)
 
     input_grad, weight_grad, bias_wide = heads_finish(

time: 144 us -> 146 us (1.014)
  waiting for transfers between devices: 47.9 us -> 64.5 us
  starting transfers between devices: 58 us -> 44.8 us
  local copies, waits for them, and re-layouts: 7.64 us -> 4.34 us
  Pallas kernels: 26.8 us -> 29.3 us
    ppermute x18 -> x15, waiting for transfers between devices: 47.8 us -> 63.8 us  [exchanged(): lax.ppermute(sends[r], 'seq', [(i, (i + direction * r) % parts) for i in...]
    ppermute x18 -> x15, starting transfers between devices: 51 us -> 37.8 us  [exchanged(): lax.ppermute(sends[r], 'seq', [(i, (i + direction * r) % parts) for i in...]
    unnamed x36 -> x22, local copies, waits for them, and re-layouts: 6.26 us -> 2.96 us
    pallas_call x1, Pallas kernels: 1.25 us -> 3.14 us  [pack_stash(): pl.pallas_call(functools.partial(pack_stash_kernel, parts, 4), out_shape=...]
  transfers between devices with their start and end apart: 24 -> 21, of which waited for: 7 -> 8; matrix products, arithmetic and copies ran while one was open for 2% -> 2% of each run, Pallas kernels for 17% -> 17%
where the time goes in v8:
time: 146 us
  waiting for transfers between devices  64.5 us (44%)
  starting transfers between devices  44.8 us (31%)
  Pallas kernels  29.3 us (20%)
  local copies, waits for them, and re-layouts  4.34 us (3%)
  other arithmetic  1.67 us (1%)
    ppermute x15, waiting for transfers between devices, exchanged(): lax.ppermute(sends[r], 'seq', [(i, (i + direction * r) % parts) for i in...  63.8 us
    ppermute x15, starting transfers between devices, exchanged(): lax.ppermute(sends[r], 'seq', [(i, (i + direction * r) % parts) for i in...  37.8 us
    pallas_call x1, Pallas kernels, heads_backward(): pl.pallas_call(functools.partial(heads_backward_kernel, parts, rows), out...  11.2 us
    pallas_call x1, Pallas kernels, heads_forward(): pl.pallas_call(functools.partial(heads_forward_kernel, parts, rows), out_...  6.95 us
    ppermute x2, starting transfers between devices, shifted(): lax.ppermute(value, axis, [(source, source + steps) for source in range(f...  3.7 us
    pallas_call x1, Pallas kernels, heads_finish(): pl.pallas_call(functools.partial(heads_finish_kernel, parts, chunks), out...  3.18 us
    pallas_call x1, Pallas kernels, pack_stash(): pl.pallas_call(functools.partial(pack_stash_kernel, parts, 4), out_shape=...  3.14 us
    unnamed x22, local copies, waits for them, and re-layouts  2.96 us
  transfers between devices with their start and end apart: 21, of which 8 were waited for; matrix products, arithmetic and copies ran while one was open for 2% of the time, Pallas kernels for 17%

profile of v8, /device:TPU:0, one launch (start us, length us, event | category | flops | bytes accessed | tf_op | source)
XLA Modules:
  0.0 145.7 jit_solution(2754547585116813670)
XLA Ops:
  0.6 0.0 copy-start
  0.6 2.4 %collective-permute-start.3 = (bf16[128,3072]{1,0:T(8,128)(2,1)}, bf16[128,3072]{1,0:T(8,128)(2,1)S(1)}, u32[]{:S(2)}, u32[]{:S(2)}) collective-permute-start(bf16[128,3072]{1,0:T(8,128)(2,1)} %bitcast.31), channel_id=1, source_target_pairs={{0,4},{4,8},{8,12},{12,16},{16,20},{20,24},{24,28},{1,5},{5,9},{9,... | collective-permute-start | bytes 2359304 | tf_op jit(solution)/shard_map/ppermute | solution.py:858
  3.1 1.3 collective-permute-start.7
  4.4 0.1 pad_add_fusion.meta_ref
  4.5 1.1 copy-done.1
  5.6 1.1 copy-done.5
  6.7 0.7 copy-done.6
  7.4 3.1 %pack_stash.1 = (f32[128,128]{1,0:T(8,128)S(1)}, bf16[224,768]{1,0:T(8,128)(2,1)S(1)}, bf16[224,768]{1,0:T(8,128)(2,1)S(1)}, bf16[224,768]{1,0:T(8,128)(2,1)S(1)}, bf16[224,768]{1,0:T(8,128)(2,1)S(1)}) custom-call(s32[3]{0:T(128)S(1)} %pad_add_fusion.meta_ref, bf16[128,3072]{1,0:T(8,128)(2,1)S(1)} %bitcast.23, f32[1,3072]{1,0:T(1,128)S(1)} %copy-done.6, ...), custom_call_target="tpu_custom_call" | custom-call | flops 1572864 | bytes 2359296 | tf_op jit(solution)/shard_map/pack_stash/pallas_call | solution.py:425
  10.5 2.5 %collective-permute-start = (bf16[224,768]{1,0:T(8,128)(2,1)S(1)}, bf16[224,768]{1,0:T(8,128)(2,1)S(1)}, u32[]{:S(2)}, u32[]{:S(2)}) collective-permute-start(bf16[224,768]{1,0:T(8,128)(2,1)S(1)} %get-tuple-element.52), channel_id=1, source_target_pairs={{0,1},{1,2},{2,3},{3,0},{4,5},{5,6},{6,7},{7,4},{8,9},{9,10},{10,1... | collective-permute-start | bytes 1032200 | tf_op jit(solution)/shard_map/ppermute | solution.py:886
  13.0 2.6 %collective-permute-start.1 = (bf16[224,768]{1,0:T(8,128)(2,1)S(1)}, bf16[224,768]{1,0:T(8,128)(2,1)S(1)}, u32[]{:S(2)}, u32[]{:S(2)}) collective-permute-start(bf16[224,768]{1,0:T(8,128)(2,1)S(1)} %get-tuple-element.53), channel_id=1, source_target_pairs={{0,2},{1,3},{2,0},{3,1},{4,6},{5,7},{6,4},{7,5},{8,10},{9,11},{10,... | collective-permute-start | bytes 1032200 | tf_op jit(solution)/shard_map/ppermute | solution.py:886
  15.6 1.3 collective-permute-start.2
  16.9 0.0 collective-permute-done.3.inner_ref
  16.9 0.9 pack_inbound.1
  17.9 0.0 copy-start.7
  17.9 0.7 collective-permute-start.4
  18.6 0.0 collective-permute-done.7.inner_ref
  18.6 0.3 collective-permute-start.5
  19.0 1.4 pack_cotangent.1
  20.3 2.0 %collective-permute-done.refs_1_ = bf16[224,768]{1,0:T(8,128)(2,1)S(1)} collective-permute-done((bf16[224,768]{1,0:T(8,128)(2,1)S(1)}, bf16[224,768]{1,0:T(8,128)(2,1)S(1)}, u32[]{:S(2)}, u32[]{:S(2)}) %collective-permute-start) | collective-permute-done | bytes 344096 | tf_op jit(solution)/shard_map/ppermute | solution.py:886
  22.4 2.1 %collective-permute-start.6 = (bf16[144,768]{1,0:T(8,128)(2,1)S(1)}, bf16[144,768]{1,0:T(8,128)(2,1)S(1)}, u32[]{:S(2)}, u32[]{:S(2)}) collective-permute-start(bf16[144,768]{1,0:T(8,128)(2,1)S(1)} %get-tuple-element.58), channel_id=1, source_target_pairs={{0,3},{1,0},{2,1},{3,2},{4,7},{5,4},{6,5},{7,6},{8,11},{9,8},{10,9... | collective-permute-start | bytes 663560 | tf_op jit(solution)/shard_map/ppermute | solution.py:886
  24.5 15.8 %collective-permute-done.1.refs_2_ = bf16[224,768]{1,0:T(8,128)(2,1)S(1)} collective-permute-done((bf16[224,768]{1,0:T(8,128)(2,1)S(1)}, bf16[224,768]{1,0:T(8,128)(2,1)S(1)}, u32[]{:S(2)}, u32[]{:S(2)}) %collective-permute-start.1) | collective-permute-done | bytes 344096 | tf_op jit(solution)/shard_map/ppermute | solution.py:886
  40.3 12.8 %collective-permute-start.8 = (bf16[128,768]{1,0:T(8,128)(2,1)S(1)}, bf16[128,768]{1,0:T(8,128)(2,1)S(1)}, u32[]{:S(2)}, u32[]{:S(2)}) collective-permute-start(bf16[128,768]{1,0:T(8,128)(2,1)S(1)} %get-tuple-element.64), channel_id=1, source_target_pairs={{0,1},{1,2},{2,3},{3,0},{4,5},{5,6},{6,7},{7,4},{8,9},{9,10},{10,1... | collective-permute-start | bytes 589832 | tf_op jit(solution)/shard_map/ppermute | solution.py:886
  53.2 0.0 collective-permute-done.2.refs_3_
  53.2 3.4 %collective-permute-start.9 = (bf16[128,768]{1,0:T(8,128)(2,1)S(1)}, bf16[128,768]{1,0:T(8,128)(2,1)S(1)}, u32[]{:S(2)}, u32[]{:S(2)}) collective-permute-start(bf16[128,768]{1,0:T(8,128)(2,1)S(1)} %get-tuple-element.65), channel_id=1, source_target_pairs={{0,2},{1,3},{2,0},{3,1},{4,6},{5,7},{6,4},{7,5},{8,10},{9,11},{10,... | collective-permute-start | bytes 589832 | tf_op jit(solution)/shard_map/ppermute | solution.py:886
  56.5 0.0 collective-permute-done.4.refs_5_
  56.6 1.9 %collective-permute-start.10 = (bf16[128,768]{1,0:T(8,128)(2,1)S(1)}, bf16[128,768]{1,0:T(8,128)(2,1)S(1)}, u32[]{:S(2)}, u32[]{:S(2)}) collective-permute-start(bf16[128,768]{1,0:T(8,128)(2,1)S(1)} %get-tuple-element.66), channel_id=1, source_target_pairs={{0,3},{1,0},{2,1},{3,2},{4,7},{5,4},{6,5},{7,6},{8,11},{9,8},{10,9... | collective-permute-start | bytes 589832 | tf_op jit(solution)/shard_map/ppermute | solution.py:886
  58.4 0.2 fusion
  58.7 0.0 copy-start.9
  58.7 10.0 %collective-permute-done.5.refs_6_ = bf16[144,768]{1,0:T(8,128)(2,1)S(1)} collective-permute-done((bf16[144,768]{1,0:T(8,128)(2,1)S(1)}, bf16[144,768]{1,0:T(8,128)(2,1)S(1)}, u32[]{:S(2)}, u32[]{:S(2)}) %collective-permute-start.5) | collective-permute-done | bytes 221216 | tf_op jit(solution)/shard_map/ppermute | solution.py:886
  68.7 0.0 collective-permute-done.6.refs_7_
  68.7 0.0 copy-done.7
  68.7 7.0 %heads_forward.1 = (bf16[144,768]{1,0:T(8,128)(2,1)S(1)}, bf16[144,768]{1,0:T(8,128)(2,1)S(1)}, bf16[144,768]{1,0:T(8,128)(2,1)S(1)}, bf16[144,768]{1,0:T(8,128)(2,1)S(1)}) custom-call(s32[3]{0:T(128)S(1)} %pad_add_fusion.meta_ref, bf16[224,768]{1,0:T(8,128)(2,1)S(1)} %get-tuple-element.51.refs_0_, bf16[224,768]{1,0:T(8,128)(2,1)S(1)} %collective-permute-done.refs_1_, ...), custom_call_target="tpu_custom_call" | custom-call | flops 3072 | bytes 512 | tf_op jit(solution)/shard_map/heads_forward/pallas_call | solution.py:703
  75.6 0.0 collective-permute-done.8.refs_5_
  75.6 2.0 %collective-permute-done.9.refs_6_ = bf16[128,768]{1,0:T(8,128)(2,1)S(1)} collective-permute-done((bf16[128,768]{1,0:T(8,128)(2,1)S(1)}, bf16[128,768]{1,0:T(8,128)(2,1)S(1)}, u32[]{:S(2)}, u32[]{:S(2)}) %collective-permute-start.9) | collective-permute-done | bytes 196640 | tf_op jit(solution)/shard_map/ppermute | solution.py:886
  77.6 0.0 collective-permute-done.10.refs_7_
  77.6 4.7 %collective-permute-start.11 = (bf16[144,768]{1,0:T(8,128)(2,1)S(1)}, bf16[144,768]{1,0:T(8,128)(2,1)S(1)}, u32[]{:S(2)}, u32[]{:S(2)}) collective-permute-start(bf16[144,768]{1,0:T(8,128)(2,1)S(1)} %get-tuple-element.76.refs_1_), channel_id=1, source_target_pairs={{0,3},{1,0},{2,1},{3,2},{4,7},{5,4},{6,5},{7,6},{8,11},{9,8},{10,9... | collective-permute-start | bytes 663560 | tf_op jit(solution)/shard_map/ppermute | solution.py:886
  82.3 1.5 %collective-permute-start.12 = (bf16[144,768]{1,0:T(8,128)(2,1)S(1)}, bf16[144,768]{1,0:T(8,128)(2,1)S(1)}, u32[]{:S(2)}, u32[]{:S(2)}) collective-permute-start(bf16[144,768]{1,0:T(8,128)(2,1)S(1)} %get-tuple-element.77.refs_2_), channel_id=1, source_target_pairs={{0,2},{1,3},{2,0},{3,1},{4,6},{5,7},{6,4},{7,5},{8,10},{9,11},{10,... | collective-permute-start | bytes 663560 | tf_op jit(solution)/shard_map/ppermute | solution.py:886
  83.9 0.0 collective-permute-start.13
  83.9 0.0 copy-done.9
  83.9 11.2 %heads_backward.1 = (bf16[240,768]{1,0:T(8,128)(2,1)S(1)}, bf16[240,768]{1,0:T(8,128)(2,1)}, bf16[240,768]{1,0:T(8,128)(2,1)}, bf16[240,768]{1,0:T(8,128)(2,1)}, f32[1,768]{1,0:T(1,128)}) custom-call(s32[3]{0:T(128)S(1)} %pad_add_fusion.meta_ref, bf16[224,768]{1,0:T(8,128)(2,1)S(1)} %get-tuple-element.51.refs_0_, ...), custom_call_target="tpu_custom_call" | custom-call | flops 1228800000 | bytes 393216 | tf_op jit(solution)/shard_map/heads_backward/pallas_call | solution.py:604
  95.1 0.0 collective-permute-done.11.refs_1_.refs_4_
  95.1 8.4 %collective-permute-done.12.refs_2_.refs_5_ = bf16[144,768]{1,0:T(8,128)(2,1)S(1)} collective-permute-done((bf16[144,768]{1,0:T(8,128)(2,1)S(1)}, bf16[144,768]{1,0:T(8,128)(2,1)S(1)}, u32[]{:S(2)}, u32[]{:S(2)}) %collective-permute-start.12) | collective-permute-done | bytes 221216 | tf_op jit(solution)/shard_map/ppermute | solution.py:886
  103.5 0.0 collective-permute-done.13.refs_3_.refs_6_
  103.5 0.9 memory_rows.1
  104.5 0.7 collective-permute-start.17
  105.1 0.7 collective-permute-start.18
  105.8 0.7 collective-permute-start.19
  106.5 0.1 collective-permute-start.14
  106.6 1.9 %collective-permute-start.15 = (bf16[240,768]{1,0:T(8,128)(2,1)}, bf16[240,768]{1,0:T(8,128)(2,1)}, u32[]{:S(2)}, u32[]{:S(2)}) collective-permute-start(bf16[240,768]{1,0:T(8,128)(2,1)} %get-tuple-element.85), channel_id=1, source_target_pairs={{0,2},{1,3},{2,0},{3,1},{4,6},{5,7},{6,4},{7,5},{8,10},{9,11},{10,... | collective-permute-start | bytes 1105928 | tf_op jit(solution)/shard_map/ppermute | solution.py:886
  108.4 0.0 collective-permute-done.17
  108.4 1.9 %collective-permute-start.16 = (bf16[240,768]{1,0:T(8,128)(2,1)}, bf16[240,768]{1,0:T(8,128)(2,1)}, u32[]{:S(2)}, u32[]{:S(2)}) collective-permute-start(bf16[240,768]{1,0:T(8,128)(2,1)} %get-tuple-element.86), channel_id=1, source_target_pairs={{0,1},{1,2},{2,3},{3,0},{4,5},{5,6},{6,7},{7,4},{8,9},{9,10},{10,1... | collective-permute-start | bytes 1105928 | tf_op jit(solution)/shard_map/ppermute | solution.py:886
  110.4 0.0 collective-permute-done.18
  110.4 0.0 collective-permute-done.19
  110.4 0.0 copy-start.2
  110.4 0.6 slice.12
  111.1 1.3 collective-permute-start.20
  112.4 1.5 %place_columns.1 = bf16[128,3072]{1,0:T(8,128)(2,1)} custom-call(s32[3]{0:T(128)S(1)} %pad_add_fusion.meta_ref, bf16[144,768]{1,0:T(8,128)(2,1)S(1)} %get-tuple-element.79.refs_11_.refs_0_, bf16[144,768]{1,0:T(8,128)(2,1)S(1)} %collective-permute-done.11.refs_1_.refs_4_, bf16[144,768]{1,0:T(8,128)(2,1)S(1)} %collective-permute-done.12.refs_2_.refs_5_, ...), custom_call_target="tpu_custom_call" | custom-call | bytes 128 | tf_op jit(solution)/shard_map/place_columns/pallas_call | solution.py:787
  113.9 0.7 collective-permute-done.20
  114.6 1.6 %slice_select_fusion = bf16[64,768]{1,0:T(8,128)(2,1)} fusion(bf16[64,768]{1,0:T(8,128)(2,1)} %collective-permute-done.20, bf16[128,768]{1,0:T(8,128)(2,1)S(1)} %add_add_fusion, pred[]{:T(512)S(6)} %eq.14), kind=kLoop, calls=%fused_computation.3 | loop fusion | flops 49152 | bytes 294913 | tf_op jit(solution)/shard_map/jit(_where)/select_n | solution.py:868
  116.2 1.0 collective-permute-done.14.refs_1_
  117.2 24.6 %collective-permute-done.15.refs_2_ = bf16[240,768]{1,0:T(8,128)(2,1)} collective-permute-done((bf16[240,768]{1,0:T(8,128)(2,1)}, bf16[240,768]{1,0:T(8,128)(2,1)}, u32[]{:S(2)}, u32[]{:S(2)}) %collective-permute-start.15) | collective-permute-done | bytes 368672 | tf_op jit(solution)/shard_map/ppermute | solution.py:886
  141.8 0.0 collective-permute-done.16.refs_3_
  141.8 3.2 %heads_finish.1 = (bf16[128,3072]{1,0:T(8,128)(2,1)}, f32[3,24,32,128]{3,2,1,0:T(8,128)}, f32[24,8,128]{2,1,0:T(8,128)S(1)}) custom-call(s32[3]{0:T(128)S(1)} %pad_add_fusion.meta_ref, bf16[240,768]{1,0:T(8,128)(2,1)S(1)} %get-tuple-element.83.refs_0_, bf16[240,768]{1,0:T(8,128)(2,1)S(1)} %collective-permute-done.14.refs_1_, ...), custom_call_target="tpu_custom_call" | custom-call | flops 4718592 | bytes 5505024 | tf_op jit(solution)/shard_map/heads_finish/pallas_call | solution.py:832
  144.9 0.7 copy.18
  (16 shorter events, 0.1 us)
Async XLA Ops:
  0.6 57.8 %copy-start = (f32[1,32,24]{1,2,0:T(8,128)S(1)}, f32[1,32,24]{1,2,0:T(8,128)}, u32[]{:S(2)}) copy-start(f32[1,32,24]{1,2,0:T(8,128)} %param.17) | copy-start | bytes 9220
  0.6 16.3 %collective-permute-start.3 = (bf16[128,3072]{1,0:T(8,128)(2,1)}, bf16[128,3072]{1,0:T(8,128)(2,1)S(1)}, u32[]{:S(2)}, u32[]{:S(2)}) collective-permute-start(bf16[128,3072]{1,0:T(8,128)(2,1)} %bitcast.31), channel_id=1, source_target_pairs={{0,4},{4,8},{8,12},{12,16},{16,20},{20,24},{24,28},{1,5},{5,9},{9,... | collective-permute-start | bytes 2359304 | tf_op jit(solution)/shard_map/ppermute | solution.py:858
  3.1 15.6 %collective-permute-start.7 = (bf16[128,3072]{1,0:T(8,128)(2,1)}, bf16[128,3072]{1,0:T(8,128)(2,1)S(1)}, u32[]{:S(2)}, u32[]{:S(2)}) collective-permute-start(bf16[128,3072]{1,0:T(8,128)(2,1)} %bitcast.32), channel_id=1, source_target_pairs={{4,0},{8,4},{12,8},{16,12},{20,16},{24,20},{28,24},{5,1},{9,5},{13... | collective-permute-start | bytes 2359304 | tf_op jit(solution)/shard_map/ppermute | solution.py:858
  4.4 1.1 copy-start.1
  5.6 1.1 copy-start.5
  6.6 0.7 copy-start.6
  7.4 9.6 %copy-start.3 = (bf16[128,3072]{1,0:T(8,128)(2,1)S(1)}, bf16[128,3072]{1,0:T(8,128)(2,1)}, u32[]{:S(2)}) copy-start(bf16[128,3072]{1,0:T(8,128)(2,1)} %edge_ref.2) | copy-start | bytes 2359300
  7.4 11.6 %copy-start.4 = (bf16[128,3072]{1,0:T(8,128)(2,1)S(1)}, bf16[128,3072]{1,0:T(8,128)(2,1)}, u32[]{:S(2)}) copy-start(bf16[128,3072]{1,0:T(8,128)(2,1)} %edge_ref.3) | copy-start | bytes 2359300
  10.5 11.9 %collective-permute-start = (bf16[224,768]{1,0:T(8,128)(2,1)S(1)}, bf16[224,768]{1,0:T(8,128)(2,1)S(1)}, u32[]{:S(2)}, u32[]{:S(2)}) collective-permute-start(bf16[224,768]{1,0:T(8,128)(2,1)S(1)} %get-tuple-element.52), channel_id=1, source_target_pairs={{0,1},{1,2},{2,3},{3,0},{4,5},{5,6},{6,7},{7,4},{8,9},{9,10},{10,1... | collective-permute-start | bytes 1032200 | tf_op jit(solution)/shard_map/ppermute | solution.py:886
  13.0 27.4 %collective-permute-start.1 = (bf16[224,768]{1,0:T(8,128)(2,1)S(1)}, bf16[224,768]{1,0:T(8,128)(2,1)S(1)}, u32[]{:S(2)}, u32[]{:S(2)}) collective-permute-start(bf16[224,768]{1,0:T(8,128)(2,1)S(1)} %get-tuple-element.53), channel_id=1, source_target_pairs={{0,2},{1,3},{2,0},{3,1},{4,6},{5,7},{6,4},{7,5},{8,10},{9,11},{10,... | collective-permute-start | bytes 1032200 | tf_op jit(solution)/shard_map/ppermute | solution.py:886
  15.6 37.6 %collective-permute-start.2 = (bf16[224,768]{1,0:T(8,128)(2,1)S(1)}, bf16[224,768]{1,0:T(8,128)(2,1)S(1)}, u32[]{:S(2)}, u32[]{:S(2)}) collective-permute-start(bf16[224,768]{1,0:T(8,128)(2,1)S(1)} %get-tuple-element.54), channel_id=1, source_target_pairs={{0,3},{1,0},{2,1},{3,2},{4,7},{5,4},{6,5},{7,6},{8,11},{9,8},{10,9... | collective-permute-start | bytes 1032200 | tf_op jit(solution)/shard_map/ppermute | solution.py:886
  17.9 40.6 %copy-start.10 = (f32[256,32]{1,0:T(8,128)S(1)}, f32[256,32]{1,0:T(8,128)}, u32[]{:S(2)}) copy-start(f32[256,32]{1,0:T(8,128)} %constant.35.clone) | copy-start | bytes 98308
  17.9 50.8 %copy-start.7 = (f32[1,3072]{1,0:T(1,128)S(1)}, f32[1,3072]{1,0:T(1,128)}, u32[]{:S(2)}) copy-start(f32[1,3072]{1,0:T(1,128)} %refs_6_.1) | copy-start | bytes 36868
  17.9 38.7 %collective-permute-start.4 = (bf16[144,768]{1,0:T(8,128)(2,1)S(1)}, bf16[144,768]{1,0:T(8,128)(2,1)S(1)}, u32[]{:S(2)}, u32[]{:S(2)}) collective-permute-start(bf16[144,768]{1,0:T(8,128)(2,1)S(1)} %get-tuple-element.56), channel_id=1, source_target_pairs={{0,1},{1,2},{2,3},{3,0},{4,5},{5,6},{6,7},{7,4},{8,9},{9,10},{10,1... | collective-permute-start | bytes 663560 | tf_op jit(solution)/shard_map/ppermute | solution.py:886
  18.6 50.0 %collective-permute-start.5 = (bf16[144,768]{1,0:T(8,128)(2,1)S(1)}, bf16[144,768]{1,0:T(8,128)(2,1)S(1)}, u32[]{:S(2)}, u32[]{:S(2)}) collective-permute-start(bf16[144,768]{1,0:T(8,128)(2,1)S(1)} %get-tuple-element.57), channel_id=1, source_target_pairs={{0,2},{1,3},{2,0},{3,1},{4,6},{5,7},{6,4},{7,5},{8,10},{9,11},{10,... | collective-permute-start | bytes 663560 | tf_op jit(solution)/shard_map/ppermute | solution.py:886
  22.4 46.3 %collective-permute-start.6 = (bf16[144,768]{1,0:T(8,128)(2,1)S(1)}, bf16[144,768]{1,0:T(8,128)(2,1)S(1)}, u32[]{:S(2)}, u32[]{:S(2)}) collective-permute-start(bf16[144,768]{1,0:T(8,128)(2,1)S(1)} %get-tuple-element.58), channel_id=1, source_target_pairs={{0,3},{1,0},{2,1},{3,2},{4,7},{5,4},{6,5},{7,6},{8,11},{9,8},{10,9... | collective-permute-start | bytes 663560 | tf_op jit(solution)/shard_map/ppermute | solution.py:886
  40.3 35.3 %collective-permute-start.8 = (bf16[128,768]{1,0:T(8,128)(2,1)S(1)}, bf16[128,768]{1,0:T(8,128)(2,1)S(1)}, u32[]{:S(2)}, u32[]{:S(2)}) collective-permute-start(bf16[128,768]{1,0:T(8,128)(2,1)S(1)} %get-tuple-element.64), channel_id=1, source_target_pairs={{0,1},{1,2},{2,3},{3,0},{4,5},{5,6},{6,7},{7,4},{8,9},{9,10},{10,1... | collective-permute-start | bytes 589832 | tf_op jit(solution)/shard_map/ppermute | solution.py:886
  53.2 24.5 %collective-permute-start.9 = (bf16[128,768]{1,0:T(8,128)(2,1)S(1)}, bf16[128,768]{1,0:T(8,128)(2,1)S(1)}, u32[]{:S(2)}, u32[]{:S(2)}) collective-permute-start(bf16[128,768]{1,0:T(8,128)(2,1)S(1)} %get-tuple-element.65), channel_id=1, source_target_pairs={{0,2},{1,3},{2,0},{3,1},{4,6},{5,7},{6,4},{7,5},{8,10},{9,11},{10,... | collective-permute-start | bytes 589832 | tf_op jit(solution)/shard_map/ppermute | solution.py:886
  56.6 21.1 %collective-permute-start.10 = (bf16[128,768]{1,0:T(8,128)(2,1)S(1)}, bf16[128,768]{1,0:T(8,128)(2,1)S(1)}, u32[]{:S(2)}, u32[]{:S(2)}) collective-permute-start(bf16[128,768]{1,0:T(8,128)(2,1)S(1)} %get-tuple-element.66), channel_id=1, source_target_pairs={{0,3},{1,0},{2,1},{3,2},{4,7},{5,4},{6,5},{7,6},{8,11},{9,8},{10,9... | collective-permute-start | bytes 589832 | tf_op jit(solution)/shard_map/ppermute | solution.py:886
  58.7 25.2 %copy-start.9 = (f32[32,256]{1,0:T(8,128)S(1)}, f32[32,256]{1,0:T(8,128)}, u32[]{:S(2)}) copy-start(f32[32,256]{1,0:T(8,128)} %constant.36.clone.refs_10_) | copy-start | bytes 98308
  77.6 25.9 %copy-start.8 = (f32[3072]{0:T(1024)S(1)}, f32[3072]{0:T(1024)}, u32[]{:S(2)}) copy-start(f32[3072]{0:T(1024)} %param.19) | copy-start | bytes 36868
  77.6 17.5 %collective-permute-start.11 = (bf16[144,768]{1,0:T(8,128)(2,1)S(1)}, bf16[144,768]{1,0:T(8,128)(2,1)S(1)}, u32[]{:S(2)}, u32[]{:S(2)}) collective-permute-start(bf16[144,768]{1,0:T(8,128)(2,1)S(1)} %get-tuple-element.76.refs_1_), channel_id=1, source_target_pairs={{0,3},{1,0},{2,1},{3,2},{4,7},{5,4},{6,5},{7,6},{8,11},{9,8},{10,9... | collective-permute-start | bytes 663560 | tf_op jit(solution)/shard_map/ppermute | solution.py:886
  82.3 21.2 %collective-permute-start.12 = (bf16[144,768]{1,0:T(8,128)(2,1)S(1)}, bf16[144,768]{1,0:T(8,128)(2,1)S(1)}, u32[]{:S(2)}, u32[]{:S(2)}) collective-permute-start(bf16[144,768]{1,0:T(8,128)(2,1)S(1)} %get-tuple-element.77.refs_2_), channel_id=1, source_target_pairs={{0,2},{1,3},{2,0},{3,1},{4,6},{5,7},{6,4},{7,5},{8,10},{9,11},{10,... | collective-permute-start | bytes 663560 | tf_op jit(solution)/shard_map/ppermute | solution.py:886
  83.9 19.6 %collective-permute-start.13 = (bf16[144,768]{1,0:T(8,128)(2,1)S(1)}, bf16[144,768]{1,0:T(8,128)(2,1)S(1)}, u32[]{:S(2)}, u32[]{:S(2)}) collective-permute-start(bf16[144,768]{1,0:T(8,128)(2,1)S(1)} %get-tuple-element.78.refs_3_), channel_id=1, source_target_pairs={{0,1},{1,2},{2,3},{3,0},{4,5},{5,6},{6,7},{7,4},{8,9},{9,10},{10,1... | collective-permute-start | bytes 663560 | tf_op jit(solution)/shard_map/ppermute | solution.py:886
  104.5 4.0 %collective-permute-start.17 = (bf16[128,768]{1,0:T(8,128)(2,1)S(1)}, bf16[128,768]{1,0:T(8,128)(2,1)S(1)}, u32[]{:S(2)}, u32[]{:S(2)}) collective-permute-start(bf16[128,768]{1,0:T(8,128)(2,1)S(1)} %get-tuple-element.93), channel_id=1, source_target_pairs={{28,4},{29,5},{30,6},{31,7}} | collective-permute-start | bytes 589832 | tf_op jit(solution)/shard_map/ppermute | solution.py:865
  105.1 5.2 %collective-permute-start.18 = (bf16[128,768]{1,0:T(8,128)(2,1)S(1)}, bf16[128,768]{1,0:T(8,128)(2,1)S(1)}, u32[]{:S(2)}, u32[]{:S(2)}) collective-permute-start(bf16[128,768]{1,0:T(8,128)(2,1)S(1)} %get-tuple-element.94), channel_id=1, source_target_pairs={{28,12},{29,13},{30,14},{31,15}} | collective-permute-start | bytes 589832 | tf_op jit(solution)/shard_map/ppermute | solution.py:865
  105.8 4.6 %collective-permute-start.19 = (bf16[128,768]{1,0:T(8,128)(2,1)S(1)}, bf16[128,768]{1,0:T(8,128)(2,1)S(1)}, u32[]{:S(2)}, u32[]{:S(2)}) collective-permute-start(bf16[128,768]{1,0:T(8,128)(2,1)S(1)} %get-tuple-element.95), channel_id=1, source_target_pairs={{28,20},{29,21},{30,22},{31,23}} | collective-permute-start | bytes 589832 | tf_op jit(solution)/shard_map/ppermute | solution.py:865
  106.5 10.7 %collective-permute-start.14 = (bf16[240,768]{1,0:T(8,128)(2,1)}, bf16[240,768]{1,0:T(8,128)(2,1)S(1)}, u32[]{:S(2)}, u32[]{:S(2)}) collective-permute-start(bf16[240,768]{1,0:T(8,128)(2,1)} %get-tuple-element.84), channel_id=1, source_target_pairs={{0,3},{1,0},{2,1},{3,2},{4,7},{5,4},{6,5},{7,6},{8,11},{9,8},{10,9... | collective-permute-start | bytes 1105928 | tf_op jit(solution)/shard_map/ppermute | solution.py:886
  106.6 35.2 %collective-permute-start.15 = (bf16[240,768]{1,0:T(8,128)(2,1)}, bf16[240,768]{1,0:T(8,128)(2,1)}, u32[]{:S(2)}, u32[]{:S(2)}) collective-permute-start(bf16[240,768]{1,0:T(8,128)(2,1)} %get-tuple-element.85), channel_id=1, source_target_pairs={{0,2},{1,3},{2,0},{3,1},{4,6},{5,7},{6,4},{7,5},{8,10},{9,11},{10,... | collective-permute-start | bytes 1105928 | tf_op jit(solution)/shard_map/ppermute | solution.py:886
  108.4 33.3 %collective-permute-start.16 = (bf16[240,768]{1,0:T(8,128)(2,1)}, bf16[240,768]{1,0:T(8,128)(2,1)}, u32[]{:S(2)}, u32[]{:S(2)}) collective-permute-start(bf16[240,768]{1,0:T(8,128)(2,1)} %get-tuple-element.86), channel_id=1, source_target_pairs={{0,1},{1,2},{2,3},{3,0},{4,5},{5,6},{6,7},{7,4},{8,9},{9,10},{10,1... | collective-permute-start | bytes 1105928 | tf_op jit(solution)/shard_map/ppermute | solution.py:886
  110.4 31.3 %copy-start.2 = (bf16[1,128,3072]{2,1,0:T(8,128)(2,1)S(1)}, bf16[1,128,3072]{2,1,0:T(8,128)(2,1)}, u32[]{:S(2)}) copy-start(bf16[1,128,3072]{2,1,0:T(8,128)(2,1)} %param.13) | copy-start | bytes 2359300
  111.1 3.5 %collective-permute-start.20 = (bf16[64,768]{1,0:T(8,128)(2,1)}, bf16[64,768]{1,0:T(8,128)(2,1)}, u32[]{:S(2)}, u32[]{:S(2)}) collective-permute-start(bf16[64,768]{1,0:T(8,128)(2,1)} %slice.12), channel_id=1, source_target_pairs={{4,0},{12,8},{20,16},{28,24},{5,1},{13,9},{21,17},{29,25},{6,2},{1... | collective-permute-start | bytes 294920 | tf_op jit(solution)/shard_map/ppermute | solution.py:867

commit v9 on v8

--- a/solution.py
+++ b/solution.py
@@ -18,6 +18,7 @@
 F32 = jnp.float32
 BF16 = jnp.bfloat16
 VMEM_LIMIT = 24 * 1024 * 1024
+EXTRA = 8
 
 
 def bucket_onehot(bucket_count):
@@ -398,9 +399,9 @@
 
     def finish_with(source_ref):
         if with_inverse:
-            tail = split_rows(row_inverse(source_ref[...]), 16, wide)
+            tail = split_rows(row_inverse(source_ref[...]), EXTRA, wide)
             for out_ref in refs:
-                out_ref[rows:] = jnp.zeros((16, wide), BF16)
+                out_ref[rows:] = jnp.zeros((EXTRA, wide), BF16)
                 out_ref[rows:, :rows] = tail
         else:
             out_refs[parts][...] = source_ref[...]
@@ -437,7 +438,7 @@
             pltpu.VMEM((rows, width), BF16),
             pltpu.SemaphoreType.DMA((8,)),
         ],
-        compiler_params=pltpu.CompilerParams(vmem_limit_bytes=VMEM_LIMIT),
+        compiler_params=pltpu.CompilerParams(vmem_limit_bytes=58 * 1024 * 1024),
         cost_estimate=pl.CostEstimate(flops=4 * rows * width, bytes_accessed=6 * rows * width, transcendentals=0),
         name="pack_stash",
     )(meta, x, gain, weight)
@@ -445,7 +446,7 @@
 
 def pack_rows(meta, edge, inner, parts, with_inverse):
     rows, width = inner.shape
-    shape = (rows + (16 if with_inverse else 0), width // parts)
+    shape = (rows + (EXTRA if with_inverse else 0), width // parts)
     extra = () if with_inverse else (jax.ShapeDtypeStruct((rows, width), BF16),)
     return pl.pallas_call(
         functools.partial(pack_rows_kernel, parts, with_inverse),
@@ -484,7 +485,7 @@
     def spread_inverse():
         for r, ref in enumerate(refs):
             source = lax.rem(meta_ref[0] + parts - r, parts)
-            tail = ref[rows : rows + 16].astype(F32)
+            tail = ref[rows : rows + EXTRA].astype(F32)
             inverse_ref[pl.ds(pl.multiple_of(source * rows, rows), rows)] = column_of(
                 tail[:1] + tail[1:2] + tail[2:3], rows
             )
@@ -576,9 +577,7 @@
                 pl.ds(pl.multiple_of(source * depth, depth), depth), j * HEAD_DIM : (j + 1) * HEAD_DIM
             ].astype(BF16)
         share = bias_ref[pl.ds(pl.multiple_of(source * buckets, buckets), buckets)]
-        out_ref[rows + 3 * depth :] = jnp.concatenate(
-            [share, jnp.zeros((16 - buckets, HEAD_DIM), F32)], axis=0
-        ).astype(BF16)
+        out_ref[rows + 3 * depth :] = share.astype(BF16)
 
 
 def head_column(rows, first=0):
@@ -599,7 +598,7 @@
     tokens = rows * parts
     buckets = onehot.shape[0]
     packed = a_slots[0].shape[0]
-    made = packed + 16
+    made = packed + buckets // parts
     width = count * HEAD_DIM
     return pl.pallas_call(
         functools.partial(heads_backward_kernel, parts, rows),
@@ -678,19 +677,19 @@
     @pl.when(pl.program_id(0) < pl.num_programs(0) - 1)
     def no_sums():
         for out_ref in out_refs:
-            out_ref[rows:] = jnp.zeros((16, HEAD_DIM), BF16)
+            out_ref[rows:] = jnp.zeros((EXTRA, HEAD_DIM), BF16)
 
     @pl.when(pl.program_id(0) == pl.num_programs(0) - 1)
     def last_head():
         rest = jnp.sum(jnp.transpose(square_ref[...]), axis=0, keepdims=True)
-        at_row = lax.broadcasted_iota(jnp.int32, (16, rows), 0)
-        tail = jnp.zeros((16, rows), F32)
-        for k in range(3):
+        at_row = lax.broadcasted_iota(jnp.int32, (EXTRA, rows), 0)
+        tail = jnp.zeros((EXTRA, rows), F32)
+        for k in range(2):
             piece = rest.astype(BF16).astype(F32)
             rest = rest - piece
             for part in range(parts):
-                row = jnp.broadcast_to(piece[:, part * rows : (part + 1) * rows], (16, rows))
-                tail = jnp.where(at_row == 3 * part + k, row, tail)
+                row = jnp.broadcast_to(piece[:, part * rows : (part + 1) * rows], (EXTRA, rows))
+                tail = jnp.where(at_row == 2 * part + k, row, tail)
         for out_ref in out_refs:
             out_ref[rows:] = tail.astype(BF16)
 
@@ -703,7 +702,7 @@
     return pl.pallas_call(
         functools.partial(heads_forward_kernel, parts, rows),
         out_shape=(
-            *[jax.ShapeDtypeStruct((rows + 16, width), BF16) for r in range(parts)],
+            *[jax.ShapeDtypeStruct((rows + EXTRA, width), BF16) for r in range(parts)],
         ),
         grid_spec=pltpu.PrefetchScalarGridSpec(
             num_scalar_prefetch=1,
@@ -714,7 +713,7 @@
                 whole_column(1, heads),
                 offset_spec(heads),
             ],
-            out_specs=(head_column(rows + 16),) * parts,
+            out_specs=(head_column(rows + EXTRA),) * parts,
             scratch_shapes=[
                 pltpu.VMEM((tokens, HEAD_DIM), F32),
                 pltpu.VMEM((tokens, HEAD_DIM), BF16),
@@ -739,10 +738,7 @@
     total = None
     for ref in (out_refs[0], *other_refs):
         tail = ref[rows:, wide - rows :].astype(F32)
-        pieces = [
-            tail[3 * p : 3 * p + 1] + tail[3 * p + 1 : 3 * p + 2] + tail[3 * p + 2 : 3 * p + 3]
-            for p in range(parts)
-        ]
+        pieces = [tail[2 * p : 2 * p + 1] + tail[2 * p + 1 : 2 * p + 2] for p in range(parts)]
         row = jnp.concatenate(pieces, axis=1)
         total = row if total is None else total + row
     inverse = lax.rsqrt(total / width + eps_norm)
@@ -760,7 +756,7 @@
 
 def memory_rows(meta, outs, others, gain, width, shares):
     parts = len(outs)
-    rows, wide = outs[0].shape[0] - 16, outs[0].shape[1]
+    rows, wide = outs[0].shape[0] - EXTRA, outs[0].shape[1]
     return pl.pallas_call(
         functools.partial(memory_kernel, parts, width),
         out_shape=[jax.ShapeDtypeStruct((rows * parts // shares, wide), BF16)] * shares,
@@ -783,7 +779,7 @@
 
 def place_columns(meta, slots):
     parts = len(slots)
-    rows, wide = slots[0].shape[0] - 16, slots[0].shape[1]
+    rows, wide = slots[0].shape[0] - EXTRA, slots[0].shape[1]
     return pl.pallas_call(
         functools.partial(place_kernel, parts),
         out_shape=jax.ShapeDtypeStruct((rows, wide * parts), BF16),
@@ -795,54 +791,64 @@
     )(meta, *slots)
 
 
-def heads_finish_kernel(parts, chunks, meta_ref, *refs):
-    g_refs = refs[: parts * chunks]
-    x_ref, inverse_ref, gain_ref, cot_ref, out_ref, weight_ref, bias_ref, scaled_ref = refs[parts * chunks :]
+def heads_finish_kernel(parts, meta_ref, *refs):
+    g_refs = refs[:parts]
+    x_ref, inverse_ref, gain_ref, cot_ref, out_ref, weight_hbm, bias_ref, scaled_ref, weight_ref, sem = refs[parts:]
     rows, width = x_ref.shape
-    wide = width // parts // chunks
+    wide = width // parts
     heads = wide // HEAD_DIM
     depth = HEAD_DIM // parts
-    buckets = bias_ref.shape[1]
-    for c in range(chunks):
-        for r in range(parts):
-            g_ref = g_refs[c * parts + r]
-            place = lax.rem(meta_ref[0] + r, parts) * chunks + c
-            columns = pl.ds(pl.multiple_of(place * wide, 128), wide)
-            scaled_ref[:, columns] = g_ref[:rows].astype(F32) * gain_ref[:, columns]
-            for h in range(heads):
-                lanes = slice(h * HEAD_DIM, (h + 1) * HEAD_DIM)
-                for j in range(3):
-                    weight_ref[j, place * heads + h] = g_ref[
-                        rows + j * depth : rows + (j + 1) * depth, lanes
-                    ].astype(F32)
-                bias_ref[place * heads + h] = g_ref[rows + 3 * depth :, lanes].astype(F32)[:buckets]
+    for r in range(parts):
+        source = lax.rem(meta_ref[0] + r, parts)
+        for h in range(heads):
+            for j in range(3):
+                weight_ref[j, source * heads + h] = g_refs[r][
+                    rows + j * depth : rows + (j + 1) * depth, h * HEAD_DIM : (h + 1) * HEAD_DIM
+                ].astype(F32)
+    weight_copy = pltpu.make_async_copy(weight_ref, weight_hbm, sem)
+    weight_copy.start()
+    lane = lax.broadcasted_iota(jnp.int32, (bias_ref.shape[0], HEAD_DIM), 1)
+    bias = jnp.zeros(lane.shape, F32)
+    for r in range(parts):
+        source = lax.rem(meta_ref[0] + r, parts)
+        columns = pl.ds(pl.multiple_of(source * wide, 128), wide)
+        scaled_ref[:, columns] = g_refs[r][:rows].astype(F32) * gain_ref[:, columns]
+        shares = g_refs[r][rows + 3 * depth :].astype(F32)
+        for h in range(heads):
+            bias = jnp.where(lane == source * heads + h, shares[:, h * HEAD_DIM : (h + 1) * HEAD_DIM], bias)
+    bias_ref[...] = bias[:, : bias_ref.shape[1]]
     x = x_ref[...].astype(F32)
     scaled = scaled_ref[...]
     inverse = inverse_ref[:, :1]
     mean = jnp.mean(scaled * x, axis=-1, keepdims=True)
     result = inverse * scaled - x * (inverse * inverse * inverse * mean)
     out_ref[...] = (cot_ref[...].astype(F32) + result).astype(BF16)
-
-
-def heads_finish(meta, g_chunks, x, inverse, gain, cotangent, buckets):
-    chunks, parts = len(g_chunks), len(g_chunks[0])
+    weight_copy.wait()
+
+
+def heads_finish(meta, g_slots, x, inverse, gain, cotangent, buckets):
+    parts = len(g_slots)
     rows, width = x.shape
     heads = width // HEAD_DIM
-    slots = [slot for g_slots in g_chunks for slot in g_slots]
+    weight_shape = (3, heads, HEAD_DIM // parts, HEAD_DIM)
     return pl.pallas_call(
-        functools.partial(heads_finish_kernel, parts, chunks),
+        functools.partial(heads_finish_kernel, parts),
         out_shape=(
             jax.ShapeDtypeStruct((rows, width), BF16),
-            jax.ShapeDtypeStruct((3, heads, HEAD_DIM // parts, HEAD_DIM), F32),
-            jax.ShapeDtypeStruct((heads, buckets // parts, HEAD_DIM), F32),
-        ),
-        in_specs=[SMEM_SPEC] + [VMEM_SPEC] * (len(slots) + 4),
-        out_specs=(VMEM_SPEC,) * 3,
-        scratch_shapes=[pltpu.VMEM((rows, width), F32)],
+            jax.ShapeDtypeStruct(weight_shape, F32),
+            jax.ShapeDtypeStruct((buckets // parts, heads), F32),
+        ),
+        in_specs=[SMEM_SPEC] + [VMEM_SPEC] * (parts + 4),
+        out_specs=(VMEM_SPEC, pl.BlockSpec(memory_space=pl.ANY), VMEM_SPEC),
+        scratch_shapes=[
+            pltpu.VMEM((rows, width), F32),
+            pltpu.VMEM(weight_shape, F32),
+            pltpu.SemaphoreType.DMA,
+        ],
         compiler_params=pltpu.CompilerParams(vmem_limit_bytes=VMEM_LIMIT),
         cost_estimate=pl.CostEstimate(flops=12 * rows * width, bytes_accessed=14 * rows * width, transcendentals=0),
         name="heads_finish",
-    )(meta, *slots, x, inverse, gain, cotangent)
+    )(meta, *g_slots, x, inverse, gain, cotangent)
 
 
 def offset_table(rel_bias):
@@ -907,15 +913,14 @@
         meta, a_slots, c_slots, norm_gain, offsets, onehot, o_sends[0], heads, 0, heads
     )
     g_sends, o_slots = lax.optimization_barrier((g_sends, o_slots))
-    g_chunks = [exchanged(g_sends, -1)]
+    g_slots = exchanged(g_sends, -1)
     output = place_columns(meta, o_slots)
     shares = memory_rows(meta, o_sends, o_slots[1:], final_gain[None], width, sections // 2)
     memory = spread_memory(shares, section, sections)
 
-    input_grad, weight_grad, bias_wide = heads_finish(
-        meta, g_chunks, stash[0], inverse_b, norm_gain, cotangent, buckets
-    )
-    bias_grad = bias_wide[:, :, 0].T
+    input_grad, weight_grad, bias_grad = heads_finish(
+        meta, g_slots, stash[0], inverse_b, norm_gain, cotangent, buckets
+    )
     return (
         output[None],
         input_grad[None],
@@ -998,7 +1003,7 @@
     even = width % (HEAD_DIM * parts) == 0 and HEAD_DIM % (32 * parts) == 0 and rows == 128
     sections = lax.axis_size("section")
     even = even and sections % 2 == 0
-    even = even and rel_bias.shape[1] == 8 * parts and rows * parts % (16 * sections) == 0
+    even = even and rel_bias.shape[1] == 8 * parts and width <= 128 * HEAD_DIM and rows * parts % (16 * sections) == 0
     chosen = heads_body if even else tokens_body
     return chosen(
         embedded, carried, stash, returned, loss_grad, qkv_weight, rel_bias, norm_gain, final_gain

time: 146 us -> 141 us (0.966)
  waiting for transfers between devices: 64.5 us -> 61.3 us
  local copies, waits for them, and re-layouts: 4.34 us -> 1.43 us
    ppermute x15, waiting for transfers between devices: 63.8 us -> 60.5 us  [exchanged(): lax.ppermute(sends[r], 'seq', [(i, (i + direction * r) % parts) for i in...]
    unnamed x22 -> x26, local copies, waits for them, and re-layouts: 2.96 us -> 0.76 us
  transfers between devices with their start and end apart: 21 -> 21, of which waited for: 8 -> 7; matrix products, arithmetic and copies ran while one was open for 2% -> 2% of each run, Pallas kernels for 17% -> 18%
where the time goes in v9:
time: 141 us; the launch traced here: 140 us
  waiting for transfers between devices  61.3 us (43%)
  starting transfers between devices  44.4 us (31%)
  Pallas kernels  30.1 us (21%)
  other arithmetic  2.2 us (2%)
  local copies, waits for them, and re-layouts  1.43 us (1%)
    ppermute x15, waiting for transfers between devices, exchanged(): lax.ppermute(sends[r], 'seq', [(i, (i + direction * r) % parts) for i in...  60.5 us
    ppermute x15, starting transfers between devices, exchanged(): lax.ppermute(sends[r], 'seq', [(i, (i + direction * r) % parts) for i in...  37.3 us
    pallas_call x1, Pallas kernels, heads_backward(): pl.pallas_call(functools.partial(heads_backward_kernel, parts, rows), out...  11.2 us
    pallas_call x1, Pallas kernels, heads_forward(): pl.pallas_call(functools.partial(heads_forward_kernel, parts, rows), out_...  6.94 us
    ppermute x2, starting transfers between devices, shifted(): lax.ppermute(value, axis, [(source, source + steps) for source in range(f...  3.83 us
    pallas_call x1, Pallas kernels, pack_stash(): pl.pallas_call(functools.partial(pack_stash_kernel, parts, 4), out_shape=...  3.63 us
    pallas_call x1, Pallas kernels, heads_finish(): pl.pallas_call(functools.partial(heads_finish_kernel, parts), out_shape=(...  3.49 us
  transfers between devices with their start and end apart: 21, of which 7 were waited for; matrix products, arithmetic and copies ran while one was open for 2% of the time, Pallas kernels for 18%

profile of v9, /device:TPU:0, one launch (start us, length us, event | category | flops | bytes accessed | tf_op | source)
XLA Modules:
  0.0 140.5 jit_solution(14596809841059697684)
XLA Ops:
  0.6 0.0 copy-start
  0.7 2.5 %collective-permute-start.3 = (bf16[128,3072]{1,0:T(8,128)(2,1)}, bf16[128,3072]{1,0:T(8,128)(2,1)S(1)}, u32[]{:S(2)}, u32[]{:S(2)}) collective-permute-start(bf16[128,3072]{1,0:T(8,128)(2,1)} %bitcast.24), channel_id=1, source_target_pairs={{0,4},{4,8},{8,12},{12,16},{16,20},{20,24},{24,28},{1,5},{5,9},{9,... | collective-permute-start | bytes 2359304 | tf_op jit(solution)/shard_map/ppermute | solution.py:864
  3.2 1.3 collective-permute-start.7
  4.5 0.6 pad_add_fusion.meta_ref
  5.1 3.6 %pack_stash.1 = (f32[128,128]{1,0:T(8,128)}, bf16[224,768]{1,0:T(8,128)(2,1)}, bf16[224,768]{1,0:T(8,128)(2,1)}, bf16[224,768]{1,0:T(8,128)(2,1)}, bf16[224,768]{1,0:T(8,128)(2,1)}) custom-call(s32[3]{0:T(128)} %pad_add_fusion.meta_ref, bf16[128,3072]{1,0:T(8,128)(2,1)} %bitcast.18, f32[1,3072]{1,0:T(1,128)} %refs_6_.1, bf16[3,24,32,128]{3,2,1,0:T(8,128)(2,1)} %bitcast.22), custom_call_target="tpu_custom_call" | custom-call | flops 1572864 | bytes 2359296 | tf_op jit(solution)/shard_map/pack_stash/pallas_call | solution.py:426
  8.7 2.5 %collective-permute-start = (bf16[224,768]{1,0:T(8,128)(2,1)}, bf16[224,768]{1,0:T(8,128)(2,1)S(1)}, u32[]{:S(2)}, u32[]{:S(2)}) collective-permute-start(bf16[224,768]{1,0:T(8,128)(2,1)} %get-tuple-element.52), channel_id=1, source_target_pairs={{0,1},{1,2},{2,3},{3,0},{4,5},{5,6},{6,7},{7,4},{8,9},{9,10},{10,1... | collective-permute-start | bytes 1032200 | tf_op jit(solution)/shard_map/ppermute | solution.py:892
  11.2 2.6 %collective-permute-start.1 = (bf16[224,768]{1,0:T(8,128)(2,1)}, bf16[224,768]{1,0:T(8,128)(2,1)S(1)}, u32[]{:S(2)}, u32[]{:S(2)}) collective-permute-start(bf16[224,768]{1,0:T(8,128)(2,1)} %get-tuple-element.53), channel_id=1, source_target_pairs={{0,2},{1,3},{2,0},{3,1},{4,6},{5,7},{6,4},{7,5},{8,10},{9,11},{10,... | collective-permute-start | bytes 1032200 | tf_op jit(solution)/shard_map/ppermute | solution.py:892
  13.8 1.3 collective-permute-start.2
  15.1 0.0 collective-permute-done.3.inner_ref
  15.2 0.0 copy-done.2
  15.2 0.9 pack_inbound.1
  16.1 0.0 copy-start.4
  16.1 0.0 copy-start.5
  16.1 0.7 collective-permute-start.4
  16.9 0.0 collective-permute-done.7.inner_ref
  16.9 0.3 collective-permute-start.5
  17.2 0.0 copy-done.3
  17.2 1.4 pack_cotangent.1
  18.6 2.2 %collective-permute-done.refs_1_ = bf16[224,768]{1,0:T(8,128)(2,1)S(1)} collective-permute-done((bf16[224,768]{1,0:T(8,128)(2,1)}, bf16[224,768]{1,0:T(8,128)(2,1)S(1)}, u32[]{:S(2)}, u32[]{:S(2)}) %collective-permute-start) | collective-permute-done | bytes 344096 | tf_op jit(solution)/shard_map/ppermute | solution.py:892
  20.8 2.1 %collective-permute-start.6 = (bf16[136,768]{1,0:T(8,128)(2,1)S(1)}, bf16[136,768]{1,0:T(8,128)(2,1)S(1)}, u32[]{:S(2)}, u32[]{:S(2)}) collective-permute-start(bf16[136,768]{1,0:T(8,128)(2,1)S(1)} %get-tuple-element.58), channel_id=1, source_target_pairs={{0,3},{1,0},{2,1},{3,2},{4,7},{5,4},{6,5},{7,6},{8,11},{9,8},{10,9... | collective-permute-start | bytes 626696 | tf_op jit(solution)/shard_map/ppermute | solution.py:892
  22.9 15.8 %collective-permute-done.1.refs_2_ = bf16[224,768]{1,0:T(8,128)(2,1)S(1)} collective-permute-done((bf16[224,768]{1,0:T(8,128)(2,1)}, bf16[224,768]{1,0:T(8,128)(2,1)S(1)}, u32[]{:S(2)}, u32[]{:S(2)}) %collective-permute-start.1) | collective-permute-done | bytes 344096 | tf_op jit(solution)/shard_map/ppermute | solution.py:892
  38.8 12.4 %collective-permute-start.8 = (bf16[128,768]{1,0:T(8,128)(2,1)S(1)}, bf16[128,768]{1,0:T(8,128)(2,1)S(1)}, u32[]{:S(2)}, u32[]{:S(2)}) collective-permute-start(bf16[128,768]{1,0:T(8,128)(2,1)S(1)} %get-tuple-element.64), channel_id=1, source_target_pairs={{0,1},{1,2},{2,3},{3,0},{4,5},{5,6},{6,7},{7,4},{8,9},{9,10},{10,1... | collective-permute-start | bytes 589832 | tf_op jit(solution)/shard_map/ppermute | solution.py:892
  51.2 0.0 collective-permute-done.2.refs_3_
  51.2 3.3 %collective-permute-start.9 = (bf16[128,768]{1,0:T(8,128)(2,1)S(1)}, bf16[128,768]{1,0:T(8,128)(2,1)S(1)}, u32[]{:S(2)}, u32[]{:S(2)}) collective-permute-start(bf16[128,768]{1,0:T(8,128)(2,1)S(1)} %get-tuple-element.65), channel_id=1, source_target_pairs={{0,2},{1,3},{2,0},{3,1},{4,6},{5,7},{6,4},{7,5},{8,10},{9,11},{10,... | collective-permute-start | bytes 589832 | tf_op jit(solution)/shard_map/ppermute | solution.py:892
  54.5 0.0 collective-permute-done.4.refs_5_
  54.5 1.9 %collective-permute-start.10 = (bf16[128,768]{1,0:T(8,128)(2,1)S(1)}, bf16[128,768]{1,0:T(8,128)(2,1)S(1)}, u32[]{:S(2)}, u32[]{:S(2)}) collective-permute-start(bf16[128,768]{1,0:T(8,128)(2,1)S(1)} %get-tuple-element.66), channel_id=1, source_target_pairs={{0,3},{1,0},{2,1},{3,2},{4,7},{5,4},{6,5},{7,6},{8,11},{9,8},{10,9... | collective-permute-start | bytes 589832 | tf_op jit(solution)/shard_map/ppermute | solution.py:892
  56.4 0.0 copy-done
  56.4 0.2 fusion
  56.6 0.0 copy-start.9
  56.6 9.7 %collective-permute-done.5.refs_6_ = bf16[136,768]{1,0:T(8,128)(2,1)S(1)} collective-permute-done((bf16[136,768]{1,0:T(8,128)(2,1)S(1)}, bf16[136,768]{1,0:T(8,128)(2,1)S(1)}, u32[]{:S(2)}, u32[]{:S(2)}) %collective-permute-start.5) | collective-permute-done | bytes 208928 | tf_op jit(solution)/shard_map/ppermute | solution.py:892
  66.3 0.0 collective-permute-done.6.refs_7_
  66.3 0.0 copy-done.4
  66.3 6.9 %heads_forward.1 = (bf16[136,768]{1,0:T(8,128)(2,1)S(1)}, bf16[136,768]{1,0:T(8,128)(2,1)S(1)}, bf16[136,768]{1,0:T(8,128)(2,1)S(1)}, bf16[136,768]{1,0:T(8,128)(2,1)S(1)}) custom-call(s32[3]{0:T(128)S(1)} %copy-done.7, bf16[224,768]{1,0:T(8,128)(2,1)S(1)} %copy-done.4, bf16[224,768]{1,0:T(8,128)(2,1)S(1)} %collective-permute-done.refs_1_, ...), custom_call_target="tpu_custom_call" | custom-call | flops 3072 | bytes 512 | tf_op jit(solution)/shard_map/heads_forward/pallas_call | solution.py:702
  73.3 0.0 collective-permute-done.8.refs_5_
  73.3 1.7 %collective-permute-done.9.refs_6_ = bf16[128,768]{1,0:T(8,128)(2,1)S(1)} collective-permute-done((bf16[128,768]{1,0:T(8,128)(2,1)S(1)}, bf16[128,768]{1,0:T(8,128)(2,1)S(1)}, u32[]{:S(2)}, u32[]{:S(2)}) %collective-permute-start.9) | collective-permute-done | bytes 196640 | tf_op jit(solution)/shard_map/ppermute | solution.py:892
  75.0 0.0 collective-permute-done.10.refs_7_
  75.0 4.7 %collective-permute-start.11 = (bf16[136,768]{1,0:T(8,128)(2,1)S(1)}, bf16[136,768]{1,0:T(8,128)(2,1)S(1)}, u32[]{:S(2)}, u32[]{:S(2)}) collective-permute-start(bf16[136,768]{1,0:T(8,128)(2,1)S(1)} %get-tuple-element.76.refs_1_), channel_id=1, source_target_pairs={{0,3},{1,0},{2,1},{3,2},{4,7},{5,4},{6,5},{7,6},{8,11},{9,8},{10,9... | collective-permute-start | bytes 626696 | tf_op jit(solution)/shard_map/ppermute | solution.py:892
  79.7 1.5 %collective-permute-start.12 = (bf16[136,768]{1,0:T(8,128)(2,1)S(1)}, bf16[136,768]{1,0:T(8,128)(2,1)S(1)}, u32[]{:S(2)}, u32[]{:S(2)}) collective-permute-start(bf16[136,768]{1,0:T(8,128)(2,1)S(1)} %get-tuple-element.77.refs_2_), channel_id=1, source_target_pairs={{0,2},{1,3},{2,0},{3,1},{4,6},{5,7},{6,4},{7,5},{8,10},{9,11},{10,... | collective-permute-start | bytes 626696 | tf_op jit(solution)/shard_map/ppermute | solution.py:892
  81.3 0.0 collective-permute-start.13
  81.3 11.2 %heads_backward.1 = (bf16[232,768]{1,0:T(8,128)(2,1)S(1)}, bf16[232,768]{1,0:T(8,128)(2,1)}, bf16[232,768]{1,0:T(8,128)(2,1)}, bf16[232,768]{1,0:T(8,128)(2,1)}, f32[1,768]{1,0:T(1,128)}) custom-call(s32[3]{0:T(128)S(1)} %copy-done.7, bf16[224,768]{1,0:T(8,128)(2,1)S(1)} %copy-done.4, bf16[224,768]{1,0:T(8,128)(2,1)S(1)} %collective-permute-done.refs_1_, ...), custom_call_target="tpu_custom_call" | custom-call | flops 1228800000 | bytes 393216 | tf_op jit(solution)/shard_map/heads_backward/pallas_call | solution.py:603
  92.5 0.0 collective-permute-done.11.refs_1_.refs_4_
  92.5 7.3 %collective-permute-done.12.refs_2_.refs_5_ = bf16[136,768]{1,0:T(8,128)(2,1)S(1)} collective-permute-done((bf16[136,768]{1,0:T(8,128)(2,1)S(1)}, bf16[136,768]{1,0:T(8,128)(2,1)S(1)}, u32[]{:S(2)}, u32[]{:S(2)}) %collective-permute-start.12) | collective-permute-done | bytes 208928 | tf_op jit(solution)/shard_map/ppermute | solution.py:892
  99.8 0.0 collective-permute-done.13.refs_3_.refs_6_
  99.9 0.9 memory_rows.1
  100.8 0.7 collective-permute-start.17
  101.5 0.7 collective-permute-start.18
  102.2 0.7 collective-permute-start.19
  102.8 0.1 collective-permute-start.14
  102.9 1.9 %collective-permute-start.15 = (bf16[232,768]{1,0:T(8,128)(2,1)}, bf16[232,768]{1,0:T(8,128)(2,1)S(1)}, u32[]{:S(2)}, u32[]{:S(2)}) collective-permute-start(bf16[232,768]{1,0:T(8,128)(2,1)} %get-tuple-element.85), channel_id=1, source_target_pairs={{0,2},{1,3},{2,0},{3,1},{4,6},{5,7},{6,4},{7,5},{8,10},{9,11},{10,... | collective-permute-start | bytes 1069064 | tf_op jit(solution)/shard_map/ppermute | solution.py:892
  104.8 0.0 collective-permute-done.17
  104.8 2.0 %collective-permute-start.16 = (bf16[232,768]{1,0:T(8,128)(2,1)}, bf16[232,768]{1,0:T(8,128)(2,1)}, u32[]{:S(2)}, u32[]{:S(2)}) collective-permute-start(bf16[232,768]{1,0:T(8,128)(2,1)} %get-tuple-element.86), channel_id=1, source_target_pairs={{0,1},{1,2},{2,3},{3,0},{4,5},{5,6},{6,7},{7,4},{8,9},{9,10},{10,1... | collective-permute-start | bytes 1069064 | tf_op jit(solution)/shard_map/ppermute | solution.py:892
  106.7 0.0 collective-permute-done.18
  106.8 0.0 collective-permute-done.19
  106.8 0.1 add_add_fusion
  106.8 0.7 copy-done.10
  107.5 0.6 slice.8
  108.2 1.3 collective-permute-start.20
  109.5 1.5 %place_columns.1 = bf16[128,3072]{1,0:T(8,128)(2,1)} custom-call(s32[3]{0:T(128)S(1)} %copy-done.7, bf16[136,768]{1,0:T(8,128)(2,1)S(1)} %get-tuple-element.79.refs_11_.refs_0_, bf16[136,768]{1,0:T(8,128)(2,1)S(1)} %collective-permute-done.11.refs_1_.refs_4_, bf16[136,768]{1,0:T(8,128)(2,1)S(1)} %collective-permute-done.12.refs_2_.refs_5_, ...), custom_call_target="tpu_custom_call" | custom-call | bytes 128 | tf_op jit(solution)/shard_map/place_columns/pallas_call | solution.py:783
  111.0 0.7 collective-permute-done.20
  111.7 1.5 %slice_select_fusion = bf16[64,768]{1,0:T(8,128)(2,1)} fusion(bf16[64,768]{1,0:T(8,128)(2,1)} %collective-permute-done.20, bf16[128,768]{1,0:T(8,128)(2,1)S(1)} %copy-done.11, pred[]{:T(512)S(6)} %eq.14), kind=kLoop, calls=%fused_computation.3 | loop fusion | flops 49152 | bytes 294913 | tf_op jit(solution)/shard_map/jit(_where)/select_n | solution.py:874
  113.2 0.0 collective-permute-done.14.refs_1_
  113.2 23.7 %collective-permute-done.15.refs_2_ = bf16[232,768]{1,0:T(8,128)(2,1)S(1)} collective-permute-done((bf16[232,768]{1,0:T(8,128)(2,1)}, bf16[232,768]{1,0:T(8,128)(2,1)S(1)}, u32[]{:S(2)}, u32[]{:S(2)}) %collective-permute-start.15) | collective-permute-done | bytes 356384 | tf_op jit(solution)/shard_map/ppermute | solution.py:892
  137.0 0.0 collective-permute-done.16.refs_3_
  137.0 3.5 %heads_finish.1 = (bf16[128,3072]{1,0:T(8,128)(2,1)}, f32[3,24,32,128]{3,2,1,0:T(8,128)}, f32[8,24]{1,0:T(8,128)}) custom-call(s32[3]{0:T(128)S(1)} %copy-done.7, bf16[232,768]{1,0:T(8,128)(2,1)S(1)} %get-tuple-element.83.refs_0_, bf16[232,768]{1,0:T(8,128)(2,1)S(1)} %collective-permute-done.14.refs_1_, ...), custom_call_target="tpu_custom_call" | custom-call | flops 4718592 | bytes 5505024 | tf_op jit(solution)/shard_map/heads_finish/pallas_call | solution.py:834
  (19 shorter events, 0.1 us)
Async XLA Ops:
  0.6 55.7 %copy-start = (f32[1,32,24]{1,2,0:T(8,128)S(1)}, f32[1,32,24]{1,2,0:T(8,128)}, u32[]{:S(2)}) copy-start(f32[1,32,24]{1,2,0:T(8,128)} %param.17) | copy-start | bytes 9220
  0.6 14.5 %copy-start.2 = (bf16[128,3072]{1,0:T(8,128)(2,1)S(1)}, bf16[128,3072]{1,0:T(8,128)(2,1)}, u32[]{:S(2)}) copy-start(bf16[128,3072]{1,0:T(8,128)(2,1)} %edge_ref.2) | copy-start | bytes 2359300
  0.7 14.5 %collective-permute-start.3 = (bf16[128,3072]{1,0:T(8,128)(2,1)}, bf16[128,3072]{1,0:T(8,128)(2,1)S(1)}, u32[]{:S(2)}, u32[]{:S(2)}) collective-permute-start(bf16[128,3072]{1,0:T(8,128)(2,1)} %bitcast.24), channel_id=1, source_target_pairs={{0,4},{4,8},{8,12},{12,16},{16,20},{20,24},{24,28},{1,5},{5,9},{9,... | collective-permute-start | bytes 2359304 | tf_op jit(solution)/shard_map/ppermute | solution.py:864
  3.2 13.7 %collective-permute-start.7 = (bf16[128,3072]{1,0:T(8,128)(2,1)}, bf16[128,3072]{1,0:T(8,128)(2,1)S(1)}, u32[]{:S(2)}, u32[]{:S(2)}) collective-permute-start(bf16[128,3072]{1,0:T(8,128)(2,1)} %bitcast.25), channel_id=1, source_target_pairs={{4,0},{8,4},{12,8},{16,12},{20,16},{24,20},{28,24},{5,1},{9,5},{13... | collective-permute-start | bytes 2359304 | tf_op jit(solution)/shard_map/ppermute | solution.py:864
  5.1 10.1 %copy-start.7 = (s32[3]{0:T(128)S(1)}, s32[3]{0:T(128)}, u32[]{:S(2)}) copy-start(s32[3]{0:T(128)} %pad_add_fusion.meta_ref) | copy-start | bytes 40
  5.1 12.1 %copy-start.3 = (bf16[128,3072]{1,0:T(8,128)(2,1)S(1)}, bf16[128,3072]{1,0:T(8,128)(2,1)}, u32[]{:S(2)}) copy-start(bf16[128,3072]{1,0:T(8,128)(2,1)} %edge_ref.3) | copy-start | bytes 2359300
  8.7 12.1 %collective-permute-start = (bf16[224,768]{1,0:T(8,128)(2,1)}, bf16[224,768]{1,0:T(8,128)(2,1)S(1)}, u32[]{:S(2)}, u32[]{:S(2)}) collective-permute-start(bf16[224,768]{1,0:T(8,128)(2,1)} %get-tuple-element.52), channel_id=1, source_target_pairs={{0,1},{1,2},{2,3},{3,0},{4,5},{5,6},{6,7},{7,4},{8,9},{9,10},{10,1... | collective-permute-start | bytes 1032200 | tf_op jit(solution)/shard_map/ppermute | solution.py:892
  11.2 27.6 %collective-permute-start.1 = (bf16[224,768]{1,0:T(8,128)(2,1)}, bf16[224,768]{1,0:T(8,128)(2,1)S(1)}, u32[]{:S(2)}, u32[]{:S(2)}) collective-permute-start(bf16[224,768]{1,0:T(8,128)(2,1)} %get-tuple-element.53), channel_id=1, source_target_pairs={{0,2},{1,3},{2,0},{3,1},{4,6},{5,7},{6,4},{7,5},{8,10},{9,11},{10,... | collective-permute-start | bytes 1032200 | tf_op jit(solution)/shard_map/ppermute | solution.py:892
  13.8 37.4 %collective-permute-start.2 = (bf16[224,768]{1,0:T(8,128)(2,1)}, bf16[224,768]{1,0:T(8,128)(2,1)S(1)}, u32[]{:S(2)}, u32[]{:S(2)}) collective-permute-start(bf16[224,768]{1,0:T(8,128)(2,1)} %get-tuple-element.54), channel_id=1, source_target_pairs={{0,3},{1,0},{2,1},{3,2},{4,7},{5,4},{6,5},{7,6},{8,11},{9,8},{10,9... | collective-permute-start | bytes 1032200 | tf_op jit(solution)/shard_map/ppermute | solution.py:892
  16.1 40.3 %copy-start.12 = (f32[256,32]{1,0:T(8,128)S(1)}, f32[256,32]{1,0:T(8,128)}, u32[]{:S(2)}) copy-start(f32[256,32]{1,0:T(8,128)} %constant.35.clone) | copy-start | bytes 98308
  16.1 50.2 %copy-start.4 = (bf16[224,768]{1,0:T(8,128)(2,1)S(1)}, bf16[224,768]{1,0:T(8,128)(2,1)}, u32[]{:S(2)}) copy-start(bf16[224,768]{1,0:T(8,128)(2,1)} %get-tuple-element.51.refs_0_) | copy-start | bytes 1032196
  16.1 50.2 %copy-start.5 = (f32[1,3072]{1,0:T(1,128)S(1)}, f32[1,3072]{1,0:T(1,128)}, u32[]{:S(2)}) copy-start(f32[1,3072]{1,0:T(1,128)} %refs_6_.1) | copy-start | bytes 36868
  16.1 38.3 %collective-permute-start.4 = (bf16[136,768]{1,0:T(8,128)(2,1)S(1)}, bf16[136,768]{1,0:T(8,128)(2,1)S(1)}, u32[]{:S(2)}, u32[]{:S(2)}) collective-permute-start(bf16[136,768]{1,0:T(8,128)(2,1)S(1)} %get-tuple-element.56), channel_id=1, source_target_pairs={{0,1},{1,2},{2,3},{3,0},{4,5},{5,6},{6,7},{7,4},{8,9},{9,10},{10,1... | collective-permute-start | bytes 626696 | tf_op jit(solution)/shard_map/ppermute | solution.py:892
  16.9 49.4 %collective-permute-start.5 = (bf16[136,768]{1,0:T(8,128)(2,1)S(1)}, bf16[136,768]{1,0:T(8,128)(2,1)S(1)}, u32[]{:S(2)}, u32[]{:S(2)}) collective-permute-start(bf16[136,768]{1,0:T(8,128)(2,1)S(1)} %get-tuple-element.57), channel_id=1, source_target_pairs={{0,2},{1,3},{2,0},{3,1},{4,6},{5,7},{6,4},{7,5},{8,10},{9,11},{10,... | collective-permute-start | bytes 626696 | tf_op jit(solution)/shard_map/ppermute | solution.py:892
  20.8 45.5 %collective-permute-start.6 = (bf16[136,768]{1,0:T(8,128)(2,1)S(1)}, bf16[136,768]{1,0:T(8,128)(2,1)S(1)}, u32[]{:S(2)}, u32[]{:S(2)}) collective-permute-start(bf16[136,768]{1,0:T(8,128)(2,1)S(1)} %get-tuple-element.58), channel_id=1, source_target_pairs={{0,3},{1,0},{2,1},{3,2},{4,7},{5,4},{6,5},{7,6},{8,11},{9,8},{10,9... | collective-permute-start | bytes 626696 | tf_op jit(solution)/shard_map/ppermute | solution.py:892
  38.8 34.5 %collective-permute-start.8 = (bf16[128,768]{1,0:T(8,128)(2,1)S(1)}, bf16[128,768]{1,0:T(8,128)(2,1)S(1)}, u32[]{:S(2)}, u32[]{:S(2)}) collective-permute-start(bf16[128,768]{1,0:T(8,128)(2,1)S(1)} %get-tuple-element.64), channel_id=1, source_target_pairs={{0,1},{1,2},{2,3},{3,0},{4,5},{5,6},{6,7},{7,4},{8,9},{9,10},{10,1... | collective-permute-start | bytes 589832 | tf_op jit(solution)/shard_map/ppermute | solution.py:892
  51.2 23.8 %collective-permute-start.9 = (bf16[128,768]{1,0:T(8,128)(2,1)S(1)}, bf16[128,768]{1,0:T(8,128)(2,1)S(1)}, u32[]{:S(2)}, u32[]{:S(2)}) collective-permute-start(bf16[128,768]{1,0:T(8,128)(2,1)S(1)} %get-tuple-element.65), channel_id=1, source_target_pairs={{0,2},{1,3},{2,0},{3,1},{4,6},{5,7},{6,4},{7,5},{8,10},{9,11},{10,... | collective-permute-start | bytes 589832 | tf_op jit(solution)/shard_map/ppermute | solution.py:892
  54.5 20.5 %collective-permute-start.10 = (bf16[128,768]{1,0:T(8,128)(2,1)S(1)}, bf16[128,768]{1,0:T(8,128)(2,1)S(1)}, u32[]{:S(2)}, u32[]{:S(2)}) collective-permute-start(bf16[128,768]{1,0:T(8,128)(2,1)S(1)} %get-tuple-element.66), channel_id=1, source_target_pairs={{0,3},{1,0},{2,1},{3,2},{4,7},{5,4},{6,5},{7,6},{8,11},{9,8},{10,9... | collective-permute-start | bytes 589832 | tf_op jit(solution)/shard_map/ppermute | solution.py:892
  56.6 24.7 %copy-start.9 = (f32[32,256]{1,0:T(8,128)S(1)}, f32[32,256]{1,0:T(8,128)}, u32[]{:S(2)}) copy-start(f32[32,256]{1,0:T(8,128)} %constant.36.clone.refs_10_) | copy-start | bytes 98308
  75.0 24.8 %copy-start.8 = (f32[3072]{0:T(1024)S(1)}, f32[3072]{0:T(1024)}, u32[]{:S(2)}) copy-start(f32[3072]{0:T(1024)} %param.19) | copy-start | bytes 36868
  75.0 17.5 %collective-permute-start.11 = (bf16[136,768]{1,0:T(8,128)(2,1)S(1)}, bf16[136,768]{1,0:T(8,128)(2,1)S(1)}, u32[]{:S(2)}, u32[]{:S(2)}) collective-permute-start(bf16[136,768]{1,0:T(8,128)(2,1)S(1)} %get-tuple-element.76.refs_1_), channel_id=1, source_target_pairs={{0,3},{1,0},{2,1},{3,2},{4,7},{5,4},{6,5},{7,6},{8,11},{9,8},{10,9... | collective-permute-start | bytes 626696 | tf_op jit(solution)/shard_map/ppermute | solution.py:892
  79.7 20.1 %collective-permute-start.12 = (bf16[136,768]{1,0:T(8,128)(2,1)S(1)}, bf16[136,768]{1,0:T(8,128)(2,1)S(1)}, u32[]{:S(2)}, u32[]{:S(2)}) collective-permute-start(bf16[136,768]{1,0:T(8,128)(2,1)S(1)} %get-tuple-element.77.refs_2_), channel_id=1, source_target_pairs={{0,2},{1,3},{2,0},{3,1},{4,6},{5,7},{6,4},{7,5},{8,10},{9,11},{10,... | collective-permute-start | bytes 626696 | tf_op jit(solution)/shard_map/ppermute | solution.py:892
  81.3 18.6 %collective-permute-start.13 = (bf16[136,768]{1,0:T(8,128)(2,1)S(1)}, bf16[136,768]{1,0:T(8,128)(2,1)S(1)}, u32[]{:S(2)}, u32[]{:S(2)}) collective-permute-start(bf16[136,768]{1,0:T(8,128)(2,1)S(1)} %get-tuple-element.78.refs_3_), channel_id=1, source_target_pairs={{0,1},{1,2},{2,3},{3,0},{4,5},{5,6},{6,7},{7,4},{8,9},{9,10},{10,1... | collective-permute-start | bytes 626696 | tf_op jit(solution)/shard_map/ppermute | solution.py:892
  100.8 4.0 %collective-permute-start.17 = (bf16[128,768]{1,0:T(8,128)(2,1)S(1)}, bf16[128,768]{1,0:T(8,128)(2,1)S(1)}, u32[]{:S(2)}, u32[]{:S(2)}) collective-permute-start(bf16[128,768]{1,0:T(8,128)(2,1)S(1)} %get-tuple-element.93), channel_id=1, source_target_pairs={{28,4},{29,5},{30,6},{31,7}} | collective-permute-start | bytes 589832 | tf_op jit(solution)/shard_map/ppermute | solution.py:871
  101.5 5.3 %collective-permute-start.18 = (bf16[128,768]{1,0:T(8,128)(2,1)S(1)}, bf16[128,768]{1,0:T(8,128)(2,1)S(1)}, u32[]{:S(2)}, u32[]{:S(2)}) collective-permute-start(bf16[128,768]{1,0:T(8,128)(2,1)S(1)} %get-tuple-element.94), channel_id=1, source_target_pairs={{28,12},{29,13},{30,14},{31,15}} | collective-permute-start | bytes 589832 | tf_op jit(solution)/shard_map/ppermute | solution.py:871
  102.2 4.6 %collective-permute-start.19 = (bf16[128,768]{1,0:T(8,128)(2,1)S(1)}, bf16[128,768]{1,0:T(8,128)(2,1)S(1)}, u32[]{:S(2)}, u32[]{:S(2)}) collective-permute-start(bf16[128,768]{1,0:T(8,128)(2,1)S(1)} %get-tuple-element.95), channel_id=1, source_target_pairs={{28,20},{29,21},{30,22},{31,23}} | collective-permute-start | bytes 589832 | tf_op jit(solution)/shard_map/ppermute | solution.py:871
  102.8 10.4 %collective-permute-start.14 = (bf16[232,768]{1,0:T(8,128)(2,1)}, bf16[232,768]{1,0:T(8,128)(2,1)S(1)}, u32[]{:S(2)}, u32[]{:S(2)}) collective-permute-start(bf16[232,768]{1,0:T(8,128)(2,1)} %get-tuple-element.84), channel_id=1, source_target_pairs={{0,3},{1,0},{2,1},{3,2},{4,7},{5,4},{6,5},{7,6},{8,11},{9,8},{10,9... | collective-permute-start | bytes 1069064 | tf_op jit(solution)/shard_map/ppermute | solution.py:892
  102.9 34.0 %collective-permute-start.15 = (bf16[232,768]{1,0:T(8,128)(2,1)}, bf16[232,768]{1,0:T(8,128)(2,1)S(1)}, u32[]{:S(2)}, u32[]{:S(2)}) collective-permute-start(bf16[232,768]{1,0:T(8,128)(2,1)} %get-tuple-element.85), channel_id=1, source_target_pairs={{0,2},{1,3},{2,0},{3,1},{4,6},{5,7},{6,4},{7,5},{8,10},{9,11},{10,... | collective-permute-start | bytes 1069064 | tf_op jit(solution)/shard_map/ppermute | solution.py:892
  104.8 32.2 %collective-permute-start.16 = (bf16[232,768]{1,0:T(8,128)(2,1)}, bf16[232,768]{1,0:T(8,128)(2,1)}, u32[]{:S(2)}, u32[]{:S(2)}) collective-permute-start(bf16[232,768]{1,0:T(8,128)(2,1)} %get-tuple-element.86), channel_id=1, source_target_pairs={{0,1},{1,2},{2,3},{3,0},{4,5},{5,6},{6,7},{7,4},{8,9},{9,10},{10,1... | collective-permute-start | bytes 1069064 | tf_op jit(solution)/shard_map/ppermute | solution.py:892
  106.8 0.7 copy-start.10
  107.5 29.4 %copy-start.1 = (bf16[1,128,3072]{2,1,0:T(8,128)(2,1)S(1)}, bf16[1,128,3072]{2,1,0:T(8,128)(2,1)}, u32[]{:S(2)}) copy-start(bf16[1,128,3072]{2,1,0:T(8,128)(2,1)} %param.13) | copy-start | bytes 2359300
  108.2 3.5 %collective-permute-start.20 = (bf16[64,768]{1,0:T(8,128)(2,1)}, bf16[64,768]{1,0:T(8,128)(2,1)}, u32[]{:S(2)}, u32[]{:S(2)}) collective-permute-start(bf16[64,768]{1,0:T(8,128)(2,1)} %slice.8), channel_id=1, source_target_pairs={{4,0},{12,8},{20,16},{28,24},{5,1},{13,9},{21,17},{29,25},{6,2},{1... | collective-permute-start | bytes 294920 | tf_op jit(solution)/shard_map/ppermute | solution.py:873
  109.5 2.2 %copy-start.11 = (bf16[128,768]{1,0:T(8,128)(2,1)S(1)}, bf16[128,768]{1,0:T(8,128)(2,1)}, u32[]{:S(2)}) copy-start(bf16[128,768]{1,0:T(8,128)(2,1)} %copy-done.10) | copy-start | bytes 589828
  109.5 27.5 %copy-start.6 = (f32[128,128]{1,0:T(8,128)S(1)}, f32[128,128]{1,0:T(8,128)}, u32[]{:S(2)}) copy-start(f32[128,128]{1,0:T(8,128)} %get-tuple-element.87.refs_5_) | copy-start | bytes 196612

commit v10 on v9

--- a/solution.py
+++ b/solution.py
@@ -640,7 +640,7 @@
     a_refs, i_refs = refs[:parts], refs[parts : 2 * parts]
     gain_ref, offset_ref = refs[2 * parts : 2 * parts + 2]
     out_refs = refs[2 * parts + 2 : 3 * parts + 2]
-    inverse_ref, x_ref, weight_ref, made_ref, square_ref = refs[3 * parts + 2 :]
+    sums_ref, inverse_ref, x_ref, weight_ref, made_ref, square_ref = refs[3 * parts + 2 :]
     tokens = rows * parts
     gather_rows(meta_ref, i_refs, rows, x_ref)
     gather_weight(meta_ref, a_refs, rows, weight_ref)
@@ -672,26 +672,12 @@
 
     for r, out_ref in enumerate(out_refs):
         source = lax.rem(meta_ref[0] + parts - r, parts)
-        out_ref[:rows] = made_ref[pl.ds(pl.multiple_of(source * rows, rows), rows)]
-
-    @pl.when(pl.program_id(0) < pl.num_programs(0) - 1)
-    def no_sums():
-        for out_ref in out_refs:
-            out_ref[rows:] = jnp.zeros((EXTRA, HEAD_DIM), BF16)
+        out_ref[...] = made_ref[pl.ds(pl.multiple_of(source * rows, rows), rows)]
 
     @pl.when(pl.program_id(0) == pl.num_programs(0) - 1)
     def last_head():
-        rest = jnp.sum(jnp.transpose(square_ref[...]), axis=0, keepdims=True)
-        at_row = lax.broadcasted_iota(jnp.int32, (EXTRA, rows), 0)
-        tail = jnp.zeros((EXTRA, rows), F32)
-        for k in range(2):
-            piece = rest.astype(BF16).astype(F32)
-            rest = rest - piece
-            for part in range(parts):
-                row = jnp.broadcast_to(piece[:, part * rows : (part + 1) * rows], (EXTRA, rows))
-                tail = jnp.where(at_row == 2 * part + k, row, tail)
-        for out_ref in out_refs:
-            out_ref[rows:] = tail.astype(BF16)
+        total = jnp.sum(jnp.transpose(square_ref[...]), axis=0, keepdims=True)
+        sums_ref[...] = jnp.broadcast_to(total, sums_ref.shape)
 
 
 def heads_forward(meta, a_slots, i_slots, gain, offsets, heads, rows):
@@ -702,7 +688,8 @@
     return pl.pallas_call(
         functools.partial(heads_forward_kernel, parts, rows),
         out_shape=(
-            *[jax.ShapeDtypeStruct((rows + EXTRA, width), BF16) for r in range(parts)],
+            *[jax.ShapeDtypeStruct((rows, width), BF16) for r in range(parts)],
+            jax.ShapeDtypeStruct((8, tokens), F32),
         ),
         grid_spec=pltpu.PrefetchScalarGridSpec(
             num_scalar_prefetch=1,
@@ -713,7 +700,10 @@
                 whole_column(1, heads),
                 offset_spec(heads),
             ],
-            out_specs=(head_column(rows + EXTRA),) * parts,
+            out_specs=(
+                *[head_column(rows)] * parts,
+                pl.BlockSpec((8, tokens), lambda i, meta: (0, 0)),
+            ),
             scratch_shapes=[
                 pltpu.VMEM((tokens, HEAD_DIM), F32),
                 pltpu.VMEM((tokens, HEAD_DIM), BF16),
@@ -731,22 +721,19 @@
 
 
 def memory_kernel(parts, width, meta_ref, *refs):
-    out_refs, other_refs = refs[:parts], refs[parts : 2 * parts - 1]
-    gain_ref, *share_refs, memory_ref = refs[2 * parts - 1 :]
+    out_refs, sum_refs = refs[:parts], refs[parts : 2 * parts]
+    gain_ref, *share_refs, memory_ref = refs[2 * parts :]
     wide = memory_ref.shape[1]
     rows = memory_ref.shape[0] // parts
-    total = None
-    for ref in (out_refs[0], *other_refs):
-        tail = ref[rows:, wide - rows :].astype(F32)
-        pieces = [tail[2 * p : 2 * p + 1] + tail[2 * p + 1 : 2 * p + 2] for p in range(parts)]
-        row = jnp.concatenate(pieces, axis=1)
-        total = row if total is None else total + row
+    total = sum_refs[0][:1]
+    for sum_ref in sum_refs[1:]:
+        total = total + sum_ref[:1]
     inverse = lax.rsqrt(total / width + eps_norm)
     gain = gain_ref[:, pl.ds(pl.multiple_of(meta_ref[0] * wide, 128), wide)]
     spread_inverse = jnp.transpose(jnp.broadcast_to(inverse, (128, inverse.shape[1])))
     for r, out_ref in enumerate(out_refs):
         source = lax.rem(meta_ref[0] + parts - r, parts)
-        memory_ref[pl.ds(pl.multiple_of(source * rows, rows), rows)] = out_ref[:rows]
+        memory_ref[pl.ds(pl.multiple_of(source * rows, rows), rows)] = out_ref[...]
     made = memory_ref[...].astype(F32)
     memory_ref[...] = (made * spread_inverse[:, :1] * gain).astype(BF16)
     for k, share_ref in enumerate(share_refs):
@@ -754,41 +741,41 @@
         share_ref[...] = memory_ref[k * size : (k + 1) * size]
 
 
-def memory_rows(meta, outs, others, gain, width, shares):
+def memory_rows(meta, outs, sums, gain, width, shares):
     parts = len(outs)
-    rows, wide = outs[0].shape[0] - EXTRA, outs[0].shape[1]
+    rows, wide = outs[0].shape
     return pl.pallas_call(
         functools.partial(memory_kernel, parts, width),
         out_shape=[jax.ShapeDtypeStruct((rows * parts // shares, wide), BF16)] * shares,
-        in_specs=[SMEM_SPEC] + [VMEM_SPEC] * (2 * parts),
+        in_specs=[SMEM_SPEC] + [VMEM_SPEC] * (2 * parts + 1),
         out_specs=[VMEM_SPEC] * shares,
         scratch_shapes=[pltpu.VMEM((rows * parts, wide), BF16)],
         compiler_params=pltpu.CompilerParams(vmem_limit_bytes=VMEM_LIMIT),
         cost_estimate=pl.CostEstimate(flops=rows, bytes_accessed=rows, transcendentals=0),
         name="memory_rows",
-    )(meta, *outs, *others, gain)
+    )(meta, *outs, *sums, gain)
 
 
 def place_kernel(parts, meta_ref, *refs):
-    out_ref = refs[parts]
+    out_ref = refs[parts + 1]
     wide = refs[0].shape[1]
     for r in range(parts):
         source = lax.rem(meta_ref[0] + r, parts)
-        out_ref[:, pl.ds(pl.multiple_of(source * wide, 128), wide)] = refs[r][: out_ref.shape[0]]
-
-
-def place_columns(meta, slots):
+        out_ref[:, pl.ds(pl.multiple_of(source * wide, 128), wide)] = refs[r][...]
+
+
+def place_columns(meta, slots, after):
     parts = len(slots)
-    rows, wide = slots[0].shape[0] - EXTRA, slots[0].shape[1]
+    rows, wide = slots[0].shape
     return pl.pallas_call(
         functools.partial(place_kernel, parts),
         out_shape=jax.ShapeDtypeStruct((rows, wide * parts), BF16),
-        in_specs=[SMEM_SPEC] + [VMEM_SPEC] * parts,
+        in_specs=[SMEM_SPEC] + [VMEM_SPEC] * parts + [pl.BlockSpec(memory_space=pl.ANY)],
         out_specs=VMEM_SPEC,
         compiler_params=pltpu.CompilerParams(vmem_limit_bytes=VMEM_LIMIT),
         cost_estimate=pl.CostEstimate(flops=0, bytes_accessed=rows, transcendentals=0),
         name="place_columns",
-    )(meta, *slots)
+    )(meta, *slots, after)
 
 
 def heads_finish_kernel(parts, meta_ref, *refs):
@@ -846,7 +833,7 @@
             pltpu.SemaphoreType.DMA,
         ],
         compiler_params=pltpu.CompilerParams(vmem_limit_bytes=VMEM_LIMIT),
-        cost_estimate=pl.CostEstimate(flops=12 * rows * width, bytes_accessed=14 * rows * width, transcendentals=0),
+        cost_estimate=pl.CostEstimate(flops=rows, bytes_accessed=rows, transcendentals=0),
         name="heads_finish",
     )(meta, *g_slots, x, inverse, gain, cotangent)
 
@@ -898,29 +885,29 @@
     a_slots = exchanged(a_sends, 1)
     arrived = shifted(carried[0], "section", 1)
     came_back = shifted(returned[0], "section", -1)
-    i_slots = exchanged(pack_rows(meta, embedded, arrived, parts, True), 1)
     *c_sends, cotangent = pack_rows(meta, loss_grad, came_back, parts, False)
     c_slots = exchanged(c_sends, 1)
     c_slots[0] = cotangent
+    i_slots = exchanged(pack_rows(meta, embedded, arrived, parts, True), 1)
 
     offsets = offset_table(rel_bias[0])
     onehot = jnp.asarray(bucket_onehot(buckets).T)
-    o_sends = heads_forward(meta, a_slots, i_slots, norm_gain, offsets, heads, rows)
-    o_sends, c_slots = lax.optimization_barrier((o_sends, c_slots))
+    *g_sends, gain_grad = heads_backward(
+        meta, a_slots, c_slots, norm_gain, offsets, onehot, norm_gain, heads, 0, heads
+    )
+    g_sends, i_slots = lax.optimization_barrier((g_sends, i_slots))
+    g_slots = exchanged(g_sends, -1)
+
+    *o_sends, sums = heads_forward(meta, a_slots, i_slots, norm_gain, offsets, heads, rows)
+    all_sums = exchanged([sums] * parts, 1)
     o_slots = exchanged(o_sends, -1)
-
-    *g_sends, gain_grad = heads_backward(
-        meta, a_slots, c_slots, norm_gain, offsets, onehot, o_sends[0], heads, 0, heads
-    )
-    g_sends, o_slots = lax.optimization_barrier((g_sends, o_slots))
-    g_slots = exchanged(g_sends, -1)
-    output = place_columns(meta, o_slots)
-    shares = memory_rows(meta, o_sends, o_slots[1:], final_gain[None], width, sections // 2)
+    shares = memory_rows(meta, o_sends, all_sums, final_gain[None], width, sections // 2)
+    shares, g_slots = lax.optimization_barrier((shares, g_slots))
     memory = spread_memory(shares, section, sections)
-
     input_grad, weight_grad, bias_grad = heads_finish(
         meta, g_slots, stash[0], inverse_b, norm_gain, cotangent, buckets
     )
+    output = place_columns(meta, o_slots, bias_grad)
     return (
         output[None],
         input_grad[None],

time: 141 us -> 147 us (1.043)
  starting transfers between devices: 44.4 us -> 55 us
  waiting for transfers between devices: 61.3 us -> 55.2 us
    ppermute x15 -> x18, starting transfers between devices: 37.3 us -> 47.2 us  [exchanged(): lax.ppermute(sends[r], 'seq', [(i, (i + direction * r) % parts) for i in...]
    ppermute x15 -> x18, waiting for transfers between devices: 60.5 us -> 55.1 us  [exchanged(): lax.ppermute(sends[r], 'seq', [(i, (i + direction * r) % parts) for i in...]
  transfers between devices with their start and end apart: 21 -> 24, of which waited for: 7 -> 7; matrix products, arithmetic and copies ran while one was open for 2% -> 1% of each run, Pallas kernels for 18% -> 21%
where the time goes in v10:
time: 147 us
  waiting for transfers between devices  55.2 us (38%)
  starting transfers between devices  55 us (37%)
  Pallas kernels  31.3 us (21%)
  other arithmetic  2.21 us (2%)
  local copies, waits for them, and re-layouts  2.06 us (1%)
    ppermute x18, waiting for transfers between devices, exchanged(): lax.ppermute(sends[r], 'seq', [(i, (i + direction * r) % parts) for i in...  55.1 us
    ppermute x18, starting transfers between devices, exchanged(): lax.ppermute(sends[r], 'seq', [(i, (i + direction * r) % parts) for i in...  47.2 us
    pallas_call x1, Pallas kernels, heads_backward(): pl.pallas_call(functools.partial(heads_backward_kernel, parts, rows), out...  11.3 us
    pallas_call x1, Pallas kernels, heads_forward(): pl.pallas_call(functools.partial(heads_forward_kernel, parts, rows), out_...  7.46 us
    ppermute x2, starting transfers between devices, shifted(): lax.ppermute(value, axis, [(source, source + steps) for source in range(f...  4.5 us
    pallas_call x1, Pallas kernels, pack_stash(): pl.pallas_call(functools.partial(pack_stash_kernel, parts, 4), out_shape=...  3.63 us
    pallas_call x1, Pallas kernels, heads_finish(): pl.pallas_call(functools.partial(heads_finish_kernel, parts), out_shape=(...  3.04 us
  transfers between devices with their start and end apart: 24, of which 7 were waited for; matrix products, arithmetic and copies ran while one was open for 1% of the time, Pallas kernels for 21%

profile of v10, /device:TPU:0, one launch (start us, length us, event | category | flops | bytes accessed | tf_op | source)
XLA Modules:
  0.0 146.8 jit_solution(17789799499577416556)
XLA Ops:
  0.6 0.0 copy-start
  0.6 0.0 copy-start.2
  0.7 1.4 collective-permute-start.3
  2.1 3.1 %collective-permute-start.7 = (bf16[128,3072]{1,0:T(8,128)(2,1)}, bf16[128,3072]{1,0:T(8,128)(2,1)S(1)}, u32[]{:S(2)}, u32[]{:S(2)}) collective-permute-start(bf16[128,3072]{1,0:T(8,128)(2,1)} %bitcast.26), channel_id=1, source_target_pairs={{0,4},{4,8},{8,12},{12,16},{16,20},{20,24},{24,28},{1,5},{5,9},{9,... | collective-permute-start | bytes 2359304 | tf_op jit(solution)/shard_map/ppermute | solution.py:851
  5.2 0.6 pad_add_fusion.meta_ref
  5.8 3.6 %pack_stash.1 = (f32[128,128]{1,0:T(8,128)}, bf16[224,768]{1,0:T(8,128)(2,1)}, bf16[224,768]{1,0:T(8,128)(2,1)}, bf16[224,768]{1,0:T(8,128)(2,1)}, bf16[224,768]{1,0:T(8,128)(2,1)}) custom-call(s32[3]{0:T(128)} %pad_add_fusion.meta_ref, bf16[128,3072]{1,0:T(8,128)(2,1)} %bitcast.18, f32[1,3072]{1,0:T(1,128)} %refs_6_.1, bf16[3,24,32,128]{3,2,1,0:T(8,128)(2,1)} %bitcast.23), custom_call_target="tpu_custom_call" | custom-call | flops 1572864 | bytes 2359296 | tf_op jit(solution)/shard_map/pack_stash/pallas_call | solution.py:426
  9.4 3.1 %collective-permute-start = (bf16[224,768]{1,0:T(8,128)(2,1)}, bf16[224,768]{1,0:T(8,128)(2,1)S(1)}, u32[]{:S(2)}, u32[]{:S(2)}) collective-permute-start(bf16[224,768]{1,0:T(8,128)(2,1)} %get-tuple-element.53), channel_id=1, source_target_pairs={{0,1},{1,2},{2,3},{3,0},{4,5},{5,6},{6,7},{7,4},{8,9},{9,10},{10,1... | collective-permute-start | bytes 1032200 | tf_op jit(solution)/shard_map/ppermute | solution.py:879
  12.5 2.6 %collective-permute-start.1 = (bf16[224,768]{1,0:T(8,128)(2,1)}, bf16[224,768]{1,0:T(8,128)(2,1)S(1)}, u32[]{:S(2)}, u32[]{:S(2)}) collective-permute-start(bf16[224,768]{1,0:T(8,128)(2,1)} %get-tuple-element.54), channel_id=1, source_target_pairs={{0,2},{1,3},{2,0},{3,1},{4,6},{5,7},{6,4},{7,5},{8,10},{9,11},{10,... | collective-permute-start | bytes 1032200 | tf_op jit(solution)/shard_map/ppermute | solution.py:879
  15.1 1.3 collective-permute-start.2
  16.5 0.0 collective-permute-done.3.inner_ref
  16.5 1.4 pack_cotangent.1
  17.9 0.7 collective-permute-start.4
  18.6 0.0 collective-permute-done.7.inner_ref
  18.6 0.3 collective-permute-start.5
  19.0 0.9 pack_inbound.1
  19.9 3.7 %collective-permute-done.refs_1_ = bf16[224,768]{1,0:T(8,128)(2,1)S(1)} collective-permute-done((bf16[224,768]{1,0:T(8,128)(2,1)}, bf16[224,768]{1,0:T(8,128)(2,1)S(1)}, u32[]{:S(2)}, u32[]{:S(2)}) %collective-permute-start) | collective-permute-done | bytes 344096 | tf_op jit(solution)/shard_map/ppermute | solution.py:879
  23.6 2.0 %collective-permute-start.6 = (bf16[128,768]{1,0:T(8,128)(2,1)S(1)}, bf16[128,768]{1,0:T(8,128)(2,1)S(1)}, u32[]{:S(2)}, u32[]{:S(2)}) collective-permute-start(bf16[128,768]{1,0:T(8,128)(2,1)S(1)} %get-tuple-element.59), channel_id=1, source_target_pairs={{0,3},{1,0},{2,1},{3,2},{4,7},{5,4},{6,5},{7,6},{8,11},{9,8},{10,9... | collective-permute-start | bytes 589832 | tf_op jit(solution)/shard_map/ppermute | solution.py:879
  25.6 13.3 %collective-permute-done.1.refs_2_ = bf16[224,768]{1,0:T(8,128)(2,1)S(1)} collective-permute-done((bf16[224,768]{1,0:T(8,128)(2,1)}, bf16[224,768]{1,0:T(8,128)(2,1)S(1)}, u32[]{:S(2)}, u32[]{:S(2)}) %collective-permute-start.1) | collective-permute-done | bytes 344096 | tf_op jit(solution)/shard_map/ppermute | solution.py:879
  38.9 17.2 %collective-permute-start.10 = (bf16[136,768]{1,0:T(8,128)(2,1)S(1)}, bf16[136,768]{1,0:T(8,128)(2,1)S(1)}, u32[]{:S(2)}, u32[]{:S(2)}) collective-permute-start(bf16[136,768]{1,0:T(8,128)(2,1)S(1)} %get-tuple-element.67), channel_id=1, source_target_pairs={{0,3},{1,0},{2,1},{3,2},{4,7},{5,4},{6,5},{7,6},{8,11},{9,8},{10,9... | collective-permute-start | bytes 626696 | tf_op jit(solution)/shard_map/ppermute | solution.py:879
  56.0 0.0 collective-permute-done.2.refs_3_
  56.0 0.0 collective-permute-start.8
  56.0 0.0 collective-permute-done.4.refs_5_
  56.0 3.3 %collective-permute-start.9 = (bf16[136,768]{1,0:T(8,128)(2,1)S(1)}, bf16[136,768]{1,0:T(8,128)(2,1)S(1)}, u32[]{:S(2)}, u32[]{:S(2)}) collective-permute-start(bf16[136,768]{1,0:T(8,128)(2,1)S(1)} %get-tuple-element.66), channel_id=1, source_target_pairs={{0,2},{1,3},{2,0},{3,1},{4,6},{5,7},{6,4},{7,5},{8,10},{9,11},{10,... | collective-permute-start | bytes 626696 | tf_op jit(solution)/shard_map/ppermute | solution.py:879
  59.4 0.2 fusion
  59.6 0.0 collective-permute-done.5.refs_6_
  59.6 0.0 collective-permute-done.6.refs_7_
  59.7 11.3 %heads_backward.1 = (bf16[232,768]{1,0:T(8,128)(2,1)S(1)}, bf16[232,768]{1,0:T(8,128)(2,1)S(1)}, bf16[232,768]{1,0:T(8,128)(2,1)S(1)}, bf16[232,768]{1,0:T(8,128)(2,1)S(1)}, f32[1,768]{1,0:T(1,128)}) custom-call(s32[3]{0:T(128)S(1)} %copy-done.7, bf16[224,768]{1,0:T(8,128)(2,1)S(1)} %copy-done.4, bf16[224,768]{1,0:T(8,128)(2,1)S(1)} %collective-permute-done.refs_1_, ...), custom_call_target="tpu_custom_call" | custom-call | flops 1228800000 | bytes 393216 | tf_op jit(solution)/shard_map/heads_backward/pallas_call | solution.py:603
  71.0 0.0 collective-permute-done.10.refs_7_
  71.0 0.0 collective-permute-done.8.refs_5_
  71.0 9.7 %collective-permute-done.9.refs_6_ = bf16[136,768]{1,0:T(8,128)(2,1)S(1)} collective-permute-done((bf16[136,768]{1,0:T(8,128)(2,1)S(1)}, bf16[136,768]{1,0:T(8,128)(2,1)S(1)}, u32[]{:S(2)}, u32[]{:S(2)}) %collective-permute-start.9) | collective-permute-done | bytes 208928 | tf_op jit(solution)/shard_map/ppermute | solution.py:879
  80.7 1.7 %collective-permute-start.17 = (bf16[232,768]{1,0:T(8,128)(2,1)S(1)}, bf16[232,768]{1,0:T(8,128)(2,1)S(1)}, u32[]{:S(2)}, u32[]{:S(2)}) collective-permute-start(bf16[232,768]{1,0:T(8,128)(2,1)S(1)} %get-tuple-element.82), channel_id=1, source_target_pairs={{0,3},{1,0},{2,1},{3,2},{4,7},{5,4},{6,5},{7,6},{8,11},{9,8},{10,9... | collective-permute-start | bytes 1069064 | tf_op jit(solution)/shard_map/ppermute | solution.py:879
  82.4 2.8 %collective-permute-start.18 = (bf16[232,768]{1,0:T(8,128)(2,1)S(1)}, bf16[232,768]{1,0:T(8,128)(2,1)S(1)}, u32[]{:S(2)}, u32[]{:S(2)}) collective-permute-start(bf16[232,768]{1,0:T(8,128)(2,1)S(1)} %get-tuple-element.83), channel_id=1, source_target_pairs={{0,2},{1,3},{2,0},{3,1},{4,6},{5,7},{6,4},{7,5},{8,10},{9,11},{10,... | collective-permute-start | bytes 1069064 | tf_op jit(solution)/shard_map/ppermute | solution.py:879
  85.2 0.0 collective-permute-start.19
  85.2 7.5 %heads_forward.1 = (bf16[128,768]{1,0:T(8,128)(2,1)S(1)}, bf16[128,768]{1,0:T(8,128)(2,1)}, bf16[128,768]{1,0:T(8,128)(2,1)}, bf16[128,768]{1,0:T(8,128)(2,1)}, f32[8,512]{1,0:T(8,128)S(1)}) custom-call(s32[3]{0:T(128)S(1)} %copy-done.7, bf16[224,768]{1,0:T(8,128)(2,1)S(1)} %copy-done.4, bf16[224,768]{1,0:T(8,128)(2,1)S(1)} %collective-permute-done.refs_1_, ...), custom_call_target="tpu_custom_call" | custom-call | flops 3072 | bytes 512 | tf_op jit(solution)/shard_map/heads_forward/pallas_call | solution.py:688
  92.7 0.8 collective-permute-start.14
  93.4 3.7 %collective-permute-start.15 = (f32[8,512]{1,0:T(8,128)S(1)}, f32[8,512]{1,0:T(8,128)S(1)}, u32[]{:S(2)}, u32[]{:S(2)}) collective-permute-start(f32[8,512]{1,0:T(8,128)S(1)} %get-tuple-element.76.refs_4_), channel_id=1, source_target_pairs={{0,2},{1,3},{2,0},{3,1},{4,6},{5,7},{6,4},{7,5},{8,10},{9,11},{10,... | collective-permute-start | bytes 49160 | tf_op jit(solution)/shard_map/ppermute | solution.py:879
  97.1 11.2 %collective-permute-done.14.refs_5_ = f32[8,512]{1,0:T(8,128)S(1)} collective-permute-done((f32[8,512]{1,0:T(8,128)S(1)}, f32[8,512]{1,0:T(8,128)S(1)}, u32[]{:S(2)}, u32[]{:S(2)}) %collective-permute-start.14) | collective-permute-done | bytes 16416 | tf_op jit(solution)/shard_map/ppermute | solution.py:879
  108.4 1.8 %collective-permute-start.16 = (f32[8,512]{1,0:T(8,128)S(1)}, f32[8,512]{1,0:T(8,128)S(1)}, u32[]{:S(2)}, u32[]{:S(2)}) collective-permute-start(f32[8,512]{1,0:T(8,128)S(1)} %get-tuple-element.76.refs_4_), channel_id=1, source_target_pairs={{0,3},{1,0},{2,1},{3,2},{4,7},{5,4},{6,5},{7,6},{8,11},{9,8},{10,9... | collective-permute-start | bytes 49160 | tf_op jit(solution)/shard_map/ppermute | solution.py:879
  110.2 7.4 %collective-permute-done.15.refs_6_ = f32[8,512]{1,0:T(8,128)S(1)} collective-permute-done((f32[8,512]{1,0:T(8,128)S(1)}, f32[8,512]{1,0:T(8,128)S(1)}, u32[]{:S(2)}, u32[]{:S(2)}) %collective-permute-start.15) | collective-permute-done | bytes 16416 | tf_op jit(solution)/shard_map/ppermute | solution.py:879
  117.5 0.3 collective-permute-done.16.refs_7_
  117.8 1.5 %memory_rows.1 = (bf16[128,768]{1,0:T(8,128)(2,1)S(1)}, bf16[128,768]{1,0:T(8,128)(2,1)S(1)}, bf16[128,768]{1,0:T(8,128)(2,1)S(1)}, bf16[128,768]{1,0:T(8,128)(2,1)S(1)}) custom-call(s32[3]{0:T(128)S(1)} %copy-done.7, bf16[128,768]{1,0:T(8,128)(2,1)S(1)} %get-tuple-element.72.refs_0_, bf16[128,768]{1,0:T(8,128)(2,1)} %get-tuple-element.73.refs_1_, ...), custom_call_target="tpu_custom_call" | custom-call | flops 128 | bytes 128 | tf_op jit(solution)/shard_map/memory_rows/pallas_call | solution.py:747
  119.3 0.0 collective-permute-done.17.refs_1_
  119.3 0.0 collective-permute-done.18.refs_2_
  119.3 0.0 collective-permute-done.19.refs_3_
  119.3 0.7 collective-permute-start.20
  120.0 0.7 collective-permute-start.21
  120.7 0.7 collective-permute-start.22
  121.4 3.0 %collective-permute-start.11 = (bf16[128,768]{1,0:T(8,128)(2,1)}, bf16[128,768]{1,0:T(8,128)(2,1)S(1)}, u32[]{:S(2)}, u32[]{:S(2)}) collective-permute-start(bf16[128,768]{1,0:T(8,128)(2,1)} %get-tuple-element.73.refs_1_), channel_id=1, source_target_pairs={{0,3},{1,0},{2,1},{3,2},{4,7},{5,4},{6,5},{7,6},{8,11},{9,8},{10,9... | collective-permute-start | bytes 589832 | tf_op jit(solution)/shard_map/ppermute | solution.py:879
  124.3 0.9 collective-permute-start.12
  125.3 0.0 collective-permute-done.20
  125.3 1.9 %collective-permute-start.13 = (bf16[128,768]{1,0:T(8,128)(2,1)}, bf16[128,768]{1,0:T(8,128)(2,1)}, u32[]{:S(2)}, u32[]{:S(2)}) collective-permute-start(bf16[128,768]{1,0:T(8,128)(2,1)} %get-tuple-element.75.refs_3_), channel_id=1, source_target_pairs={{0,1},{1,2},{2,3},{3,0},{4,5},{5,6},{6,7},{7,4},{8,9},{9,10},{10,1... | collective-permute-start | bytes 589832 | tf_op jit(solution)/shard_map/ppermute | solution.py:879
  127.2 0.0 collective-permute-done.21
  127.2 0.0 collective-permute-done.22
  127.3 0.7 copy-done.11
  127.9 0.6 slice.8
  128.6 1.3 collective-permute-start.23
  129.9 3.0 %heads_finish.1 = (bf16[128,3072]{1,0:T(8,128)(2,1)}, f32[3,24,32,128]{3,2,1,0:T(8,128)}, f32[8,24]{1,0:T(8,128)}) custom-call(s32[3]{0:T(128)S(1)} %copy-done.7, bf16[232,768]{1,0:T(8,128)(2,1)S(1)} %get-tuple-element.85.refs_0_, bf16[232,768]{1,0:T(8,128)(2,1)S(1)} %collective-permute-done.17.refs_1_, ...), custom_call_target="tpu_custom_call" | custom-call | flops 128 | bytes 128 | tf_op jit(solution)/shard_map/heads_finish/pallas_call | solution.py:821
  133.0 0.0 collective-permute-done.11.refs_1_
  133.0 9.6 %collective-permute-done.12.refs_2_ = bf16[128,768]{1,0:T(8,128)(2,1)} collective-permute-done((bf16[128,768]{1,0:T(8,128)(2,1)}, bf16[128,768]{1,0:T(8,128)(2,1)}, u32[]{:S(2)}, u32[]{:S(2)}) %collective-permute-start.12) | collective-permute-done | bytes 196640 | tf_op jit(solution)/shard_map/ppermute | solution.py:879
  142.6 0.0 collective-permute-done.13.refs_3_
  142.6 0.7 copy-done.9
  143.3 2.0 %place_columns.1 = bf16[128,3072]{1,0:T(8,128)(2,1)} custom-call(s32[3]{0:T(128)S(1)} %copy-done.7, bf16[128,768]{1,0:T(8,128)(2,1)S(1)} %get-tuple-element.72.refs_0_, bf16[128,768]{1,0:T(8,128)(2,1)S(1)} %collective-permute-done.11.refs_1_, bf16[128,768]{1,0:T(8,128)(2,1)} %collective-permute-done.12.refs_2_, ...), custom_call_target="tpu_custom_call" | custom-call | bytes 128 | tf_op jit(solution)/shard_map/place_columns/pallas_call | solution.py:770
  145.3 0.0 collective-permute-done.23
  145.3 1.5 %slice_select_fusion = bf16[64,768]{1,0:T(8,128)(2,1)} fusion(bf16[64,768]{1,0:T(8,128)(2,1)} %collective-permute-done.23, bf16[128,768]{1,0:T(8,128)(2,1)S(1)} %copy-done.12, pred[]{:T(512)S(6)} %eq.14), kind=kLoop, calls=%fused_computation.3 | loop fusion | flops 49152 | bytes 294913 | tf_op jit(solution)/shard_map/jit(_where)/select_n | solution.py:861
  (27 shorter events, 0.1 us)
Async XLA Ops:
  0.6 58.7 %copy-start = (f32[1,32,24]{1,2,0:T(8,128)S(1)}, f32[1,32,24]{1,2,0:T(8,128)}, u32[]{:S(2)}) copy-start(f32[1,32,24]{1,2,0:T(8,128)} %param.17) | copy-start | bytes 9220
  0.6 15.8 %copy-start.2 = (bf16[128,3072]{1,0:T(8,128)(2,1)S(1)}, bf16[128,3072]{1,0:T(8,128)(2,1)}, u32[]{:S(2)}) copy-start(bf16[128,3072]{1,0:T(8,128)(2,1)} %edge_ref.2) | copy-start | bytes 2359300
  0.7 15.8 %collective-permute-start.3 = (bf16[128,3072]{1,0:T(8,128)(2,1)}, bf16[128,3072]{1,0:T(8,128)(2,1)S(1)}, u32[]{:S(2)}, u32[]{:S(2)}) collective-permute-start(bf16[128,3072]{1,0:T(8,128)(2,1)} %bitcast.25), channel_id=1, source_target_pairs={{4,0},{8,4},{12,8},{16,12},{20,16},{24,20},{28,24},{5,1},{9,5},{13... | collective-permute-start | bytes 2359304 | tf_op jit(solution)/shard_map/ppermute | solution.py:851
  2.1 16.5 %collective-permute-start.7 = (bf16[128,3072]{1,0:T(8,128)(2,1)}, bf16[128,3072]{1,0:T(8,128)(2,1)S(1)}, u32[]{:S(2)}, u32[]{:S(2)}) collective-permute-start(bf16[128,3072]{1,0:T(8,128)(2,1)} %bitcast.26), channel_id=1, source_target_pairs={{0,4},{4,8},{8,12},{12,16},{16,20},{20,24},{24,28},{1,5},{5,9},{9,... | collective-permute-start | bytes 2359304 | tf_op jit(solution)/shard_map/ppermute | solution.py:851
  5.8 10.7 %copy-start.7 = (s32[3]{0:T(128)S(1)}, s32[3]{0:T(128)}, u32[]{:S(2)}) copy-start(s32[3]{0:T(128)} %pad_add_fusion.meta_ref) | copy-start | bytes 40
  5.8 13.2 %copy-start.3 = (bf16[128,3072]{1,0:T(8,128)(2,1)S(1)}, bf16[128,3072]{1,0:T(8,128)(2,1)}, u32[]{:S(2)}) copy-start(bf16[128,3072]{1,0:T(8,128)(2,1)} %edge_ref.3) | copy-start | bytes 2359300
  9.4 14.1 %collective-permute-start = (bf16[224,768]{1,0:T(8,128)(2,1)}, bf16[224,768]{1,0:T(8,128)(2,1)S(1)}, u32[]{:S(2)}, u32[]{:S(2)}) collective-permute-start(bf16[224,768]{1,0:T(8,128)(2,1)} %get-tuple-element.53), channel_id=1, source_target_pairs={{0,1},{1,2},{2,3},{3,0},{4,5},{5,6},{6,7},{7,4},{8,9},{9,10},{10,1... | collective-permute-start | bytes 1032200 | tf_op jit(solution)/shard_map/ppermute | solution.py:879
  12.5 26.3 %collective-permute-start.1 = (bf16[224,768]{1,0:T(8,128)(2,1)}, bf16[224,768]{1,0:T(8,128)(2,1)S(1)}, u32[]{:S(2)}, u32[]{:S(2)}) collective-permute-start(bf16[224,768]{1,0:T(8,128)(2,1)} %get-tuple-element.54), channel_id=1, source_target_pairs={{0,2},{1,3},{2,0},{3,1},{4,6},{5,7},{6,4},{7,5},{8,10},{9,11},{10,... | collective-permute-start | bytes 1032200 | tf_op jit(solution)/shard_map/ppermute | solution.py:879
  15.1 40.9 %collective-permute-start.2 = (bf16[224,768]{1,0:T(8,128)(2,1)}, bf16[224,768]{1,0:T(8,128)(2,1)S(1)}, u32[]{:S(2)}, u32[]{:S(2)}) collective-permute-start(bf16[224,768]{1,0:T(8,128)(2,1)} %get-tuple-element.55), channel_id=1, source_target_pairs={{0,3},{1,0},{2,1},{3,2},{4,7},{5,4},{6,5},{7,6},{8,11},{9,8},{10,9... | collective-permute-start | bytes 1032200 | tf_op jit(solution)/shard_map/ppermute | solution.py:879
  17.9 41.5 %copy-start.13 = (f32[256,32]{1,0:T(8,128)S(1)}, f32[256,32]{1,0:T(8,128)}, u32[]{:S(2)}) copy-start(f32[256,32]{1,0:T(8,128)} %constant.35.clone) | copy-start | bytes 98308
  17.9 41.8 %copy-start.4 = (bf16[224,768]{1,0:T(8,128)(2,1)S(1)}, bf16[224,768]{1,0:T(8,128)(2,1)}, u32[]{:S(2)}) copy-start(bf16[224,768]{1,0:T(8,128)(2,1)} %get-tuple-element.52.refs_0_) | copy-start | bytes 1032196
  17.9 41.8 %copy-start.5 = (f32[1,3072]{1,0:T(1,128)S(1)}, f32[1,3072]{1,0:T(1,128)}, u32[]{:S(2)}) copy-start(f32[1,3072]{1,0:T(1,128)} %refs_6_.1) | copy-start | bytes 36868
  17.9 41.8 %copy-start.10 = (f32[32,256]{1,0:T(8,128)S(1)}, f32[32,256]{1,0:T(8,128)}, u32[]{:S(2)}) copy-start(f32[32,256]{1,0:T(8,128)} %constant.36.clone.refs_10_) | copy-start | bytes 98308
  17.9 38.2 %collective-permute-start.4 = (bf16[128,768]{1,0:T(8,128)(2,1)S(1)}, bf16[128,768]{1,0:T(8,128)(2,1)S(1)}, u32[]{:S(2)}, u32[]{:S(2)}) collective-permute-start(bf16[128,768]{1,0:T(8,128)(2,1)S(1)} %get-tuple-element.57), channel_id=1, source_target_pairs={{0,1},{1,2},{2,3},{3,0},{4,5},{5,6},{6,7},{7,4},{8,9},{9,10},{10,1... | collective-permute-start | bytes 589832 | tf_op jit(solution)/shard_map/ppermute | solution.py:879
  18.6 41.0 %collective-permute-start.5 = (bf16[128,768]{1,0:T(8,128)(2,1)S(1)}, bf16[128,768]{1,0:T(8,128)(2,1)S(1)}, u32[]{:S(2)}, u32[]{:S(2)}) collective-permute-start(bf16[128,768]{1,0:T(8,128)(2,1)S(1)} %get-tuple-element.58), channel_id=1, source_target_pairs={{0,2},{1,3},{2,0},{3,1},{4,6},{5,7},{6,4},{7,5},{8,10},{9,11},{10,... | collective-permute-start | bytes 589832 | tf_op jit(solution)/shard_map/ppermute | solution.py:879
  23.6 36.0 %collective-permute-start.6 = (bf16[128,768]{1,0:T(8,128)(2,1)S(1)}, bf16[128,768]{1,0:T(8,128)(2,1)S(1)}, u32[]{:S(2)}, u32[]{:S(2)}) collective-permute-start(bf16[128,768]{1,0:T(8,128)(2,1)S(1)} %get-tuple-element.59), channel_id=1, source_target_pairs={{0,3},{1,0},{2,1},{3,2},{4,7},{5,4},{6,5},{7,6},{8,11},{9,8},{10,9... | collective-permute-start | bytes 589832 | tf_op jit(solution)/shard_map/ppermute | solution.py:879
  38.9 32.2 %collective-permute-start.10 = (bf16[136,768]{1,0:T(8,128)(2,1)S(1)}, bf16[136,768]{1,0:T(8,128)(2,1)S(1)}, u32[]{:S(2)}, u32[]{:S(2)}) collective-permute-start(bf16[136,768]{1,0:T(8,128)(2,1)S(1)} %get-tuple-element.67), channel_id=1, source_target_pairs={{0,3},{1,0},{2,1},{3,2},{4,7},{5,4},{6,5},{7,6},{8,11},{9,8},{10,9... | collective-permute-start | bytes 626696 | tf_op jit(solution)/shard_map/ppermute | solution.py:879
  56.0 15.0 %collective-permute-start.8 = (bf16[136,768]{1,0:T(8,128)(2,1)S(1)}, bf16[136,768]{1,0:T(8,128)(2,1)S(1)}, u32[]{:S(2)}, u32[]{:S(2)}) collective-permute-start(bf16[136,768]{1,0:T(8,128)(2,1)S(1)} %get-tuple-element.65), channel_id=1, source_target_pairs={{0,1},{1,2},{2,3},{3,0},{4,5},{5,6},{6,7},{7,4},{8,9},{9,10},{10,1... | collective-permute-start | bytes 626696 | tf_op jit(solution)/shard_map/ppermute | solution.py:879
  56.0 24.6 %collective-permute-start.9 = (bf16[136,768]{1,0:T(8,128)(2,1)S(1)}, bf16[136,768]{1,0:T(8,128)(2,1)S(1)}, u32[]{:S(2)}, u32[]{:S(2)}) collective-permute-start(bf16[136,768]{1,0:T(8,128)(2,1)S(1)} %get-tuple-element.66), channel_id=1, source_target_pairs={{0,2},{1,3},{2,0},{3,1},{4,6},{5,7},{6,4},{7,5},{8,10},{9,11},{10,... | collective-permute-start | bytes 626696 | tf_op jit(solution)/shard_map/ppermute | solution.py:879
  71.0 46.8 %copy-start.8 = (f32[3072]{0:T(1024)S(1)}, f32[3072]{0:T(1024)}, u32[]{:S(2)}) copy-start(f32[3072]{0:T(1024)} %param.19) | copy-start | bytes 36868
  80.7 38.6 %collective-permute-start.17 = (bf16[232,768]{1,0:T(8,128)(2,1)S(1)}, bf16[232,768]{1,0:T(8,128)(2,1)S(1)}, u32[]{:S(2)}, u32[]{:S(2)}) collective-permute-start(bf16[232,768]{1,0:T(8,128)(2,1)S(1)} %get-tuple-element.82), channel_id=1, source_target_pairs={{0,3},{1,0},{2,1},{3,2},{4,7},{5,4},{6,5},{7,6},{8,11},{9,8},{10,9... | collective-permute-start | bytes 1069064 | tf_op jit(solution)/shard_map/ppermute | solution.py:879
  82.4 36.9 %collective-permute-start.18 = (bf16[232,768]{1,0:T(8,128)(2,1)S(1)}, bf16[232,768]{1,0:T(8,128)(2,1)S(1)}, u32[]{:S(2)}, u32[]{:S(2)}) collective-permute-start(bf16[232,768]{1,0:T(8,128)(2,1)S(1)} %get-tuple-element.83), channel_id=1, source_target_pairs={{0,2},{1,3},{2,0},{3,1},{4,6},{5,7},{6,4},{7,5},{8,10},{9,11},{10,... | collective-permute-start | bytes 1069064 | tf_op jit(solution)/shard_map/ppermute | solution.py:879
  85.2 34.1 %collective-permute-start.19 = (bf16[232,768]{1,0:T(8,128)(2,1)S(1)}, bf16[232,768]{1,0:T(8,128)(2,1)S(1)}, u32[]{:S(2)}, u32[]{:S(2)}) collective-permute-start(bf16[232,768]{1,0:T(8,128)(2,1)S(1)} %get-tuple-element.84), channel_id=1, source_target_pairs={{0,1},{1,2},{2,3},{3,0},{4,5},{5,6},{6,7},{7,4},{8,9},{9,10},{10,1... | collective-permute-start | bytes 1069064 | tf_op jit(solution)/shard_map/ppermute | solution.py:879
  92.7 37.2 %copy-start.1 = (bf16[1,128,3072]{2,1,0:T(8,128)(2,1)S(1)}, bf16[1,128,3072]{2,1,0:T(8,128)(2,1)}, u32[]{:S(2)}) copy-start(bf16[1,128,3072]{2,1,0:T(8,128)(2,1)} %param.13) | copy-start | bytes 2359300
  92.7 37.2 %copy-start.6 = (f32[128,128]{1,0:T(8,128)S(1)}, f32[128,128]{1,0:T(8,128)}, u32[]{:S(2)}) copy-start(f32[128,128]{1,0:T(8,128)} %get-tuple-element.89.refs_5_) | copy-start | bytes 196612
  92.7 15.7 %collective-permute-start.14 = (f32[8,512]{1,0:T(8,128)S(1)}, f32[8,512]{1,0:T(8,128)S(1)}, u32[]{:S(2)}, u32[]{:S(2)}) collective-permute-start(f32[8,512]{1,0:T(8,128)S(1)} %get-tuple-element.76.refs_4_), channel_id=1, source_target_pairs={{0,1},{1,2},{2,3},{3,0},{4,5},{5,6},{6,7},{7,4},{8,9},{9,10},{10,1... | collective-permute-start | bytes 49160 | tf_op jit(solution)/shard_map/ppermute | solution.py:879
  93.4 24.1 %collective-permute-start.15 = (f32[8,512]{1,0:T(8,128)S(1)}, f32[8,512]{1,0:T(8,128)S(1)}, u32[]{:S(2)}, u32[]{:S(2)}) collective-permute-start(f32[8,512]{1,0:T(8,128)S(1)} %get-tuple-element.76.refs_4_), channel_id=1, source_target_pairs={{0,2},{1,3},{2,0},{3,1},{4,6},{5,7},{6,4},{7,5},{8,10},{9,11},{10,... | collective-permute-start | bytes 49160 | tf_op jit(solution)/shard_map/ppermute | solution.py:879
  108.4 9.4 %collective-permute-start.16 = (f32[8,512]{1,0:T(8,128)S(1)}, f32[8,512]{1,0:T(8,128)S(1)}, u32[]{:S(2)}, u32[]{:S(2)}) collective-permute-start(f32[8,512]{1,0:T(8,128)S(1)} %get-tuple-element.76.refs_4_), channel_id=1, source_target_pairs={{0,3},{1,0},{2,1},{3,2},{4,7},{5,4},{6,5},{7,6},{8,11},{9,8},{10,9... | collective-permute-start | bytes 49160 | tf_op jit(solution)/shard_map/ppermute | solution.py:879
  119.3 5.9 %collective-permute-start.20 = (bf16[128,768]{1,0:T(8,128)(2,1)S(1)}, bf16[128,768]{1,0:T(8,128)(2,1)S(1)}, u32[]{:S(2)}, u32[]{:S(2)}) collective-permute-start(bf16[128,768]{1,0:T(8,128)(2,1)S(1)} %get-tuple-element.95), channel_id=1, source_target_pairs={{28,4},{29,5},{30,6},{31,7}} | collective-permute-start | bytes 589832 | tf_op jit(solution)/shard_map/ppermute | solution.py:858
  120.0 7.2 %collective-permute-start.21 = (bf16[128,768]{1,0:T(8,128)(2,1)S(1)}, bf16[128,768]{1,0:T(8,128)(2,1)S(1)}, u32[]{:S(2)}, u32[]{:S(2)}) collective-permute-start(bf16[128,768]{1,0:T(8,128)(2,1)S(1)} %get-tuple-element.96), channel_id=1, source_target_pairs={{28,12},{29,13},{30,14},{31,15}} | collective-permute-start | bytes 589832 | tf_op jit(solution)/shard_map/ppermute | solution.py:858
  120.7 6.5 %collective-permute-start.22 = (bf16[128,768]{1,0:T(8,128)(2,1)S(1)}, bf16[128,768]{1,0:T(8,128)(2,1)S(1)}, u32[]{:S(2)}, u32[]{:S(2)}) collective-permute-start(bf16[128,768]{1,0:T(8,128)(2,1)S(1)} %get-tuple-element.97), channel_id=1, source_target_pairs={{28,20},{29,21},{30,22},{31,23}} | collective-permute-start | bytes 589832 | tf_op jit(solution)/shard_map/ppermute | solution.py:858
  121.4 11.6 %collective-permute-start.11 = (bf16[128,768]{1,0:T(8,128)(2,1)}, bf16[128,768]{1,0:T(8,128)(2,1)S(1)}, u32[]{:S(2)}, u32[]{:S(2)}) collective-permute-start(bf16[128,768]{1,0:T(8,128)(2,1)} %get-tuple-element.73.refs_1_), channel_id=1, source_target_pairs={{0,3},{1,0},{2,1},{3,2},{4,7},{5,4},{6,5},{7,6},{8,11},{9,8},{10,9... | collective-permute-start | bytes 589832 | tf_op jit(solution)/shard_map/ppermute | solution.py:879
  124.3 18.2 %collective-permute-start.12 = (bf16[128,768]{1,0:T(8,128)(2,1)}, bf16[128,768]{1,0:T(8,128)(2,1)}, u32[]{:S(2)}, u32[]{:S(2)}) collective-permute-start(bf16[128,768]{1,0:T(8,128)(2,1)} %get-tuple-element.74.refs_2_), channel_id=1, source_target_pairs={{0,2},{1,3},{2,0},{3,1},{4,6},{5,7},{6,4},{7,5},{8,10},{9,11},{10,... | collective-permute-start | bytes 589832 | tf_op jit(solution)/shard_map/ppermute | solution.py:879
  125.3 17.3 %collective-permute-start.13 = (bf16[128,768]{1,0:T(8,128)(2,1)}, bf16[128,768]{1,0:T(8,128)(2,1)}, u32[]{:S(2)}, u32[]{:S(2)}) collective-permute-start(bf16[128,768]{1,0:T(8,128)(2,1)} %get-tuple-element.75.refs_3_), channel_id=1, source_target_pairs={{0,1},{1,2},{2,3},{3,0},{4,5},{5,6},{6,7},{7,4},{8,9},{9,10},{10,1... | collective-permute-start | bytes 589832 | tf_op jit(solution)/shard_map/ppermute | solution.py:879
  127.3 0.7 copy-start.11
  128.6 16.7 %collective-permute-start.23 = (bf16[64,768]{1,0:T(8,128)(2,1)}, bf16[64,768]{1,0:T(8,128)(2,1)}, u32[]{:S(2)}, u32[]{:S(2)}) collective-permute-start(bf16[64,768]{1,0:T(8,128)(2,1)} %slice.8), channel_id=1, source_target_pairs={{4,0},{12,8},{20,16},{28,24},{5,1},{13,9},{21,17},{29,25},{6,2},{1... | collective-permute-start | bytes 294920 | tf_op jit(solution)/shard_map/ppermute | solution.py:860
  129.9 15.4 %copy-start.12 = (bf16[128,768]{1,0:T(8,128)(2,1)S(1)}, bf16[128,768]{1,0:T(8,128)(2,1)}, u32[]{:S(2)}) copy-start(bf16[128,768]{1,0:T(8,128)(2,1)} %copy-done.11) | copy-start | bytes 589828
  142.6 0.7 copy-start.9

commit v11 on v9

--- a/solution.py
+++ b/solution.py
@@ -341,7 +341,7 @@
     return lax.rsqrt(jnp.mean(x * x, axis=-1, keepdims=True) + eps_norm)
 
 
-def pack_stash_kernel(parts, pieces, meta_ref, x_hbm, gain_hbm, weight_hbm, inverse_ref, *refs):
+def pack_stash_kernel(parts, pieces, x_hbm, gain_hbm, weight_hbm, inverse_ref, *refs):
     out_refs = refs[:parts]
     x_ref, gain_ref, weight_ref, normed_ref, sems = refs[parts:]
     rows, width = x_ref.shape
@@ -368,12 +368,12 @@
         inverse_ref[part] = jnp.broadcast_to(inverse, (step, 128))
         normed_ref[part] = (x_ref[part].astype(F32) * inverse * gain).astype(BF16)
     for r, out_ref in enumerate(out_refs):
-        target = lax.rem(meta_ref[0] + r, parts)
+        target = lax.rem(lax.axis_index("seq") + r, parts)
         out_ref[:rows] = normed_ref[:, pl.ds(pl.multiple_of(target * wide, 128), wide)]
     for j, copy in enumerate(weight_copies):
         copy.wait()
         for r, out_ref in enumerate(out_refs):
-            target = lax.rem(meta_ref[0] + r, parts)
+            target = lax.rem(lax.axis_index("seq") + r, parts)
             for h in range(heads):
                 out_ref[rows + j * depth : rows + (j + 1) * depth, h * HEAD_DIM : (h + 1) * HEAD_DIM] = weight_ref[
                     j, target * heads + h
@@ -419,7 +419,7 @@
 VMEM_SPEC = pl.BlockSpec(memory_space=pltpu.VMEM)
 
 
-def pack_stash(meta, x, gain, weight, parts):
+def pack_stash(x, gain, weight, parts):
     rows, width = x.shape
     depth = weight.shape[2]
     shape = (rows + 3 * depth, width // parts)
@@ -429,7 +429,7 @@
             jax.ShapeDtypeStruct((rows, 128), F32),
             *[jax.ShapeDtypeStruct(shape, BF16) for r in range(parts)],
         ),
-        in_specs=[SMEM_SPEC] + [pl.BlockSpec(memory_space=pl.ANY)] * 3,
+        in_specs=[pl.BlockSpec(memory_space=pl.ANY)] * 3,
         out_specs=(VMEM_SPEC,) * (parts + 1),
         scratch_shapes=[
             pltpu.VMEM((rows, width), BF16),
@@ -441,7 +441,7 @@
         compiler_params=pltpu.CompilerParams(vmem_limit_bytes=58 * 1024 * 1024),
         cost_estimate=pl.CostEstimate(flops=4 * rows * width, bytes_accessed=6 * rows * width, transcendentals=0),
         name="pack_stash",
-    )(meta, x, gain, weight)
+    )(x, gain, weight)
 
 
 def pack_rows(meta, edge, inner, parts, with_inverse):
@@ -894,7 +894,7 @@
         ]
         return [sends[0]] + moved
 
-    inverse_b, *a_sends = pack_stash(meta, stash[0], norm_gain, qkv_weight[0], parts)
+    inverse_b, *a_sends = pack_stash(stash[0], norm_gain, qkv_weight[0], parts)
     a_slots = exchanged(a_sends, 1)
     arrived = shifted(carried[0], "section", 1)
     came_back = shifted(returned[0], "section", -1)
@@ -906,7 +906,6 @@
     offsets = offset_table(rel_bias[0])
     onehot = jnp.asarray(bucket_onehot(buckets).T)
     o_sends = heads_forward(meta, a_slots, i_slots, norm_gain, offsets, heads, rows)
-    o_sends, c_slots = lax.optimization_barrier((o_sends, c_slots))
     o_slots = exchanged(o_sends, -1)
 
     *g_sends, gain_grad = heads_backward(

time: 141 us -> 138 us (0.979)
  waiting for transfers between devices: 61.3 us -> 58.7 us
    ppermute x15, waiting for transfers between devices: 60.5 us -> 57.5 us  [exchanged(): lax.ppermute(sends[r], 'seq', [(i, (i + direction * r) % parts) for i in...]
  transfers between devices with their start and end apart: 21 -> 21, of which waited for: 7 -> 6; matrix products, arithmetic and copies ran while one was open for 2% -> 2% of each run, Pallas kernels for 18% -> 19%
where the time goes in v11:
time: 138 us
  waiting for transfers between devices  58.7 us (43%)
  starting transfers between devices  44.3 us (32%)
  Pallas kernels  30.5 us (22%)
  other arithmetic  1.67 us (1%)
  local copies, waits for them, and re-layouts  1.42 us (1%)
    ppermute x15, waiting for transfers between devices, exchanged(): lax.ppermute(sends[r], 'seq', [(i, (i + direction * r) % parts) for i in...  57.5 us
    ppermute x15, starting transfers between devices, exchanged(): lax.ppermute(sends[r], 'seq', [(i, (i + direction * r) % parts) for i in...  37.1 us
    pallas_call x1, Pallas kernels, heads_backward(): pl.pallas_call(functools.partial(heads_backward_kernel, parts, rows), out...  11.8 us
    pallas_call x1, Pallas kernels, heads_forward(): pl.pallas_call(functools.partial(heads_forward_kernel, parts, rows), out_...  7.54 us
    ppermute x2, starting transfers between devices, shifted(): lax.ppermute(value, axis, [(source, source + steps) for source in range(f...  3.83 us
    pallas_call x1, Pallas kernels, heads_finish(): pl.pallas_call(functools.partial(heads_finish_kernel, parts), out_shape=(...  3.49 us
    pallas_call x1, Pallas kernels, pack_stash(): pl.pallas_call(functools.partial(pack_stash_kernel, parts, 4), out_shape=...  2.9 us
  transfers between devices with their start and end apart: 21, of which 6 were waited for; matrix products, arithmetic and copies ran while one was open for 2% of the time, Pallas kernels for 19%

profile of v11, /device:TPU:0, one launch (start us, length us, event | category | flops | bytes accessed | tf_op | source)
XLA Modules:
  0.0 137.6 jit_solution(9402309338223585498)
XLA Ops:
  0.6 0.0 copy-start
  0.6 0.0 copy-start.2
  0.7 2.5 %collective-permute-start.7 = (bf16[128,3072]{1,0:T(8,128)(2,1)}, bf16[128,3072]{1,0:T(8,128)(2,1)S(1)}, u32[]{:S(2)}, u32[]{:S(2)}) collective-permute-start(bf16[128,3072]{1,0:T(8,128)(2,1)} %bitcast.24), channel_id=1, source_target_pairs={{0,4},{4,8},{8,12},{12,16},{16,20},{20,24},{24,28},{1,5},{5,9},{9,... | collective-permute-start | bytes 2359304 | tf_op jit(solution)/shard_map/ppermute | solution.py:864
  3.2 1.3 collective-permute-start.3
  4.5 2.9 %pack_stash.1 = (f32[128,128]{1,0:T(8,128)}, bf16[224,768]{1,0:T(8,128)(2,1)}, bf16[224,768]{1,0:T(8,128)(2,1)}, bf16[224,768]{1,0:T(8,128)(2,1)}, bf16[224,768]{1,0:T(8,128)(2,1)}) custom-call(bf16[128,3072]{1,0:T(8,128)(2,1)} %bitcast.18, f32[1,3072]{1,0:T(1,128)} %refs_6_.1, bf16[3,24,32,128]{3,2,1,0:T(8,128)(2,1)} %bitcast.22), custom_call_target="tpu_custom_call" | custom-call | flops 1572864 | bytes 2359296 | tf_op jit(solution)/shard_map/pack_stash/pallas_call | solution.py:426
  7.4 2.5 %collective-permute-start = (bf16[224,768]{1,0:T(8,128)(2,1)}, bf16[224,768]{1,0:T(8,128)(2,1)S(1)}, u32[]{:S(2)}, u32[]{:S(2)}) collective-permute-start(bf16[224,768]{1,0:T(8,128)(2,1)} %get-tuple-element.44), channel_id=1, source_target_pairs={{0,1},{1,2},{2,3},{3,0},{4,5},{5,6},{6,7},{7,4},{8,9},{9,10},{10,1... | collective-permute-start | bytes 1032200 | tf_op jit(solution)/shard_map/ppermute | solution.py:892
  9.9 2.6 %collective-permute-start.1 = (bf16[224,768]{1,0:T(8,128)(2,1)}, bf16[224,768]{1,0:T(8,128)(2,1)}, u32[]{:S(2)}, u32[]{:S(2)}) collective-permute-start(bf16[224,768]{1,0:T(8,128)(2,1)} %get-tuple-element.45), channel_id=1, source_target_pairs={{0,2},{1,3},{2,0},{3,1},{4,6},{5,7},{6,4},{7,5},{8,10},{9,11},{10,... | collective-permute-start | bytes 1032200 | tf_op jit(solution)/shard_map/ppermute | solution.py:892
  12.5 1.3 collective-permute-start.2
  13.8 0.1 pad_add_fusion.meta_ref
  13.9 0.0 collective-permute-done.7.inner_ref
  13.9 0.9 pack_inbound.1
  14.8 0.0 copy-start.4
  14.9 0.0 copy-start.5
  14.9 0.7 collective-permute-start.8
  15.6 0.0 collective-permute-done.3.inner_ref
  15.6 0.3 collective-permute-start.9
  16.0 1.4 %pack_cotangent.1 = (bf16[128,768]{1,0:T(8,128)(2,1)}, bf16[128,768]{1,0:T(8,128)(2,1)S(1)}, bf16[128,768]{1,0:T(8,128)(2,1)S(1)}, bf16[128,768]{1,0:T(8,128)(2,1)S(1)}, bf16[128,3072]{1,0:T(8,128)(2,1)S(1)}) custom-call(s32[3]{0:T(128)S(1)} %pad_add_fusion.meta_ref, bf16[128,3072]{1,0:T(8,128)(2,1)S(1)} %copy-done.3, ...), custom_call_target="tpu_custom_call" | custom-call | flops 1572864 | bytes 2359296 | tf_op jit(solution)/shard_map/pack_cotangent/pallas_call | solution.py:451
  17.4 2.1 %collective-permute-done.refs_1_ = bf16[224,768]{1,0:T(8,128)(2,1)S(1)} collective-permute-done((bf16[224,768]{1,0:T(8,128)(2,1)}, bf16[224,768]{1,0:T(8,128)(2,1)S(1)}, u32[]{:S(2)}, u32[]{:S(2)}) %collective-permute-start) | collective-permute-done | bytes 344096 | tf_op jit(solution)/shard_map/ppermute | solution.py:892
  19.5 2.1 %collective-permute-start.10 = (bf16[136,768]{1,0:T(8,128)(2,1)S(1)}, bf16[136,768]{1,0:T(8,128)(2,1)S(1)}, u32[]{:S(2)}, u32[]{:S(2)}) collective-permute-start(bf16[136,768]{1,0:T(8,128)(2,1)S(1)} %get-tuple-element.54), channel_id=1, source_target_pairs={{0,3},{1,0},{2,1},{3,2},{4,7},{5,4},{6,5},{7,6},{8,11},{9,8},{10,9... | collective-permute-start | bytes 626696 | tf_op jit(solution)/shard_map/ppermute | solution.py:892
  21.6 15.9 %collective-permute-done.1.refs_2_ = bf16[224,768]{1,0:T(8,128)(2,1)} collective-permute-done((bf16[224,768]{1,0:T(8,128)(2,1)}, bf16[224,768]{1,0:T(8,128)(2,1)}, u32[]{:S(2)}, u32[]{:S(2)}) %collective-permute-start.1) | collective-permute-done | bytes 344096 | tf_op jit(solution)/shard_map/ppermute | solution.py:892
  37.6 12.3 %collective-permute-start.4 = (bf16[128,768]{1,0:T(8,128)(2,1)S(1)}, bf16[128,768]{1,0:T(8,128)(2,1)S(1)}, u32[]{:S(2)}, u32[]{:S(2)}) collective-permute-start(bf16[128,768]{1,0:T(8,128)(2,1)S(1)} %get-tuple-element.48), channel_id=1, source_target_pairs={{0,1},{1,2},{2,3},{3,0},{4,5},{5,6},{6,7},{7,4},{8,9},{9,10},{10,1... | collective-permute-start | bytes 589832 | tf_op jit(solution)/shard_map/ppermute | solution.py:892
  49.9 0.0 collective-permute-done.2.refs_3_
  49.9 3.4 %collective-permute-start.5 = (bf16[128,768]{1,0:T(8,128)(2,1)S(1)}, bf16[128,768]{1,0:T(8,128)(2,1)S(1)}, u32[]{:S(2)}, u32[]{:S(2)}) collective-permute-start(bf16[128,768]{1,0:T(8,128)(2,1)S(1)} %get-tuple-element.49), channel_id=1, source_target_pairs={{0,2},{1,3},{2,0},{3,1},{4,6},{5,7},{6,4},{7,5},{8,10},{9,11},{10,... | collective-permute-start | bytes 589832 | tf_op jit(solution)/shard_map/ppermute | solution.py:892
  53.2 0.0 collective-permute-done.8.refs_5_
  53.2 1.9 %collective-permute-start.6 = (bf16[128,768]{1,0:T(8,128)(2,1)S(1)}, bf16[128,768]{1,0:T(8,128)(2,1)S(1)}, u32[]{:S(2)}, u32[]{:S(2)}) collective-permute-start(bf16[128,768]{1,0:T(8,128)(2,1)S(1)} %get-tuple-element.50), channel_id=1, source_target_pairs={{0,3},{1,0},{2,1},{3,2},{4,7},{5,4},{6,5},{7,6},{8,11},{9,8},{10,9... | collective-permute-start | bytes 589832 | tf_op jit(solution)/shard_map/ppermute | solution.py:892
  55.1 0.2 fusion
  55.4 0.0 copy-start.8
  55.4 9.6 %collective-permute-done.9.refs_6_ = bf16[136,768]{1,0:T(8,128)(2,1)S(1)} collective-permute-done((bf16[136,768]{1,0:T(8,128)(2,1)S(1)}, bf16[136,768]{1,0:T(8,128)(2,1)S(1)}, u32[]{:S(2)}, u32[]{:S(2)}) %collective-permute-start.9) | collective-permute-done | bytes 208928 | tf_op jit(solution)/shard_map/ppermute | solution.py:892
  65.0 0.0 collective-permute-done.10.refs_7_
  65.0 7.5 %heads_forward.1 = (bf16[136,768]{1,0:T(8,128)(2,1)S(1)}, bf16[136,768]{1,0:T(8,128)(2,1)S(1)}, bf16[136,768]{1,0:T(8,128)(2,1)S(1)}, bf16[136,768]{1,0:T(8,128)(2,1)S(1)}) custom-call(s32[3]{0:T(128)S(1)} %pad_add_fusion.meta_ref, bf16[224,768]{1,0:T(8,128)(2,1)S(1)} %copy-done.4, bf16[224,768]{1,0:T(8,128)(2,1)S(1)} %collective-permute-done.refs_1_, ...), custom_call_target="tpu_custom_call" | custom-call | flops 3072 | bytes 512 | tf_op jit(solution)/shard_map/heads_forward/pallas_call | solution.py:702
  72.6 5.0 %collective-permute-start.11 = (bf16[136,768]{1,0:T(8,128)(2,1)S(1)}, bf16[136,768]{1,0:T(8,128)(2,1)S(1)}, u32[]{:S(2)}, u32[]{:S(2)}) collective-permute-start(bf16[136,768]{1,0:T(8,128)(2,1)S(1)} %get-tuple-element.60.refs_1_), channel_id=1, source_target_pairs={{0,3},{1,0},{2,1},{3,2},{4,7},{5,4},{6,5},{7,6},{8,11},{9,8},{10,9... | collective-permute-start | bytes 626696 | tf_op jit(solution)/shard_map/ppermute | solution.py:892
  77.6 1.5 %collective-permute-start.12 = (bf16[136,768]{1,0:T(8,128)(2,1)S(1)}, bf16[136,768]{1,0:T(8,128)(2,1)S(1)}, u32[]{:S(2)}, u32[]{:S(2)}) collective-permute-start(bf16[136,768]{1,0:T(8,128)(2,1)S(1)} %get-tuple-element.61.refs_2_), channel_id=1, source_target_pairs={{0,2},{1,3},{2,0},{3,1},{4,6},{5,7},{6,4},{7,5},{8,10},{9,11},{10,... | collective-permute-start | bytes 626696 | tf_op jit(solution)/shard_map/ppermute | solution.py:892
  79.1 0.0 collective-permute-done.4.refs_5_
  79.1 0.0 collective-permute-start.13
  79.1 0.0 collective-permute-done.5.refs_6_
  79.1 0.0 collective-permute-done.6.refs_7_
  79.1 0.0 copy-start.7
  79.1 11.8 %heads_backward.1 = (bf16[232,768]{1,0:T(8,128)(2,1)S(1)}, bf16[232,768]{1,0:T(8,128)(2,1)}, bf16[232,768]{1,0:T(8,128)(2,1)}, bf16[232,768]{1,0:T(8,128)(2,1)}, f32[1,768]{1,0:T(1,128)}) custom-call(s32[3]{0:T(128)S(1)} %pad_add_fusion.meta_ref, bf16[224,768]{1,0:T(8,128)(2,1)S(1)} %copy-done.4, bf16[224,768]{1,0:T(8,128)(2,1)S(1)} %collective-permute-done.refs_1_, ...), custom_call_target="tpu_custom_call" | custom-call | flops 1228800000 | bytes 393216 | tf_op jit(solution)/shard_map/heads_backward/pallas_call | solution.py:603
  90.9 0.0 collective-permute-done.11.refs_1_.refs_4_
  90.9 6.8 %collective-permute-done.12.refs_2_.refs_5_ = bf16[136,768]{1,0:T(8,128)(2,1)S(1)} collective-permute-done((bf16[136,768]{1,0:T(8,128)(2,1)S(1)}, bf16[136,768]{1,0:T(8,128)(2,1)S(1)}, u32[]{:S(2)}, u32[]{:S(2)}) %collective-permute-start.12) | collective-permute-done | bytes 208928 | tf_op jit(solution)/shard_map/ppermute | solution.py:892
  97.7 0.0 collective-permute-done.13.refs_3_.refs_6_
  97.7 0.9 memory_rows.1
  98.7 0.7 collective-permute-start.17
  99.3 0.7 collective-permute-start.18
  100.0 0.7 collective-permute-start.19
  100.7 0.1 collective-permute-start.14
  100.8 1.4 %collective-permute-start.15 = (bf16[232,768]{1,0:T(8,128)(2,1)}, bf16[232,768]{1,0:T(8,128)(2,1)S(1)}, u32[]{:S(2)}, u32[]{:S(2)}) collective-permute-start(bf16[232,768]{1,0:T(8,128)(2,1)} %get-tuple-element.69), channel_id=1, source_target_pairs={{0,2},{1,3},{2,0},{3,1},{4,6},{5,7},{6,4},{7,5},{8,10},{9,11},{10,... | collective-permute-start | bytes 1069064 | tf_op jit(solution)/shard_map/ppermute | solution.py:892
  102.2 0.0 collective-permute-done.17
  102.2 1.9 %collective-permute-start.16 = (bf16[232,768]{1,0:T(8,128)(2,1)}, bf16[232,768]{1,0:T(8,128)(2,1)}, u32[]{:S(2)}, u32[]{:S(2)}) collective-permute-start(bf16[232,768]{1,0:T(8,128)(2,1)} %get-tuple-element.70), channel_id=1, source_target_pairs={{0,1},{1,2},{2,3},{3,0},{4,5},{5,6},{6,7},{7,4},{8,9},{9,10},{10,1... | collective-permute-start | bytes 1069064 | tf_op jit(solution)/shard_map/ppermute | solution.py:892
  104.1 0.0 collective-permute-done.18
  104.1 0.0 collective-permute-done.19
  104.2 0.7 copy-done.9
  104.9 0.6 slice.8
  105.5 1.3 collective-permute-start.20
  106.8 0.0 copy-start.10
  106.9 0.0 copy-start.6
  106.9 1.5 %place_columns.1 = bf16[128,3072]{1,0:T(8,128)(2,1)} custom-call(s32[3]{0:T(128)S(1)} %pad_add_fusion.meta_ref, bf16[136,768]{1,0:T(8,128)(2,1)S(1)} %get-tuple-element.63.refs_11_.refs_0_, bf16[136,768]{1,0:T(8,128)(2,1)S(1)} %collective-permute-done.11.refs_1_.refs_4_, bf16[136,768]{1,0:T(8,128)(2,1)S(1)} %collective-permute-done.12.refs_2_.refs_5_, ...), custom_call_target="tpu_custom_call" | custom-call | bytes 128 | tf_op jit(solution)/shard_map/place_columns/pallas_call | solution.py:783
  108.4 1.2 collective-permute-done.20
  109.6 1.5 %slice_select_fusion = bf16[64,768]{1,0:T(8,128)(2,1)} fusion(bf16[64,768]{1,0:T(8,128)(2,1)} %collective-permute-done.20, bf16[128,768]{1,0:T(8,128)(2,1)S(1)} %copy-done.10, pred[]{:T(512)S(6)} %eq.14), kind=kLoop, calls=%fused_computation.3 | loop fusion | flops 49152 | bytes 294913 | tf_op jit(solution)/shard_map/jit(_where)/select_n | solution.py:874
  111.1 0.0 collective-permute-done.14.refs_1_
  111.1 23.0 %collective-permute-done.15.refs_2_ = bf16[232,768]{1,0:T(8,128)(2,1)S(1)} collective-permute-done((bf16[232,768]{1,0:T(8,128)(2,1)}, bf16[232,768]{1,0:T(8,128)(2,1)S(1)}, u32[]{:S(2)}, u32[]{:S(2)}) %collective-permute-start.15) | collective-permute-done | bytes 356384 | tf_op jit(solution)/shard_map/ppermute | solution.py:892
  134.1 0.0 collective-permute-done.16.refs_3_
  134.1 0.0 copy-done.6
  134.2 3.5 %heads_finish.1 = (bf16[128,3072]{1,0:T(8,128)(2,1)}, f32[3,24,32,128]{3,2,1,0:T(8,128)}, f32[8,24]{1,0:T(8,128)}) custom-call(s32[3]{0:T(128)S(1)} %pad_add_fusion.meta_ref, bf16[232,768]{1,0:T(8,128)(2,1)S(1)} %get-tuple-element.67.refs_0_, bf16[232,768]{1,0:T(8,128)(2,1)S(1)} %collective-permute-done.14.refs_1_, ...), custom_call_target="tpu_custom_call" | custom-call | flops 4718592 | bytes 5505024 | tf_op jit(solution)/shard_map/heads_finish/pallas_call | solution.py:834
  (17 shorter events, 0.1 us)
Async XLA Ops:
  0.6 54.5 %copy-start = (f32[1,32,24]{1,2,0:T(8,128)S(1)}, f32[1,32,24]{1,2,0:T(8,128)}, u32[]{:S(2)}) copy-start(f32[1,32,24]{1,2,0:T(8,128)} %param.17) | copy-start | bytes 9220
  0.6 13.2 %copy-start.2 = (bf16[128,3072]{1,0:T(8,128)(2,1)S(1)}, bf16[128,3072]{1,0:T(8,128)(2,1)}, u32[]{:S(2)}) copy-start(bf16[128,3072]{1,0:T(8,128)(2,1)} %edge_ref.3) | copy-start | bytes 2359300
  0.7 13.2 %collective-permute-start.7 = (bf16[128,3072]{1,0:T(8,128)(2,1)}, bf16[128,3072]{1,0:T(8,128)(2,1)S(1)}, u32[]{:S(2)}, u32[]{:S(2)}) collective-permute-start(bf16[128,3072]{1,0:T(8,128)(2,1)} %bitcast.24), channel_id=1, source_target_pairs={{0,4},{4,8},{8,12},{12,16},{16,20},{20,24},{24,28},{1,5},{5,9},{9,... | collective-permute-start | bytes 2359304 | tf_op jit(solution)/shard_map/ppermute | solution.py:864
  3.2 12.4 %collective-permute-start.3 = (bf16[128,3072]{1,0:T(8,128)(2,1)}, bf16[128,3072]{1,0:T(8,128)(2,1)S(1)}, u32[]{:S(2)}, u32[]{:S(2)}) collective-permute-start(bf16[128,3072]{1,0:T(8,128)(2,1)} %bitcast.25), channel_id=1, source_target_pairs={{4,0},{8,4},{12,8},{16,12},{20,16},{24,20},{28,24},{5,1},{9,5},{13... | collective-permute-start | bytes 2359304 | tf_op jit(solution)/shard_map/ppermute | solution.py:864
  4.5 11.5 %copy-start.3 = (bf16[128,3072]{1,0:T(8,128)(2,1)S(1)}, bf16[128,3072]{1,0:T(8,128)(2,1)}, u32[]{:S(2)}) copy-start(bf16[128,3072]{1,0:T(8,128)(2,1)} %edge_ref.2) | copy-start | bytes 2359300
  7.4 12.1 %collective-permute-start = (bf16[224,768]{1,0:T(8,128)(2,1)}, bf16[224,768]{1,0:T(8,128)(2,1)S(1)}, u32[]{:S(2)}, u32[]{:S(2)}) collective-permute-start(bf16[224,768]{1,0:T(8,128)(2,1)} %get-tuple-element.44), channel_id=1, source_target_pairs={{0,1},{1,2},{2,3},{3,0},{4,5},{5,6},{6,7},{7,4},{8,9},{9,10},{10,1... | collective-permute-start | bytes 1032200 | tf_op jit(solution)/shard_map/ppermute | solution.py:892
  9.9 27.7 %collective-permute-start.1 = (bf16[224,768]{1,0:T(8,128)(2,1)}, bf16[224,768]{1,0:T(8,128)(2,1)}, u32[]{:S(2)}, u32[]{:S(2)}) collective-permute-start(bf16[224,768]{1,0:T(8,128)(2,1)} %get-tuple-element.45), channel_id=1, source_target_pairs={{0,2},{1,3},{2,0},{3,1},{4,6},{5,7},{6,4},{7,5},{8,10},{9,11},{10,... | collective-permute-start | bytes 1032200 | tf_op jit(solution)/shard_map/ppermute | solution.py:892
  12.5 37.4 %collective-permute-start.2 = (bf16[224,768]{1,0:T(8,128)(2,1)}, bf16[224,768]{1,0:T(8,128)(2,1)}, u32[]{:S(2)}, u32[]{:S(2)}) collective-permute-start(bf16[224,768]{1,0:T(8,128)(2,1)} %get-tuple-element.46), channel_id=1, source_target_pairs={{0,3},{1,0},{2,1},{3,2},{4,7},{5,4},{6,5},{7,6},{8,11},{9,8},{10,9... | collective-permute-start | bytes 1032200 | tf_op jit(solution)/shard_map/ppermute | solution.py:892
  14.8 40.3 %copy-start.11 = (f32[256,32]{1,0:T(8,128)S(1)}, f32[256,32]{1,0:T(8,128)}, u32[]{:S(2)}) copy-start(f32[256,32]{1,0:T(8,128)} %constant.35.clone) | copy-start | bytes 98308
  14.8 50.2 %copy-start.4 = (bf16[224,768]{1,0:T(8,128)(2,1)S(1)}, bf16[224,768]{1,0:T(8,128)(2,1)}, u32[]{:S(2)}) copy-start(bf16[224,768]{1,0:T(8,128)(2,1)} %get-tuple-element.43.refs_0_) | copy-start | bytes 1032196
  14.9 50.1 %copy-start.5 = (f32[1,3072]{1,0:T(1,128)S(1)}, f32[1,3072]{1,0:T(1,128)}, u32[]{:S(2)}) copy-start(f32[1,3072]{1,0:T(1,128)} %refs_6_.1) | copy-start | bytes 36868
  14.9 38.4 %collective-permute-start.8 = (bf16[136,768]{1,0:T(8,128)(2,1)S(1)}, bf16[136,768]{1,0:T(8,128)(2,1)S(1)}, u32[]{:S(2)}, u32[]{:S(2)}) collective-permute-start(bf16[136,768]{1,0:T(8,128)(2,1)S(1)} %get-tuple-element.52), channel_id=1, source_target_pairs={{0,1},{1,2},{2,3},{3,0},{4,5},{5,6},{6,7},{7,4},{8,9},{9,10},{10,1... | collective-permute-start | bytes 626696 | tf_op jit(solution)/shard_map/ppermute | solution.py:892
  15.6 49.4 %collective-permute-start.9 = (bf16[136,768]{1,0:T(8,128)(2,1)S(1)}, bf16[136,768]{1,0:T(8,128)(2,1)S(1)}, u32[]{:S(2)}, u32[]{:S(2)}) collective-permute-start(bf16[136,768]{1,0:T(8,128)(2,1)S(1)} %get-tuple-element.53), channel_id=1, source_target_pairs={{0,2},{1,3},{2,0},{3,1},{4,6},{5,7},{6,4},{7,5},{8,10},{9,11},{10,... | collective-permute-start | bytes 626696 | tf_op jit(solution)/shard_map/ppermute | solution.py:892
  19.5 45.5 %collective-permute-start.10 = (bf16[136,768]{1,0:T(8,128)(2,1)S(1)}, bf16[136,768]{1,0:T(8,128)(2,1)S(1)}, u32[]{:S(2)}, u32[]{:S(2)}) collective-permute-start(bf16[136,768]{1,0:T(8,128)(2,1)S(1)} %get-tuple-element.54), channel_id=1, source_target_pairs={{0,3},{1,0},{2,1},{3,2},{4,7},{5,4},{6,5},{7,6},{8,11},{9,8},{10,9... | collective-permute-start | bytes 626696 | tf_op jit(solution)/shard_map/ppermute | solution.py:892
  37.6 41.5 %collective-permute-start.4 = (bf16[128,768]{1,0:T(8,128)(2,1)S(1)}, bf16[128,768]{1,0:T(8,128)(2,1)S(1)}, u32[]{:S(2)}, u32[]{:S(2)}) collective-permute-start(bf16[128,768]{1,0:T(8,128)(2,1)S(1)} %get-tuple-element.48), channel_id=1, source_target_pairs={{0,1},{1,2},{2,3},{3,0},{4,5},{5,6},{6,7},{7,4},{8,9},{9,10},{10,1... | collective-permute-start | bytes 589832 | tf_op jit(solution)/shard_map/ppermute | solution.py:892
  49.9 29.2 %collective-permute-start.5 = (bf16[128,768]{1,0:T(8,128)(2,1)S(1)}, bf16[128,768]{1,0:T(8,128)(2,1)S(1)}, u32[]{:S(2)}, u32[]{:S(2)}) collective-permute-start(bf16[128,768]{1,0:T(8,128)(2,1)S(1)} %get-tuple-element.49), channel_id=1, source_target_pairs={{0,2},{1,3},{2,0},{3,1},{4,6},{5,7},{6,4},{7,5},{8,10},{9,11},{10,... | collective-permute-start | bytes 589832 | tf_op jit(solution)/shard_map/ppermute | solution.py:892
  53.2 25.9 %collective-permute-start.6 = (bf16[128,768]{1,0:T(8,128)(2,1)S(1)}, bf16[128,768]{1,0:T(8,128)(2,1)S(1)}, u32[]{:S(2)}, u32[]{:S(2)}) collective-permute-start(bf16[128,768]{1,0:T(8,128)(2,1)S(1)} %get-tuple-element.50), channel_id=1, source_target_pairs={{0,3},{1,0},{2,1},{3,2},{4,7},{5,4},{6,5},{7,6},{8,11},{9,8},{10,9... | collective-permute-start | bytes 589832 | tf_op jit(solution)/shard_map/ppermute | solution.py:892
  55.4 23.8 %copy-start.8 = (f32[32,256]{1,0:T(8,128)S(1)}, f32[32,256]{1,0:T(8,128)}, u32[]{:S(2)}) copy-start(f32[32,256]{1,0:T(8,128)} %constant.36.clone.refs_10_) | copy-start | bytes 98308
  72.6 18.4 %collective-permute-start.11 = (bf16[136,768]{1,0:T(8,128)(2,1)S(1)}, bf16[136,768]{1,0:T(8,128)(2,1)S(1)}, u32[]{:S(2)}, u32[]{:S(2)}) collective-permute-start(bf16[136,768]{1,0:T(8,128)(2,1)S(1)} %get-tuple-element.60.refs_1_), channel_id=1, source_target_pairs={{0,3},{1,0},{2,1},{3,2},{4,7},{5,4},{6,5},{7,6},{8,11},{9,8},{10,9... | collective-permute-start | bytes 626696 | tf_op jit(solution)/shard_map/ppermute | solution.py:892
  77.6 20.1 %collective-permute-start.12 = (bf16[136,768]{1,0:T(8,128)(2,1)S(1)}, bf16[136,768]{1,0:T(8,128)(2,1)S(1)}, u32[]{:S(2)}, u32[]{:S(2)}) collective-permute-start(bf16[136,768]{1,0:T(8,128)(2,1)S(1)} %get-tuple-element.61.refs_2_), channel_id=1, source_target_pairs={{0,2},{1,3},{2,0},{3,1},{4,6},{5,7},{6,4},{7,5},{8,10},{9,11},{10,... | collective-permute-start | bytes 626696 | tf_op jit(solution)/shard_map/ppermute | solution.py:892
  79.1 18.6 %collective-permute-start.13 = (bf16[136,768]{1,0:T(8,128)(2,1)S(1)}, bf16[136,768]{1,0:T(8,128)(2,1)S(1)}, u32[]{:S(2)}, u32[]{:S(2)}) collective-permute-start(bf16[136,768]{1,0:T(8,128)(2,1)S(1)} %get-tuple-element.62.refs_3_), channel_id=1, source_target_pairs={{0,1},{1,2},{2,3},{3,0},{4,5},{5,6},{6,7},{7,4},{8,9},{9,10},{10,1... | collective-permute-start | bytes 626696 | tf_op jit(solution)/shard_map/ppermute | solution.py:892
  79.1 18.6 %copy-start.7 = (f32[3072]{0:T(1024)S(1)}, f32[3072]{0:T(1024)}, u32[]{:S(2)}) copy-start(f32[3072]{0:T(1024)} %param.19) | copy-start | bytes 36868
  98.7 3.5 %collective-permute-start.17 = (bf16[128,768]{1,0:T(8,128)(2,1)S(1)}, bf16[128,768]{1,0:T(8,128)(2,1)S(1)}, u32[]{:S(2)}, u32[]{:S(2)}) collective-permute-start(bf16[128,768]{1,0:T(8,128)(2,1)S(1)} %get-tuple-element.77), channel_id=1, source_target_pairs={{28,4},{29,5},{30,6},{31,7}} | collective-permute-start | bytes 589832 | tf_op jit(solution)/shard_map/ppermute | solution.py:871
  99.3 4.8 %collective-permute-start.18 = (bf16[128,768]{1,0:T(8,128)(2,1)S(1)}, bf16[128,768]{1,0:T(8,128)(2,1)S(1)}, u32[]{:S(2)}, u32[]{:S(2)}) collective-permute-start(bf16[128,768]{1,0:T(8,128)(2,1)S(1)} %get-tuple-element.78), channel_id=1, source_target_pairs={{28,12},{29,13},{30,14},{31,15}} | collective-permute-start | bytes 589832 | tf_op jit(solution)/shard_map/ppermute | solution.py:871
  100.0 4.1 %collective-permute-start.19 = (bf16[128,768]{1,0:T(8,128)(2,1)S(1)}, bf16[128,768]{1,0:T(8,128)(2,1)S(1)}, u32[]{:S(2)}, u32[]{:S(2)}) collective-permute-start(bf16[128,768]{1,0:T(8,128)(2,1)S(1)} %get-tuple-element.79), channel_id=1, source_target_pairs={{28,20},{29,21},{30,22},{31,23}} | collective-permute-start | bytes 589832 | tf_op jit(solution)/shard_map/ppermute | solution.py:871
  100.7 10.4 %collective-permute-start.14 = (bf16[232,768]{1,0:T(8,128)(2,1)}, bf16[232,768]{1,0:T(8,128)(2,1)S(1)}, u32[]{:S(2)}, u32[]{:S(2)}) collective-permute-start(bf16[232,768]{1,0:T(8,128)(2,1)} %get-tuple-element.68), channel_id=1, source_target_pairs={{0,3},{1,0},{2,1},{3,2},{4,7},{5,4},{6,5},{7,6},{8,11},{9,8},{10,9... | collective-permute-start | bytes 1069064 | tf_op jit(solution)/shard_map/ppermute | solution.py:892
  100.8 33.4 %collective-permute-start.15 = (bf16[232,768]{1,0:T(8,128)(2,1)}, bf16[232,768]{1,0:T(8,128)(2,1)S(1)}, u32[]{:S(2)}, u32[]{:S(2)}) collective-permute-start(bf16[232,768]{1,0:T(8,128)(2,1)} %get-tuple-element.69), channel_id=1, source_target_pairs={{0,2},{1,3},{2,0},{3,1},{4,6},{5,7},{6,4},{7,5},{8,10},{9,11},{10,... | collective-permute-start | bytes 1069064 | tf_op jit(solution)/shard_map/ppermute | solution.py:892
  102.2 31.9 %collective-permute-start.16 = (bf16[232,768]{1,0:T(8,128)(2,1)}, bf16[232,768]{1,0:T(8,128)(2,1)}, u32[]{:S(2)}, u32[]{:S(2)}) collective-permute-start(bf16[232,768]{1,0:T(8,128)(2,1)} %get-tuple-element.70), channel_id=1, source_target_pairs={{0,1},{1,2},{2,3},{3,0},{4,5},{5,6},{6,7},{7,4},{8,9},{9,10},{10,1... | collective-permute-start | bytes 1069064 | tf_op jit(solution)/shard_map/ppermute | solution.py:892
  104.2 0.7 copy-start.9
  104.9 29.2 %copy-start.1 = (bf16[1,128,3072]{2,1,0:T(8,128)(2,1)S(1)}, bf16[1,128,3072]{2,1,0:T(8,128)(2,1)}, u32[]{:S(2)}) copy-start(bf16[1,128,3072]{2,1,0:T(8,128)(2,1)} %param.13) | copy-start | bytes 2359300
  105.5 4.0 %collective-permute-start.20 = (bf16[64,768]{1,0:T(8,128)(2,1)}, bf16[64,768]{1,0:T(8,128)(2,1)}, u32[]{:S(2)}, u32[]{:S(2)}) collective-permute-start(bf16[64,768]{1,0:T(8,128)(2,1)} %slice.8), channel_id=1, source_target_pairs={{4,0},{12,8},{20,16},{28,24},{5,1},{13,9},{21,17},{29,25},{6,2},{1... | collective-permute-start | bytes 294920 | tf_op jit(solution)/shard_map/ppermute | solution.py:873
  106.8 2.7 %copy-start.10 = (bf16[128,768]{1,0:T(8,128)(2,1)S(1)}, bf16[128,768]{1,0:T(8,128)(2,1)}, u32[]{:S(2)}) copy-start(bf16[128,768]{1,0:T(8,128)(2,1)} %copy-done.9) | copy-start | bytes 589828
  106.9 27.3 %copy-start.6 = (f32[128,128]{1,0:T(8,128)S(1)}, f32[128,128]{1,0:T(8,128)}, u32[]{:S(2)}) copy-start(f32[128,128]{1,0:T(8,128)} %get-tuple-element.71.refs_5_) | copy-start | bytes 196612

commit v12 on v11

--- a/solution.py
+++ b/solution.py
@@ -459,9 +459,13 @@
     )(meta, edge, inner)
 
 
+def slot_order(parts):
+    return sorted(range(parts), key=lambda r: min(r, parts - r))
+
+
 def gather_rows(meta_ref, refs, rows, x_ref):
     parts = len(refs)
-    for r, ref in enumerate(refs):
+    for r, ref in zip(slot_order(parts), refs):
         source = lax.rem(meta_ref[0] + parts - r, parts)
         x_ref[pl.ds(pl.multiple_of(source * rows, rows), rows)] = ref[:rows]
 
@@ -469,7 +473,7 @@
 def gather_weight(meta_ref, refs, rows, weight_ref):
     parts = len(refs)
     depth = HEAD_DIM // parts
-    for r, ref in enumerate(refs):
+    for r, ref in zip(slot_order(parts), refs):
         source = lax.rem(meta_ref[0] + parts - r, parts)
         depth_at = pl.ds(pl.multiple_of(source * depth, depth), depth)
         for j in range(3):
@@ -483,7 +487,7 @@
 
     @pl.when(pl.program_id(0) == 0)
     def spread_inverse():
-        for r, ref in enumerate(refs):
+        for r, ref in zip(slot_order(parts), refs):
             source = lax.rem(meta_ref[0] + parts - r, parts)
             tail = ref[rows : rows + EXTRA].astype(F32)
             inverse_ref[pl.ds(pl.multiple_of(source * rows, rows), rows)] = column_of(
@@ -772,9 +776,9 @@
 def place_kernel(parts, meta_ref, *refs):
     out_ref = refs[parts]
     wide = refs[0].shape[1]
-    for r in range(parts):
+    for r, ref in zip(slot_order(parts), refs):
         source = lax.rem(meta_ref[0] + r, parts)
-        out_ref[:, pl.ds(pl.multiple_of(source * wide, 128), wide)] = refs[r][: out_ref.shape[0]]
+        out_ref[:, pl.ds(pl.multiple_of(source * wide, 128), wide)] = ref[: out_ref.shape[0]]
 
 
 def place_columns(meta, slots):
@@ -798,22 +802,22 @@
     wide = width // parts
     heads = wide // HEAD_DIM
     depth = HEAD_DIM // parts
-    for r in range(parts):
+    for r, g_ref in zip(slot_order(parts), g_refs):
         source = lax.rem(meta_ref[0] + r, parts)
         for h in range(heads):
             for j in range(3):
-                weight_ref[j, source * heads + h] = g_refs[r][
+                weight_ref[j, source * heads + h] = g_ref[
                     rows + j * depth : rows + (j + 1) * depth, h * HEAD_DIM : (h + 1) * HEAD_DIM
                 ].astype(F32)
     weight_copy = pltpu.make_async_copy(weight_ref, weight_hbm, sem)
     weight_copy.start()
     lane = lax.broadcasted_iota(jnp.int32, (bias_ref.shape[0], HEAD_DIM), 1)
     bias = jnp.zeros(lane.shape, F32)
-    for r in range(parts):
+    for r, g_ref in zip(slot_order(parts), g_refs):
         source = lax.rem(meta_ref[0] + r, parts)
         columns = pl.ds(pl.multiple_of(source * wide, 128), wide)
-        scaled_ref[:, columns] = g_refs[r][:rows].astype(F32) * gain_ref[:, columns]
-        shares = g_refs[r][rows + 3 * depth :].astype(F32)
+        scaled_ref[:, columns] = g_ref[:rows].astype(F32) * gain_ref[:, columns]
+        shares = g_ref[rows + 3 * depth :].astype(F32)
         for h in range(heads):
             bias = jnp.where(lane == source * heads + h, shares[:, h * HEAD_DIM : (h + 1) * HEAD_DIM], bias)
     bias_ref[...] = bias[:, : bias_ref.shape[1]]
@@ -888,11 +892,10 @@
     ).astype(jnp.int32)
 
     def exchanged(sends, direction):
-        moved = [
-            lax.ppermute(sends[r], "seq", [(i, (i + direction * r) % parts) for i in range(parts)])
-            for r in range(1, parts)
+        return [
+            lax.ppermute(sends[r], "seq", [(i, (i + direction * r) % parts) for i in range(parts)]) if r else sends[0]
+            for r in slot_order(parts)
         ]
-        return [sends[0]] + moved
 
     inverse_b, *a_sends = pack_stash(stash[0], norm_gain, qkv_weight[0], parts)
     a_slots = exchanged(a_sends, 1)

time: 138 us -> 138 us (level)
  starting transfers between devices: 44.3 us -> 26.3 us
  waiting for transfers between devices: 58.7 us -> 76.3 us
    ppermute x15, waiting for transfers between devices: 57.5 us -> 75.6 us  [exchanged(): lax.ppermute(sends[r], 'seq', [(i, (i + direction * r) % parts) for i in...]
    ppermute x15, starting transfers between devices: 37.1 us -> 19.2 us  [exchanged(): lax.ppermute(sends[r], 'seq', [(i, (i + direction * r) % parts) for i in...]
  transfers between devices with their start and end apart: 21 -> 21, of which waited for: 6 -> 9; matrix products, arithmetic and copies ran while one was open for 2% -> 2% of each run, Pallas kernels for 19% -> 19%
where the time goes in v12:
time: 138 us; the launch traced here: 137 us
  waiting for transfers between devices  76.3 us (55%)
  Pallas kernels  30.5 us (22%)
  starting transfers between devices  26.3 us (19%)
  other arithmetic  1.67 us (1%)
  local copies, waits for them, and re-layouts  1.42 us (1%)
    ppermute x15, waiting for transfers between devices, exchanged(): lax.ppermute(sends[r], 'seq', [(i, (i + direction * r) % parts) for i in...  75.6 us
    ppermute x15, starting transfers between devices, exchanged(): lax.ppermute(sends[r], 'seq', [(i, (i + direction * r) % parts) for i in...  19.2 us
    pallas_call x1, Pallas kernels, heads_backward(): pl.pallas_call(functools.partial(heads_backward_kernel, parts, rows), out...  11.8 us
    pallas_call x1, Pallas kernels, heads_forward(): pl.pallas_call(functools.partial(heads_forward_kernel, parts, rows), out_...  7.55 us
    ppermute x2, starting transfers between devices, shifted(): lax.ppermute(value, axis, [(source, source + steps) for source in range(f...  3.83 us
    pallas_call x1, Pallas kernels, heads_finish(): pl.pallas_call(functools.partial(heads_finish_kernel, parts), out_shape=(...  3.49 us
    pallas_call x1, Pallas kernels, pack_stash(): pl.pallas_call(functools.partial(pack_stash_kernel, parts, 4), out_shape=...  2.9 us
  transfers between devices with their start and end apart: 21, of which 9 were waited for; matrix products, arithmetic and copies ran while one was open for 2% of the time, Pallas kernels for 19%

profile of v12, /device:TPU:0, one launch (start us, length us, event | category | flops | bytes accessed | tf_op | source)
XLA Modules:
  0.0 137.3 jit_solution(3954608020382472317)
XLA Ops:
  0.6 0.0 copy-start
  0.7 2.5 %collective-permute-start.7 = (bf16[128,3072]{1,0:T(8,128)(2,1)}, bf16[128,3072]{1,0:T(8,128)(2,1)S(1)}, u32[]{:S(2)}, u32[]{:S(2)}) collective-permute-start(bf16[128,3072]{1,0:T(8,128)(2,1)} %bitcast.24), channel_id=1, source_target_pairs={{0,4},{4,8},{8,12},{12,16},{16,20},{20,24},{24,28},{1,5},{5,9},{9,... | collective-permute-start | bytes 2359304 | tf_op jit(solution)/shard_map/ppermute | solution.py:868
  3.2 1.3 collective-permute-start.3
  4.5 2.9 %pack_stash.1 = (f32[128,128]{1,0:T(8,128)}, bf16[224,768]{1,0:T(8,128)(2,1)}, bf16[224,768]{1,0:T(8,128)(2,1)}, bf16[224,768]{1,0:T(8,128)(2,1)}, bf16[224,768]{1,0:T(8,128)(2,1)}) custom-call(bf16[128,3072]{1,0:T(8,128)(2,1)} %bitcast.18, f32[1,3072]{1,0:T(1,128)} %refs_6_.1, bf16[3,24,32,128]{3,2,1,0:T(8,128)(2,1)} %bitcast.22), custom_call_target="tpu_custom_call" | custom-call | flops 1572864 | bytes 2359296 | tf_op jit(solution)/shard_map/pack_stash/pallas_call | solution.py:426
  7.4 2.5 %collective-permute-start = (bf16[224,768]{1,0:T(8,128)(2,1)}, bf16[224,768]{1,0:T(8,128)(2,1)S(1)}, u32[]{:S(2)}, u32[]{:S(2)}) collective-permute-start(bf16[224,768]{1,0:T(8,128)(2,1)} %get-tuple-element.44), channel_id=1, source_target_pairs={{0,1},{1,2},{2,3},{3,0},{4,5},{5,6},{6,7},{7,4},{8,9},{9,10},{10,1... | collective-permute-start | bytes 1032200 | tf_op jit(solution)/shard_map/ppermute | solution.py:896
  9.9 2.1 %collective-permute-start.1 = (bf16[224,768]{1,0:T(8,128)(2,1)}, bf16[224,768]{1,0:T(8,128)(2,1)}, u32[]{:S(2)}, u32[]{:S(2)}) collective-permute-start(bf16[224,768]{1,0:T(8,128)(2,1)} %get-tuple-element.45), channel_id=1, source_target_pairs={{0,3},{1,0},{2,1},{3,2},{4,7},{5,4},{6,5},{7,6},{8,11},{9,8},{10,9... | collective-permute-start | bytes 1032200 | tf_op jit(solution)/shard_map/ppermute | solution.py:896
  12.0 0.9 collective-permute-start.2
  12.9 0.1 pad_add_fusion.meta_ref
  13.0 0.0 collective-permute-done.7.inner_ref
  13.0 0.0 copy-done.2
  13.0 0.9 pack_inbound.1
  13.9 0.0 copy-start.4
  14.0 0.0 copy-start.5
  14.0 1.6 %collective-permute-start.8 = (bf16[136,768]{1,0:T(8,128)(2,1)S(1)}, bf16[136,768]{1,0:T(8,128)(2,1)S(1)}, u32[]{:S(2)}, u32[]{:S(2)}) collective-permute-start(bf16[136,768]{1,0:T(8,128)(2,1)S(1)} %get-tuple-element.52), channel_id=1, source_target_pairs={{0,1},{1,2},{2,3},{3,0},{4,5},{5,6},{6,7},{7,4},{8,9},{9,10},{10,1... | collective-permute-start | bytes 626696 | tf_op jit(solution)/shard_map/ppermute | solution.py:896
  15.6 0.0 collective-permute-done.3.inner_ref
  15.6 2.2 %collective-permute-start.9 = (bf16[136,768]{1,0:T(8,128)(2,1)S(1)}, bf16[136,768]{1,0:T(8,128)(2,1)S(1)}, u32[]{:S(2)}, u32[]{:S(2)}) collective-permute-start(bf16[136,768]{1,0:T(8,128)(2,1)S(1)} %get-tuple-element.53), channel_id=1, source_target_pairs={{0,3},{1,0},{2,1},{3,2},{4,7},{5,4},{6,5},{7,6},{8,11},{9,8},{10,9... | collective-permute-start | bytes 626696 | tf_op jit(solution)/shard_map/ppermute | solution.py:896
  17.9 1.4 %pack_cotangent.1 = (bf16[128,768]{1,0:T(8,128)(2,1)}, bf16[128,768]{1,0:T(8,128)(2,1)S(1)}, bf16[128,768]{1,0:T(8,128)(2,1)S(1)}, bf16[128,768]{1,0:T(8,128)(2,1)S(1)}, bf16[128,3072]{1,0:T(8,128)(2,1)S(1)}) custom-call(s32[3]{0:T(128)S(1)} %pad_add_fusion.meta_ref, bf16[128,3072]{1,0:T(8,128)(2,1)S(1)} %copy-done.3, ...), custom_call_target="tpu_custom_call" | custom-call | flops 1572864 | bytes 2359296 | tf_op jit(solution)/shard_map/pack_cotangent/pallas_call | solution.py:451
  19.3 0.2 collective-permute-done.refs_1_
  19.5 1.2 collective-permute-start.10
  20.7 7.7 %collective-permute-done.1.refs_2_ = bf16[224,768]{1,0:T(8,128)(2,1)} collective-permute-done((bf16[224,768]{1,0:T(8,128)(2,1)}, bf16[224,768]{1,0:T(8,128)(2,1)}, u32[]{:S(2)}, u32[]{:S(2)}) %collective-permute-start.1) | collective-permute-done | bytes 344096 | tf_op jit(solution)/shard_map/ppermute | solution.py:896
  28.4 2.2 %collective-permute-start.4 = (bf16[128,768]{1,0:T(8,128)(2,1)S(1)}, bf16[128,768]{1,0:T(8,128)(2,1)S(1)}, u32[]{:S(2)}, u32[]{:S(2)}) collective-permute-start(bf16[128,768]{1,0:T(8,128)(2,1)S(1)} %get-tuple-element.48), channel_id=1, source_target_pairs={{0,1},{1,2},{2,3},{3,0},{4,5},{5,6},{6,7},{7,4},{8,9},{9,10},{10,1... | collective-permute-start | bytes 589832 | tf_op jit(solution)/shard_map/ppermute | solution.py:896
  30.6 25.8 %collective-permute-done.2.refs_3_ = bf16[224,768]{1,0:T(8,128)(2,1)} collective-permute-done((bf16[224,768]{1,0:T(8,128)(2,1)}, bf16[224,768]{1,0:T(8,128)(2,1)}, u32[]{:S(2)}, u32[]{:S(2)}) %collective-permute-start.2) | collective-permute-done | bytes 344096 | tf_op jit(solution)/shard_map/ppermute | solution.py:896
  56.4 0.0 collective-permute-start.5
  56.4 0.0 collective-permute-done.8.refs_5_
  56.4 0.0 collective-permute-start.6
  56.4 0.2 fusion
  56.6 0.0 copy-start.8
  56.7 0.0 collective-permute-done.9.refs_6_
  56.7 12.7 %collective-permute-done.10.refs_7_ = bf16[136,768]{1,0:T(8,128)(2,1)S(1)} collective-permute-done((bf16[136,768]{1,0:T(8,128)(2,1)S(1)}, bf16[136,768]{1,0:T(8,128)(2,1)S(1)}, u32[]{:S(2)}, u32[]{:S(2)}) %collective-permute-start.10) | collective-permute-done | bytes 208928 | tf_op jit(solution)/shard_map/ppermute | solution.py:896
  69.4 0.0 copy-done.4
  69.4 7.5 %heads_forward.1 = (bf16[136,768]{1,0:T(8,128)(2,1)S(1)}, bf16[136,768]{1,0:T(8,128)(2,1)S(1)}, bf16[136,768]{1,0:T(8,128)(2,1)S(1)}, bf16[136,768]{1,0:T(8,128)(2,1)S(1)}) custom-call(s32[3]{0:T(128)S(1)} %pad_add_fusion.meta_ref, bf16[224,768]{1,0:T(8,128)(2,1)S(1)} %copy-done.4, bf16[224,768]{1,0:T(8,128)(2,1)S(1)} %collective-permute-done.refs_1_, ...), custom_call_target="tpu_custom_call" | custom-call | flops 3072 | bytes 512 | tf_op jit(solution)/shard_map/heads_forward/pallas_call | solution.py:706
  77.0 0.6 collective-permute-start.11
  77.6 1.5 %collective-permute-start.12 = (bf16[136,768]{1,0:T(8,128)(2,1)S(1)}, bf16[136,768]{1,0:T(8,128)(2,1)S(1)}, u32[]{:S(2)}, u32[]{:S(2)}) collective-permute-start(bf16[136,768]{1,0:T(8,128)(2,1)S(1)} %get-tuple-element.61.refs_3_), channel_id=1, source_target_pairs={{0,1},{1,2},{2,3},{3,0},{4,5},{5,6},{6,7},{7,4},{8,9},{9,10},{10,1... | collective-permute-start | bytes 626696 | tf_op jit(solution)/shard_map/ppermute | solution.py:896
  79.1 0.0 collective-permute-done.4.refs_5_
  79.1 0.0 collective-permute-start.13
  79.1 0.0 collective-permute-done.5.refs_6_
  79.1 0.0 collective-permute-done.6.refs_7_
  79.1 0.0 copy-start.7
  79.1 11.8 %heads_backward.1 = (bf16[232,768]{1,0:T(8,128)(2,1)S(1)}, bf16[232,768]{1,0:T(8,128)(2,1)}, bf16[232,768]{1,0:T(8,128)(2,1)}, bf16[232,768]{1,0:T(8,128)(2,1)}, f32[1,768]{1,0:T(1,128)}) custom-call(s32[3]{0:T(128)S(1)} %pad_add_fusion.meta_ref, bf16[224,768]{1,0:T(8,128)(2,1)S(1)} %copy-done.4, bf16[224,768]{1,0:T(8,128)(2,1)S(1)} %collective-permute-done.refs_1_, ...), custom_call_target="tpu_custom_call" | custom-call | flops 1228800000 | bytes 393216 | tf_op jit(solution)/shard_map/heads_backward/pallas_call | solution.py:607
  90.9 0.0 collective-permute-done.11.refs_1_.refs_4_
  90.9 0.0 collective-permute-done.12.refs_2_.refs_5_
  90.9 5.8 %collective-permute-done.13.refs_3_.refs_6_ = bf16[136,768]{1,0:T(8,128)(2,1)S(1)} collective-permute-done((bf16[136,768]{1,0:T(8,128)(2,1)S(1)}, bf16[136,768]{1,0:T(8,128)(2,1)S(1)}, u32[]{:S(2)}, u32[]{:S(2)}) %collective-permute-start.13) | collective-permute-done | bytes 208928 | tf_op jit(solution)/shard_map/ppermute | solution.py:896
  96.7 0.9 memory_rows.1
  97.7 0.7 collective-permute-start.17
  98.4 0.7 collective-permute-start.18
  99.0 0.7 collective-permute-start.19
  99.7 3.7 %collective-permute-start.14 = (bf16[232,768]{1,0:T(8,128)(2,1)}, bf16[232,768]{1,0:T(8,128)(2,1)S(1)}, u32[]{:S(2)}, u32[]{:S(2)}) collective-permute-start(bf16[232,768]{1,0:T(8,128)(2,1)} %get-tuple-element.68), channel_id=1, source_target_pairs={{0,3},{1,0},{2,1},{3,2},{4,7},{5,4},{6,5},{7,6},{8,11},{9,8},{10,9... | collective-permute-start | bytes 1069064 | tf_op jit(solution)/shard_map/ppermute | solution.py:896
  103.4 0.0 collective-permute-start.15
  103.4 0.0 collective-permute-done.17
  103.4 0.6 collective-permute-start.16
  104.0 0.0 collective-permute-done.18
  104.0 0.0 collective-permute-done.19
  104.1 0.7 copy-done.9
  104.8 0.6 slice.8
  105.4 1.3 collective-permute-start.20
  106.7 0.0 copy-start.10
  106.7 0.0 copy-start.6
  106.7 1.5 %place_columns.1 = bf16[128,3072]{1,0:T(8,128)(2,1)} custom-call(s32[3]{0:T(128)S(1)} %pad_add_fusion.meta_ref, bf16[136,768]{1,0:T(8,128)(2,1)S(1)} %get-tuple-element.63.refs_11_.refs_0_, bf16[136,768]{1,0:T(8,128)(2,1)S(1)} %collective-permute-done.11.refs_1_.refs_4_, bf16[136,768]{1,0:T(8,128)(2,1)S(1)} %collective-permute-done.12.refs_2_.refs_5_, ...), custom_call_target="tpu_custom_call" | custom-call | bytes 128 | tf_op jit(solution)/shard_map/place_columns/pallas_call | solution.py:787
  108.2 0.7 collective-permute-done.20
  109.0 1.5 %slice_select_fusion = bf16[64,768]{1,0:T(8,128)(2,1)} fusion(bf16[64,768]{1,0:T(8,128)(2,1)} %collective-permute-done.20, bf16[128,768]{1,0:T(8,128)(2,1)S(1)} %copy-done.10, pred[]{:T(512)S(6)} %eq.14), kind=kLoop, calls=%fused_computation.3 | loop fusion | flops 49152 | bytes 294913 | tf_op jit(solution)/shard_map/jit(_where)/select_n | solution.py:878
  110.5 9.5 %collective-permute-done.14.refs_1_ = bf16[232,768]{1,0:T(8,128)(2,1)S(1)} collective-permute-done((bf16[232,768]{1,0:T(8,128)(2,1)}, bf16[232,768]{1,0:T(8,128)(2,1)S(1)}, u32[]{:S(2)}, u32[]{:S(2)}) %collective-permute-start.14) | collective-permute-done | bytes 356384 | tf_op jit(solution)/shard_map/ppermute | solution.py:896
  120.0 0.3 collective-permute-done.15.refs_2_
  120.3 13.5 %collective-permute-done.16.refs_3_ = bf16[232,768]{1,0:T(8,128)(2,1)} collective-permute-done((bf16[232,768]{1,0:T(8,128)(2,1)}, bf16[232,768]{1,0:T(8,128)(2,1)}, u32[]{:S(2)}, u32[]{:S(2)}) %collective-permute-start.16) | collective-permute-done | bytes 356384 | tf_op jit(solution)/shard_map/ppermute | solution.py:896
  133.8 3.5 %heads_finish.1 = (bf16[128,3072]{1,0:T(8,128)(2,1)}, f32[3,24,32,128]{3,2,1,0:T(8,128)}, f32[8,24]{1,0:T(8,128)}) custom-call(s32[3]{0:T(128)S(1)} %pad_add_fusion.meta_ref, bf16[232,768]{1,0:T(8,128)(2,1)S(1)} %get-tuple-element.67.refs_0_, bf16[232,768]{1,0:T(8,128)(2,1)S(1)} %collective-permute-done.14.refs_1_, ...), custom_call_target="tpu_custom_call" | custom-call | flops 4718592 | bytes 5505024 | tf_op jit(solution)/shard_map/heads_finish/pallas_call | solution.py:838
  (17 shorter events, 0.1 us)
Async XLA Ops:
  0.6 55.7 %copy-start = (f32[1,32,24]{1,2,0:T(8,128)S(1)}, f32[1,32,24]{1,2,0:T(8,128)}, u32[]{:S(2)}) copy-start(f32[1,32,24]{1,2,0:T(8,128)} %param.17) | copy-start | bytes 9220
  0.6 12.4 %copy-start.2 = (bf16[128,3072]{1,0:T(8,128)(2,1)S(1)}, bf16[128,3072]{1,0:T(8,128)(2,1)}, u32[]{:S(2)}) copy-start(bf16[128,3072]{1,0:T(8,128)(2,1)} %edge_ref.3) | copy-start | bytes 2359300
  0.7 12.3 %collective-permute-start.7 = (bf16[128,3072]{1,0:T(8,128)(2,1)}, bf16[128,3072]{1,0:T(8,128)(2,1)S(1)}, u32[]{:S(2)}, u32[]{:S(2)}) collective-permute-start(bf16[128,3072]{1,0:T(8,128)(2,1)} %bitcast.24), channel_id=1, source_target_pairs={{0,4},{4,8},{8,12},{12,16},{16,20},{20,24},{24,28},{1,5},{5,9},{9,... | collective-permute-start | bytes 2359304 | tf_op jit(solution)/shard_map/ppermute | solution.py:868
  3.2 12.4 %collective-permute-start.3 = (bf16[128,3072]{1,0:T(8,128)(2,1)}, bf16[128,3072]{1,0:T(8,128)(2,1)S(1)}, u32[]{:S(2)}, u32[]{:S(2)}) collective-permute-start(bf16[128,3072]{1,0:T(8,128)(2,1)} %bitcast.25), channel_id=1, source_target_pairs={{4,0},{8,4},{12,8},{16,12},{20,16},{24,20},{28,24},{5,1},{9,5},{13... | collective-permute-start | bytes 2359304 | tf_op jit(solution)/shard_map/ppermute | solution.py:868
  4.5 13.4 %copy-start.3 = (bf16[128,3072]{1,0:T(8,128)(2,1)S(1)}, bf16[128,3072]{1,0:T(8,128)(2,1)}, u32[]{:S(2)}) copy-start(bf16[128,3072]{1,0:T(8,128)(2,1)} %edge_ref.2) | copy-start | bytes 2359300
  7.4 12.1 %collective-permute-start = (bf16[224,768]{1,0:T(8,128)(2,1)}, bf16[224,768]{1,0:T(8,128)(2,1)S(1)}, u32[]{:S(2)}, u32[]{:S(2)}) collective-permute-start(bf16[224,768]{1,0:T(8,128)(2,1)} %get-tuple-element.44), channel_id=1, source_target_pairs={{0,1},{1,2},{2,3},{3,0},{4,5},{5,6},{6,7},{7,4},{8,9},{9,10},{10,1... | collective-permute-start | bytes 1032200 | tf_op jit(solution)/shard_map/ppermute | solution.py:896
  9.9 18.5 %collective-permute-start.1 = (bf16[224,768]{1,0:T(8,128)(2,1)}, bf16[224,768]{1,0:T(8,128)(2,1)}, u32[]{:S(2)}, u32[]{:S(2)}) collective-permute-start(bf16[224,768]{1,0:T(8,128)(2,1)} %get-tuple-element.45), channel_id=1, source_target_pairs={{0,3},{1,0},{2,1},{3,2},{4,7},{5,4},{6,5},{7,6},{8,11},{9,8},{10,9... | collective-permute-start | bytes 1032200 | tf_op jit(solution)/shard_map/ppermute | solution.py:896
  12.0 44.4 %collective-permute-start.2 = (bf16[224,768]{1,0:T(8,128)(2,1)}, bf16[224,768]{1,0:T(8,128)(2,1)}, u32[]{:S(2)}, u32[]{:S(2)}) collective-permute-start(bf16[224,768]{1,0:T(8,128)(2,1)} %get-tuple-element.46), channel_id=1, source_target_pairs={{0,2},{1,3},{2,0},{3,1},{4,6},{5,7},{6,4},{7,5},{8,10},{9,11},{10,... | collective-permute-start | bytes 1032200 | tf_op jit(solution)/shard_map/ppermute | solution.py:896
  13.9 42.4 %copy-start.11 = (f32[256,32]{1,0:T(8,128)S(1)}, f32[256,32]{1,0:T(8,128)}, u32[]{:S(2)}) copy-start(f32[256,32]{1,0:T(8,128)} %constant.35.clone) | copy-start | bytes 98308
  13.9 55.5 %copy-start.4 = (bf16[224,768]{1,0:T(8,128)(2,1)S(1)}, bf16[224,768]{1,0:T(8,128)(2,1)}, u32[]{:S(2)}) copy-start(bf16[224,768]{1,0:T(8,128)(2,1)} %get-tuple-element.43.refs_0_) | copy-start | bytes 1032196
  14.0 55.5 %copy-start.5 = (f32[1,3072]{1,0:T(1,128)S(1)}, f32[1,3072]{1,0:T(1,128)}, u32[]{:S(2)}) copy-start(f32[1,3072]{1,0:T(1,128)} %refs_6_.1) | copy-start | bytes 36868
  14.0 42.4 %collective-permute-start.8 = (bf16[136,768]{1,0:T(8,128)(2,1)S(1)}, bf16[136,768]{1,0:T(8,128)(2,1)S(1)}, u32[]{:S(2)}, u32[]{:S(2)}) collective-permute-start(bf16[136,768]{1,0:T(8,128)(2,1)S(1)} %get-tuple-element.52), channel_id=1, source_target_pairs={{0,1},{1,2},{2,3},{3,0},{4,5},{5,6},{6,7},{7,4},{8,9},{9,10},{10,1... | collective-permute-start | bytes 626696 | tf_op jit(solution)/shard_map/ppermute | solution.py:896
  15.6 41.1 %collective-permute-start.9 = (bf16[136,768]{1,0:T(8,128)(2,1)S(1)}, bf16[136,768]{1,0:T(8,128)(2,1)S(1)}, u32[]{:S(2)}, u32[]{:S(2)}) collective-permute-start(bf16[136,768]{1,0:T(8,128)(2,1)S(1)} %get-tuple-element.53), channel_id=1, source_target_pairs={{0,3},{1,0},{2,1},{3,2},{4,7},{5,4},{6,5},{7,6},{8,11},{9,8},{10,9... | collective-permute-start | bytes 626696 | tf_op jit(solution)/shard_map/ppermute | solution.py:896
  19.5 49.9 %collective-permute-start.10 = (bf16[136,768]{1,0:T(8,128)(2,1)S(1)}, bf16[136,768]{1,0:T(8,128)(2,1)S(1)}, u32[]{:S(2)}, u32[]{:S(2)}) collective-permute-start(bf16[136,768]{1,0:T(8,128)(2,1)S(1)} %get-tuple-element.54), channel_id=1, source_target_pairs={{0,2},{1,3},{2,0},{3,1},{4,6},{5,7},{6,4},{7,5},{8,10},{9,11},{10,... | collective-permute-start | bytes 626696 | tf_op jit(solution)/shard_map/ppermute | solution.py:896
  28.4 50.7 %collective-permute-start.4 = (bf16[128,768]{1,0:T(8,128)(2,1)S(1)}, bf16[128,768]{1,0:T(8,128)(2,1)S(1)}, u32[]{:S(2)}, u32[]{:S(2)}) collective-permute-start(bf16[128,768]{1,0:T(8,128)(2,1)S(1)} %get-tuple-element.48), channel_id=1, source_target_pairs={{0,1},{1,2},{2,3},{3,0},{4,5},{5,6},{6,7},{7,4},{8,9},{9,10},{10,1... | collective-permute-start | bytes 589832 | tf_op jit(solution)/shard_map/ppermute | solution.py:896
  56.4 22.7 %collective-permute-start.5 = (bf16[128,768]{1,0:T(8,128)(2,1)S(1)}, bf16[128,768]{1,0:T(8,128)(2,1)S(1)}, u32[]{:S(2)}, u32[]{:S(2)}) collective-permute-start(bf16[128,768]{1,0:T(8,128)(2,1)S(1)} %get-tuple-element.49), channel_id=1, source_target_pairs={{0,3},{1,0},{2,1},{3,2},{4,7},{5,4},{6,5},{7,6},{8,11},{9,8},{10,9... | collective-permute-start | bytes 589832 | tf_op jit(solution)/shard_map/ppermute | solution.py:896
  56.4 22.7 %collective-permute-start.6 = (bf16[128,768]{1,0:T(8,128)(2,1)S(1)}, bf16[128,768]{1,0:T(8,128)(2,1)S(1)}, u32[]{:S(2)}, u32[]{:S(2)}) collective-permute-start(bf16[128,768]{1,0:T(8,128)(2,1)S(1)} %get-tuple-element.50), channel_id=1, source_target_pairs={{0,2},{1,3},{2,0},{3,1},{4,6},{5,7},{6,4},{7,5},{8,10},{9,11},{10,... | collective-permute-start | bytes 589832 | tf_op jit(solution)/shard_map/ppermute | solution.py:896
  56.6 22.5 %copy-start.8 = (f32[32,256]{1,0:T(8,128)S(1)}, f32[32,256]{1,0:T(8,128)}, u32[]{:S(2)}) copy-start(f32[32,256]{1,0:T(8,128)} %constant.36.clone.refs_10_) | copy-start | bytes 98308
  77.0 13.9 %collective-permute-start.11 = (bf16[136,768]{1,0:T(8,128)(2,1)S(1)}, bf16[136,768]{1,0:T(8,128)(2,1)S(1)}, u32[]{:S(2)}, u32[]{:S(2)}) collective-permute-start(bf16[136,768]{1,0:T(8,128)(2,1)S(1)} %get-tuple-element.60.refs_1_), channel_id=1, source_target_pairs={{0,3},{1,0},{2,1},{3,2},{4,7},{5,4},{6,5},{7,6},{8,11},{9,8},{10,9... | collective-permute-start | bytes 626696 | tf_op jit(solution)/shard_map/ppermute | solution.py:896
  77.6 13.3 %collective-permute-start.12 = (bf16[136,768]{1,0:T(8,128)(2,1)S(1)}, bf16[136,768]{1,0:T(8,128)(2,1)S(1)}, u32[]{:S(2)}, u32[]{:S(2)}) collective-permute-start(bf16[136,768]{1,0:T(8,128)(2,1)S(1)} %get-tuple-element.61.refs_3_), channel_id=1, source_target_pairs={{0,1},{1,2},{2,3},{3,0},{4,5},{5,6},{6,7},{7,4},{8,9},{9,10},{10,1... | collective-permute-start | bytes 626696 | tf_op jit(solution)/shard_map/ppermute | solution.py:896
  79.1 17.7 %collective-permute-start.13 = (bf16[136,768]{1,0:T(8,128)(2,1)S(1)}, bf16[136,768]{1,0:T(8,128)(2,1)S(1)}, u32[]{:S(2)}, u32[]{:S(2)}) collective-permute-start(bf16[136,768]{1,0:T(8,128)(2,1)S(1)} %get-tuple-element.62.refs_2_), channel_id=1, source_target_pairs={{0,2},{1,3},{2,0},{3,1},{4,6},{5,7},{6,4},{7,5},{8,10},{9,11},{10,... | collective-permute-start | bytes 626696 | tf_op jit(solution)/shard_map/ppermute | solution.py:896
  79.1 17.6 %copy-start.7 = (f32[3072]{0:T(1024)S(1)}, f32[3072]{0:T(1024)}, u32[]{:S(2)}) copy-start(f32[3072]{0:T(1024)} %param.19) | copy-start | bytes 36868
  97.7 5.7 %collective-permute-start.17 = (bf16[128,768]{1,0:T(8,128)(2,1)S(1)}, bf16[128,768]{1,0:T(8,128)(2,1)S(1)}, u32[]{:S(2)}, u32[]{:S(2)}) collective-permute-start(bf16[128,768]{1,0:T(8,128)(2,1)S(1)} %get-tuple-element.77), channel_id=1, source_target_pairs={{28,4},{29,5},{30,6},{31,7}} | collective-permute-start | bytes 589832 | tf_op jit(solution)/shard_map/ppermute | solution.py:875
  98.4 5.7 %collective-permute-start.18 = (bf16[128,768]{1,0:T(8,128)(2,1)S(1)}, bf16[128,768]{1,0:T(8,128)(2,1)S(1)}, u32[]{:S(2)}, u32[]{:S(2)}) collective-permute-start(bf16[128,768]{1,0:T(8,128)(2,1)S(1)} %get-tuple-element.78), channel_id=1, source_target_pairs={{28,12},{29,13},{30,14},{31,15}} | collective-permute-start | bytes 589832 | tf_op jit(solution)/shard_map/ppermute | solution.py:875
  99.0 5.0 %collective-permute-start.19 = (bf16[128,768]{1,0:T(8,128)(2,1)S(1)}, bf16[128,768]{1,0:T(8,128)(2,1)S(1)}, u32[]{:S(2)}, u32[]{:S(2)}) collective-permute-start(bf16[128,768]{1,0:T(8,128)(2,1)S(1)} %get-tuple-element.79), channel_id=1, source_target_pairs={{28,20},{29,21},{30,22},{31,23}} | collective-permute-start | bytes 589832 | tf_op jit(solution)/shard_map/ppermute | solution.py:875
  99.7 20.3 %collective-permute-start.14 = (bf16[232,768]{1,0:T(8,128)(2,1)}, bf16[232,768]{1,0:T(8,128)(2,1)S(1)}, u32[]{:S(2)}, u32[]{:S(2)}) collective-permute-start(bf16[232,768]{1,0:T(8,128)(2,1)} %get-tuple-element.68), channel_id=1, source_target_pairs={{0,3},{1,0},{2,1},{3,2},{4,7},{5,4},{6,5},{7,6},{8,11},{9,8},{10,9... | collective-permute-start | bytes 1069064 | tf_op jit(solution)/shard_map/ppermute | solution.py:896
  103.4 16.9 %collective-permute-start.15 = (bf16[232,768]{1,0:T(8,128)(2,1)}, bf16[232,768]{1,0:T(8,128)(2,1)S(1)}, u32[]{:S(2)}, u32[]{:S(2)}) collective-permute-start(bf16[232,768]{1,0:T(8,128)(2,1)} %get-tuple-element.69), channel_id=1, source_target_pairs={{0,1},{1,2},{2,3},{3,0},{4,5},{5,6},{6,7},{7,4},{8,9},{9,10},{10,1... | collective-permute-start | bytes 1069064 | tf_op jit(solution)/shard_map/ppermute | solution.py:896
  103.4 30.4 %collective-permute-start.16 = (bf16[232,768]{1,0:T(8,128)(2,1)}, bf16[232,768]{1,0:T(8,128)(2,1)}, u32[]{:S(2)}, u32[]{:S(2)}) collective-permute-start(bf16[232,768]{1,0:T(8,128)(2,1)} %get-tuple-element.70), channel_id=1, source_target_pairs={{0,2},{1,3},{2,0},{3,1},{4,6},{5,7},{6,4},{7,5},{8,10},{9,11},{10,... | collective-permute-start | bytes 1069064 | tf_op jit(solution)/shard_map/ppermute | solution.py:896
  104.1 0.7 copy-start.9
  104.8 29.0 %copy-start.1 = (bf16[1,128,3072]{2,1,0:T(8,128)(2,1)S(1)}, bf16[1,128,3072]{2,1,0:T(8,128)(2,1)}, u32[]{:S(2)}) copy-start(bf16[1,128,3072]{2,1,0:T(8,128)(2,1)} %param.13) | copy-start | bytes 2359300
  105.4 3.5 %collective-permute-start.20 = (bf16[64,768]{1,0:T(8,128)(2,1)}, bf16[64,768]{1,0:T(8,128)(2,1)}, u32[]{:S(2)}, u32[]{:S(2)}) collective-permute-start(bf16[64,768]{1,0:T(8,128)(2,1)} %slice.8), channel_id=1, source_target_pairs={{4,0},{12,8},{20,16},{28,24},{5,1},{13,9},{21,17},{29,25},{6,2},{1... | collective-permute-start | bytes 294920 | tf_op jit(solution)/shard_map/ppermute | solution.py:877
  106.7 2.2 %copy-start.10 = (bf16[128,768]{1,0:T(8,128)(2,1)S(1)}, bf16[128,768]{1,0:T(8,128)(2,1)}, u32[]{:S(2)}) copy-start(bf16[128,768]{1,0:T(8,128)(2,1)} %copy-done.9) | copy-start | bytes 589828
  106.7 27.1 %copy-start.6 = (f32[128,128]{1,0:T(8,128)S(1)}, f32[128,128]{1,0:T(8,128)}, u32[]{:S(2)}) copy-start(f32[128,128]{1,0:T(8,128)} %get-tuple-element.71.refs_5_) | copy-start | bytes 196612

commit v13 on v12

--- a/solution.py
+++ b/solution.py
@@ -795,64 +795,128 @@
     )(meta, *slots)
 
 
-def heads_finish_kernel(parts, meta_ref, *refs):
-    g_refs = refs[:parts]
-    x_ref, inverse_ref, gain_ref, cot_ref, out_ref, weight_hbm, bias_ref, scaled_ref, weight_ref, sem = refs[parts:]
+def store_weights(g_ref, weight_ref, rows, depth, heads):
+    for h in range(heads):
+        for j in range(3):
+            weight_ref[j, h] = g_ref[
+                rows + j * depth : rows + (j + 1) * depth, h * HEAD_DIM : (h + 1) * HEAD_DIM
+            ].astype(F32)
+
+
+def weight_copies(weight_ref, weight_hbm, first_head, heads, sems):
+    return [
+        pltpu.make_async_copy(weight_ref.at[j], weight_hbm.at[j, pl.ds(first_head, heads)], sems.at[j])
+        for j in range(3)
+    ]
+
+
+def add_bias(bias, g_ref, first_row, first_head, heads):
+    lane = lax.broadcasted_iota(jnp.int32, bias.shape, 1)
+    shares = g_ref[first_row:].astype(F32)
+    for h in range(heads):
+        bias = jnp.where(lane == first_head + h, shares[:, h * HEAD_DIM : (h + 1) * HEAD_DIM], bias)
+    return bias
+
+
+def early_finish_kernel(parts, meta_ref, *refs):
+    g_refs = refs[: parts - 1]
+    x_ref, inverse_ref, gain_ref, cot_ref = refs[parts - 1 : parts + 3]
+    base_ref, row_ref, weight_hbm, bias_ref, weight_ref, sems = refs[parts + 3 :]
     rows, width = x_ref.shape
     wide = width // parts
     heads = wide // HEAD_DIM
     depth = HEAD_DIM // parts
-    for r, g_ref in zip(slot_order(parts), g_refs):
-        source = lax.rem(meta_ref[0] + r, parts)
-        for h in range(heads):
-            for j in range(3):
-                weight_ref[j, source * heads + h] = g_ref[
-                    rows + j * depth : rows + (j + 1) * depth, h * HEAD_DIM : (h + 1) * HEAD_DIM
-                ].astype(F32)
-    weight_copy = pltpu.make_async_copy(weight_ref, weight_hbm, sem)
-    weight_copy.start()
-    lane = lax.broadcasted_iota(jnp.int32, (bias_ref.shape[0], HEAD_DIM), 1)
-    bias = jnp.zeros(lane.shape, F32)
-    for r, g_ref in zip(slot_order(parts), g_refs):
-        source = lax.rem(meta_ref[0] + r, parts)
+    order = slot_order(parts)
+    inverse = inverse_ref[:, :1]
+    bias = jnp.zeros(bias_ref.shape, F32)
+    total = jnp.zeros((rows, 1), F32)
+    copies = []
+    for k, g_ref in enumerate(g_refs):
+        source = lax.rem(meta_ref[0] + order[k], parts)
+        store_weights(g_ref, weight_ref.at[k], rows, depth, heads)
+        for copy in weight_copies(weight_ref.at[k], weight_hbm, source * heads, heads, sems.at[k]):
+            copy.start()
+            copies.append(copy)
+        bias = add_bias(bias, g_ref, rows + 3 * depth, source * heads, heads)
         columns = pl.ds(pl.multiple_of(source * wide, 128), wide)
-        scaled_ref[:, columns] = g_ref[:rows].astype(F32) * gain_ref[:, columns]
-        shares = g_ref[rows + 3 * depth :].astype(F32)
-        for h in range(heads):
-            bias = jnp.where(lane == source * heads + h, shares[:, h * HEAD_DIM : (h + 1) * HEAD_DIM], bias)
+        scaled = g_ref[:rows].astype(F32) * gain_ref[:, columns]
+        total = total + jnp.sum(scaled * x_ref[:, columns].astype(F32), axis=-1, keepdims=True)
+        base_ref[:, columns] = cot_ref[:, columns].astype(F32) + inverse * scaled
+    last = pl.ds(pl.multiple_of(lax.rem(meta_ref[0] + order[-1], parts) * wide, 128), wide)
+    base_ref[:, last] = cot_ref[:, last].astype(F32)
+    row_ref[...] = jnp.broadcast_to(total, row_ref.shape)
+    bias_ref[...] = bias
+    for copy in copies:
+        copy.wait()
+
+
+def late_finish_kernel(parts, meta_ref, *refs):
+    base_ref, row_ref, early_bias_ref, g_ref, x_ref, inverse_ref, gain_ref, early_hbm = refs[:8]
+    out_ref, weight_hbm, bias_ref, weight_ref, sems = refs[8:]
+    rows, width = x_ref.shape
+    wide = width // parts
+    heads = wide // HEAD_DIM
+    depth = HEAD_DIM // parts
+    source = lax.rem(meta_ref[0] + slot_order(parts)[-1], parts)
+    store_weights(g_ref, weight_ref, rows, depth, heads)
+    copies = weight_copies(weight_ref, weight_hbm, source * heads, heads, sems)
+    for copy in copies:
+        copy.start()
+    bias = add_bias(early_bias_ref[...], g_ref, rows + 3 * depth, source * heads, heads)
     bias_ref[...] = bias[:, : bias_ref.shape[1]]
-    x = x_ref[...].astype(F32)
-    scaled = scaled_ref[...]
+    columns = pl.ds(pl.multiple_of(source * wide, 128), wide)
     inverse = inverse_ref[:, :1]
-    mean = jnp.mean(scaled * x, axis=-1, keepdims=True)
-    result = inverse * scaled - x * (inverse * inverse * inverse * mean)
-    out_ref[...] = (cot_ref[...].astype(F32) + result).astype(BF16)
-    weight_copy.wait()
+    scaled = g_ref[:rows].astype(F32) * gain_ref[:, columns]
+    total = row_ref[:, :1] + jnp.sum(scaled * x_ref[:, columns].astype(F32), axis=-1, keepdims=True)
+    factor = inverse * inverse * inverse * (total / width)
+    out_ref[...] = (base_ref[...] - x_ref[...].astype(F32) * factor).astype(BF16)
+    out_ref[:, columns] = (
+        base_ref[:, columns] + (inverse * scaled - x_ref[:, columns].astype(F32) * factor)
+    ).astype(BF16)
+    for copy in copies:
+        copy.wait()
 
 
 def heads_finish(meta, g_slots, x, inverse, gain, cotangent, buckets):
     parts = len(g_slots)
     rows, width = x.shape
     heads = width // HEAD_DIM
-    weight_shape = (3, heads, HEAD_DIM // parts, HEAD_DIM)
+    depth = HEAD_DIM // parts
+    any_spec = pl.BlockSpec(memory_space=pl.ANY)
+    weight = jax.ShapeDtypeStruct((3, heads, depth, HEAD_DIM), F32)
+    piece = (3, heads // parts, depth, HEAD_DIM)
+    cost = pl.CostEstimate(flops=rows * width, bytes_accessed=rows * width, transcendentals=0)
+    params = pltpu.CompilerParams(vmem_limit_bytes=VMEM_LIMIT)
+    base, row, early, bias = pl.pallas_call(
+        functools.partial(early_finish_kernel, parts),
+        out_shape=(
+            jax.ShapeDtypeStruct((rows, width), F32),
+            jax.ShapeDtypeStruct((rows, 128), F32),
+            weight,
+            jax.ShapeDtypeStruct((buckets // parts, HEAD_DIM), F32),
+        ),
+        in_specs=[SMEM_SPEC] + [VMEM_SPEC] * (parts + 3),
+        out_specs=(VMEM_SPEC, VMEM_SPEC, any_spec, VMEM_SPEC),
+        scratch_shapes=[pltpu.VMEM((parts - 1, *piece), F32), pltpu.SemaphoreType.DMA((parts - 1, 3))],
+        compiler_params=params,
+        cost_estimate=cost,
+        name="early_finish",
+    )(meta, *g_slots[:-1], x, inverse, gain, cotangent)
     return pl.pallas_call(
-        functools.partial(heads_finish_kernel, parts),
+        functools.partial(late_finish_kernel, parts),
         out_shape=(
             jax.ShapeDtypeStruct((rows, width), BF16),
-            jax.ShapeDtypeStruct(weight_shape, F32),
+            weight,
             jax.ShapeDtypeStruct((buckets // parts, heads), F32),
         ),
-        in_specs=[SMEM_SPEC] + [VMEM_SPEC] * (parts + 4),
-        out_specs=(VMEM_SPEC, pl.BlockSpec(memory_space=pl.ANY), VMEM_SPEC),
-        scratch_shapes=[
-            pltpu.VMEM((rows, width), F32),
-            pltpu.VMEM(weight_shape, F32),
-            pltpu.SemaphoreType.DMA,
-        ],
-        compiler_params=pltpu.CompilerParams(vmem_limit_bytes=VMEM_LIMIT),
-        cost_estimate=pl.CostEstimate(flops=12 * rows * width, bytes_accessed=14 * rows * width, transcendentals=0),
-        name="heads_finish",
-    )(meta, *g_slots, x, inverse, gain, cotangent)
+        in_specs=[SMEM_SPEC] + [VMEM_SPEC] * 7 + [any_spec],
+        out_specs=(VMEM_SPEC, any_spec, VMEM_SPEC),
+        input_output_aliases={8: 1},
+        scratch_shapes=[pltpu.VMEM(piece, F32), pltpu.SemaphoreType.DMA((3,))],
+        compiler_params=params,
+        cost_estimate=cost,
+        name="late_finish",
+    )(meta, base, row, bias, g_slots[-1], x, inverse, gain, early)
 
 
 def offset_table(rel_bias):
@@ -1002,7 +1066,7 @@
 def choose_body(embedded, carried, stash, returned, loss_grad, qkv_weight, rel_bias, norm_gain, final_gain):
     parts = lax.axis_size("seq")
     rows, width = embedded.shape
-    even = width % (HEAD_DIM * parts) == 0 and HEAD_DIM % (32 * parts) == 0 and rows == 128
+    even = parts > 1 and width % (HEAD_DIM * parts) == 0 and HEAD_DIM % (32 * parts) == 0 and rows == 128
     sections = lax.axis_size("section")
     even = even and sections % 2 == 0
     even = even and rel_bias.shape[1] == 8 * parts and width <= 128 * HEAD_DIM and rows * parts % (16 * sections) == 0

time: 138 us -> 137 us (level)
  waiting for transfers between devices: 76.3 us -> 73 us
  Pallas kernels: 30.5 us -> 32 us
    ppermute x15, waiting for transfers between devices: 75.6 us -> 72.2 us  [exchanged(): lax.ppermute(sends[r], 'seq', [(i, (i + direction * r) % parts) for i in...]
    pallas_call x1 -> x2, Pallas kernels: 3.49 us -> 5.01 us  [the longest x1 2.62 us: heads_finish(): pl.pallas_call(functools.partial(late_finish_kernel, parts), out_shape=(j...]
  transfers between devices with their start and end apart: 21 -> 21, of which waited for: 9 -> 9; matrix products, arithmetic and copies ran while one was open for 2% -> 2% of each run, Pallas kernels for 19% -> 21%
where the time goes in v13:
time: 137 us; the launch traced here: 136 us
  waiting for transfers between devices  73 us (53%)
  Pallas kernels  32 us (23%)
  starting transfers between devices  26.3 us (19%)
  local copies, waits for them, and re-layouts  2.26 us (2%)
  other arithmetic  1.67 us (1%)
    ppermute x15, waiting for transfers between devices, exchanged(): lax.ppermute(sends[r], 'seq', [(i, (i + direction * r) % parts) for i in...  72.2 us
    ppermute x15, starting transfers between devices, exchanged(): lax.ppermute(sends[r], 'seq', [(i, (i + direction * r) % parts) for i in...  19.2 us
    pallas_call x1, Pallas kernels, heads_backward(): pl.pallas_call(functools.partial(heads_backward_kernel, parts, rows), out...  11.8 us
    pallas_call x1, Pallas kernels, heads_forward(): pl.pallas_call(functools.partial(heads_forward_kernel, parts, rows), out_...  7.54 us
    ppermute x2, starting transfers between devices, shifted(): lax.ppermute(value, axis, [(source, source + steps) for source in range(f...  3.83 us
    pallas_call x1, Pallas kernels, pack_stash(): pl.pallas_call(functools.partial(pack_stash_kernel, parts, 4), out_shape=...  2.9 us
  transfers between devices with their start and end apart: 21, of which 9 were waited for; matrix products, arithmetic and copies ran while one was open for 2% of the time, Pallas kernels for 21%

profile of v13, /device:TPU:0, one launch (start us, length us, event | category | flops | bytes accessed | tf_op | source)
XLA Modules:
  0.0 136.3 jit_solution(16613776506778273555)
XLA Ops:
  0.6 0.0 copy-start
  0.7 2.5 %collective-permute-start.7 = (bf16[128,3072]{1,0:T(8,128)(2,1)}, bf16[128,3072]{1,0:T(8,128)(2,1)S(1)}, u32[]{:S(2)}, u32[]{:S(2)}) collective-permute-start(bf16[128,3072]{1,0:T(8,128)(2,1)} %bitcast.25), channel_id=1, source_target_pairs={{0,4},{4,8},{8,12},{12,16},{16,20},{20,24},{24,28},{1,5},{5,9},{9,... | collective-permute-start | bytes 2359304 | tf_op jit(solution)/shard_map/ppermute | solution.py:932
  3.2 1.3 collective-permute-start.3
  4.5 2.9 %pack_stash.1 = (f32[128,128]{1,0:T(8,128)}, bf16[224,768]{1,0:T(8,128)(2,1)}, bf16[224,768]{1,0:T(8,128)(2,1)}, bf16[224,768]{1,0:T(8,128)(2,1)}, bf16[224,768]{1,0:T(8,128)(2,1)}) custom-call(bf16[128,3072]{1,0:T(8,128)(2,1)} %bitcast.18, f32[1,3072]{1,0:T(1,128)} %refs_6_.1, bf16[3,24,32,128]{3,2,1,0:T(8,128)(2,1)} %bitcast.24), custom_call_target="tpu_custom_call" | custom-call | flops 1572864 | bytes 2359296 | tf_op jit(solution)/shard_map/pack_stash/pallas_call | solution.py:426
  7.4 2.5 %collective-permute-start = (bf16[224,768]{1,0:T(8,128)(2,1)}, bf16[224,768]{1,0:T(8,128)(2,1)S(1)}, u32[]{:S(2)}, u32[]{:S(2)}) collective-permute-start(bf16[224,768]{1,0:T(8,128)(2,1)} %get-tuple-element.48), channel_id=1, source_target_pairs={{0,1},{1,2},{2,3},{3,0},{4,5},{5,6},{6,7},{7,4},{8,9},{9,10},{10,1... | collective-permute-start | bytes 1032200 | tf_op jit(solution)/shard_map/ppermute | solution.py:960
  9.9 2.1 %collective-permute-start.1 = (bf16[224,768]{1,0:T(8,128)(2,1)}, bf16[224,768]{1,0:T(8,128)(2,1)}, u32[]{:S(2)}, u32[]{:S(2)}) collective-permute-start(bf16[224,768]{1,0:T(8,128)(2,1)} %get-tuple-element.49), channel_id=1, source_target_pairs={{0,3},{1,0},{2,1},{3,2},{4,7},{5,4},{6,5},{7,6},{8,11},{9,8},{10,9... | collective-permute-start | bytes 1032200 | tf_op jit(solution)/shard_map/ppermute | solution.py:960
  12.0 0.9 collective-permute-start.2
  12.9 0.1 pad_add_fusion.meta_ref
  13.0 0.0 collective-permute-done.7.inner_ref
  13.0 0.9 pack_inbound.1
  14.0 0.0 copy-start.4
  14.0 0.0 copy-start.6
  14.0 1.6 %collective-permute-start.8 = (bf16[136,768]{1,0:T(8,128)(2,1)S(1)}, bf16[136,768]{1,0:T(8,128)(2,1)S(1)}, u32[]{:S(2)}, u32[]{:S(2)}) collective-permute-start(bf16[136,768]{1,0:T(8,128)(2,1)S(1)} %get-tuple-element.56), channel_id=1, source_target_pairs={{0,1},{1,2},{2,3},{3,0},{4,5},{5,6},{6,7},{7,4},{8,9},{9,10},{10,1... | collective-permute-start | bytes 626696 | tf_op jit(solution)/shard_map/ppermute | solution.py:960
  15.6 0.0 collective-permute-done.3.inner_ref
  15.6 2.2 %collective-permute-start.9 = (bf16[136,768]{1,0:T(8,128)(2,1)S(1)}, bf16[136,768]{1,0:T(8,128)(2,1)S(1)}, u32[]{:S(2)}, u32[]{:S(2)}) collective-permute-start(bf16[136,768]{1,0:T(8,128)(2,1)S(1)} %get-tuple-element.57), channel_id=1, source_target_pairs={{0,3},{1,0},{2,1},{3,2},{4,7},{5,4},{6,5},{7,6},{8,11},{9,8},{10,9... | collective-permute-start | bytes 626696 | tf_op jit(solution)/shard_map/ppermute | solution.py:960
  17.9 1.4 %pack_cotangent.1 = (bf16[128,768]{1,0:T(8,128)(2,1)}, bf16[128,768]{1,0:T(8,128)(2,1)S(1)}, bf16[128,768]{1,0:T(8,128)(2,1)S(1)}, bf16[128,768]{1,0:T(8,128)(2,1)S(1)}, bf16[128,3072]{1,0:T(8,128)(2,1)S(1)}) custom-call(s32[3]{0:T(128)S(1)} %pad_add_fusion.meta_ref, bf16[128,3072]{1,0:T(8,128)(2,1)S(1)} %copy-done.3, ...), custom_call_target="tpu_custom_call" | custom-call | flops 1572864 | bytes 2359296 | tf_op jit(solution)/shard_map/pack_cotangent/pallas_call | solution.py:451
  19.3 0.2 collective-permute-done.refs_1_
  19.5 1.2 collective-permute-start.10
  20.7 7.7 %collective-permute-done.1.refs_2_ = bf16[224,768]{1,0:T(8,128)(2,1)} collective-permute-done((bf16[224,768]{1,0:T(8,128)(2,1)}, bf16[224,768]{1,0:T(8,128)(2,1)}, u32[]{:S(2)}, u32[]{:S(2)}) %collective-permute-start.1) | collective-permute-done | bytes 344096 | tf_op jit(solution)/shard_map/ppermute | solution.py:960
  28.4 2.2 %collective-permute-start.4 = (bf16[128,768]{1,0:T(8,128)(2,1)S(1)}, bf16[128,768]{1,0:T(8,128)(2,1)S(1)}, u32[]{:S(2)}, u32[]{:S(2)}) collective-permute-start(bf16[128,768]{1,0:T(8,128)(2,1)S(1)} %get-tuple-element.52), channel_id=1, source_target_pairs={{0,1},{1,2},{2,3},{3,0},{4,5},{5,6},{6,7},{7,4},{8,9},{9,10},{10,1... | collective-permute-start | bytes 589832 | tf_op jit(solution)/shard_map/ppermute | solution.py:960
  30.6 25.8 %collective-permute-done.2.refs_3_ = bf16[224,768]{1,0:T(8,128)(2,1)} collective-permute-done((bf16[224,768]{1,0:T(8,128)(2,1)}, bf16[224,768]{1,0:T(8,128)(2,1)}, u32[]{:S(2)}, u32[]{:S(2)}) %collective-permute-start.2) | collective-permute-done | bytes 344096 | tf_op jit(solution)/shard_map/ppermute | solution.py:960
  56.4 0.0 collective-permute-start.5
  56.4 0.0 collective-permute-done.8.refs_5_
  56.4 0.0 collective-permute-start.6
  56.4 0.2 fusion
  56.6 0.0 copy-start.8
  56.7 0.0 collective-permute-done.9.refs_6_
  56.7 12.7 %collective-permute-done.10.refs_7_ = bf16[136,768]{1,0:T(8,128)(2,1)S(1)} collective-permute-done((bf16[136,768]{1,0:T(8,128)(2,1)S(1)}, bf16[136,768]{1,0:T(8,128)(2,1)S(1)}, u32[]{:S(2)}, u32[]{:S(2)}) %collective-permute-start.10) | collective-permute-done | bytes 208928 | tf_op jit(solution)/shard_map/ppermute | solution.py:960
  69.4 7.5 %heads_forward.1 = (bf16[136,768]{1,0:T(8,128)(2,1)S(1)}, bf16[136,768]{1,0:T(8,128)(2,1)S(1)}, bf16[136,768]{1,0:T(8,128)(2,1)S(1)}, bf16[136,768]{1,0:T(8,128)(2,1)S(1)}) custom-call(s32[3]{0:T(128)S(1)} %pad_add_fusion.meta_ref, bf16[224,768]{1,0:T(8,128)(2,1)S(1)} %copy-done.4, bf16[224,768]{1,0:T(8,128)(2,1)S(1)} %collective-permute-done.refs_1_, ...), custom_call_target="tpu_custom_call" | custom-call | flops 3072 | bytes 512 | tf_op jit(solution)/shard_map/heads_forward/pallas_call | solution.py:706
  77.0 0.6 collective-permute-start.11
  77.6 1.4 %collective-permute-start.12 = (bf16[136,768]{1,0:T(8,128)(2,1)S(1)}, bf16[136,768]{1,0:T(8,128)(2,1)S(1)}, u32[]{:S(2)}, u32[]{:S(2)}) collective-permute-start(bf16[136,768]{1,0:T(8,128)(2,1)S(1)} %get-tuple-element.65.refs_3_), channel_id=1, source_target_pairs={{0,1},{1,2},{2,3},{3,0},{4,5},{5,6},{6,7},{7,4},{8,9},{9,10},{10,1... | collective-permute-start | bytes 626696 | tf_op jit(solution)/shard_map/ppermute | solution.py:960
  79.1 0.0 collective-permute-done.4.refs_5_
  79.1 0.0 collective-permute-start.13
  79.1 0.0 collective-permute-done.5.refs_6_
  79.1 0.0 collective-permute-done.6.refs_7_
  79.1 0.0 copy-start.7
  79.1 11.8 %heads_backward.1 = (bf16[232,768]{1,0:T(8,128)(2,1)S(1)}, bf16[232,768]{1,0:T(8,128)(2,1)}, bf16[232,768]{1,0:T(8,128)(2,1)}, bf16[232,768]{1,0:T(8,128)(2,1)}, f32[1,768]{1,0:T(1,128)}) custom-call(s32[3]{0:T(128)S(1)} %pad_add_fusion.meta_ref, bf16[224,768]{1,0:T(8,128)(2,1)S(1)} %copy-done.4, bf16[224,768]{1,0:T(8,128)(2,1)S(1)} %collective-permute-done.refs_1_, ...), custom_call_target="tpu_custom_call" | custom-call | flops 1228800000 | bytes 393216 | tf_op jit(solution)/shard_map/heads_backward/pallas_call | solution.py:607
  90.9 0.0 collective-permute-done.11.refs_1_.refs_4_
  90.9 0.0 collective-permute-done.12.refs_2_.refs_5_
  90.9 5.9 %collective-permute-done.13.refs_3_.refs_6_ = bf16[136,768]{1,0:T(8,128)(2,1)S(1)} collective-permute-done((bf16[136,768]{1,0:T(8,128)(2,1)S(1)}, bf16[136,768]{1,0:T(8,128)(2,1)S(1)}, u32[]{:S(2)}, u32[]{:S(2)}) %collective-permute-start.13) | collective-permute-done | bytes 208928 | tf_op jit(solution)/shard_map/ppermute | solution.py:960
  96.8 0.0 copy-done.7
  96.8 0.9 memory_rows.1
  97.7 0.7 collective-permute-start.17
  98.4 0.7 collective-permute-start.18
  99.1 0.7 collective-permute-start.19
  99.8 3.7 %collective-permute-start.14 = (bf16[232,768]{1,0:T(8,128)(2,1)}, bf16[232,768]{1,0:T(8,128)(2,1)S(1)}, u32[]{:S(2)}, u32[]{:S(2)}) collective-permute-start(bf16[232,768]{1,0:T(8,128)(2,1)} %get-tuple-element.72), channel_id=1, source_target_pairs={{0,3},{1,0},{2,1},{3,2},{4,7},{5,4},{6,5},{7,6},{8,11},{9,8},{10,9... | collective-permute-start | bytes 1069064 | tf_op jit(solution)/shard_map/ppermute | solution.py:960
  103.4 0.0 collective-permute-start.15
  103.4 0.0 collective-permute-done.17
  103.4 0.6 collective-permute-start.16
  104.0 0.0 collective-permute-done.18
  104.0 0.0 collective-permute-done.19
  104.1 0.7 copy-done.9
  104.8 0.6 slice.8
  105.4 1.3 collective-permute-start.20
  106.8 1.5 %place_columns.1 = bf16[128,3072]{1,0:T(8,128)(2,1)} custom-call(s32[3]{0:T(128)S(1)} %pad_add_fusion.meta_ref, bf16[136,768]{1,0:T(8,128)(2,1)S(1)} %get-tuple-element.67.refs_11_.refs_0_, bf16[136,768]{1,0:T(8,128)(2,1)S(1)} %collective-permute-done.11.refs_1_.refs_4_, bf16[136,768]{1,0:T(8,128)(2,1)S(1)} %collective-permute-done.12.refs_2_.refs_5_, ...), custom_call_target="tpu_custom_call" | custom-call | bytes 128 | tf_op jit(solution)/shard_map/place_columns/pallas_call | solution.py:787
  108.3 0.7 collective-permute-done.20
  109.0 1.5 %slice_select_fusion = bf16[64,768]{1,0:T(8,128)(2,1)} fusion(bf16[64,768]{1,0:T(8,128)(2,1)} %collective-permute-done.20, bf16[128,768]{1,0:T(8,128)(2,1)S(1)} %copy-done.10, pred[]{:T(512)S(6)} %eq.14), kind=kLoop, calls=%fused_computation.3 | loop fusion | flops 49152 | bytes 294913 | tf_op jit(solution)/shard_map/jit(_where)/select_n | solution.py:942
  110.5 9.5 %collective-permute-done.14.refs_1_ = bf16[232,768]{1,0:T(8,128)(2,1)S(1)} collective-permute-done((bf16[232,768]{1,0:T(8,128)(2,1)}, bf16[232,768]{1,0:T(8,128)(2,1)S(1)}, u32[]{:S(2)}, u32[]{:S(2)}) %collective-permute-start.14) | collective-permute-done | bytes 356384 | tf_op jit(solution)/shard_map/ppermute | solution.py:960
  120.1 0.4 collective-permute-done.15.refs_2_
  120.4 0.0 copy-done.1
  120.5 0.8 copy-done.5
  121.3 2.4 %early_finish.1 = (f32[128,3072]{1,0:T(8,128)S(1)}, f32[128,128]{1,0:T(8,128)S(1)}, f32[3,24,32,128]{3,2,1,0:T(8,128)}, f32[8,128]{1,0:T(8,128)S(1)}) custom-call(s32[3]{0:T(128)S(1)} %pad_add_fusion.meta_ref, bf16[232,768]{1,0:T(8,128)(2,1)S(1)} %get-tuple-element.71.refs_0_, bf16[232,768]{1,0:T(8,128)(2,1)S(1)} %collective-permute-done.14.refs_1_, ...), custom_call_target="tpu_custom_call" | custom-call | flops 393216 | bytes 393216 | tf_op jit(solution)/shard_map/early_finish/pallas_call | solution.py:890
  123.7 10.0 %collective-permute-done.16.refs_3_ = bf16[232,768]{1,0:T(8,128)(2,1)S(1)} collective-permute-done((bf16[232,768]{1,0:T(8,128)(2,1)}, bf16[232,768]{1,0:T(8,128)(2,1)S(1)}, u32[]{:S(2)}, u32[]{:S(2)}) %collective-permute-start.16) | collective-permute-done | bytes 356384 | tf_op jit(solution)/shard_map/ppermute | solution.py:960
  133.7 2.6 %late_finish.1 = (bf16[128,3072]{1,0:T(8,128)(2,1)}, f32[3,24,32,128]{3,2,1,0:T(8,128)}, f32[8,24]{1,0:T(8,128)}) custom-call(s32[3]{0:T(128)S(1)} %pad_add_fusion.meta_ref, f32[128,3072]{1,0:T(8,128)S(1)} %get-tuple-element.75.refs_0_, f32[128,128]{1,0:T(8,128)S(1)} %get-tuple-element.76.refs_1_, ...), custom_call_target="tpu_custom_call", output_to_operand_aliasing={{1}: (8, {})} | custom-call | flops 393216 | bytes 393216 | tf_op jit(solution)/shard_map/late_finish/pallas_call | solution.py:905
  (18 shorter events, 0.1 us)
Async XLA Ops:
  0.6 55.8 %copy-start = (f32[1,32,24]{1,2,0:T(8,128)S(1)}, f32[1,32,24]{1,2,0:T(8,128)}, u32[]{:S(2)}) copy-start(f32[1,32,24]{1,2,0:T(8,128)} %param.17) | copy-start | bytes 9220
  0.6 12.4 %copy-start.2 = (bf16[128,3072]{1,0:T(8,128)(2,1)S(1)}, bf16[128,3072]{1,0:T(8,128)(2,1)}, u32[]{:S(2)}) copy-start(bf16[128,3072]{1,0:T(8,128)(2,1)} %edge_ref.3) | copy-start | bytes 2359300
  0.7 12.3 %collective-permute-start.7 = (bf16[128,3072]{1,0:T(8,128)(2,1)}, bf16[128,3072]{1,0:T(8,128)(2,1)S(1)}, u32[]{:S(2)}, u32[]{:S(2)}) collective-permute-start(bf16[128,3072]{1,0:T(8,128)(2,1)} %bitcast.25), channel_id=1, source_target_pairs={{0,4},{4,8},{8,12},{12,16},{16,20},{20,24},{24,28},{1,5},{5,9},{9,... | collective-permute-start | bytes 2359304 | tf_op jit(solution)/shard_map/ppermute | solution.py:932
  3.2 12.4 %collective-permute-start.3 = (bf16[128,3072]{1,0:T(8,128)(2,1)}, bf16[128,3072]{1,0:T(8,128)(2,1)S(1)}, u32[]{:S(2)}, u32[]{:S(2)}) collective-permute-start(bf16[128,3072]{1,0:T(8,128)(2,1)} %bitcast.26), channel_id=1, source_target_pairs={{4,0},{8,4},{12,8},{16,12},{20,16},{24,20},{28,24},{5,1},{9,5},{13... | collective-permute-start | bytes 2359304 | tf_op jit(solution)/shard_map/ppermute | solution.py:932
  4.5 13.4 %copy-start.3 = (bf16[128,3072]{1,0:T(8,128)(2,1)S(1)}, bf16[128,3072]{1,0:T(8,128)(2,1)}, u32[]{:S(2)}) copy-start(bf16[128,3072]{1,0:T(8,128)(2,1)} %edge_ref.2) | copy-start | bytes 2359300
  7.4 12.1 %collective-permute-start = (bf16[224,768]{1,0:T(8,128)(2,1)}, bf16[224,768]{1,0:T(8,128)(2,1)S(1)}, u32[]{:S(2)}, u32[]{:S(2)}) collective-permute-start(bf16[224,768]{1,0:T(8,128)(2,1)} %get-tuple-element.48), channel_id=1, source_target_pairs={{0,1},{1,2},{2,3},{3,0},{4,5},{5,6},{6,7},{7,4},{8,9},{9,10},{10,1... | collective-permute-start | bytes 1032200 | tf_op jit(solution)/shard_map/ppermute | solution.py:960
  9.9 18.5 %collective-permute-start.1 = (bf16[224,768]{1,0:T(8,128)(2,1)}, bf16[224,768]{1,0:T(8,128)(2,1)}, u32[]{:S(2)}, u32[]{:S(2)}) collective-permute-start(bf16[224,768]{1,0:T(8,128)(2,1)} %get-tuple-element.49), channel_id=1, source_target_pairs={{0,3},{1,0},{2,1},{3,2},{4,7},{5,4},{6,5},{7,6},{8,11},{9,8},{10,9... | collective-permute-start | bytes 1032200 | tf_op jit(solution)/shard_map/ppermute | solution.py:960
  12.0 44.4 %collective-permute-start.2 = (bf16[224,768]{1,0:T(8,128)(2,1)}, bf16[224,768]{1,0:T(8,128)(2,1)}, u32[]{:S(2)}, u32[]{:S(2)}) collective-permute-start(bf16[224,768]{1,0:T(8,128)(2,1)} %get-tuple-element.50), channel_id=1, source_target_pairs={{0,2},{1,3},{2,0},{3,1},{4,6},{5,7},{6,4},{7,5},{8,10},{9,11},{10,... | collective-permute-start | bytes 1032200 | tf_op jit(solution)/shard_map/ppermute | solution.py:960
  13.9 42.4 %copy-start.11 = (f32[256,32]{1,0:T(8,128)S(1)}, f32[256,32]{1,0:T(8,128)}, u32[]{:S(2)}) copy-start(f32[256,32]{1,0:T(8,128)} %constant.35.clone) | copy-start | bytes 98308
  14.0 55.5 %copy-start.4 = (bf16[224,768]{1,0:T(8,128)(2,1)S(1)}, bf16[224,768]{1,0:T(8,128)(2,1)}, u32[]{:S(2)}) copy-start(bf16[224,768]{1,0:T(8,128)(2,1)} %get-tuple-element.47.refs_0_) | copy-start | bytes 1032196
  14.0 55.5 %copy-start.6 = (f32[1,3072]{1,0:T(1,128)S(1)}, f32[1,3072]{1,0:T(1,128)}, u32[]{:S(2)}) copy-start(f32[1,3072]{1,0:T(1,128)} %refs_6_.1) | copy-start | bytes 36868
  14.0 42.4 %collective-permute-start.8 = (bf16[136,768]{1,0:T(8,128)(2,1)S(1)}, bf16[136,768]{1,0:T(8,128)(2,1)S(1)}, u32[]{:S(2)}, u32[]{:S(2)}) collective-permute-start(bf16[136,768]{1,0:T(8,128)(2,1)S(1)} %get-tuple-element.56), channel_id=1, source_target_pairs={{0,1},{1,2},{2,3},{3,0},{4,5},{5,6},{6,7},{7,4},{8,9},{9,10},{10,1... | collective-permute-start | bytes 626696 | tf_op jit(solution)/shard_map/ppermute | solution.py:960
  15.6 41.1 %collective-permute-start.9 = (bf16[136,768]{1,0:T(8,128)(2,1)S(1)}, bf16[136,768]{1,0:T(8,128)(2,1)S(1)}, u32[]{:S(2)}, u32[]{:S(2)}) collective-permute-start(bf16[136,768]{1,0:T(8,128)(2,1)S(1)} %get-tuple-element.57), channel_id=1, source_target_pairs={{0,3},{1,0},{2,1},{3,2},{4,7},{5,4},{6,5},{7,6},{8,11},{9,8},{10,9... | collective-permute-start | bytes 626696 | tf_op jit(solution)/shard_map/ppermute | solution.py:960
  19.5 49.9 %collective-permute-start.10 = (bf16[136,768]{1,0:T(8,128)(2,1)S(1)}, bf16[136,768]{1,0:T(8,128)(2,1)S(1)}, u32[]{:S(2)}, u32[]{:S(2)}) collective-permute-start(bf16[136,768]{1,0:T(8,128)(2,1)S(1)} %get-tuple-element.58), channel_id=1, source_target_pairs={{0,2},{1,3},{2,0},{3,1},{4,6},{5,7},{6,4},{7,5},{8,10},{9,11},{10,... | collective-permute-start | bytes 626696 | tf_op jit(solution)/shard_map/ppermute | solution.py:960
  28.4 50.7 %collective-permute-start.4 = (bf16[128,768]{1,0:T(8,128)(2,1)S(1)}, bf16[128,768]{1,0:T(8,128)(2,1)S(1)}, u32[]{:S(2)}, u32[]{:S(2)}) collective-permute-start(bf16[128,768]{1,0:T(8,128)(2,1)S(1)} %get-tuple-element.52), channel_id=1, source_target_pairs={{0,1},{1,2},{2,3},{3,0},{4,5},{5,6},{6,7},{7,4},{8,9},{9,10},{10,1... | collective-permute-start | bytes 589832 | tf_op jit(solution)/shard_map/ppermute | solution.py:960
  56.4 22.7 %collective-permute-start.5 = (bf16[128,768]{1,0:T(8,128)(2,1)S(1)}, bf16[128,768]{1,0:T(8,128)(2,1)S(1)}, u32[]{:S(2)}, u32[]{:S(2)}) collective-permute-start(bf16[128,768]{1,0:T(8,128)(2,1)S(1)} %get-tuple-element.53), channel_id=1, source_target_pairs={{0,3},{1,0},{2,1},{3,2},{4,7},{5,4},{6,5},{7,6},{8,11},{9,8},{10,9... | collective-permute-start | bytes 589832 | tf_op jit(solution)/shard_map/ppermute | solution.py:960
  56.4 22.7 %collective-permute-start.6 = (bf16[128,768]{1,0:T(8,128)(2,1)S(1)}, bf16[128,768]{1,0:T(8,128)(2,1)S(1)}, u32[]{:S(2)}, u32[]{:S(2)}) collective-permute-start(bf16[128,768]{1,0:T(8,128)(2,1)S(1)} %get-tuple-element.54), channel_id=1, source_target_pairs={{0,2},{1,3},{2,0},{3,1},{4,6},{5,7},{6,4},{7,5},{8,10},{9,11},{10,... | collective-permute-start | bytes 589832 | tf_op jit(solution)/shard_map/ppermute | solution.py:960
  56.6 22.5 %copy-start.8 = (f32[32,256]{1,0:T(8,128)S(1)}, f32[32,256]{1,0:T(8,128)}, u32[]{:S(2)}) copy-start(f32[32,256]{1,0:T(8,128)} %constant.36.clone.refs_10_) | copy-start | bytes 98308
  77.0 13.9 %collective-permute-start.11 = (bf16[136,768]{1,0:T(8,128)(2,1)S(1)}, bf16[136,768]{1,0:T(8,128)(2,1)S(1)}, u32[]{:S(2)}, u32[]{:S(2)}) collective-permute-start(bf16[136,768]{1,0:T(8,128)(2,1)S(1)} %get-tuple-element.64.refs_1_), channel_id=1, source_target_pairs={{0,3},{1,0},{2,1},{3,2},{4,7},{5,4},{6,5},{7,6},{8,11},{9,8},{10,9... | collective-permute-start | bytes 626696 | tf_op jit(solution)/shard_map/ppermute | solution.py:960
  77.6 13.3 %collective-permute-start.12 = (bf16[136,768]{1,0:T(8,128)(2,1)S(1)}, bf16[136,768]{1,0:T(8,128)(2,1)S(1)}, u32[]{:S(2)}, u32[]{:S(2)}) collective-permute-start(bf16[136,768]{1,0:T(8,128)(2,1)S(1)} %get-tuple-element.65.refs_3_), channel_id=1, source_target_pairs={{0,1},{1,2},{2,3},{3,0},{4,5},{5,6},{6,7},{7,4},{8,9},{9,10},{10,1... | collective-permute-start | bytes 626696 | tf_op jit(solution)/shard_map/ppermute | solution.py:960
  79.1 17.7 %collective-permute-start.13 = (bf16[136,768]{1,0:T(8,128)(2,1)S(1)}, bf16[136,768]{1,0:T(8,128)(2,1)S(1)}, u32[]{:S(2)}, u32[]{:S(2)}) collective-permute-start(bf16[136,768]{1,0:T(8,128)(2,1)S(1)} %get-tuple-element.66.refs_2_), channel_id=1, source_target_pairs={{0,2},{1,3},{2,0},{3,1},{4,6},{5,7},{6,4},{7,5},{8,10},{9,11},{10,... | collective-permute-start | bytes 626696 | tf_op jit(solution)/shard_map/ppermute | solution.py:960
  79.1 17.7 %copy-start.7 = (f32[3072]{0:T(1024)S(1)}, f32[3072]{0:T(1024)}, u32[]{:S(2)}) copy-start(f32[3072]{0:T(1024)} %param.19) | copy-start | bytes 36868
  97.7 5.7 %collective-permute-start.17 = (bf16[128,768]{1,0:T(8,128)(2,1)S(1)}, bf16[128,768]{1,0:T(8,128)(2,1)S(1)}, u32[]{:S(2)}, u32[]{:S(2)}) collective-permute-start(bf16[128,768]{1,0:T(8,128)(2,1)S(1)} %get-tuple-element.85), channel_id=1, source_target_pairs={{28,4},{29,5},{30,6},{31,7}} | collective-permute-start | bytes 589832 | tf_op jit(solution)/shard_map/ppermute | solution.py:939
  98.4 5.7 %collective-permute-start.18 = (bf16[128,768]{1,0:T(8,128)(2,1)S(1)}, bf16[128,768]{1,0:T(8,128)(2,1)S(1)}, u32[]{:S(2)}, u32[]{:S(2)}) collective-permute-start(bf16[128,768]{1,0:T(8,128)(2,1)S(1)} %get-tuple-element.86), channel_id=1, source_target_pairs={{28,12},{29,13},{30,14},{31,15}} | collective-permute-start | bytes 589832 | tf_op jit(solution)/shard_map/ppermute | solution.py:939
  99.1 5.0 %collective-permute-start.19 = (bf16[128,768]{1,0:T(8,128)(2,1)S(1)}, bf16[128,768]{1,0:T(8,128)(2,1)S(1)}, u32[]{:S(2)}, u32[]{:S(2)}) collective-permute-start(bf16[128,768]{1,0:T(8,128)(2,1)S(1)} %get-tuple-element.87), channel_id=1, source_target_pairs={{28,20},{29,21},{30,22},{31,23}} | collective-permute-start | bytes 589832 | tf_op jit(solution)/shard_map/ppermute | solution.py:939
  99.8 20.3 %collective-permute-start.14 = (bf16[232,768]{1,0:T(8,128)(2,1)}, bf16[232,768]{1,0:T(8,128)(2,1)S(1)}, u32[]{:S(2)}, u32[]{:S(2)}) collective-permute-start(bf16[232,768]{1,0:T(8,128)(2,1)} %get-tuple-element.72), channel_id=1, source_target_pairs={{0,3},{1,0},{2,1},{3,2},{4,7},{5,4},{6,5},{7,6},{8,11},{9,8},{10,9... | collective-permute-start | bytes 1069064 | tf_op jit(solution)/shard_map/ppermute | solution.py:960
  103.4 17.0 %collective-permute-start.15 = (bf16[232,768]{1,0:T(8,128)(2,1)}, bf16[232,768]{1,0:T(8,128)(2,1)}, u32[]{:S(2)}, u32[]{:S(2)}) collective-permute-start(bf16[232,768]{1,0:T(8,128)(2,1)} %get-tuple-element.73), channel_id=1, source_target_pairs={{0,1},{1,2},{2,3},{3,0},{4,5},{5,6},{6,7},{7,4},{8,9},{9,10},{10,1... | collective-permute-start | bytes 1069064 | tf_op jit(solution)/shard_map/ppermute | solution.py:960
  103.4 30.3 %collective-permute-start.16 = (bf16[232,768]{1,0:T(8,128)(2,1)}, bf16[232,768]{1,0:T(8,128)(2,1)S(1)}, u32[]{:S(2)}, u32[]{:S(2)}) collective-permute-start(bf16[232,768]{1,0:T(8,128)(2,1)} %get-tuple-element.78), channel_id=1, source_target_pairs={{0,2},{1,3},{2,0},{3,1},{4,6},{5,7},{6,4},{7,5},{8,10},{9,11},{10,... | collective-permute-start | bytes 1069064 | tf_op jit(solution)/shard_map/ppermute | solution.py:960
  104.1 0.7 copy-start.9
  104.8 15.7 %copy-start.1 = (bf16[1,128,3072]{2,1,0:T(8,128)(2,1)S(1)}, bf16[1,128,3072]{2,1,0:T(8,128)(2,1)}, u32[]{:S(2)}) copy-start(bf16[1,128,3072]{2,1,0:T(8,128)(2,1)} %param.13) | copy-start | bytes 2359300
  105.4 3.5 %collective-permute-start.20 = (bf16[64,768]{1,0:T(8,128)(2,1)}, bf16[64,768]{1,0:T(8,128)(2,1)}, u32[]{:S(2)}, u32[]{:S(2)}) collective-permute-start(bf16[64,768]{1,0:T(8,128)(2,1)} %slice.8), channel_id=1, source_target_pairs={{4,0},{12,8},{20,16},{28,24},{5,1},{13,9},{21,17},{29,25},{6,2},{1... | collective-permute-start | bytes 294920 | tf_op jit(solution)/shard_map/ppermute | solution.py:941
  106.7 2.2 %copy-start.10 = (bf16[128,768]{1,0:T(8,128)(2,1)S(1)}, bf16[128,768]{1,0:T(8,128)(2,1)}, u32[]{:S(2)}) copy-start(bf16[128,768]{1,0:T(8,128)(2,1)} %copy-done.9) | copy-start | bytes 589828
  120.5 0.8 copy-start.5

commit v14 on v13

--- a/solution.py
+++ b/solution.py
@@ -734,7 +734,7 @@
     )(meta, *a_slots, *i_slots, gain, offsets)
 
 
-def memory_kernel(parts, width, meta_ref, *refs):
+def memory_kernel(parts, width, sections, meta_ref, *refs):
     out_refs, other_refs = refs[:parts], refs[parts : 2 * parts - 1]
     gain_ref, *share_refs, memory_ref = refs[2 * parts - 1 :]
     wide = memory_ref.shape[1]
@@ -754,18 +754,19 @@
     made = memory_ref[...].astype(F32)
     memory_ref[...] = (made * spread_inverse[:, :1] * gain).astype(BF16)
     for k, share_ref in enumerate(share_refs):
-        size = share_ref.shape[0]
-        share_ref[...] = memory_ref[k * size : (k + 1) * size]
-
-
-def memory_rows(meta, outs, others, gain, width, shares):
+        size = 2 * share_ref.shape[0] // sections
+        for i in range(sections // 2):
+            share_ref[i * size : (i + 1) * size] = memory_ref[(2 * i + k) * size : (2 * i + k + 1) * size]
+
+
+def memory_rows(meta, outs, others, gain, width, sections):
     parts = len(outs)
     rows, wide = outs[0].shape[0] - EXTRA, outs[0].shape[1]
     return pl.pallas_call(
-        functools.partial(memory_kernel, parts, width),
-        out_shape=[jax.ShapeDtypeStruct((rows * parts // shares, wide), BF16)] * shares,
+        functools.partial(memory_kernel, parts, width, sections),
+        out_shape=[jax.ShapeDtypeStruct((rows * parts // 2, wide), BF16)] * 2,
         in_specs=[SMEM_SPEC] + [VMEM_SPEC] * (2 * parts),
-        out_specs=[VMEM_SPEC] * shares,
+        out_specs=[VMEM_SPEC] * 2,
         scratch_shapes=[pltpu.VMEM((rows * parts, wide), BF16)],
         compiler_params=pltpu.CompilerParams(vmem_limit_bytes=VMEM_LIMIT),
         cost_estimate=pl.CostEstimate(flops=rows, bytes_accessed=rows, transcendentals=0),
@@ -851,8 +852,8 @@
 
 
 def late_finish_kernel(parts, meta_ref, *refs):
-    base_ref, row_ref, early_bias_ref, g_ref, x_ref, inverse_ref, gain_ref, early_hbm = refs[:8]
-    out_ref, weight_hbm, bias_ref, weight_ref, sems = refs[8:]
+    base_ref, row_ref, early_bias_ref, g_ref, x_ref, inverse_ref, gain_ref, early_hbm, after_hbm = refs[:9]
+    out_ref, weight_hbm, bias_ref, weight_ref, sems = refs[9:]
     rows, width = x_ref.shape
     wide = width // parts
     heads = wide // HEAD_DIM
@@ -877,7 +878,7 @@
         copy.wait()
 
 
-def heads_finish(meta, g_slots, x, inverse, gain, cotangent, buckets):
+def heads_finish(meta, g_slots, x, inverse, gain, cotangent, after, buckets):
     parts = len(g_slots)
     rows, width = x.shape
     heads = width // HEAD_DIM
@@ -909,14 +910,14 @@
             weight,
             jax.ShapeDtypeStruct((buckets // parts, heads), F32),
         ),
-        in_specs=[SMEM_SPEC] + [VMEM_SPEC] * 7 + [any_spec],
+        in_specs=[SMEM_SPEC] + [VMEM_SPEC] * 7 + [any_spec] * 2,
         out_specs=(VMEM_SPEC, any_spec, VMEM_SPEC),
         input_output_aliases={8: 1},
         scratch_shapes=[pltpu.VMEM(piece, F32), pltpu.SemaphoreType.DMA((3,))],
         compiler_params=params,
         cost_estimate=cost,
         name="late_finish",
-    )(meta, base, row, bias, g_slots[-1], x, inverse, gain, early)
+    )(meta, base, row, bias, g_slots[-1], x, inverse, gain, early, after)
 
 
 def offset_table(rel_bias):
@@ -932,14 +933,16 @@
     return lax.ppermute(value, axis, [(source, source + steps) for source in range(first, last)])
 
 
-def spread_memory(shares, section, sections):
+def spread_memory(even, odd, section, sections):
     last = sections - 1
-    couple = jnp.where(section == last, shares[-1], 0)
-    for s, share in enumerate(shares[:-1]):
-        couple = couple + lax.ppermute(share, "section", [(last, 2 * s + 1)])
-    half = couple.shape[0] // 2
-    even = lax.ppermute(couple[:half], "section", [(s + 1, s) for s in range(0, sections, 2)])
-    return jnp.where(section % 2 == 0, even, couple[half:])
+    share = 2 * even.shape[0] // sections
+    held = jnp.where(section == last - 1, lax.ppermute(even, "section", [(last, last - 1)]), odd)
+    memory = jnp.where(section >= last - 1, held[even.shape[0] - share :], 0)
+    for i in range(sections // 2 - 1):
+        memory = memory + lax.ppermute(
+            held[i * share : (i + 1) * share], "section", [(last, 2 * i + 1), (last - 1, 2 * i)]
+        )
+    return memory
 
 
 def heads_body(
@@ -981,11 +984,11 @@
     g_sends, o_slots = lax.optimization_barrier((g_sends, o_slots))
     g_slots = exchanged(g_sends, -1)
     output = place_columns(meta, o_slots)
-    shares = memory_rows(meta, o_sends, o_slots[1:], final_gain[None], width, sections // 2)
-    memory = spread_memory(shares, section, sections)
+    shares = memory_rows(meta, o_sends, o_slots[1:], final_gain[None], width, sections)
+    memory = spread_memory(*shares, section, sections)
 
     input_grad, weight_grad, bias_grad = heads_finish(
-        meta, g_slots, stash[0], inverse_b, norm_gain, cotangent, buckets
+        meta, g_slots, stash[0], inverse_b, norm_gain, cotangent, memory, buckets
     )
     return (
         output[None],

time: 137 us -> 136 us (level)
  waiting for transfers between devices: 73 us -> 69.2 us
  starting transfers between devices: 26.3 us -> 27.7 us
    ppermute x15, waiting for transfers between devices: 72.2 us -> 69.2 us  [exchanged(): lax.ppermute(sends[r], 'seq', [(i, (i + direction * r) % parts) for i in...]
    select_n x1, other arithmetic: 1.55 us -> 0.04 us  [spread_memory(): jnp.where(section == last - 1, lax.ppermute(even, 'section', [(last, last...]
    ppermute x4, starting transfers between devices: 3.3 us -> 4.69 us  [the longest x3 4 us: spread_memory(): lax.ppermute(held[i * share:(i + 1) * share], 'section', [(last, 2 * i +...]
  transfers between devices with their start and end apart: 21 -> 21, of which waited for: 9 -> 7; matrix products, arithmetic and copies ran while one was open for 2% -> 2% of each run, Pallas kernels for 21% -> 21%
where the time goes in v14:
time: 136 us; the launch traced here: 134 us
  waiting for transfers between devices  69.2 us (51%)
  Pallas kernels  32 us (24%)
  starting transfers between devices  27.7 us (20%)
  local copies, waits for them, and re-layouts  3.15 us (2%)
    ppermute x15, waiting for transfers between devices, exchanged(): lax.ppermute(sends[r], 'seq', [(i, (i + direction * r) % parts) for i in...  69.2 us
    ppermute x15, starting transfers between devices, exchanged(): lax.ppermute(sends[r], 'seq', [(i, (i + direction * r) % parts) for i in...  19.2 us
    pallas_call x1, Pallas kernels, heads_backward(): pl.pallas_call(functools.partial(heads_backward_kernel, parts, rows), out...  11.8 us
    pallas_call x1, Pallas kernels, heads_forward(): pl.pallas_call(functools.partial(heads_forward_kernel, parts, rows), out_...  7.53 us
    ppermute x3, starting transfers between devices, spread_memory(): lax.ppermute(held[i * share:(i + 1) * share], 'section', [(last, 2 * i +...  4 us
    ppermute x2, starting transfers between devices, shifted(): lax.ppermute(value, axis, [(source, source + steps) for source in range(f...  3.83 us
    pallas_call x1, Pallas kernels, pack_stash(): pl.pallas_call(functools.partial(pack_stash_kernel, parts, 4), out_shape=...  2.89 us
  transfers between devices with their start and end apart: 21, of which 7 were waited for; matrix products, arithmetic and copies ran while one was open for 2% of the time, Pallas kernels for 21%

profile of v14, /device:TPU:0, one launch (start us, length us, event | category | flops | bytes accessed | tf_op | source)
XLA Modules:
  0.0 134.4 jit_solution(9425843266367673804)
XLA Ops:
  0.6 0.0 copy-start
  0.7 2.5 %collective-permute-start.7 = (bf16[128,3072]{1,0:T(8,128)(2,1)}, bf16[128,3072]{1,0:T(8,128)(2,1)S(1)}, u32[]{:S(2)}, u32[]{:S(2)}) collective-permute-start(bf16[128,3072]{1,0:T(8,128)(2,1)} %bitcast.25), channel_id=1, source_target_pairs={{0,4},{4,8},{8,12},{12,16},{16,20},{20,24},{24,28},{1,5},{5,9},{9,... | collective-permute-start | bytes 2359304 | tf_op jit(solution)/shard_map/ppermute | solution.py:933
  3.2 1.3 collective-permute-start.3
  4.5 2.9 %pack_stash.1 = (f32[128,128]{1,0:T(8,128)}, bf16[224,768]{1,0:T(8,128)(2,1)}, bf16[224,768]{1,0:T(8,128)(2,1)}, bf16[224,768]{1,0:T(8,128)(2,1)}, bf16[224,768]{1,0:T(8,128)(2,1)}) custom-call(bf16[128,3072]{1,0:T(8,128)(2,1)} %bitcast.18, f32[1,3072]{1,0:T(1,128)} %refs_6_.1, bf16[3,24,32,128]{3,2,1,0:T(8,128)(2,1)} %bitcast.24), custom_call_target="tpu_custom_call" | custom-call | flops 1572864 | bytes 2359296 | tf_op jit(solution)/shard_map/pack_stash/pallas_call | solution.py:426
  7.4 2.5 %collective-permute-start = (bf16[224,768]{1,0:T(8,128)(2,1)}, bf16[224,768]{1,0:T(8,128)(2,1)S(1)}, u32[]{:S(2)}, u32[]{:S(2)}) collective-permute-start(bf16[224,768]{1,0:T(8,128)(2,1)} %get-tuple-element.46), channel_id=1, source_target_pairs={{0,1},{1,2},{2,3},{3,0},{4,5},{5,6},{6,7},{7,4},{8,9},{9,10},{10,1... | collective-permute-start | bytes 1032200 | tf_op jit(solution)/shard_map/ppermute | solution.py:963
  9.9 2.1 %collective-permute-start.1 = (bf16[224,768]{1,0:T(8,128)(2,1)}, bf16[224,768]{1,0:T(8,128)(2,1)}, u32[]{:S(2)}, u32[]{:S(2)}) collective-permute-start(bf16[224,768]{1,0:T(8,128)(2,1)} %get-tuple-element.47), channel_id=1, source_target_pairs={{0,3},{1,0},{2,1},{3,2},{4,7},{5,4},{6,5},{7,6},{8,11},{9,8},{10,9... | collective-permute-start | bytes 1032200 | tf_op jit(solution)/shard_map/ppermute | solution.py:963
  12.0 0.9 collective-permute-start.2
  12.9 0.1 pad_add_fusion.meta_ref
  13.0 0.0 collective-permute-done.7.inner_ref
  13.0 0.9 pack_inbound.1
  13.9 0.0 copy-start.9
  14.0 0.0 copy-start.11
  14.0 1.6 %collective-permute-start.8 = (bf16[136,768]{1,0:T(8,128)(2,1)S(1)}, bf16[136,768]{1,0:T(8,128)(2,1)S(1)}, u32[]{:S(2)}, u32[]{:S(2)}) collective-permute-start(bf16[136,768]{1,0:T(8,128)(2,1)S(1)} %get-tuple-element.54), channel_id=1, source_target_pairs={{0,1},{1,2},{2,3},{3,0},{4,5},{5,6},{6,7},{7,4},{8,9},{9,10},{10,1... | collective-permute-start | bytes 626696 | tf_op jit(solution)/shard_map/ppermute | solution.py:963
  15.6 0.0 collective-permute-done.3.inner_ref
  15.6 2.2 %collective-permute-start.9 = (bf16[136,768]{1,0:T(8,128)(2,1)S(1)}, bf16[136,768]{1,0:T(8,128)(2,1)S(1)}, u32[]{:S(2)}, u32[]{:S(2)}) collective-permute-start(bf16[136,768]{1,0:T(8,128)(2,1)S(1)} %get-tuple-element.55), channel_id=1, source_target_pairs={{0,3},{1,0},{2,1},{3,2},{4,7},{5,4},{6,5},{7,6},{8,11},{9,8},{10,9... | collective-permute-start | bytes 626696 | tf_op jit(solution)/shard_map/ppermute | solution.py:963
  17.9 1.4 %pack_cotangent.1 = (bf16[128,768]{1,0:T(8,128)(2,1)}, bf16[128,768]{1,0:T(8,128)(2,1)S(1)}, bf16[128,768]{1,0:T(8,128)(2,1)S(1)}, bf16[128,768]{1,0:T(8,128)(2,1)S(1)}, bf16[128,3072]{1,0:T(8,128)(2,1)S(1)}) custom-call(s32[3]{0:T(128)S(1)} %pad_add_fusion.meta_ref, bf16[128,3072]{1,0:T(8,128)(2,1)S(1)} %copy-done.3, ...), custom_call_target="tpu_custom_call" | custom-call | flops 1572864 | bytes 2359296 | tf_op jit(solution)/shard_map/pack_cotangent/pallas_call | solution.py:451
  19.3 0.2 collective-permute-done.refs_1_
  19.5 1.2 collective-permute-start.10
  20.7 7.7 %collective-permute-done.1.refs_2_ = bf16[224,768]{1,0:T(8,128)(2,1)} collective-permute-done((bf16[224,768]{1,0:T(8,128)(2,1)}, bf16[224,768]{1,0:T(8,128)(2,1)}, u32[]{:S(2)}, u32[]{:S(2)}) %collective-permute-start.1) | collective-permute-done | bytes 344096 | tf_op jit(solution)/shard_map/ppermute | solution.py:963
  28.4 2.2 %collective-permute-start.4 = (bf16[128,768]{1,0:T(8,128)(2,1)S(1)}, bf16[128,768]{1,0:T(8,128)(2,1)S(1)}, u32[]{:S(2)}, u32[]{:S(2)}) collective-permute-start(bf16[128,768]{1,0:T(8,128)(2,1)S(1)} %get-tuple-element.50), channel_id=1, source_target_pairs={{0,1},{1,2},{2,3},{3,0},{4,5},{5,6},{6,7},{7,4},{8,9},{9,10},{10,1... | collective-permute-start | bytes 589832 | tf_op jit(solution)/shard_map/ppermute | solution.py:963
  30.6 25.8 %collective-permute-done.2.refs_3_ = bf16[224,768]{1,0:T(8,128)(2,1)} collective-permute-done((bf16[224,768]{1,0:T(8,128)(2,1)}, bf16[224,768]{1,0:T(8,128)(2,1)}, u32[]{:S(2)}, u32[]{:S(2)}) %collective-permute-start.2) | collective-permute-done | bytes 344096 | tf_op jit(solution)/shard_map/ppermute | solution.py:963
  56.4 0.0 collective-permute-start.5
  56.4 0.0 collective-permute-done.8.refs_5_
  56.4 0.0 collective-permute-start.6
  56.4 0.2 fusion
  56.6 0.0 copy-start.13
  56.7 0.0 collective-permute-done.9.refs_6_
  56.7 12.7 %collective-permute-done.10.refs_7_ = bf16[136,768]{1,0:T(8,128)(2,1)S(1)} collective-permute-done((bf16[136,768]{1,0:T(8,128)(2,1)S(1)}, bf16[136,768]{1,0:T(8,128)(2,1)S(1)}, u32[]{:S(2)}, u32[]{:S(2)}) %collective-permute-start.10) | collective-permute-done | bytes 208928 | tf_op jit(solution)/shard_map/ppermute | solution.py:963
  69.4 7.5 %heads_forward.1 = (bf16[136,768]{1,0:T(8,128)(2,1)S(1)}, bf16[136,768]{1,0:T(8,128)(2,1)S(1)}, bf16[136,768]{1,0:T(8,128)(2,1)S(1)}, bf16[136,768]{1,0:T(8,128)(2,1)S(1)}) custom-call(s32[3]{0:T(128)S(1)} %pad_add_fusion.meta_ref, bf16[224,768]{1,0:T(8,128)(2,1)S(1)} %copy-done.9, bf16[224,768]{1,0:T(8,128)(2,1)S(1)} %collective-permute-done.refs_1_, ...), custom_call_target="tpu_custom_call" | custom-call | flops 3072 | bytes 512 | tf_op jit(solution)/shard_map/heads_forward/pallas_call | solution.py:706
  77.0 0.6 collective-permute-start.11
  77.6 1.4 %collective-permute-start.12 = (bf16[136,768]{1,0:T(8,128)(2,1)S(1)}, bf16[136,768]{1,0:T(8,128)(2,1)S(1)}, u32[]{:S(2)}, u32[]{:S(2)}) collective-permute-start(bf16[136,768]{1,0:T(8,128)(2,1)S(1)} %get-tuple-element.63.refs_3_), channel_id=1, source_target_pairs={{0,1},{1,2},{2,3},{3,0},{4,5},{5,6},{6,7},{7,4},{8,9},{9,10},{10,1... | collective-permute-start | bytes 626696 | tf_op jit(solution)/shard_map/ppermute | solution.py:963
  79.0 0.0 collective-permute-done.4.refs_5_
  79.1 0.0 collective-permute-start.13
  79.1 0.0 collective-permute-done.5.refs_6_
  79.1 0.0 collective-permute-done.6.refs_7_
  79.1 0.0 copy-start.12
  79.1 11.8 %heads_backward.1 = (bf16[232,768]{1,0:T(8,128)(2,1)S(1)}, bf16[232,768]{1,0:T(8,128)(2,1)}, bf16[232,768]{1,0:T(8,128)(2,1)}, bf16[232,768]{1,0:T(8,128)(2,1)}, f32[1,768]{1,0:T(1,128)}) custom-call(s32[3]{0:T(128)S(1)} %pad_add_fusion.meta_ref, bf16[224,768]{1,0:T(8,128)(2,1)S(1)} %copy-done.9, bf16[224,768]{1,0:T(8,128)(2,1)S(1)} %collective-permute-done.refs_1_, ...), custom_call_target="tpu_custom_call" | custom-call | flops 1228800000 | bytes 393216 | tf_op jit(solution)/shard_map/heads_backward/pallas_call | solution.py:607
  90.9 0.8 copy-done.5
  91.6 0.0 collective-permute-done.11.refs_1_.refs_4_
  91.6 0.0 collective-permute-done.12.refs_2_.refs_5_
  91.6 5.1 %collective-permute-done.13.refs_3_.refs_6_ = bf16[136,768]{1,0:T(8,128)(2,1)S(1)} collective-permute-done((bf16[136,768]{1,0:T(8,128)(2,1)S(1)}, bf16[136,768]{1,0:T(8,128)(2,1)S(1)}, u32[]{:S(2)}, u32[]{:S(2)}) %collective-permute-start.13) | collective-permute-done | bytes 208928 | tf_op jit(solution)/shard_map/ppermute | solution.py:963
  96.7 0.9 memory_rows.1
  97.7 0.7 collective-permute-start.17
  98.4 3.7 %collective-permute-start.14 = (bf16[232,768]{1,0:T(8,128)(2,1)}, bf16[232,768]{1,0:T(8,128)(2,1)S(1)}, u32[]{:S(2)}, u32[]{:S(2)}) collective-permute-start(bf16[232,768]{1,0:T(8,128)(2,1)} %get-tuple-element.70), channel_id=1, source_target_pairs={{0,3},{1,0},{2,1},{3,2},{4,7},{5,4},{6,5},{7,6},{8,11},{9,8},{10,9... | collective-permute-start | bytes 1069064 | tf_op jit(solution)/shard_map/ppermute | solution.py:963
  102.1 0.0 collective-permute-start.15
  102.1 0.6 collective-permute-start.16
  102.8 0.0 copy-start.14
  102.8 0.0 copy-start.1
  102.8 0.7 fusion.5
  103.5 1.3 collective-permute-start.18
  104.8 1.3 collective-permute-start.20
  106.1 11.4 %collective-permute-done.14.refs_1_ = bf16[232,768]{1,0:T(8,128)(2,1)S(1)} collective-permute-done((bf16[232,768]{1,0:T(8,128)(2,1)}, bf16[232,768]{1,0:T(8,128)(2,1)S(1)}, u32[]{:S(2)}, u32[]{:S(2)}) %collective-permute-start.14) | collective-permute-done | bytes 356384 | tf_op jit(solution)/shard_map/ppermute | solution.py:963
  117.5 0.7 copy-done.7
  118.3 1.4 %collective-permute-start.19 = (bf16[64,768]{1,0:T(8,128)(2,1)}, bf16[64,768]{1,0:T(8,128)(2,1)}, u32[]{:S(2)}, u32[]{:S(2)}) collective-permute-start(bf16[64,768]{1,0:T(8,128)(2,1)} %get-tuple-element.86), channel_id=1, source_target_pairs={{28,12},{24,8},{29,13},{25,9},{30,14},{26,10},{31,15},{27,11}} | collective-permute-start | bytes 294920 | tf_op jit(solution)/shard_map/ppermute | solution.py:942
  119.7 1.5 %place_columns.1 = bf16[128,3072]{1,0:T(8,128)(2,1)} custom-call(s32[3]{0:T(128)S(1)} %pad_add_fusion.meta_ref, bf16[136,768]{1,0:T(8,128)(2,1)S(1)} %get-tuple-element.65.refs_11_.refs_0_, bf16[136,768]{1,0:T(8,128)(2,1)S(1)} %collective-permute-done.11.refs_1_.refs_4_, bf16[136,768]{1,0:T(8,128)(2,1)S(1)} %collective-permute-done.12.refs_2_.refs_5_, ...), custom_call_target="tpu_custom_call" | custom-call | bytes 128 | tf_op jit(solution)/shard_map/place_columns/pallas_call | solution.py:788
  121.2 0.0 collective-permute-done.15.refs_2_
  121.2 0.8 copy-done.10
  122.1 2.4 %early_finish.1 = (f32[128,3072]{1,0:T(8,128)S(1)}, f32[128,128]{1,0:T(8,128)S(1)}, f32[3,24,32,128]{3,2,1,0:T(8,128)}, f32[8,128]{1,0:T(8,128)S(1)}) custom-call(s32[3]{0:T(128)S(1)} %pad_add_fusion.meta_ref, bf16[232,768]{1,0:T(8,128)(2,1)S(1)} %copy-done.6, bf16[232,768]{1,0:T(8,128)(2,1)S(1)} %copy-done.8, ...), custom_call_target="tpu_custom_call" | custom-call | flops 393216 | bytes 393216 | tf_op jit(solution)/shard_map/early_finish/pallas_call | solution.py:891
  124.5 0.0 collective-permute-done.20
  124.5 0.0 collective-permute-done.19
  124.5 1.1 fusion.3.refs_8_
  125.6 0.0 copy-start.4
  125.6 6.2 %collective-permute-done.16.refs_3_ = bf16[232,768]{1,0:T(8,128)(2,1)S(1)} collective-permute-done((bf16[232,768]{1,0:T(8,128)(2,1)}, bf16[232,768]{1,0:T(8,128)(2,1)S(1)}, u32[]{:S(2)}, u32[]{:S(2)}) %collective-permute-start.16) | collective-permute-done | bytes 356384 | tf_op jit(solution)/shard_map/ppermute | solution.py:963
  131.8 2.6 %late_finish.1 = (bf16[128,3072]{1,0:T(8,128)(2,1)}, f32[3,24,32,128]{3,2,1,0:T(8,128)}, f32[8,24]{1,0:T(8,128)}) custom-call(s32[3]{0:T(128)S(1)} %pad_add_fusion.meta_ref, f32[128,3072]{1,0:T(8,128)S(1)} %get-tuple-element.73.refs_0_, f32[128,128]{1,0:T(8,128)S(1)} %get-tuple-element.74.refs_1_, ...), custom_call_target="tpu_custom_call", output_to_operand_aliasing={{1}: (8, {})} | custom-call | flops 393216 | bytes 393216 | tf_op jit(solution)/shard_map/late_finish/pallas_call | solution.py:906
  (26 shorter events, 0.1 us)
Async XLA Ops:
  0.6 55.7 %copy-start = (f32[1,32,24]{1,2,0:T(8,128)S(1)}, f32[1,32,24]{1,2,0:T(8,128)}, u32[]{:S(2)}) copy-start(f32[1,32,24]{1,2,0:T(8,128)} %param.17) | copy-start | bytes 9220
  0.6 12.3 %copy-start.2 = (bf16[128,3072]{1,0:T(8,128)(2,1)S(1)}, bf16[128,3072]{1,0:T(8,128)(2,1)}, u32[]{:S(2)}) copy-start(bf16[128,3072]{1,0:T(8,128)(2,1)} %edge_ref.3) | copy-start | bytes 2359300
  0.7 12.3 %collective-permute-start.7 = (bf16[128,3072]{1,0:T(8,128)(2,1)}, bf16[128,3072]{1,0:T(8,128)(2,1)S(1)}, u32[]{:S(2)}, u32[]{:S(2)}) collective-permute-start(bf16[128,3072]{1,0:T(8,128)(2,1)} %bitcast.25), channel_id=1, source_target_pairs={{0,4},{4,8},{8,12},{12,16},{16,20},{20,24},{24,28},{1,5},{5,9},{9,... | collective-permute-start | bytes 2359304 | tf_op jit(solution)/shard_map/ppermute | solution.py:933
  3.2 12.4 %collective-permute-start.3 = (bf16[128,3072]{1,0:T(8,128)(2,1)}, bf16[128,3072]{1,0:T(8,128)(2,1)S(1)}, u32[]{:S(2)}, u32[]{:S(2)}) collective-permute-start(bf16[128,3072]{1,0:T(8,128)(2,1)} %bitcast.26), channel_id=1, source_target_pairs={{4,0},{8,4},{12,8},{16,12},{20,16},{24,20},{28,24},{5,1},{9,5},{13... | collective-permute-start | bytes 2359304 | tf_op jit(solution)/shard_map/ppermute | solution.py:933
  4.5 13.4 %copy-start.3 = (bf16[128,3072]{1,0:T(8,128)(2,1)S(1)}, bf16[128,3072]{1,0:T(8,128)(2,1)}, u32[]{:S(2)}) copy-start(bf16[128,3072]{1,0:T(8,128)(2,1)} %edge_ref.2) | copy-start | bytes 2359300
  7.4 12.1 %collective-permute-start = (bf16[224,768]{1,0:T(8,128)(2,1)}, bf16[224,768]{1,0:T(8,128)(2,1)S(1)}, u32[]{:S(2)}, u32[]{:S(2)}) collective-permute-start(bf16[224,768]{1,0:T(8,128)(2,1)} %get-tuple-element.46), channel_id=1, source_target_pairs={{0,1},{1,2},{2,3},{3,0},{4,5},{5,6},{6,7},{7,4},{8,9},{9,10},{10,1... | collective-permute-start | bytes 1032200 | tf_op jit(solution)/shard_map/ppermute | solution.py:963
  9.9 18.5 %collective-permute-start.1 = (bf16[224,768]{1,0:T(8,128)(2,1)}, bf16[224,768]{1,0:T(8,128)(2,1)}, u32[]{:S(2)}, u32[]{:S(2)}) collective-permute-start(bf16[224,768]{1,0:T(8,128)(2,1)} %get-tuple-element.47), channel_id=1, source_target_pairs={{0,3},{1,0},{2,1},{3,2},{4,7},{5,4},{6,5},{7,6},{8,11},{9,8},{10,9... | collective-permute-start | bytes 1032200 | tf_op jit(solution)/shard_map/ppermute | solution.py:963
  12.0 44.4 %collective-permute-start.2 = (bf16[224,768]{1,0:T(8,128)(2,1)}, bf16[224,768]{1,0:T(8,128)(2,1)}, u32[]{:S(2)}, u32[]{:S(2)}) collective-permute-start(bf16[224,768]{1,0:T(8,128)(2,1)} %get-tuple-element.48), channel_id=1, source_target_pairs={{0,2},{1,3},{2,0},{3,1},{4,6},{5,7},{6,4},{7,5},{8,10},{9,11},{10,... | collective-permute-start | bytes 1032200 | tf_op jit(solution)/shard_map/ppermute | solution.py:963
  13.9 42.4 %copy-start.15 = (f32[256,32]{1,0:T(8,128)S(1)}, f32[256,32]{1,0:T(8,128)}, u32[]{:S(2)}) copy-start(f32[256,32]{1,0:T(8,128)} %constant.25.clone) | copy-start | bytes 98308
  13.9 55.5 %copy-start.9 = (bf16[224,768]{1,0:T(8,128)(2,1)S(1)}, bf16[224,768]{1,0:T(8,128)(2,1)}, u32[]{:S(2)}) copy-start(bf16[224,768]{1,0:T(8,128)(2,1)} %get-tuple-element.45.refs_0_) | copy-start | bytes 1032196
  14.0 55.5 %copy-start.11 = (f32[1,3072]{1,0:T(1,128)S(1)}, f32[1,3072]{1,0:T(1,128)}, u32[]{:S(2)}) copy-start(f32[1,3072]{1,0:T(1,128)} %refs_6_.1) | copy-start | bytes 36868
  14.0 42.4 %collective-permute-start.8 = (bf16[136,768]{1,0:T(8,128)(2,1)S(1)}, bf16[136,768]{1,0:T(8,128)(2,1)S(1)}, u32[]{:S(2)}, u32[]{:S(2)}) collective-permute-start(bf16[136,768]{1,0:T(8,128)(2,1)S(1)} %get-tuple-element.54), channel_id=1, source_target_pairs={{0,1},{1,2},{2,3},{3,0},{4,5},{5,6},{6,7},{7,4},{8,9},{9,10},{10,1... | collective-permute-start | bytes 626696 | tf_op jit(solution)/shard_map/ppermute | solution.py:963
  15.6 41.1 %collective-permute-start.9 = (bf16[136,768]{1,0:T(8,128)(2,1)S(1)}, bf16[136,768]{1,0:T(8,128)(2,1)S(1)}, u32[]{:S(2)}, u32[]{:S(2)}) collective-permute-start(bf16[136,768]{1,0:T(8,128)(2,1)S(1)} %get-tuple-element.55), channel_id=1, source_target_pairs={{0,3},{1,0},{2,1},{3,2},{4,7},{5,4},{6,5},{7,6},{8,11},{9,8},{10,9... | collective-permute-start | bytes 626696 | tf_op jit(solution)/shard_map/ppermute | solution.py:963
  19.5 49.9 %collective-permute-start.10 = (bf16[136,768]{1,0:T(8,128)(2,1)S(1)}, bf16[136,768]{1,0:T(8,128)(2,1)S(1)}, u32[]{:S(2)}, u32[]{:S(2)}) collective-permute-start(bf16[136,768]{1,0:T(8,128)(2,1)S(1)} %get-tuple-element.56), channel_id=1, source_target_pairs={{0,2},{1,3},{2,0},{3,1},{4,6},{5,7},{6,4},{7,5},{8,10},{9,11},{10,... | collective-permute-start | bytes 626696 | tf_op jit(solution)/shard_map/ppermute | solution.py:963
  28.4 50.7 %collective-permute-start.4 = (bf16[128,768]{1,0:T(8,128)(2,1)S(1)}, bf16[128,768]{1,0:T(8,128)(2,1)S(1)}, u32[]{:S(2)}, u32[]{:S(2)}) collective-permute-start(bf16[128,768]{1,0:T(8,128)(2,1)S(1)} %get-tuple-element.50), channel_id=1, source_target_pairs={{0,1},{1,2},{2,3},{3,0},{4,5},{5,6},{6,7},{7,4},{8,9},{9,10},{10,1... | collective-permute-start | bytes 589832 | tf_op jit(solution)/shard_map/ppermute | solution.py:963
  56.4 22.7 %collective-permute-start.5 = (bf16[128,768]{1,0:T(8,128)(2,1)S(1)}, bf16[128,768]{1,0:T(8,128)(2,1)S(1)}, u32[]{:S(2)}, u32[]{:S(2)}) collective-permute-start(bf16[128,768]{1,0:T(8,128)(2,1)S(1)} %get-tuple-element.51), channel_id=1, source_target_pairs={{0,3},{1,0},{2,1},{3,2},{4,7},{5,4},{6,5},{7,6},{8,11},{9,8},{10,9... | collective-permute-start | bytes 589832 | tf_op jit(solution)/shard_map/ppermute | solution.py:963
  56.4 22.7 %collective-permute-start.6 = (bf16[128,768]{1,0:T(8,128)(2,1)S(1)}, bf16[128,768]{1,0:T(8,128)(2,1)S(1)}, u32[]{:S(2)}, u32[]{:S(2)}) collective-permute-start(bf16[128,768]{1,0:T(8,128)(2,1)S(1)} %get-tuple-element.52), channel_id=1, source_target_pairs={{0,2},{1,3},{2,0},{3,1},{4,6},{5,7},{6,4},{7,5},{8,10},{9,11},{10,... | collective-permute-start | bytes 589832 | tf_op jit(solution)/shard_map/ppermute | solution.py:963
  56.6 22.4 %copy-start.13 = (f32[32,256]{1,0:T(8,128)S(1)}, f32[32,256]{1,0:T(8,128)}, u32[]{:S(2)}) copy-start(f32[32,256]{1,0:T(8,128)} %constant.26.clone.refs_10_) | copy-start | bytes 98308
  77.0 14.7 %collective-permute-start.11 = (bf16[136,768]{1,0:T(8,128)(2,1)S(1)}, bf16[136,768]{1,0:T(8,128)(2,1)S(1)}, u32[]{:S(2)}, u32[]{:S(2)}) collective-permute-start(bf16[136,768]{1,0:T(8,128)(2,1)S(1)} %get-tuple-element.62.refs_1_), channel_id=1, source_target_pairs={{0,3},{1,0},{2,1},{3,2},{4,7},{5,4},{6,5},{7,6},{8,11},{9,8},{10,9... | collective-permute-start | bytes 626696 | tf_op jit(solution)/shard_map/ppermute | solution.py:963
  77.6 14.0 %collective-permute-start.12 = (bf16[136,768]{1,0:T(8,128)(2,1)S(1)}, bf16[136,768]{1,0:T(8,128)(2,1)S(1)}, u32[]{:S(2)}, u32[]{:S(2)}) collective-permute-start(bf16[136,768]{1,0:T(8,128)(2,1)S(1)} %get-tuple-element.63.refs_3_), channel_id=1, source_target_pairs={{0,1},{1,2},{2,3},{3,0},{4,5},{5,6},{6,7},{7,4},{8,9},{9,10},{10,1... | collective-permute-start | bytes 626696 | tf_op jit(solution)/shard_map/ppermute | solution.py:963
  79.1 17.7 %collective-permute-start.13 = (bf16[136,768]{1,0:T(8,128)(2,1)S(1)}, bf16[136,768]{1,0:T(8,128)(2,1)S(1)}, u32[]{:S(2)}, u32[]{:S(2)}) collective-permute-start(bf16[136,768]{1,0:T(8,128)(2,1)S(1)} %get-tuple-element.64.refs_2_), channel_id=1, source_target_pairs={{0,2},{1,3},{2,0},{3,1},{4,6},{5,7},{6,4},{7,5},{8,10},{9,11},{10,... | collective-permute-start | bytes 626696 | tf_op jit(solution)/shard_map/ppermute | solution.py:963
  79.1 17.7 %copy-start.12 = (f32[3072]{0:T(1024)S(1)}, f32[3072]{0:T(1024)}, u32[]{:S(2)}) copy-start(f32[3072]{0:T(1024)} %param.19) | copy-start | bytes 36868
  90.9 0.8 copy-start.5
  97.7 5.0 %collective-permute-start.17 = (bf16[256,768]{1,0:T(8,128)(2,1)S(1)}, bf16[256,768]{1,0:T(8,128)(2,1)S(1)}, u32[]{:S(2)}, u32[]{:S(2)}) collective-permute-start(bf16[256,768]{1,0:T(8,128)(2,1)S(1)} %get-tuple-element.78), channel_id=1, source_target_pairs={{28,24},{29,25},{30,26},{31,27}} | collective-permute-start | bytes 1179656 | tf_op jit(solution)/shard_map/ppermute | solution.py:939
  98.4 19.1 %collective-permute-start.14 = (bf16[232,768]{1,0:T(8,128)(2,1)}, bf16[232,768]{1,0:T(8,128)(2,1)S(1)}, u32[]{:S(2)}, u32[]{:S(2)}) collective-permute-start(bf16[232,768]{1,0:T(8,128)(2,1)} %get-tuple-element.70), channel_id=1, source_target_pairs={{0,3},{1,0},{2,1},{3,2},{4,7},{5,4},{6,5},{7,6},{8,11},{9,8},{10,9... | collective-permute-start | bytes 1069064 | tf_op jit(solution)/shard_map/ppermute | solution.py:963
  102.1 19.1 %collective-permute-start.15 = (bf16[232,768]{1,0:T(8,128)(2,1)}, bf16[232,768]{1,0:T(8,128)(2,1)}, u32[]{:S(2)}, u32[]{:S(2)}) collective-permute-start(bf16[232,768]{1,0:T(8,128)(2,1)} %get-tuple-element.71), channel_id=1, source_target_pairs={{0,1},{1,2},{2,3},{3,0},{4,5},{5,6},{6,7},{7,4},{8,9},{9,10},{10,1... | collective-permute-start | bytes 1069064 | tf_op jit(solution)/shard_map/ppermute | solution.py:963
  102.1 29.7 %collective-permute-start.16 = (bf16[232,768]{1,0:T(8,128)(2,1)}, bf16[232,768]{1,0:T(8,128)(2,1)S(1)}, u32[]{:S(2)}, u32[]{:S(2)}) collective-permute-start(bf16[232,768]{1,0:T(8,128)(2,1)} %get-tuple-element.76), channel_id=1, source_target_pairs={{0,2},{1,3},{2,0},{3,1},{4,6},{5,7},{6,4},{7,5},{8,10},{9,11},{10,... | collective-permute-start | bytes 1069064 | tf_op jit(solution)/shard_map/ppermute | solution.py:963
  102.8 14.8 %copy-start.14 = (bf16[256,768]{1,0:T(8,128)(2,1)}, bf16[256,768]{1,0:T(8,128)(2,1)S(1)}, u32[]{:S(2)}) copy-start(bf16[256,768]{1,0:T(8,128)(2,1)S(1)} %broadcast_select_fusion) | copy-start | bytes 1179652
  102.8 18.4 %copy-start.1 = (bf16[1,128,3072]{2,1,0:T(8,128)(2,1)S(1)}, bf16[1,128,3072]{2,1,0:T(8,128)(2,1)}, u32[]{:S(2)}) copy-start(bf16[1,128,3072]{2,1,0:T(8,128)(2,1)} %param.13) | copy-start | bytes 2359300
  102.8 18.4 %copy-start.6 = (bf16[232,768]{1,0:T(8,128)(2,1)S(1)}, bf16[232,768]{1,0:T(8,128)(2,1)}, u32[]{:S(2)}) copy-start(bf16[232,768]{1,0:T(8,128)(2,1)} %copy-done.5) | copy-start | bytes 1069060
  103.5 21.0 %collective-permute-start.18 = (bf16[64,768]{1,0:T(8,128)(2,1)}, bf16[64,768]{1,0:T(8,128)(2,1)}, u32[]{:S(2)}, u32[]{:S(2)}) collective-permute-start(bf16[64,768]{1,0:T(8,128)(2,1)} %get-tuple-element.84), channel_id=1, source_target_pairs={{28,4},{24,0},{29,5},{25,1},{30,6},{26,2},{31,7},{27,3}} | collective-permute-start | bytes 294920 | tf_op jit(solution)/shard_map/ppermute | solution.py:942
  104.8 19.7 %collective-permute-start.20 = (bf16[64,768]{1,0:T(8,128)(2,1)}, bf16[64,768]{1,0:T(8,128)(2,1)}, u32[]{:S(2)}, u32[]{:S(2)}) collective-permute-start(bf16[64,768]{1,0:T(8,128)(2,1)} %get-tuple-element.85), channel_id=1, source_target_pairs={{28,20},{24,16},{29,21},{25,17},{30,22},{26,18},{31,23},{27,19}} | collective-permute-start | bytes 294920 | tf_op jit(solution)/shard_map/ppermute | solution.py:942
  117.5 0.7 copy-start.7
  118.3 2.9 %copy-start.8 = (bf16[232,768]{1,0:T(8,128)(2,1)S(1)}, bf16[232,768]{1,0:T(8,128)(2,1)}, u32[]{:S(2)}) copy-start(bf16[232,768]{1,0:T(8,128)(2,1)} %copy-done.7) | copy-start | bytes 1069060
  118.3 6.2 %collective-permute-start.19 = (bf16[64,768]{1,0:T(8,128)(2,1)}, bf16[64,768]{1,0:T(8,128)(2,1)}, u32[]{:S(2)}, u32[]{:S(2)}) collective-permute-start(bf16[64,768]{1,0:T(8,128)(2,1)} %get-tuple-element.86), channel_id=1, source_target_pairs={{28,12},{24,8},{29,13},{25,9},{30,14},{26,10},{31,15},{27,11}} | collective-permute-start | bytes 294920 | tf_op jit(solution)/shard_map/ppermute | solution.py:942
  121.2 0.8 copy-start.10
  125.6 8.8 %copy-start.4 = (bf16[64,768]{1,0:T(8,128)(2,1)}, bf16[64,768]{1,0:T(8,128)(2,1)S(1)}, u32[]{:S(2)}) copy-start(bf16[64,768]{1,0:T(8,128)(2,1)S(1)} %fusion.3.refs_8_) | copy-start | bytes 294916

commit v15 on v14

--- a/solution.py
+++ b/solution.py
@@ -17,7 +17,7 @@
 masked_score = -1e30
 F32 = jnp.float32
 BF16 = jnp.bfloat16
-VMEM_LIMIT = 24 * 1024 * 1024
+VMEM_LIMIT = 14 * 1024 * 1024
 EXTRA = 8
 
 

time: 136 us -> 136 us (level)
  no operation moved by 1% of the time
where the time goes in v15:
time: 136 us; the launch traced here: 134 us
  waiting for transfers between devices  69.2 us (51%)
  Pallas kernels  32 us (24%)
  starting transfers between devices  27.7 us (20%)
  local copies, waits for them, and re-layouts  3.15 us (2%)
    ppermute x15, waiting for transfers between devices, exchanged(): lax.ppermute(sends[r], 'seq', [(i, (i + direction * r) % parts) for i in...  69.2 us
    ppermute x15, starting transfers between devices, exchanged(): lax.ppermute(sends[r], 'seq', [(i, (i + direction * r) % parts) for i in...  19.2 us
    pallas_call x1, Pallas kernels, heads_backward(): pl.pallas_call(functools.partial(heads_backward_kernel, parts, rows), out...  11.8 us
    pallas_call x1, Pallas kernels, heads_forward(): pl.pallas_call(functools.partial(heads_forward_kernel, parts, rows), out_...  7.53 us
    ppermute x3, starting transfers between devices, spread_memory(): lax.ppermute(held[i * share:(i + 1) * share], 'section', [(last, 2 * i +...  4 us
    ppermute x2, starting transfers between devices, shifted(): lax.ppermute(value, axis, [(source, source + steps) for source in range(f...  3.83 us
    pallas_call x1, Pallas kernels, pack_stash(): pl.pallas_call(functools.partial(pack_stash_kernel, parts, 4), out_shape=...  2.89 us
  transfers between devices with their start and end apart: 21, of which 7 were waited for; matrix products, arithmetic and copies ran while one was open for 2% of the time, Pallas kernels for 21%

profile of v15, /device:TPU:0, one launch (start us, length us, event | category | flops | bytes accessed | tf_op | source)
XLA Modules:
  0.0 134.4 jit_solution(2682967088451682339)
XLA Ops:
  0.6 0.0 copy-start
  0.7 2.5 %collective-permute-start.7 = (bf16[128,3072]{1,0:T(8,128)(2,1)}, bf16[128,3072]{1,0:T(8,128)(2,1)S(1)}, u32[]{:S(2)}, u32[]{:S(2)}) collective-permute-start(bf16[128,3072]{1,0:T(8,128)(2,1)} %bitcast.25), channel_id=1, source_target_pairs={{0,4},{4,8},{8,12},{12,16},{16,20},{20,24},{24,28},{1,5},{5,9},{9,... | collective-permute-start | bytes 2359304 | tf_op jit(solution)/shard_map/ppermute | solution.py:933
  3.2 1.3 collective-permute-start.3
  4.5 2.9 %pack_stash.1 = (f32[128,128]{1,0:T(8,128)}, bf16[224,768]{1,0:T(8,128)(2,1)}, bf16[224,768]{1,0:T(8,128)(2,1)}, bf16[224,768]{1,0:T(8,128)(2,1)}, bf16[224,768]{1,0:T(8,128)(2,1)}) custom-call(bf16[128,3072]{1,0:T(8,128)(2,1)} %bitcast.18, f32[1,3072]{1,0:T(1,128)} %refs_6_.1, bf16[3,24,32,128]{3,2,1,0:T(8,128)(2,1)} %bitcast.24), custom_call_target="tpu_custom_call" | custom-call | flops 1572864 | bytes 2359296 | tf_op jit(solution)/shard_map/pack_stash/pallas_call | solution.py:426
  7.4 2.5 %collective-permute-start = (bf16[224,768]{1,0:T(8,128)(2,1)}, bf16[224,768]{1,0:T(8,128)(2,1)S(1)}, u32[]{:S(2)}, u32[]{:S(2)}) collective-permute-start(bf16[224,768]{1,0:T(8,128)(2,1)} %get-tuple-element.46), channel_id=1, source_target_pairs={{0,1},{1,2},{2,3},{3,0},{4,5},{5,6},{6,7},{7,4},{8,9},{9,10},{10,1... | collective-permute-start | bytes 1032200 | tf_op jit(solution)/shard_map/ppermute | solution.py:963
  9.9 2.1 %collective-permute-start.1 = (bf16[224,768]{1,0:T(8,128)(2,1)}, bf16[224,768]{1,0:T(8,128)(2,1)}, u32[]{:S(2)}, u32[]{:S(2)}) collective-permute-start(bf16[224,768]{1,0:T(8,128)(2,1)} %get-tuple-element.47), channel_id=1, source_target_pairs={{0,3},{1,0},{2,1},{3,2},{4,7},{5,4},{6,5},{7,6},{8,11},{9,8},{10,9... | collective-permute-start | bytes 1032200 | tf_op jit(solution)/shard_map/ppermute | solution.py:963
  12.0 0.9 collective-permute-start.2
  12.9 0.1 pad_add_fusion.meta_ref
  13.0 0.0 collective-permute-done.7.inner_ref
  13.0 0.9 pack_inbound.1
  13.9 0.0 copy-start.9
  14.0 0.0 copy-start.11
  14.0 1.6 %collective-permute-start.8 = (bf16[136,768]{1,0:T(8,128)(2,1)S(1)}, bf16[136,768]{1,0:T(8,128)(2,1)S(1)}, u32[]{:S(2)}, u32[]{:S(2)}) collective-permute-start(bf16[136,768]{1,0:T(8,128)(2,1)S(1)} %get-tuple-element.54), channel_id=1, source_target_pairs={{0,1},{1,2},{2,3},{3,0},{4,5},{5,6},{6,7},{7,4},{8,9},{9,10},{10,1... | collective-permute-start | bytes 626696 | tf_op jit(solution)/shard_map/ppermute | solution.py:963
  15.6 0.0 collective-permute-done.3.inner_ref
  15.6 2.2 %collective-permute-start.9 = (bf16[136,768]{1,0:T(8,128)(2,1)S(1)}, bf16[136,768]{1,0:T(8,128)(2,1)S(1)}, u32[]{:S(2)}, u32[]{:S(2)}) collective-permute-start(bf16[136,768]{1,0:T(8,128)(2,1)S(1)} %get-tuple-element.55), channel_id=1, source_target_pairs={{0,3},{1,0},{2,1},{3,2},{4,7},{5,4},{6,5},{7,6},{8,11},{9,8},{10,9... | collective-permute-start | bytes 626696 | tf_op jit(solution)/shard_map/ppermute | solution.py:963
  17.9 1.4 %pack_cotangent.1 = (bf16[128,768]{1,0:T(8,128)(2,1)}, bf16[128,768]{1,0:T(8,128)(2,1)S(1)}, bf16[128,768]{1,0:T(8,128)(2,1)S(1)}, bf16[128,768]{1,0:T(8,128)(2,1)S(1)}, bf16[128,3072]{1,0:T(8,128)(2,1)S(1)}) custom-call(s32[3]{0:T(128)S(1)} %pad_add_fusion.meta_ref, bf16[128,3072]{1,0:T(8,128)(2,1)S(1)} %copy-done.3, ...), custom_call_target="tpu_custom_call" | custom-call | flops 1572864 | bytes 2359296 | tf_op jit(solution)/shard_map/pack_cotangent/pallas_call | solution.py:451
  19.3 0.2 collective-permute-done.refs_1_
  19.5 1.2 collective-permute-start.10
  20.7 7.7 %collective-permute-done.1.refs_2_ = bf16[224,768]{1,0:T(8,128)(2,1)} collective-permute-done((bf16[224,768]{1,0:T(8,128)(2,1)}, bf16[224,768]{1,0:T(8,128)(2,1)}, u32[]{:S(2)}, u32[]{:S(2)}) %collective-permute-start.1) | collective-permute-done | bytes 344096 | tf_op jit(solution)/shard_map/ppermute | solution.py:963
  28.4 2.2 %collective-permute-start.4 = (bf16[128,768]{1,0:T(8,128)(2,1)S(1)}, bf16[128,768]{1,0:T(8,128)(2,1)S(1)}, u32[]{:S(2)}, u32[]{:S(2)}) collective-permute-start(bf16[128,768]{1,0:T(8,128)(2,1)S(1)} %get-tuple-element.50), channel_id=1, source_target_pairs={{0,1},{1,2},{2,3},{3,0},{4,5},{5,6},{6,7},{7,4},{8,9},{9,10},{10,1... | collective-permute-start | bytes 589832 | tf_op jit(solution)/shard_map/ppermute | solution.py:963
  30.6 25.8 %collective-permute-done.2.refs_3_ = bf16[224,768]{1,0:T(8,128)(2,1)} collective-permute-done((bf16[224,768]{1,0:T(8,128)(2,1)}, bf16[224,768]{1,0:T(8,128)(2,1)}, u32[]{:S(2)}, u32[]{:S(2)}) %collective-permute-start.2) | collective-permute-done | bytes 344096 | tf_op jit(solution)/shard_map/ppermute | solution.py:963
  56.4 0.0 collective-permute-start.5
  56.4 0.0 collective-permute-done.8.refs_5_
  56.4 0.0 collective-permute-start.6
  56.4 0.2 fusion
  56.6 0.0 copy-start.13
  56.7 0.0 collective-permute-done.9.refs_6_
  56.7 12.7 %collective-permute-done.10.refs_7_ = bf16[136,768]{1,0:T(8,128)(2,1)S(1)} collective-permute-done((bf16[136,768]{1,0:T(8,128)(2,1)S(1)}, bf16[136,768]{1,0:T(8,128)(2,1)S(1)}, u32[]{:S(2)}, u32[]{:S(2)}) %collective-permute-start.10) | collective-permute-done | bytes 208928 | tf_op jit(solution)/shard_map/ppermute | solution.py:963
  69.4 7.5 %heads_forward.1 = (bf16[136,768]{1,0:T(8,128)(2,1)S(1)}, bf16[136,768]{1,0:T(8,128)(2,1)S(1)}, bf16[136,768]{1,0:T(8,128)(2,1)S(1)}, bf16[136,768]{1,0:T(8,128)(2,1)S(1)}) custom-call(s32[3]{0:T(128)S(1)} %pad_add_fusion.meta_ref, bf16[224,768]{1,0:T(8,128)(2,1)S(1)} %copy-done.9, bf16[224,768]{1,0:T(8,128)(2,1)S(1)} %collective-permute-done.refs_1_, ...), custom_call_target="tpu_custom_call" | custom-call | flops 3072 | bytes 512 | tf_op jit(solution)/shard_map/heads_forward/pallas_call | solution.py:706
  77.0 0.6 collective-permute-start.11
  77.6 1.4 %collective-permute-start.12 = (bf16[136,768]{1,0:T(8,128)(2,1)S(1)}, bf16[136,768]{1,0:T(8,128)(2,1)S(1)}, u32[]{:S(2)}, u32[]{:S(2)}) collective-permute-start(bf16[136,768]{1,0:T(8,128)(2,1)S(1)} %get-tuple-element.63.refs_3_), channel_id=1, source_target_pairs={{0,1},{1,2},{2,3},{3,0},{4,5},{5,6},{6,7},{7,4},{8,9},{9,10},{10,1... | collective-permute-start | bytes 626696 | tf_op jit(solution)/shard_map/ppermute | solution.py:963
  79.0 0.0 collective-permute-done.4.refs_5_
  79.1 0.0 collective-permute-start.13
  79.1 0.0 collective-permute-done.5.refs_6_
  79.1 0.0 collective-permute-done.6.refs_7_
  79.1 0.0 copy-start.12
  79.1 11.8 %heads_backward.1 = (bf16[232,768]{1,0:T(8,128)(2,1)S(1)}, bf16[232,768]{1,0:T(8,128)(2,1)}, bf16[232,768]{1,0:T(8,128)(2,1)}, bf16[232,768]{1,0:T(8,128)(2,1)}, f32[1,768]{1,0:T(1,128)}) custom-call(s32[3]{0:T(128)S(1)} %pad_add_fusion.meta_ref, bf16[224,768]{1,0:T(8,128)(2,1)S(1)} %copy-done.9, bf16[224,768]{1,0:T(8,128)(2,1)S(1)} %collective-permute-done.refs_1_, ...), custom_call_target="tpu_custom_call" | custom-call | flops 1228800000 | bytes 393216 | tf_op jit(solution)/shard_map/heads_backward/pallas_call | solution.py:607
  90.9 0.8 copy-done.5
  91.6 0.0 collective-permute-done.11.refs_1_.refs_4_
  91.6 0.0 collective-permute-done.12.refs_2_.refs_5_
  91.6 5.1 %collective-permute-done.13.refs_3_.refs_6_ = bf16[136,768]{1,0:T(8,128)(2,1)S(1)} collective-permute-done((bf16[136,768]{1,0:T(8,128)(2,1)S(1)}, bf16[136,768]{1,0:T(8,128)(2,1)S(1)}, u32[]{:S(2)}, u32[]{:S(2)}) %collective-permute-start.13) | collective-permute-done | bytes 208928 | tf_op jit(solution)/shard_map/ppermute | solution.py:963
  96.7 0.9 memory_rows.1
  97.7 0.7 collective-permute-start.17
  98.4 3.7 %collective-permute-start.14 = (bf16[232,768]{1,0:T(8,128)(2,1)}, bf16[232,768]{1,0:T(8,128)(2,1)S(1)}, u32[]{:S(2)}, u32[]{:S(2)}) collective-permute-start(bf16[232,768]{1,0:T(8,128)(2,1)} %get-tuple-element.70), channel_id=1, source_target_pairs={{0,3},{1,0},{2,1},{3,2},{4,7},{5,4},{6,5},{7,6},{8,11},{9,8},{10,9... | collective-permute-start | bytes 1069064 | tf_op jit(solution)/shard_map/ppermute | solution.py:963
  102.1 0.0 collective-permute-start.15
  102.1 0.6 collective-permute-start.16
  102.8 0.0 copy-start.14
  102.8 0.0 copy-start.1
  102.8 0.7 fusion.5
  103.5 1.3 collective-permute-start.18
  104.8 1.3 collective-permute-start.20
  106.1 11.4 %collective-permute-done.14.refs_1_ = bf16[232,768]{1,0:T(8,128)(2,1)S(1)} collective-permute-done((bf16[232,768]{1,0:T(8,128)(2,1)}, bf16[232,768]{1,0:T(8,128)(2,1)S(1)}, u32[]{:S(2)}, u32[]{:S(2)}) %collective-permute-start.14) | collective-permute-done | bytes 356384 | tf_op jit(solution)/shard_map/ppermute | solution.py:963
  117.5 0.7 copy-done.7
  118.3 1.4 %collective-permute-start.19 = (bf16[64,768]{1,0:T(8,128)(2,1)}, bf16[64,768]{1,0:T(8,128)(2,1)}, u32[]{:S(2)}, u32[]{:S(2)}) collective-permute-start(bf16[64,768]{1,0:T(8,128)(2,1)} %get-tuple-element.86), channel_id=1, source_target_pairs={{28,12},{24,8},{29,13},{25,9},{30,14},{26,10},{31,15},{27,11}} | collective-permute-start | bytes 294920 | tf_op jit(solution)/shard_map/ppermute | solution.py:942
  119.7 1.5 %place_columns.1 = bf16[128,3072]{1,0:T(8,128)(2,1)} custom-call(s32[3]{0:T(128)S(1)} %pad_add_fusion.meta_ref, bf16[136,768]{1,0:T(8,128)(2,1)S(1)} %get-tuple-element.65.refs_11_.refs_0_, bf16[136,768]{1,0:T(8,128)(2,1)S(1)} %collective-permute-done.11.refs_1_.refs_4_, bf16[136,768]{1,0:T(8,128)(2,1)S(1)} %collective-permute-done.12.refs_2_.refs_5_, ...), custom_call_target="tpu_custom_call" | custom-call | bytes 128 | tf_op jit(solution)/shard_map/place_columns/pallas_call | solution.py:788
  121.2 0.0 collective-permute-done.15.refs_2_
  121.2 0.8 copy-done.10
  122.1 2.4 %early_finish.1 = (f32[128,3072]{1,0:T(8,128)S(1)}, f32[128,128]{1,0:T(8,128)S(1)}, f32[3,24,32,128]{3,2,1,0:T(8,128)}, f32[8,128]{1,0:T(8,128)S(1)}) custom-call(s32[3]{0:T(128)S(1)} %pad_add_fusion.meta_ref, bf16[232,768]{1,0:T(8,128)(2,1)S(1)} %copy-done.6, bf16[232,768]{1,0:T(8,128)(2,1)S(1)} %copy-done.8, ...), custom_call_target="tpu_custom_call" | custom-call | flops 393216 | bytes 393216 | tf_op jit(solution)/shard_map/early_finish/pallas_call | solution.py:891
  124.5 0.0 collective-permute-done.20
  124.5 0.0 collective-permute-done.19
  124.5 1.1 fusion.3.refs_8_
  125.6 0.0 copy-start.4
  125.6 6.2 %collective-permute-done.16.refs_3_ = bf16[232,768]{1,0:T(8,128)(2,1)S(1)} collective-permute-done((bf16[232,768]{1,0:T(8,128)(2,1)}, bf16[232,768]{1,0:T(8,128)(2,1)S(1)}, u32[]{:S(2)}, u32[]{:S(2)}) %collective-permute-start.16) | collective-permute-done | bytes 356384 | tf_op jit(solution)/shard_map/ppermute | solution.py:963
  131.8 2.6 %late_finish.1 = (bf16[128,3072]{1,0:T(8,128)(2,1)}, f32[3,24,32,128]{3,2,1,0:T(8,128)}, f32[8,24]{1,0:T(8,128)}) custom-call(s32[3]{0:T(128)S(1)} %pad_add_fusion.meta_ref, f32[128,3072]{1,0:T(8,128)S(1)} %get-tuple-element.73.refs_0_, f32[128,128]{1,0:T(8,128)S(1)} %get-tuple-element.74.refs_1_, ...), custom_call_target="tpu_custom_call", output_to_operand_aliasing={{1}: (8, {})} | custom-call | flops 393216 | bytes 393216 | tf_op jit(solution)/shard_map/late_finish/pallas_call | solution.py:906
  (26 shorter events, 0.1 us)
Async XLA Ops:
  0.6 55.7 %copy-start = (f32[1,32,24]{1,2,0:T(8,128)S(1)}, f32[1,32,24]{1,2,0:T(8,128)}, u32[]{:S(2)}) copy-start(f32[1,32,24]{1,2,0:T(8,128)} %param.17) | copy-start | bytes 9220
  0.6 12.3 %copy-start.2 = (bf16[128,3072]{1,0:T(8,128)(2,1)S(1)}, bf16[128,3072]{1,0:T(8,128)(2,1)}, u32[]{:S(2)}) copy-start(bf16[128,3072]{1,0:T(8,128)(2,1)} %edge_ref.3) | copy-start | bytes 2359300
  0.7 12.3 %collective-permute-start.7 = (bf16[128,3072]{1,0:T(8,128)(2,1)}, bf16[128,3072]{1,0:T(8,128)(2,1)S(1)}, u32[]{:S(2)}, u32[]{:S(2)}) collective-permute-start(bf16[128,3072]{1,0:T(8,128)(2,1)} %bitcast.25), channel_id=1, source_target_pairs={{0,4},{4,8},{8,12},{12,16},{16,20},{20,24},{24,28},{1,5},{5,9},{9,... | collective-permute-start | bytes 2359304 | tf_op jit(solution)/shard_map/ppermute | solution.py:933
  3.2 12.4 %collective-permute-start.3 = (bf16[128,3072]{1,0:T(8,128)(2,1)}, bf16[128,3072]{1,0:T(8,128)(2,1)S(1)}, u32[]{:S(2)}, u32[]{:S(2)}) collective-permute-start(bf16[128,3072]{1,0:T(8,128)(2,1)} %bitcast.26), channel_id=1, source_target_pairs={{4,0},{8,4},{12,8},{16,12},{20,16},{24,20},{28,24},{5,1},{9,5},{13... | collective-permute-start | bytes 2359304 | tf_op jit(solution)/shard_map/ppermute | solution.py:933
  4.5 13.4 %copy-start.3 = (bf16[128,3072]{1,0:T(8,128)(2,1)S(1)}, bf16[128,3072]{1,0:T(8,128)(2,1)}, u32[]{:S(2)}) copy-start(bf16[128,3072]{1,0:T(8,128)(2,1)} %edge_ref.2) | copy-start | bytes 2359300
  7.4 12.1 %collective-permute-start = (bf16[224,768]{1,0:T(8,128)(2,1)}, bf16[224,768]{1,0:T(8,128)(2,1)S(1)}, u32[]{:S(2)}, u32[]{:S(2)}) collective-permute-start(bf16[224,768]{1,0:T(8,128)(2,1)} %get-tuple-element.46), channel_id=1, source_target_pairs={{0,1},{1,2},{2,3},{3,0},{4,5},{5,6},{6,7},{7,4},{8,9},{9,10},{10,1... | collective-permute-start | bytes 1032200 | tf_op jit(solution)/shard_map/ppermute | solution.py:963
  9.9 18.5 %collective-permute-start.1 = (bf16[224,768]{1,0:T(8,128)(2,1)}, bf16[224,768]{1,0:T(8,128)(2,1)}, u32[]{:S(2)}, u32[]{:S(2)}) collective-permute-start(bf16[224,768]{1,0:T(8,128)(2,1)} %get-tuple-element.47), channel_id=1, source_target_pairs={{0,3},{1,0},{2,1},{3,2},{4,7},{5,4},{6,5},{7,6},{8,11},{9,8},{10,9... | collective-permute-start | bytes 1032200 | tf_op jit(solution)/shard_map/ppermute | solution.py:963
  12.0 44.4 %collective-permute-start.2 = (bf16[224,768]{1,0:T(8,128)(2,1)}, bf16[224,768]{1,0:T(8,128)(2,1)}, u32[]{:S(2)}, u32[]{:S(2)}) collective-permute-start(bf16[224,768]{1,0:T(8,128)(2,1)} %get-tuple-element.48), channel_id=1, source_target_pairs={{0,2},{1,3},{2,0},{3,1},{4,6},{5,7},{6,4},{7,5},{8,10},{9,11},{10,... | collective-permute-start | bytes 1032200 | tf_op jit(solution)/shard_map/ppermute | solution.py:963
  13.9 42.4 %copy-start.15 = (f32[256,32]{1,0:T(8,128)S(1)}, f32[256,32]{1,0:T(8,128)}, u32[]{:S(2)}) copy-start(f32[256,32]{1,0:T(8,128)} %constant.25.clone) | copy-start | bytes 98308
  13.9 55.5 %copy-start.9 = (bf16[224,768]{1,0:T(8,128)(2,1)S(1)}, bf16[224,768]{1,0:T(8,128)(2,1)}, u32[]{:S(2)}) copy-start(bf16[224,768]{1,0:T(8,128)(2,1)} %get-tuple-element.45.refs_0_) | copy-start | bytes 1032196
  14.0 55.5 %copy-start.11 = (f32[1,3072]{1,0:T(1,128)S(1)}, f32[1,3072]{1,0:T(1,128)}, u32[]{:S(2)}) copy-start(f32[1,3072]{1,0:T(1,128)} %refs_6_.1) | copy-start | bytes 36868
  14.0 42.4 %collective-permute-start.8 = (bf16[136,768]{1,0:T(8,128)(2,1)S(1)}, bf16[136,768]{1,0:T(8,128)(2,1)S(1)}, u32[]{:S(2)}, u32[]{:S(2)}) collective-permute-start(bf16[136,768]{1,0:T(8,128)(2,1)S(1)} %get-tuple-element.54), channel_id=1, source_target_pairs={{0,1},{1,2},{2,3},{3,0},{4,5},{5,6},{6,7},{7,4},{8,9},{9,10},{10,1... | collective-permute-start | bytes 626696 | tf_op jit(solution)/shard_map/ppermute | solution.py:963
  15.6 41.1 %collective-permute-start.9 = (bf16[136,768]{1,0:T(8,128)(2,1)S(1)}, bf16[136,768]{1,0:T(8,128)(2,1)S(1)}, u32[]{:S(2)}, u32[]{:S(2)}) collective-permute-start(bf16[136,768]{1,0:T(8,128)(2,1)S(1)} %get-tuple-element.55), channel_id=1, source_target_pairs={{0,3},{1,0},{2,1},{3,2},{4,7},{5,4},{6,5},{7,6},{8,11},{9,8},{10,9... | collective-permute-start | bytes 626696 | tf_op jit(solution)/shard_map/ppermute | solution.py:963
  19.5 49.9 %collective-permute-start.10 = (bf16[136,768]{1,0:T(8,128)(2,1)S(1)}, bf16[136,768]{1,0:T(8,128)(2,1)S(1)}, u32[]{:S(2)}, u32[]{:S(2)}) collective-permute-start(bf16[136,768]{1,0:T(8,128)(2,1)S(1)} %get-tuple-element.56), channel_id=1, source_target_pairs={{0,2},{1,3},{2,0},{3,1},{4,6},{5,7},{6,4},{7,5},{8,10},{9,11},{10,... | collective-permute-start | bytes 626696 | tf_op jit(solution)/shard_map/ppermute | solution.py:963
  28.4 50.7 %collective-permute-start.4 = (bf16[128,768]{1,0:T(8,128)(2,1)S(1)}, bf16[128,768]{1,0:T(8,128)(2,1)S(1)}, u32[]{:S(2)}, u32[]{:S(2)}) collective-permute-start(bf16[128,768]{1,0:T(8,128)(2,1)S(1)} %get-tuple-element.50), channel_id=1, source_target_pairs={{0,1},{1,2},{2,3},{3,0},{4,5},{5,6},{6,7},{7,4},{8,9},{9,10},{10,1... | collective-permute-start | bytes 589832 | tf_op jit(solution)/shard_map/ppermute | solution.py:963
  56.4 22.7 %collective-permute-start.5 = (bf16[128,768]{1,0:T(8,128)(2,1)S(1)}, bf16[128,768]{1,0:T(8,128)(2,1)S(1)}, u32[]{:S(2)}, u32[]{:S(2)}) collective-permute-start(bf16[128,768]{1,0:T(8,128)(2,1)S(1)} %get-tuple-element.51), channel_id=1, source_target_pairs={{0,3},{1,0},{2,1},{3,2},{4,7},{5,4},{6,5},{7,6},{8,11},{9,8},{10,9... | collective-permute-start | bytes 589832 | tf_op jit(solution)/shard_map/ppermute | solution.py:963
  56.4 22.7 %collective-permute-start.6 = (bf16[128,768]{1,0:T(8,128)(2,1)S(1)}, bf16[128,768]{1,0:T(8,128)(2,1)S(1)}, u32[]{:S(2)}, u32[]{:S(2)}) collective-permute-start(bf16[128,768]{1,0:T(8,128)(2,1)S(1)} %get-tuple-element.52), channel_id=1, source_target_pairs={{0,2},{1,3},{2,0},{3,1},{4,6},{5,7},{6,4},{7,5},{8,10},{9,11},{10,... | collective-permute-start | bytes 589832 | tf_op jit(solution)/shard_map/ppermute | solution.py:963
  56.6 22.4 %copy-start.13 = (f32[32,256]{1,0:T(8,128)S(1)}, f32[32,256]{1,0:T(8,128)}, u32[]{:S(2)}) copy-start(f32[32,256]{1,0:T(8,128)} %constant.26.clone.refs_10_) | copy-start | bytes 98308
  77.0 14.7 %collective-permute-start.11 = (bf16[136,768]{1,0:T(8,128)(2,1)S(1)}, bf16[136,768]{1,0:T(8,128)(2,1)S(1)}, u32[]{:S(2)}, u32[]{:S(2)}) collective-permute-start(bf16[136,768]{1,0:T(8,128)(2,1)S(1)} %get-tuple-element.62.refs_1_), channel_id=1, source_target_pairs={{0,3},{1,0},{2,1},{3,2},{4,7},{5,4},{6,5},{7,6},{8,11},{9,8},{10,9... | collective-permute-start | bytes 626696 | tf_op jit(solution)/shard_map/ppermute | solution.py:963
  77.6 14.0 %collective-permute-start.12 = (bf16[136,768]{1,0:T(8,128)(2,1)S(1)}, bf16[136,768]{1,0:T(8,128)(2,1)S(1)}, u32[]{:S(2)}, u32[]{:S(2)}) collective-permute-start(bf16[136,768]{1,0:T(8,128)(2,1)S(1)} %get-tuple-element.63.refs_3_), channel_id=1, source_target_pairs={{0,1},{1,2},{2,3},{3,0},{4,5},{5,6},{6,7},{7,4},{8,9},{9,10},{10,1... | collective-permute-start | bytes 626696 | tf_op jit(solution)/shard_map/ppermute | solution.py:963
  79.1 17.7 %collective-permute-start.13 = (bf16[136,768]{1,0:T(8,128)(2,1)S(1)}, bf16[136,768]{1,0:T(8,128)(2,1)S(1)}, u32[]{:S(2)}, u32[]{:S(2)}) collective-permute-start(bf16[136,768]{1,0:T(8,128)(2,1)S(1)} %get-tuple-element.64.refs_2_), channel_id=1, source_target_pairs={{0,2},{1,3},{2,0},{3,1},{4,6},{5,7},{6,4},{7,5},{8,10},{9,11},{10,... | collective-permute-start | bytes 626696 | tf_op jit(solution)/shard_map/ppermute | solution.py:963
  79.1 17.7 %copy-start.12 = (f32[3072]{0:T(1024)S(1)}, f32[3072]{0:T(1024)}, u32[]{:S(2)}) copy-start(f32[3072]{0:T(1024)} %param.19) | copy-start | bytes 36868
  90.9 0.8 copy-start.5
  97.7 5.0 %collective-permute-start.17 = (bf16[256,768]{1,0:T(8,128)(2,1)S(1)}, bf16[256,768]{1,0:T(8,128)(2,1)S(1)}, u32[]{:S(2)}, u32[]{:S(2)}) collective-permute-start(bf16[256,768]{1,0:T(8,128)(2,1)S(1)} %get-tuple-element.78), channel_id=1, source_target_pairs={{28,24},{29,25},{30,26},{31,27}} | collective-permute-start | bytes 1179656 | tf_op jit(solution)/shard_map/ppermute | solution.py:939
  98.4 19.1 %collective-permute-start.14 = (bf16[232,768]{1,0:T(8,128)(2,1)}, bf16[232,768]{1,0:T(8,128)(2,1)S(1)}, u32[]{:S(2)}, u32[]{:S(2)}) collective-permute-start(bf16[232,768]{1,0:T(8,128)(2,1)} %get-tuple-element.70), channel_id=1, source_target_pairs={{0,3},{1,0},{2,1},{3,2},{4,7},{5,4},{6,5},{7,6},{8,11},{9,8},{10,9... | collective-permute-start | bytes 1069064 | tf_op jit(solution)/shard_map/ppermute | solution.py:963
  102.1 19.1 %collective-permute-start.15 = (bf16[232,768]{1,0:T(8,128)(2,1)}, bf16[232,768]{1,0:T(8,128)(2,1)}, u32[]{:S(2)}, u32[]{:S(2)}) collective-permute-start(bf16[232,768]{1,0:T(8,128)(2,1)} %get-tuple-element.71), channel_id=1, source_target_pairs={{0,1},{1,2},{2,3},{3,0},{4,5},{5,6},{6,7},{7,4},{8,9},{9,10},{10,1... | collective-permute-start | bytes 1069064 | tf_op jit(solution)/shard_map/ppermute | solution.py:963
  102.1 29.7 %collective-permute-start.16 = (bf16[232,768]{1,0:T(8,128)(2,1)}, bf16[232,768]{1,0:T(8,128)(2,1)S(1)}, u32[]{:S(2)}, u32[]{:S(2)}) collective-permute-start(bf16[232,768]{1,0:T(8,128)(2,1)} %get-tuple-element.76), channel_id=1, source_target_pairs={{0,2},{1,3},{2,0},{3,1},{4,6},{5,7},{6,4},{7,5},{8,10},{9,11},{10,... | collective-permute-start | bytes 1069064 | tf_op jit(solution)/shard_map/ppermute | solution.py:963
  102.8 14.8 %copy-start.14 = (bf16[256,768]{1,0:T(8,128)(2,1)}, bf16[256,768]{1,0:T(8,128)(2,1)S(1)}, u32[]{:S(2)}) copy-start(bf16[256,768]{1,0:T(8,128)(2,1)S(1)} %broadcast_select_fusion) | copy-start | bytes 1179652
  102.8 18.4 %copy-start.1 = (bf16[1,128,3072]{2,1,0:T(8,128)(2,1)S(1)}, bf16[1,128,3072]{2,1,0:T(8,128)(2,1)}, u32[]{:S(2)}) copy-start(bf16[1,128,3072]{2,1,0:T(8,128)(2,1)} %param.13) | copy-start | bytes 2359300
  102.8 18.4 %copy-start.6 = (bf16[232,768]{1,0:T(8,128)(2,1)S(1)}, bf16[232,768]{1,0:T(8,128)(2,1)}, u32[]{:S(2)}) copy-start(bf16[232,768]{1,0:T(8,128)(2,1)} %copy-done.5) | copy-start | bytes 1069060
  103.5 21.0 %collective-permute-start.18 = (bf16[64,768]{1,0:T(8,128)(2,1)}, bf16[64,768]{1,0:T(8,128)(2,1)}, u32[]{:S(2)}, u32[]{:S(2)}) collective-permute-start(bf16[64,768]{1,0:T(8,128)(2,1)} %get-tuple-element.84), channel_id=1, source_target_pairs={{28,4},{24,0},{29,5},{25,1},{30,6},{26,2},{31,7},{27,3}} | collective-permute-start | bytes 294920 | tf_op jit(solution)/shard_map/ppermute | solution.py:942
  104.8 19.7 %collective-permute-start.20 = (bf16[64,768]{1,0:T(8,128)(2,1)}, bf16[64,768]{1,0:T(8,128)(2,1)}, u32[]{:S(2)}, u32[]{:S(2)}) collective-permute-start(bf16[64,768]{1,0:T(8,128)(2,1)} %get-tuple-element.85), channel_id=1, source_target_pairs={{28,20},{24,16},{29,21},{25,17},{30,22},{26,18},{31,23},{27,19}} | collective-permute-start | bytes 294920 | tf_op jit(solution)/shard_map/ppermute | solution.py:942
  117.5 0.7 copy-start.7
  118.3 2.9 %copy-start.8 = (bf16[232,768]{1,0:T(8,128)(2,1)S(1)}, bf16[232,768]{1,0:T(8,128)(2,1)}, u32[]{:S(2)}) copy-start(bf16[232,768]{1,0:T(8,128)(2,1)} %copy-done.7) | copy-start | bytes 1069060
  118.3 6.2 %collective-permute-start.19 = (bf16[64,768]{1,0:T(8,128)(2,1)}, bf16[64,768]{1,0:T(8,128)(2,1)}, u32[]{:S(2)}, u32[]{:S(2)}) collective-permute-start(bf16[64,768]{1,0:T(8,128)(2,1)} %get-tuple-element.86), channel_id=1, source_target_pairs={{28,12},{24,8},{29,13},{25,9},{30,14},{26,10},{31,15},{27,11}} | collective-permute-start | bytes 294920 | tf_op jit(solution)/shard_map/ppermute | solution.py:942
  121.2 0.8 copy-start.10
  125.6 8.8 %copy-start.4 = (bf16[64,768]{1,0:T(8,128)(2,1)}, bf16[64,768]{1,0:T(8,128)(2,1)S(1)}, u32[]{:S(2)}) copy-start(bf16[64,768]{1,0:T(8,128)(2,1)S(1)} %fusion.3.refs_8_) | copy-start | bytes 294916
